TPU v7x, 32 devices: a whole 2x2x4 slice. The times are simulated.
32 devices in a mesh: groups: 2 (over x), tm: 8 (over z, y), space: 2 (over core).
Axes of the slice: x: 2, y: 2, z: 4, core: 2. Of those that a mesh axis runs over, the one named last changes fastest.
Arguments:
- video: bfloat16 [32, 16, 64, 1152], P(('groups', 'tm'), 'space'), parts along dimension 0, may hold values from -6 to 6
- w_query: bfloat16 [1152, 1152], replicated, may hold values from -0.1875 to 0.1875
- w_key: bfloat16 [1152, 1152], replicated, may hold values from -0.1875 to 0.1875
- w_value: bfloat16 [1152, 1152], replicated, may hold values from -0.1875 to 0.1875
- w_out: bfloat16 [1152, 1152], replicated, may hold values from -0.1875 to 0.1875
- w_latent: bfloat16 [1152, 128], replicated, may hold values from -0.1875 to 0.1875
- conv_weight: bfloat16 [3, 3, 128, 256], replicated, may hold values from -0.1875 to 0.1875
- conv_bias: float32 [256], replicated, may hold values from -3 to 3
Outputs:
- decoded: bfloat16 [32, 32, 128, 256], P('groups', 'space', 'tm'), parts along dimension 0
There are 2 independent parts, one for each index of `groups`. A program takes and returns all parts, laid end to end along the dimension named above; an argument that names none is the same for every part. Nothing has to cross between parts.
All inputs are finite; a program needn't handle non-finite values.
Results may differ from a plain program's by a relative error of at most 0.008.
Values may be sent and summed in bfloat16 or wider, within the bound.
No kernel may reach another device: no remote copies, remote signals or barrier semaphores. Data moves between devices by JAX's collectives and lax.ppermute only.
A program may use at most 128 MiB of HBM per device.

v0:
```python
import functools

import jax
import jax.numpy as jnp
from jax import lax
from jax.experimental import pallas as pl
from jax.experimental.pallas import tpu as pltpu
from jax.sharding import PartitionSpec as P


HEAD = 128
EPS = 1e-06
BF16 = jnp.bfloat16
F32 = jnp.float32


IN_HBM = pl.BlockSpec(memory_space=pltpu.HBM)
IN_VMEM = pl.BlockSpec(memory_space=pltpu.VMEM)
IN_SMEM = pl.BlockSpec(memory_space=pltpu.SMEM)


def shape(dims, dtype):
    return jax.ShapeDtypeStruct(dims, dtype)


def params(megabytes):
    return pltpu.CompilerParams(vmem_limit_bytes=megabytes << 20)


def in_hbm(x):
    return pltpu.with_memory_space_constraint(x, pltpu.HBM)


def matmul(a, b):
    return jnp.dot(a, b, preferred_element_type=F32)


def features(x):
    return jnp.where(x > 0.0, x + 1.0, jnp.exp(jnp.minimum(x, 0.0)))


def states_kernel(
    frames, first, load, core, video_in, wk_hbm, wv_hbm,
    parts_out, mine_out, theirs_out, *refs,
):
    if load:
        video, wk, wv, key, value, wk_sem, wv_sem, video_sem = refs
    else:
        wk, wv, key, value, wk_sem, wv_sem = refs
        video = video_in
    per = video.shape[0] // frames
    heads = wk.shape[1] // HEAD
    half = HEAD // 2

    def weight_copies(h):
        source = pl.ds(pl.multiple_of((first + h) * HEAD, HEAD), HEAD)
        cols = pl.ds(pl.multiple_of(h * HEAD, HEAD), HEAD)
        return (
            pltpu.make_async_copy(wk_hbm.at[:, source], wk.at[:, cols], wk_sem.at[h]),
            pltpu.make_async_copy(wv_hbm.at[:, source], wv.at[:, cols], wv_sem.at[h]),
        )

    def video_copy(f):
        rows = pl.ds(f * per, per)
        return pltpu.make_async_copy(video_in.at[rows], video.at[rows], video_sem.at[f])

    for c in weight_copies(0):
        c.start()
    if load:
        for f in range(frames):
            video_copy(f).start()
    for h in range(1, heads):
        for c in weight_copies(h):
            c.start()
    if load:
        for f in range(frames):
            video_copy(f).wait()

    def project(h, carry):
        for c in weight_copies(h):
            c.wait()
        cols = pl.ds(pl.multiple_of(h * HEAD, HEAD), HEAD)
        both = jnp.concatenate([wk[:, cols], wv[:, cols]], axis=1)
        for f in range(frames):
            rows = slice(f * per, (f + 1) * per)
            kv = matmul(video[rows, :], both)
            key[h, rows, :] = features(kv[:, :HEAD]).astype(BF16)
            value[h, rows, :] = kv[:, HEAD:].astype(BF16)
        return carry

    lax.fori_loop(0, heads, project, 0)
    low = core[0] == 0
    for h in range(heads):
        total = None
        for f in range(frames):
            rows = slice(f * per, (f + 1) * per)
            state = lax.dot_general(
                key[h, rows, :], value[h, rows, :], (((0,), (0,)), ((), ())),
                preferred_element_type=F32,
            )
            parts_out[f, h] = state.astype(BF16)
            total = state if total is None else total + state
        mine_out[h] = jnp.where(low, total[:half], total[half:])
        theirs_out[h] = jnp.where(low, total[half:], total[:half]).astype(BF16)


def states_call(core, video, wk, wv, frames, first, heads, load):
    tokens, d = video.shape
    width = heads * HEAD
    half = (heads, HEAD // 2, HEAD)
    out_shape = [
        shape((frames, heads, HEAD, HEAD), BF16),
        shape(half, F32),
        shape(half, BF16),
    ]
    scratch = [
        pltpu.VMEM((d, width), BF16),
        pltpu.VMEM((d, width), BF16),
        pltpu.VMEM((heads, tokens, HEAD), BF16),
        pltpu.VMEM((heads, tokens, HEAD), BF16),
        pltpu.SemaphoreType.DMA((heads,)),
        pltpu.SemaphoreType.DMA((heads,)),
    ]
    if load:
        out_shape.append(shape((tokens, d), BF16))
        scratch.append(pltpu.SemaphoreType.DMA((frames,)))
        video = in_hbm(video)
    return pl.pallas_call(
        functools.partial(states_kernel, frames, first, load),
        out_shape=out_shape,
        in_specs=[IN_SMEM, IN_HBM if load else IN_VMEM, IN_HBM, IN_HBM],
        out_specs=[IN_VMEM] * len(out_shape),
        scratch_shapes=scratch,
        name="states",
        compiler_params=params(20),
    )(core, video, in_hbm(wk), in_hbm(wv))


def query_call(video, w, first, width):
    def kernel(video, w, out):
        out[...] = features(matmul(video[...], w[:, first : first + width])).astype(BF16)

    return pl.pallas_call(
        kernel,
        out_shape=shape((video.shape[0], width), BF16),
        in_specs=[IN_VMEM] * 2,
        out_specs=IN_VMEM,
        name="query",
        compiler_params=params(16),
    )(video, w)


def attend(frames, core, query, parts, other_parts, carry, other_carry, used, head_out):
    heads = carry.shape[0]
    per = query.shape[0] // frames
    low = core[0] == 0
    used[...] = jnp.zeros_like(used)
    for h in range(heads):
        mine, theirs = carry[h].astype(F32), other_carry[h].astype(F32)
        running = jnp.concatenate(
            [jnp.where(low, mine, theirs), jnp.where(low, theirs, mine)], axis=0
        )
        at = (h % 2) * HEAD
        for f in range(frames):
            running = running + parts[f, h].astype(F32) + other_parts[f, h].astype(F32)
            used[f, h // 2, at : at + HEAD, at : at + HEAD] = running.astype(BF16)
    for f in range(frames):
        rows = slice(f * per, (f + 1) * per)
        for p in range(pl.cdiv(heads, 2)):
            width = min(2, heads - 2 * p) * HEAD
            first = 2 * p * HEAD
            attended = matmul(
                query[rows, first : first + width], used[f, p, :width, :width]
            )
            for h in range(width // HEAD):
                one = attended[:, h * HEAD : (h + 1) * HEAD]
                scale = lax.rsqrt(jnp.mean(one * one, axis=1, keepdims=True) + EPS)
                at = first + h * HEAD
                head_out[rows, at : at + HEAD] = (one * scale).astype(BF16)


def used_shape(frames, heads):
    return pltpu.VMEM((frames, pl.cdiv(heads, 2), 2 * HEAD, 2 * HEAD), BF16)


def partial_call(core, video, chunk, w_out, frames):
    tokens, d = video.shape
    heads = chunk[3].shape[0]

    def kernel(core, video, query, parts, other_parts, carry, other_carry, w_out, out,
               used, head_out):
        attend(frames, core, query, parts, other_parts, carry, other_carry, used, head_out)
        per = tokens // frames
        for f in range(frames):
            rows = slice(f * per, (f + 1) * per)
            out[rows, :] = video[rows, :].astype(F32) + matmul(
                head_out[rows, :], w_out[: heads * HEAD, :]
            )

    return pl.pallas_call(
        kernel,
        out_shape=shape((tokens, d), F32),
        in_specs=[IN_SMEM] + [IN_VMEM] * 7,
        out_specs=IN_VMEM,
        scratch_shapes=[used_shape(frames, heads), pltpu.VMEM((tokens, heads * HEAD), BF16)],
        name="partial",
        compiler_params=params(20),
    )(core, video, *chunk, w_out)


def latent_kernel(
    frames, columns, tiles, core, partial, query, parts, other_parts, carry, other_carry,
    w_out, w_latent, out, used, head_out, latent,
):
    tokens, d = partial.shape
    per = tokens // frames
    width = head_out.shape[1]
    attend(frames, core, query, parts, other_parts, carry, other_carry, used, head_out)
    for f in range(frames):
        rows = slice(f * per, (f + 1) * per)
        summed = partial[rows, :] + matmul(head_out[rows, :], w_out[d - width :, :])
        scale = lax.rsqrt(jnp.mean(summed * summed, axis=1, keepdims=True) + EPS)
        latent[rows, :] = matmul((summed * scale).astype(BF16), w_latent[...])

    own = columns // tiles
    grid_rows = per // columns
    main = grid_rows * frames * own
    for t in range(tiles):
        for r in range(grid_rows):
            block = [
                latent[pl.ds(f * per + r * columns + t * own, own), :] for f in range(frames)
            ]
            at = r * frames * own
            out[t, at : at + frames * own, :] = jnp.concatenate(block, axis=0).astype(BF16)
        sides = []
        for column in (t * own - 1, (t + 1) * own):
            for f in range(frames):
                if 0 <= column < columns:
                    at = f * per + column
                    sides.append(latent[pl.ds(at, grid_rows, stride=columns), :])
                else:
                    sides.append(jnp.zeros((grid_rows, out.shape[2]), F32))
        out[t, main:, :] = jnp.concatenate(sides, axis=0).astype(BF16)


def latent_call(core, partial, chunk, w_out, w_latent, frames, columns, tiles):
    tokens, _ = partial.shape
    channels = w_latent.shape[1]
    heads = chunk[3].shape[0]
    rows = tokens // columns * (columns // tiles + 2)
    return pl.pallas_call(
        functools.partial(latent_kernel, frames, columns, tiles),
        out_shape=shape((tiles, rows, channels), BF16),
        in_specs=[IN_SMEM] + [IN_VMEM] * 8,
        out_specs=IN_VMEM,
        scratch_shapes=[
            used_shape(frames, heads),
            pltpu.VMEM((tokens, heads * HEAD), BF16),
            pltpu.VMEM((tokens, channels), F32),
        ],
        name="latent",
        compiler_params=params(20),
    )(core, partial, *chunk, w_out, w_latent)


def decode_kernel(
    frames, tiles, grid_rows, own, core, blocks, edge, weight, bias,
    out, left, middle, right, taps, wide,
):
    group = frames * own
    main = grid_rows * group
    column = lax.broadcasted_iota(jnp.int32, (group, 1), 0) % own
    channels = weight.shape[2]

    def place(row, t, body, sides):
        at = slice(t * group, (t + 1) * group)
        first = jnp.concatenate(
            [jnp.broadcast_to(sides[f : f + 1], (own, channels)) for f in range(frames)], axis=0
        )
        last = jnp.concatenate(
            [jnp.broadcast_to(sides[frames + f : frames + f + 1], (own, channels))
             for f in range(frames)], axis=0
        )
        down = pltpu.roll(body, 1, 0)
        up = pltpu.roll(body, group - 1, 0)
        left[row, at, :] = jnp.where(column == 0, first, down).astype(BF16)
        middle[row, at, :] = body.astype(BF16)
        right[row, at, :] = jnp.where(column == own - 1, last, up).astype(BF16)

    for t in range(tiles):
        everything = blocks[t].astype(F32)
        for r in range(grid_rows):
            body = everything[r * group : (r + 1) * group]
            sides = [
                everything[main + s * grid_rows + r : main + s * grid_rows + r + 1]
                for s in range(2 * frames)
            ]
            place(r + 1, t, body, jnp.concatenate(sides, axis=0))
        beside = edge[t].astype(F32)
        for row, present in ((0, core[0] == 1), (grid_rows + 1, core[0] == 0)):
            there = jnp.where(present, beside, 0.0)
            place(row, t, there[:group], there[group:])

    w = weight[...].astype(F32)
    row_sets = (((0,), (1, 2)), ((0, 1), (2,)))
    for a in range(2):
        for b in range(2):
            for i, rows in enumerate(row_sets[a]):
                for j, cols in enumerate(row_sets[b]):
                    tap = sum(w[r, c] for r in rows for c in cols)
                    at = (2 * i + j) * channels
                    taps[2 * a + b, at : at + channels, :] = tap.astype(BF16)

    views = ((left, middle), (middle, right))
    total = tiles * group
    for a in range(2):
        for b in range(2):
            lhs = jnp.concatenate(
                [v[a + i : a + i + grid_rows].reshape(grid_rows * total, channels)
                 for i in range(2) for v in views[b]], axis=1
            )
            mapped = matmul(lhs, taps[2 * a + b]) + bias[...]
            value = 0.5 * mapped * (1.0 + jnp.tanh(0.5 * mapped))
            for n in range(wide.shape[0]):
                wide[n, pl.ds(b, grid_rows * total, stride=2), :] = value[:, n * 128 : (n + 1) * 128]
        for n in range(wide.shape[0]):
            shaped = wide[n].reshape(grid_rows, tiles * frames, 2 * own, 128)
            for r in range(grid_rows):
                out[:, 2 * r + a, :, n * 128 : (n + 1) * 128] = shaped[r].astype(BF16)


def prefix_rounds(total, tiles, here):
    carry = jnp.zeros_like(total)
    step, number = 1, 0
    while step < tiles:
        sent = total.astype(BF16)
        if 2 * step < tiles:
            pairs = [(i, i ^ step) for i in range(tiles)]
            got = lax.ppermute(sent, "tm", pairs).astype(F32)
            carry = carry + jnp.where((here & step) != 0, got, 0.0)
            total = total + got
        else:
            pairs = [(i, i + step) for i in range(step)]
            carry = carry + lax.ppermute(sent, "tm", pairs).astype(F32)
        step *= 2
        number += 1
    return carry.astype(BF16)


SWAP = [(0, 1), (1, 0)]


def body(video, w_query, w_key, w_value, w_out, w_latent, conv_weight, conv_bias):
    frames, grid_rows, columns, d = video.shape
    tiles = lax.axis_size("tm")
    own = columns // tiles
    flat = video.reshape(-1, d)
    core = lax.axis_index("space").astype(jnp.int32).reshape(1)
    here = lax.axis_index("tm")
    heads = d // HEAD
    split = heads // 3 * 2
    chunks = (("a", 0, split), ("b", split, heads - split))

    loaded = flat
    sent = {}
    for name, first, count in chunks:
        made = states_call(
            core, loaded, w_key, w_value, frames, first, count, name == "a"
        )
        parts, mine, theirs = made[:3]
        if name == "a":
            loaded = made[3]
        total = mine + lax.ppermute(theirs, "space", SWAP).astype(F32)
        other_parts = lax.ppermute(parts, "space", SWAP)
        sent[name] = (parts, other_parts, total)

    ready = {}
    for name, first, count in chunks:
        parts, other_parts, total = sent[name]
        query = query_call(loaded, w_query, first * HEAD, count * HEAD)
        carry = prefix_rounds(total, tiles, here)
        other_carry = lax.ppermute(carry, "space", SWAP)
        ready[name] = (query, parts, other_parts, carry, other_carry)

    partial = partial_call(core, loaded, ready["a"], w_out, frames)
    blocks = latent_call(
        core, partial, ready["b"], w_out, w_latent, frames, columns, tiles
    )
    blocks = lax.all_to_all(blocks, "tm", 0, 0, tiled=True)
    return decode(core, blocks, conv_weight, conv_bias, frames, grid_rows, own, tiles)


def decode(core, blocks, conv_weight, conv_bias, frames, grid_rows, own, tiles):
    channels = conv_weight.shape[2]
    width = conv_weight.shape[3]
    group = frames * own
    main = grid_rows * group
    sides = blocks[:, main:].reshape(tiles, 2 * frames, grid_rows, channels)

    def edge(r):
        return jnp.concatenate([blocks[:, r * group : (r + 1) * group], sides[:, :, r]], axis=1)

    mine = jnp.where(core[0] == 0, edge(grid_rows - 1), edge(0))
    beside = lax.ppermute(mine, "space", SWAP)
    total = tiles * group
    return pl.pallas_call(
        functools.partial(decode_kernel, frames, tiles, grid_rows, own),
        out_shape=shape((tiles * frames, 2 * grid_rows, 2 * own, width), BF16),
        in_specs=[IN_SMEM] + [IN_VMEM] * 4,
        out_specs=IN_VMEM,
        scratch_shapes=[pltpu.VMEM((grid_rows + 2, total, channels), BF16)] * 3
        + [
            pltpu.VMEM((4, 4 * channels, width), BF16),
            pltpu.VMEM((width // 128, 2 * grid_rows * total, 128), F32),
        ],
        name="decode",
        compiler_params=params(36),
    )(core, blocks, beside, conv_weight, conv_bias.reshape(1, width))


def solution(mesh):
    assert mesh.shape["space"] == 2
    tiles = mesh.shape["tm"]
    assert tiles & (tiles - 1) == 0
    placed = (P(("groups", "tm"), "space", None, None), P(), P(), P(), P(), P(), P(), P())
    return jax.shard_map(
        body,
        mesh=mesh,
        in_specs=placed,
        out_specs=P("groups", "space", "tm", None),
        check_vma=False,
    )
```

profile of v0, /device:TPU:0, one launch (start us, length us, event | category | flops | bytes accessed | tf_op | source)
XLA Modules:
  0.0 72.6 jit_solution(18339731029960986477)
XLA Ops:
  0.0 8.5 %states.2 = (bf16[2,6,128,128]{3,2,1,0:T(8,128)(2,1)S(1)}, f32[6,64,128]{2,1,0:T(8,128)S(1)}, bf16[6,64,128]{2,1,0:T(8,128)(2,1)S(1)}, bf16[1024,1152]{1,0:T(8,128)(2,1)S(1)}) custom-call(s32[1]{0:T(128)} %bitcast.core, bf16[1024,1152]{1,0:T(8,128)(2,1)} %bitcast.10, bf16[1152,1152]{1,0:T(8,128)(2,1)} %wk_hbm.3, bf16[1152,1152]{1,0:T(8,128)(2,1)} %wv_hbm.3), custom_call_target="tpu_custom_call" | custom-call | tf_op jit(solution)/shard_map/states/pallas_call | solution.py:128
  8.5 0.6 collective-permute-start.1
  9.1 0.1 collective-permute-start
  9.2 4.8 %states.3 = (bf16[2,3,128,128]{3,2,1,0:T(8,128)(2,1)}, f32[3,64,128]{2,1,0:T(8,128)S(1)}, bf16[3,64,128]{2,1,0:T(8,128)(2,1)}) custom-call(s32[1]{0:T(128)} %bitcast.core, bf16[1024,1152]{1,0:T(8,128)(2,1)S(1)} %get-tuple-element.12.video.video_in, bf16[1152,1152]{1,0:T(8,128)(2,1)} %wk_hbm.3, bf16[1152,1152]{1,0:T(8,128)(2,1)} %wv_hbm.3), custom_call_target="tpu_custom_call" | custom-call | tf_op jit(solution)/shard_map/states/pallas_call | solution.py:128
  14.0 0.5 collective-permute-start.6
  14.5 0.1 collective-permute-start.7
  14.5 1.1 %fusion.4 = bf16[6,64,128]{2,1,0:T(8,128)(2,1)S(1)} fusion(f32[6,64,128]{2,1,0:T(8,128)S(1)} %get-tuple-element.14, bf16[6,64,128]{2,1,0:T(8,128)(2,1)} %collective-permute-done.1), kind=kLoop, calls=%fused_computation.9 | loop fusion | flops 147456 | bytes 393216 | tf_op jit(solution)/shard_map/convert_element_type | solution.py:336
  15.6 3.0 %collective-permute-start.2 = (bf16[6,64,128]{2,1,0:T(8,128)(2,1)S(1)}, bf16[6,64,128]{2,1,0:T(8,128)(2,1)S(1)}, u32[]{:S(2)}, u32[]{:S(2)}) collective-permute-start(bf16[6,64,128]{2,1,0:T(8,128)(2,1)S(1)} %fusion.4), channel_id=1, source_target_pairs={{0,2},{2,0},{4,6},{6,4},{8,10},{10,8},{12,14},{14,12},{1,3},{3,1},... | collective-permute-start | bytes 294920 | tf_op jit(solution)/shard_map/ppermute | solution.py:339
  18.6 0.8 %fusion.10 = bf16[3,64,128]{2,1,0:T(8,128)(2,1)S(1)} fusion(f32[3,64,128]{2,1,0:T(8,128)S(1)} %get-tuple-element.17, bf16[3,64,128]{2,1,0:T(8,128)(2,1)} %collective-permute-done.7), kind=kLoop, calls=%fused_computation.20 | loop fusion | flops 73728 | bytes 196608 | tf_op jit(solution)/shard_map/convert_element_type | solution.py:336
  19.4 0.3 collective-permute-start.8
  19.7 2.0 %collective-permute-done.2 = bf16[6,64,128]{2,1,0:T(8,128)(2,1)S(1)} collective-permute-done((bf16[6,64,128]{2,1,0:T(8,128)(2,1)S(1)}, bf16[6,64,128]{2,1,0:T(8,128)(2,1)S(1)}, u32[]{:S(2)}, u32[]{:S(2)}) %collective-permute-start.2) | collective-permute-done | bytes 98336 | tf_op jit(solution)/shard_map/ppermute | solution.py:339
  21.6 0.9 %fusion.9 = bf16[6,64,128]{2,1,0:T(8,128)(2,1)S(1)} fusion(bf16[6,64,128]{2,1,0:T(8,128)(2,1)S(1)} %collective-permute-done.2, f32[6,64,128]{2,1,0:T(8,128)S(1)} %get-tuple-element.14, bf16[6,64,128]{2,1,0:T(8,128)(2,1)} %collective-permute-done.1), kind=kLoop, calls=%fused_computation.19 | loop fusion | flops 245760 | bytes 491520 | tf_op jit(solution)/shard_map/convert_element_type | solution.py:336
  22.6 1.9 %collective-permute-start.3 = (bf16[6,64,128]{2,1,0:T(8,128)(2,1)S(1)}, bf16[6,64,128]{2,1,0:T(8,128)(2,1)S(1)}, u32[]{:S(2)}, u32[]{:S(2)}) collective-permute-start(bf16[6,64,128]{2,1,0:T(8,128)(2,1)S(1)} %fusion.9), channel_id=1, source_target_pairs={{0,4},{2,6},{4,0},{6,2},{8,12},{10,14},{12,8},{14,10},{1,5},{3,7},... | collective-permute-start | bytes 294920 | tf_op jit(solution)/shard_map/ppermute | solution.py:339
  24.4 0.8 %fusion.11 = bf16[3,64,128]{2,1,0:T(8,128)(2,1)S(1)} fusion(bf16[3,64,128]{2,1,0:T(8,128)(2,1)S(1)} %collective-permute-done.8, f32[3,64,128]{2,1,0:T(8,128)S(1)} %get-tuple-element.17, bf16[3,64,128]{2,1,0:T(8,128)(2,1)} %collective-permute-done.7), kind=kLoop, calls=%fused_computation.23 | loop fusion | flops 122880 | bytes 245760 | tf_op jit(solution)/shard_map/convert_element_type | solution.py:336
  25.3 0.8 %collective-permute-start.9 = (bf16[3,64,128]{2,1,0:T(8,128)(2,1)S(1)}, bf16[3,64,128]{2,1,0:T(8,128)(2,1)S(1)}, u32[]{:S(2)}, u32[]{:S(2)}) collective-permute-start(bf16[3,64,128]{2,1,0:T(8,128)(2,1)S(1)} %fusion.11), channel_id=1, source_target_pairs={{0,4},{2,6},{4,0},{6,2},{8,12},{10,14},{12,8},{14,10},{1,5},{3,7},... | collective-permute-start | bytes 147464 | tf_op jit(solution)/shard_map/ppermute | solution.py:339
  26.0 1.6 %collective-permute-done.3 = bf16[6,64,128]{2,1,0:T(8,128)(2,1)S(1)} collective-permute-done((bf16[6,64,128]{2,1,0:T(8,128)(2,1)S(1)}, bf16[6,64,128]{2,1,0:T(8,128)(2,1)S(1)}, u32[]{:S(2)}, u32[]{:S(2)}) %collective-permute-start.3) | collective-permute-done | bytes 98336 | tf_op jit(solution)/shard_map/ppermute | solution.py:339
  27.6 0.9 %fusion.3 = bf16[6,64,128]{2,1,0:T(8,128)(2,1)S(1)} fusion(bf16[6,64,128]{2,1,0:T(8,128)(2,1)S(1)} %collective-permute-done.3, bf16[6,64,128]{2,1,0:T(8,128)(2,1)S(1)} %collective-permute-done.2, f32[6,64,128]{2,1,0:T(8,128)S(1)} %get-tuple-element.14, bf16[6,64,128]{2,1,0:T(8,128)(2,1)} %collective-permute-done.1), kind=kLoop, calls=%fused_computation.7 | loop fusion | flops 344064 | bytes 589824 | tf_op jit(solution)/shard_map/convert_element_type | solution.py:336
  28.6 4.9 %collective-permute-start.4 = (bf16[6,64,128]{2,1,0:T(8,128)(2,1)S(1)}, bf16[6,64,128]{2,1,0:T(8,128)(2,1)S(1)}, u32[]{:S(2)}, u32[]{:S(2)}) collective-permute-start(bf16[6,64,128]{2,1,0:T(8,128)(2,1)S(1)} %fusion.3), channel_id=1, source_target_pairs={{0,8},{2,10},{4,12},{6,14},{1,9},{3,11},{5,13},{7,15},{16,24},{18,... | collective-permute-start | bytes 294920 | tf_op jit(solution)/shard_map/ppermute | solution.py:344
  33.5 0.8 %fusion.8 = bf16[3,64,128]{2,1,0:T(8,128)(2,1)S(1)} fusion(bf16[3,64,128]{2,1,0:T(8,128)(2,1)S(1)} %collective-permute-done.9, bf16[3,64,128]{2,1,0:T(8,128)(2,1)S(1)} %collective-permute-done.8, f32[3,64,128]{2,1,0:T(8,128)S(1)} %get-tuple-element.17, bf16[3,64,128]{2,1,0:T(8,128)(2,1)} %collective-permute-done.7), kind=kLoop, calls=%fused_computation.17 | loop fusion | flops 172032 | bytes 294912 | tf_op jit(solution)/shard_map/convert_element_type | solution.py:336
  34.3 1.3 %collective-permute-start.10 = (bf16[3,64,128]{2,1,0:T(8,128)(2,1)S(1)}, bf16[3,64,128]{2,1,0:T(8,128)(2,1)S(1)}, u32[]{:S(2)}, u32[]{:S(2)}) collective-permute-start(bf16[3,64,128]{2,1,0:T(8,128)(2,1)S(1)} %fusion.8), channel_id=1, source_target_pairs={{0,8},{2,10},{4,12},{6,14},{1,9},{3,11},{5,13},{7,15},{16,24},{18,... | collective-permute-start | bytes 147464 | tf_op jit(solution)/shard_map/ppermute | solution.py:344
  35.7 0.1 collective-permute-start.5
  35.8 1.5 %collective-permute-done.10 = bf16[3,64,128]{2,1,0:T(8,128)(2,1)S(1)} collective-permute-done((bf16[3,64,128]{2,1,0:T(8,128)(2,1)S(1)}, bf16[3,64,128]{2,1,0:T(8,128)(2,1)S(1)}, u32[]{:S(2)}, u32[]{:S(2)}) %collective-permute-start.10) | collective-permute-done | bytes 49184 | tf_op jit(solution)/shard_map/ppermute | solution.py:344
  37.4 0.1 collective-permute-start.11
  37.5 2.4 %query.2 = bf16[1024,768]{1,0:T(8,128)(2,1)S(1)} custom-call(bf16[1024,1152]{1,0:T(8,128)(2,1)S(1)} %get-tuple-element.12.video.video_in, bf16[1152,1152]{1,0:T(8,128)(2,1)S(1)} %copy-done.1), custom_call_target="tpu_custom_call" | custom-call | tf_op jit(solution)/shard_map/query/pallas_call | solution.py:143
  39.8 1.6 %query.3 = bf16[1024,384]{1,0:T(8,128)(2,1)S(1)} custom-call(bf16[1024,1152]{1,0:T(8,128)(2,1)S(1)} %get-tuple-element.12.video.video_in, bf16[1152,1152]{1,0:T(8,128)(2,1)S(1)} %copy-done.1), custom_call_target="tpu_custom_call" | custom-call | tf_op jit(solution)/shard_map/query/pallas_call | solution.py:143
  41.4 0.1 copy-done
  41.6 2.9 %partial.1 = f32[1024,1152]{1,0:T(8,128)S(1)} custom-call(s32[1]{0:T(128)} %bitcast.core, bf16[1024,1152]{1,0:T(8,128)(2,1)S(1)} %get-tuple-element.12.video.video_in, bf16[1024,768]{1,0:T(8,128)(2,1)S(1)} %query.2, bf16[2,6,128,128]{3,2,1,0:T(8,128)(2,1)S(1)} %get-tuple-element.13.parts, bf16[2,6,128,128]{3,2,1,0:T(8,128)(2,1)S(1)} %collective-permute-done.other_parts, ...), custom_call_target="tpu_custom_call" | custom-call | tf_op jit(solution)/shard_map/partial/pallas_call | solution.py:200
  44.5 5.4 %latent.1 = bf16[8,160,128]{2,1,0:T(8,128)(2,1)} custom-call(s32[1]{0:T(128)} %bitcast.core, f32[1024,1152]{1,0:T(8,128)S(1)} %partial.1, bf16[1024,384]{1,0:T(8,128)(2,1)S(1)} %query.3, bf16[2,3,128,128]{3,2,1,0:T(8,128)(2,1)} %get-tuple-element.16.parts, bf16[2,3,128,128]{3,2,1,0:T(8,128)(2,1)} %collective-permute-done.6.other_parts, ...), custom_call_target="tpu_custom_call" | custom-call | tf_op jit(solution)/shard_map/latent/pallas_call | solution.py:251
  49.9 7.0 %all-to-all-start = ((bf16[8,160,128]{2,1,0:T(8,128)(2,1)}), bf16[8,160,128]{2,1,0:T(8,128)(2,1)S(1)}, u32[]{:S(2)}, u32[]{:S(2)}) async-start(bf16[8,160,128]{2,1,0:T(8,128)(2,1)} %latent.1), calls=%async_computation | async-start | bytes 655360 | tf_op jit(solution)/shard_map/all_to_all | solution.py:389
  56.9 10.9 %all-to-all-done.blocks = bf16[8,160,128]{2,1,0:T(8,128)(2,1)S(1)} async-done(((bf16[8,160,128]{2,1,0:T(8,128)(2,1)}), bf16[8,160,128]{2,1,0:T(8,128)(2,1)S(1)}, u32[]{:S(2)}, u32[]{:S(2)}) %all-to-all-start) | async-done | bytes 327712 | tf_op jit(solution)/shard_map/all_to_all | solution.py:389
  68.0 1.2 %collective-permute-done.12.edge = bf16[8,20,128]{2,1,0:T(8,128)(2,1)S(1)} collective-permute-done((bf16[8,20,128]{2,1,0:T(8,128)(2,1)S(1)}, bf16[8,20,128]{2,1,0:T(8,128)(2,1)S(1)}, u32[]{:S(2)}, u32[]{:S(2)}) %collective-permute-start.12) | collective-permute-done | bytes 40992 | tf_op jit(solution)/shard_map/ppermute | solution.py:404
  69.3 3.4 %decode.1 = bf16[16,16,16,256]{3,2,1,0:T(8,128)(2,1)} custom-call(s32[1]{0:T(128)} %bitcast.core, bf16[8,160,128]{2,1,0:T(8,128)(2,1)S(1)} %all-to-all-done.blocks, bf16[8,20,128]{2,1,0:T(8,128)(2,1)S(1)} %collective-permute-done.12.edge, bf16[3,3,128,256]{3,2,1,0:T(8,128)(2,1)S(1)} %copy-done.2, f32[1,256]{1,0:T(1,128)S(1)} %bitcast.9), custom_call_target="tpu_custom_call" | custom-call | tf_op jit(solution)/shard_map/decode/pallas_call | solution.py:406
  (26 shorter events, 0.3 us)
Async XLA Ops:
  8.5 6.0 %collective-permute-start.1 = (bf16[6,64,128]{2,1,0:T(8,128)(2,1)S(1)}, bf16[6,64,128]{2,1,0:T(8,128)(2,1)}, u32[]{:S(2)}, u32[]{:S(2)}) collective-permute-start(bf16[6,64,128]{2,1,0:T(8,128)(2,1)S(1)} %get-tuple-element.15), channel_id=1, source_target_pairs={{0,1},{1,0},{2,3},{3,2},{4,5},{5,4},{6,7},{7,6},{8,9},{9,8},{10,11... | collective-permute-start | bytes 294920 | tf_op jit(solution)/shard_map/ppermute | solution.py:373
  9.1 32.3 %collective-permute-start = (bf16[2,6,128,128]{3,2,1,0:T(8,128)(2,1)S(1)}, bf16[2,6,128,128]{3,2,1,0:T(8,128)(2,1)S(1)}, u32[]{:S(2)}, u32[]{:S(2)}) collective-permute-start(bf16[2,6,128,128]{3,2,1,0:T(8,128)(2,1)S(1)} %get-tuple-element.13.parts), channel_id=1, source_target_pairs={{0,1},{1,0},{2,3},{3,2},{4,5},{5,4},{6,7},{7,6},{8,9},{9,8},{10,11... | collective-permute-start | bytes 1179656 | tf_op jit(solution)/shard_map/ppermute | solution.py:374
  14.0 30.5 %collective-permute-start.6 = (bf16[2,3,128,128]{3,2,1,0:T(8,128)(2,1)}, bf16[2,3,128,128]{3,2,1,0:T(8,128)(2,1)}, u32[]{:S(2)}, u32[]{:S(2)}) collective-permute-start(bf16[2,3,128,128]{3,2,1,0:T(8,128)(2,1)} %get-tuple-element.16.parts), channel_id=1, source_target_pairs={{0,1},{1,0},{2,3},{3,2},{4,5},{5,4},{6,7},{7,6},{8,9},{9,8},{10,11... | collective-permute-start | bytes 589832 | tf_op jit(solution)/shard_map/ppermute | solution.py:374
  14.5 4.2 %collective-permute-start.7 = (bf16[3,64,128]{2,1,0:T(8,128)(2,1)}, bf16[3,64,128]{2,1,0:T(8,128)(2,1)}, u32[]{:S(2)}, u32[]{:S(2)}) collective-permute-start(bf16[3,64,128]{2,1,0:T(8,128)(2,1)} %get-tuple-element.18), channel_id=1, source_target_pairs={{0,1},{1,0},{2,3},{3,2},{4,5},{5,4},{6,7},{7,6},{8,9},{9,8},{10,11... | collective-permute-start | bytes 147464 | tf_op jit(solution)/shard_map/ppermute | solution.py:373
  14.5 22.9 %copy-start.1 = (bf16[1152,1152]{1,0:T(8,128)(2,1)S(1)}, bf16[1152,1152]{1,0:T(8,128)(2,1)}, u32[]{:S(2)}) copy-start(bf16[1152,1152]{1,0:T(8,128)(2,1)} %w.3) | copy-start | bytes 7962628
  15.6 6.0 %collective-permute-start.2 = (bf16[6,64,128]{2,1,0:T(8,128)(2,1)S(1)}, bf16[6,64,128]{2,1,0:T(8,128)(2,1)S(1)}, u32[]{:S(2)}, u32[]{:S(2)}) collective-permute-start(bf16[6,64,128]{2,1,0:T(8,128)(2,1)S(1)} %fusion.4), channel_id=1, source_target_pairs={{0,2},{2,0},{4,6},{6,4},{8,10},{10,8},{12,14},{14,12},{1,3},{3,1},... | collective-permute-start | bytes 294920 | tf_op jit(solution)/shard_map/ppermute | solution.py:339
  19.4 5.0 %collective-permute-start.8 = (bf16[3,64,128]{2,1,0:T(8,128)(2,1)S(1)}, bf16[3,64,128]{2,1,0:T(8,128)(2,1)S(1)}, u32[]{:S(2)}, u32[]{:S(2)}) collective-permute-start(bf16[3,64,128]{2,1,0:T(8,128)(2,1)S(1)} %fusion.10), channel_id=1, source_target_pairs={{0,2},{2,0},{4,6},{6,4},{8,10},{10,8},{12,14},{14,12},{1,3},{3,1},... | collective-permute-start | bytes 147464 | tf_op jit(solution)/shard_map/ppermute | solution.py:339
  22.6 5.1 %collective-permute-start.3 = (bf16[6,64,128]{2,1,0:T(8,128)(2,1)S(1)}, bf16[6,64,128]{2,1,0:T(8,128)(2,1)S(1)}, u32[]{:S(2)}, u32[]{:S(2)}) collective-permute-start(bf16[6,64,128]{2,1,0:T(8,128)(2,1)S(1)} %fusion.9), channel_id=1, source_target_pairs={{0,4},{2,6},{4,0},{6,2},{8,12},{10,14},{12,8},{14,10},{1,5},{3,7},... | collective-permute-start | bytes 294920 | tf_op jit(solution)/shard_map/ppermute | solution.py:339
  25.3 8.2 %collective-permute-start.9 = (bf16[3,64,128]{2,1,0:T(8,128)(2,1)S(1)}, bf16[3,64,128]{2,1,0:T(8,128)(2,1)S(1)}, u32[]{:S(2)}, u32[]{:S(2)}) collective-permute-start(bf16[3,64,128]{2,1,0:T(8,128)(2,1)S(1)} %fusion.11), channel_id=1, source_target_pairs={{0,4},{2,6},{4,0},{6,2},{8,12},{10,14},{12,8},{14,10},{1,5},{3,7},... | collective-permute-start | bytes 147464 | tf_op jit(solution)/shard_map/ppermute | solution.py:339
  28.6 7.1 %collective-permute-start.4 = (bf16[6,64,128]{2,1,0:T(8,128)(2,1)S(1)}, bf16[6,64,128]{2,1,0:T(8,128)(2,1)S(1)}, u32[]{:S(2)}, u32[]{:S(2)}) collective-permute-start(bf16[6,64,128]{2,1,0:T(8,128)(2,1)S(1)} %fusion.3), channel_id=1, source_target_pairs={{0,8},{2,10},{4,12},{6,14},{1,9},{3,11},{5,13},{7,15},{16,24},{18,... | collective-permute-start | bytes 294920 | tf_op jit(solution)/shard_map/ppermute | solution.py:344
  34.3 3.0 %collective-permute-start.10 = (bf16[3,64,128]{2,1,0:T(8,128)(2,1)S(1)}, bf16[3,64,128]{2,1,0:T(8,128)(2,1)S(1)}, u32[]{:S(2)}, u32[]{:S(2)}) collective-permute-start(bf16[3,64,128]{2,1,0:T(8,128)(2,1)S(1)} %fusion.8), channel_id=1, source_target_pairs={{0,8},{2,10},{4,12},{6,14},{1,9},{3,11},{5,13},{7,15},{16,24},{18,... | collective-permute-start | bytes 147464 | tf_op jit(solution)/shard_map/ppermute | solution.py:344
  35.7 5.7 %collective-permute-start.5 = (bf16[6,64,128]{2,1,0:T(8,128)(2,1)S(1)}, bf16[6,64,128]{2,1,0:T(8,128)(2,1)S(1)}, u32[]{:S(2)}, u32[]{:S(2)}) collective-permute-start(bf16[6,64,128]{2,1,0:T(8,128)(2,1)S(1)} %fusion.2.carry), channel_id=1, source_target_pairs={{0,1},{1,0},{2,3},{3,2},{4,5},{5,4},{6,7},{7,6},{8,9},{9,8},{10,11... | collective-permute-start | bytes 294920 | tf_op jit(solution)/shard_map/ppermute | solution.py:382
  37.4 7.2 %collective-permute-start.11 = (bf16[3,64,128]{2,1,0:T(8,128)(2,1)S(1)}, bf16[3,64,128]{2,1,0:T(8,128)(2,1)S(1)}, u32[]{:S(2)}, u32[]{:S(2)}) collective-permute-start(bf16[3,64,128]{2,1,0:T(8,128)(2,1)S(1)} %fusion.7.carry), channel_id=1, source_target_pairs={{0,1},{1,0},{2,3},{3,2},{4,5},{5,4},{6,7},{7,6},{8,9},{9,8},{10,11... | collective-permute-start | bytes 147464 | tf_op jit(solution)/shard_map/ppermute | solution.py:382
  39.8 1.8 %copy-start = (bf16[1152,1152]{1,0:T(8,128)(2,1)S(1)}, bf16[1152,1152]{1,0:T(8,128)(2,1)}, u32[]{:S(2)}) copy-start(bf16[1152,1152]{1,0:T(8,128)(2,1)} %w_out.3) | copy-start | bytes 7962628
  41.4 3.1 %copy-start.3 = (bf16[1152,128]{1,0:T(8,128)(2,1)S(1)}, bf16[1152,128]{1,0:T(8,128)(2,1)}, u32[]{:S(2)}) copy-start(bf16[1152,128]{1,0:T(8,128)(2,1)} %w_latent.1) | copy-start | bytes 884740
  44.5 24.8 %copy-start.2 = (bf16[3,3,128,256]{3,2,1,0:T(8,128)(2,1)S(1)}, bf16[3,3,128,256]{3,2,1,0:T(8,128)(2,1)}, u32[]{:S(2)}) copy-start(bf16[3,3,128,256]{3,2,1,0:T(8,128)(2,1)} %weight.1) | copy-start | bytes 1769476
  44.5 24.8 %copy-start.4 = (f32[256]{0:T(256)S(1)}, f32[256]{0:T(256)}, u32[]{:S(2)}) copy-start(f32[256]{0:T(256)} %param.15) | copy-start | bytes 3076
  49.9 17.9 %all-to-all-start = ((bf16[8,160,128]{2,1,0:T(8,128)(2,1)}), bf16[8,160,128]{2,1,0:T(8,128)(2,1)S(1)}, u32[]{:S(2)}, u32[]{:S(2)}) async-start(bf16[8,160,128]{2,1,0:T(8,128)(2,1)} %latent.1), calls=%async_computation | async-start | bytes 655360 | tf_op jit(solution)/shard_map/all_to_all | solution.py:389
  68.0 1.3 %collective-permute-start.12 = (bf16[8,20,128]{2,1,0:T(8,128)(2,1)S(1)}, bf16[8,20,128]{2,1,0:T(8,128)(2,1)S(1)}, u32[]{:S(2)}, u32[]{:S(2)}) collective-permute-start(bf16[8,20,128]{2,1,0:T(8,128)(2,1)S(1)} %maximum_select_fusion), channel_id=1, source_target_pairs={{0,1},{1,0},{2,3},{3,2},{4,5},{5,4},{6,7},{7,6},{8,9},{9,8},{10,11... | collective-permute-start | bytes 122888 | tf_op jit(solution)/shard_map/ppermute | solution.py:404
where the time goes:
time: 73.2 us; the launch traced here: 72.6 us
  Pallas kernels  28.9 us (39%)
  starting transfers between devices  20.5 us (28%)
  waiting for transfers between devices  17.3 us (24%)
  other arithmetic  5.5 us (8%)
    pallas_call x2, Pallas kernels, states_call(): pl.pallas_call(functools.partial(states_kernel, frames, first, load), out...  13.3 us
    all_to_all x1, waiting for transfers between devices, body(): blocks = lax.all_to_all(blocks, 'tm', 0, 0, tiled=True)  10.9 us
    all_to_all x1, starting transfers between devices, body(): blocks = lax.all_to_all(blocks, 'tm', 0, 0, tiled=True)  7.01 us
    ppermute x2, starting transfers between devices, prefix_rounds(): carry = carry + lax.ppermute(sent, 'tm', pairs).astype(F32)  6.15 us
    ppermute x4, starting transfers between devices, prefix_rounds(): got = lax.ppermute(sent, 'tm', pairs).astype(F32)  5.9 us
    convert_element_type x6, other arithmetic, prefix_rounds(): sent = total.astype(BF16)  5.4 us
    pallas_call x1, Pallas kernels, latent_call(): pl.pallas_call(functools.partial(latent_kernel, frames, columns, tiles),...  5.39 us
    pallas_call x2, Pallas kernels, query_call(): pl.pallas_call(kernel, out_shape=shape((video.shape[0], width), BF16), in...  3.93 us
  transfers between devices with their start and end apart: 14, of which 5 were waited for; matrix products, arithmetic and copies ran while one was open for 8% of the time, Pallas kernels for 16%

commit v1 on v0

--- a/solution.py
+++ b/solution.py
@@ -31,6 +31,10 @@
     return pltpu.with_memory_space_constraint(x, pltpu.HBM)
 
 
+def in_vmem(x):
+    return pltpu.with_memory_space_constraint(x, pltpu.VMEM)
+
+
 def matmul(a, b):
     return jnp.dot(a, b, preferred_element_type=F32)
 
@@ -39,18 +43,18 @@
     return jnp.where(x > 0.0, x + 1.0, jnp.exp(jnp.minimum(x, 0.0)))
 
 
-def states_kernel(
-    frames, first, load, core, video_in, wk_hbm, wv_hbm,
-    parts_out, mine_out, theirs_out, *refs,
-):
-    if load:
-        video, wk, wv, key, value, wk_sem, wv_sem, video_sem = refs
+def states_kernel(frames, first, heads, later, fetched, place, video_in, wk_hbm, wv_hbm, *refs):
+    refs = list(refs)
+    wq_hbm = refs.pop(0) if fetched else None
+    parts_out = refs.pop(0)
+    if fetched:
+        wq_out, key, value, wq_sem = refs
+        video, wk, wv = video_in, wk_hbm, wv_hbm
     else:
-        wk, wv, key, value, wk_sem, wv_sem = refs
-        video = video_in
+        video, wk_out, wv_out, wk, wv, key, value, wk_sem, wv_sem, video_sem, late_sem = refs
     per = video.shape[0] // frames
-    heads = wk.shape[1] // HEAD
-    half = HEAD // 2
+    blocks = 2 * frames
+    rows_of = video.shape[0] // blocks
 
     def weight_copies(h):
         source = pl.ds(pl.multiple_of((first + h) * HEAD, HEAD), HEAD)
@@ -60,38 +64,57 @@
             pltpu.make_async_copy(wv_hbm.at[:, source], wv.at[:, cols], wv_sem.at[h]),
         )
 
-    def video_copy(f):
-        rows = pl.ds(f * per, per)
-        return pltpu.make_async_copy(video_in.at[rows], video.at[rows], video_sem.at[f])
-
-    for c in weight_copies(0):
-        c.start()
-    if load:
+    def video_copy(i):
+        rows = pl.ds(i * rows_of, rows_of)
+        return pltpu.make_async_copy(video_in.at[rows], video.at[rows], video_sem.at[i])
+
+    def project(h, rows, both):
+        kv = matmul(video[rows, :], both)
+        key[h, rows, :] = features(kv[:, :HEAD]).astype(BF16)
+        value[h, rows, :] = kv[:, HEAD:].astype(BF16)
+
+    def weights(h):
+        cols = pl.ds(pl.multiple_of(h * HEAD, HEAD), HEAD)
+        return jnp.concatenate([wk[:, cols], wv[:, cols]], axis=1)
+
+    def one_head(h, carry):
+        if not fetched:
+            for c in weight_copies(h):
+                c.wait()
+        both = weights(h)
         for f in range(frames):
-            video_copy(f).start()
-    for h in range(1, heads):
-        for c in weight_copies(h):
+            project(h, slice(f * per, (f + 1) * per), both)
+        return carry
+
+    if fetched:
+        late = [pltpu.make_async_copy(wq_hbm, wq_out, wq_sem)]
+        late[0].start()
+        lax.fori_loop(0, heads, one_head, 0)
+    else:
+        for c in weight_copies(0):
             c.start()
-    if load:
-        for f in range(frames):
-            video_copy(f).wait()
-
-    def project(h, carry):
-        for c in weight_copies(h):
+        for i in range(blocks):
+            video_copy(i).start()
+        for c in weight_copies(0):
             c.wait()
-        cols = pl.ds(pl.multiple_of(h * HEAD, HEAD), HEAD)
-        both = jnp.concatenate([wk[:, cols], wv[:, cols]], axis=1)
-        for f in range(frames):
-            rows = slice(f * per, (f + 1) * per)
-            kv = matmul(video[rows, :], both)
-            key[h, rows, :] = features(kv[:, :HEAD]).astype(BF16)
-            value[h, rows, :] = kv[:, HEAD:].astype(BF16)
-        return carry
-
-    lax.fori_loop(0, heads, project, 0)
-    low = core[0] == 0
+        both = weights(0)
+        for i in range(blocks):
+            video_copy(i).wait()
+            if i == 0:
+                for h in range(1, heads):
+                    for c in weight_copies(h):
+                        c.start()
+            project(0, slice(i * rows_of, (i + 1) * rows_of), both)
+        source = pl.ds((first + heads) * HEAD, later * HEAD)
+        late = [
+            pltpu.make_async_copy(wk_hbm.at[:, source], wk_out, late_sem.at[0]),
+            pltpu.make_async_copy(wv_hbm.at[:, source], wv_out, late_sem.at[1]),
+        ]
+        for c in late:
+            c.start()
+        lax.fori_loop(1, heads, one_head, 0)
+
     for h in range(heads):
-        total = None
         for f in range(frames):
             rows = slice(f * per, (f + 1) * per)
             state = lax.dot_general(
@@ -99,41 +122,83 @@
                 preferred_element_type=F32,
             )
             parts_out[f, h] = state.astype(BF16)
-            total = state if total is None else total + state
-        mine_out[h] = jnp.where(low, total[:half], total[half:])
-        theirs_out[h] = jnp.where(low, total[half:], total[:half]).astype(BF16)
-
-
-def states_call(core, video, wk, wv, frames, first, heads, load):
+    for c in late:
+        c.wait()
+
+
+def first_states(place, video, wk, wv, frames, heads, later):
     tokens, d = video.shape
     width = heads * HEAD
-    half = (heads, HEAD // 2, HEAD)
-    out_shape = [
-        shape((frames, heads, HEAD, HEAD), BF16),
-        shape(half, F32),
-        shape(half, BF16),
-    ]
-    scratch = [
-        pltpu.VMEM((d, width), BF16),
-        pltpu.VMEM((d, width), BF16),
-        pltpu.VMEM((heads, tokens, HEAD), BF16),
-        pltpu.VMEM((heads, tokens, HEAD), BF16),
-        pltpu.SemaphoreType.DMA((heads,)),
-        pltpu.SemaphoreType.DMA((heads,)),
-    ]
-    if load:
-        out_shape.append(shape((tokens, d), BF16))
-        scratch.append(pltpu.SemaphoreType.DMA((frames,)))
-        video = in_hbm(video)
-    return pl.pallas_call(
-        functools.partial(states_kernel, frames, first, load),
-        out_shape=out_shape,
-        in_specs=[IN_SMEM, IN_HBM if load else IN_VMEM, IN_HBM, IN_HBM],
-        out_specs=[IN_VMEM] * len(out_shape),
-        scratch_shapes=scratch,
+    return pl.pallas_call(
+        functools.partial(states_kernel, frames, 0, heads, later, False),
+        out_shape=[
+            shape((frames, heads, HEAD, HEAD), BF16),
+            shape((tokens, d), BF16),
+            shape((d, later * HEAD), BF16),
+            shape((d, later * HEAD), BF16),
+        ],
+        in_specs=[IN_SMEM] + [IN_HBM] * 3,
+        out_specs=[IN_VMEM] * 4,
+        scratch_shapes=[
+            pltpu.VMEM((d, width), BF16),
+            pltpu.VMEM((d, width), BF16),
+            pltpu.VMEM((heads, tokens, HEAD), BF16),
+            pltpu.VMEM((heads, tokens, HEAD), BF16),
+            pltpu.SemaphoreType.DMA((heads,)),
+            pltpu.SemaphoreType.DMA((heads,)),
+            pltpu.SemaphoreType.DMA((2 * frames,)),
+            pltpu.SemaphoreType.DMA((2,)),
+        ],
         name="states",
         compiler_params=params(20),
-    )(core, video, in_hbm(wk), in_hbm(wv))
+    )(place, in_hbm(video), in_hbm(wk), in_hbm(wv))
+
+
+def second_states(place, video, wk, wv, wq, frames):
+    tokens, _ = video.shape
+    heads = wk.shape[1] // HEAD
+    return pl.pallas_call(
+        functools.partial(states_kernel, frames, 0, heads, 0, True),
+        out_shape=[
+            shape((frames, heads, HEAD, HEAD), BF16),
+            shape(wq.shape, BF16),
+        ],
+        in_specs=[IN_SMEM] + [IN_VMEM] * 3 + [IN_HBM],
+        out_specs=[IN_VMEM] * 2,
+        scratch_shapes=[
+            pltpu.VMEM((heads, tokens, HEAD), BF16),
+            pltpu.VMEM((heads, tokens, HEAD), BF16),
+            pltpu.SemaphoreType.DMA,
+        ],
+        name="states",
+        compiler_params=params(20),
+    )(place, video, wk, wv, in_hbm(wq))
+
+
+def total_call(place, parts, other_parts):
+    frames, heads = parts.shape[:2]
+    half = HEAD // 2
+
+    def kernel(place, parts, other_parts, out, sent):
+        low = place[0] == 0
+        for h in range(heads):
+            total = None
+            for f in range(frames):
+                one = parts[f, h].astype(F32) + other_parts[f, h].astype(F32)
+                total = one if total is None else total + one
+            total = jnp.where(low, total[:half], total[half:])
+            out[h] = total
+            sent[h] = total.astype(BF16)
+
+    dims = (heads, half, HEAD)
+    return pl.pallas_call(
+        kernel,
+        out_shape=[shape(dims, F32), shape(dims, BF16)],
+        in_specs=[IN_SMEM] + [IN_VMEM] * 2,
+        out_specs=[IN_VMEM] * 2,
+        name="total",
+        compiler_params=params(4),
+    )(place, in_vmem(parts), in_vmem(other_parts))
 
 
 def query_call(video, w, first, width):
@@ -150,10 +215,10 @@
     )(video, w)
 
 
-def attend(frames, core, query, parts, other_parts, carry, other_carry, used, head_out):
+def attend(frames, place, query, parts, other_parts, carry, other_carry, used, head_out):
     heads = carry.shape[0]
     per = query.shape[0] // frames
-    low = core[0] == 0
+    low = place[0] == 0
     used[...] = jnp.zeros_like(used)
     for h in range(heads):
         mine, theirs = carry[h].astype(F32), other_carry[h].astype(F32)
@@ -183,13 +248,13 @@
     return pltpu.VMEM((frames, pl.cdiv(heads, 2), 2 * HEAD, 2 * HEAD), BF16)
 
 
-def partial_call(core, video, chunk, w_out, frames):
+def partial_call(place, video, chunk, w_out, frames):
     tokens, d = video.shape
     heads = chunk[3].shape[0]
 
-    def kernel(core, video, query, parts, other_parts, carry, other_carry, w_out, out,
+    def kernel(place, video, query, parts, other_parts, carry, other_carry, w_out, out,
                used, head_out):
-        attend(frames, core, query, parts, other_parts, carry, other_carry, used, head_out)
+        attend(frames, place, query, parts, other_parts, carry, other_carry, used, head_out)
         per = tokens // frames
         for f in range(frames):
             rows = slice(f * per, (f + 1) * per)
@@ -205,17 +270,17 @@
         scratch_shapes=[used_shape(frames, heads), pltpu.VMEM((tokens, heads * HEAD), BF16)],
         name="partial",
         compiler_params=params(20),
-    )(core, video, *chunk, w_out)
+    )(place, video, *chunk, w_out)
 
 
 def latent_kernel(
-    frames, columns, tiles, core, partial, query, parts, other_parts, carry, other_carry,
+    frames, columns, tiles, place, partial, query, parts, other_parts, carry, other_carry,
     w_out, w_latent, out, used, head_out, latent,
 ):
     tokens, d = partial.shape
     per = tokens // frames
     width = head_out.shape[1]
-    attend(frames, core, query, parts, other_parts, carry, other_carry, used, head_out)
+    attend(frames, place, query, parts, other_parts, carry, other_carry, used, head_out)
     for f in range(frames):
         rows = slice(f * per, (f + 1) * per)
         summed = partial[rows, :] + matmul(head_out[rows, :], w_out[d - width :, :])
@@ -243,7 +308,7 @@
         out[t, main:, :] = jnp.concatenate(sides, axis=0).astype(BF16)
 
 
-def latent_call(core, partial, chunk, w_out, w_latent, frames, columns, tiles):
+def latent_call(place, partial, chunk, w_out, w_latent, frames, columns, tiles):
     tokens, _ = partial.shape
     channels = w_latent.shape[1]
     heads = chunk[3].shape[0]
@@ -260,11 +325,11 @@
         ],
         name="latent",
         compiler_params=params(20),
-    )(core, partial, *chunk, w_out, w_latent)
+    )(place, partial, *chunk, w_out, w_latent)
 
 
 def decode_kernel(
-    frames, tiles, grid_rows, own, core, blocks, edge, weight, bias,
+    frames, tiles, grid_rows, own, place, blocks, edge, weight, bias,
     out, left, middle, right, taps, wide,
 ):
     group = frames * own
@@ -272,7 +337,7 @@
     column = lax.broadcasted_iota(jnp.int32, (group, 1), 0) % own
     channels = weight.shape[2]
 
-    def place(row, t, body, sides):
+    def lay(row, t, body, sides):
         at = slice(t * group, (t + 1) * group)
         first = jnp.concatenate(
             [jnp.broadcast_to(sides[f : f + 1], (own, channels)) for f in range(frames)], axis=0
@@ -295,11 +360,11 @@
                 everything[main + s * grid_rows + r : main + s * grid_rows + r + 1]
                 for s in range(2 * frames)
             ]
-            place(r + 1, t, body, jnp.concatenate(sides, axis=0))
+            lay(r + 1, t, body, jnp.concatenate(sides, axis=0))
         beside = edge[t].astype(F32)
-        for row, present in ((0, core[0] == 1), (grid_rows + 1, core[0] == 0)):
+        for row, present in ((0, place[0] == 1), (grid_rows + 1, place[0] == 0)):
             there = jnp.where(present, beside, 0.0)
-            place(row, t, there[:group], there[group:])
+            lay(row, t, there[:group], there[group:])
 
     w = weight[...].astype(F32)
     row_sets = (((0,), (1, 2)), ((0, 1), (2,)))
@@ -329,22 +394,52 @@
                 out[:, 2 * r + a, :, n * 128 : (n + 1) * 128] = shaped[r].astype(BF16)
 
 
-def prefix_rounds(total, tiles, here):
-    carry = jnp.zeros_like(total)
+def round_call(place, step, last, got, total, carry):
+    def kernel(place, got, total, *refs):
+        upper = (place[1] // step) % 2 == 1
+        received = got[...].astype(F32)
+        before = jnp.where(upper, received, 0.0)
+        if carry is not None:
+            before = refs[0][...] + before
+            refs = refs[1:]
+        if last:
+            refs[0][...] = before.astype(BF16)
+        else:
+            carry_out, total_out, sent_out = refs
+            carry_out[...] = before
+            both = total[...] + received
+            total_out[...] = both
+            sent_out[...] = both.astype(BF16)
+
+    near = [got, total] + ([] if carry is None else [carry])
+    kinds = [BF16] if last else [F32, F32, BF16]
+    return pl.pallas_call(
+        kernel,
+        out_shape=[shape(total.shape, kind) for kind in kinds],
+        in_specs=[IN_SMEM] + [IN_VMEM] * len(near),
+        out_specs=[IN_VMEM] * len(kinds),
+        name="round",
+        compiler_params=params(4),
+    )(place, *near)
+
+
+def prefix_rounds(place, total, sent, tiles):
+    carry = None
     step, number = 1, 0
     while step < tiles:
-        sent = total.astype(BF16)
-        if 2 * step < tiles:
+        last = 2 * step >= tiles
+        if last:
+            pairs = [(i, i + step) for i in range(step)]
+        else:
             pairs = [(i, i ^ step) for i in range(tiles)]
-            got = lax.ppermute(sent, "tm", pairs).astype(F32)
-            carry = carry + jnp.where((here & step) != 0, got, 0.0)
-            total = total + got
-        else:
-            pairs = [(i, i + step) for i in range(step)]
-            carry = carry + lax.ppermute(sent, "tm", pairs).astype(F32)
+        got = lax.ppermute(sent, "tm", pairs)
+        out = round_call(place, step, last, got, total, carry)
+        if last:
+            return out[0]
+        carry, total, sent = out
         step *= 2
         number += 1
-    return carry.astype(BF16)
+    return jnp.zeros_like(sent)
 
 
 SWAP = [(0, 1), (1, 0)]
@@ -355,42 +450,31 @@
     tiles = lax.axis_size("tm")
     own = columns // tiles
     flat = video.reshape(-1, d)
-    core = lax.axis_index("space").astype(jnp.int32).reshape(1)
-    here = lax.axis_index("tm")
+    place = jnp.stack([lax.axis_index("space"), lax.axis_index("tm")]).astype(jnp.int32)
     heads = d // HEAD
     split = heads // 3 * 2
-    chunks = (("a", 0, split), ("b", split, heads - split))
-
-    loaded = flat
-    sent = {}
-    for name, first, count in chunks:
-        made = states_call(
-            core, loaded, w_key, w_value, frames, first, count, name == "a"
-        )
-        parts, mine, theirs = made[:3]
-        if name == "a":
-            loaded = made[3]
-        total = mine + lax.ppermute(theirs, "space", SWAP).astype(F32)
-        other_parts = lax.ppermute(parts, "space", SWAP)
-        sent[name] = (parts, other_parts, total)
+    rest = heads - split
+    parts_a, near, wk_b, wv_b = first_states(place, flat, w_key, w_value, frames, split, rest)
+    other_a = lax.ppermute(parts_a, "space", SWAP)
+    parts_b, near_query = second_states(place, near, wk_b, wv_b, w_query, frames)
+    other_b = lax.ppermute(parts_b, "space", SWAP)
 
     ready = {}
-    for name, first, count in chunks:
-        parts, other_parts, total = sent[name]
-        query = query_call(loaded, w_query, first * HEAD, count * HEAD)
-        carry = prefix_rounds(total, tiles, here)
+    for name, first, parts, other in (("a", 0, parts_a, other_a), ("b", split, parts_b, other_b)):
+        count = parts.shape[1]
+        total, sent = total_call(place, parts, other)
+        query = query_call(near, near_query, first * HEAD, count * HEAD)
+        carry = prefix_rounds(place, total, sent, tiles)
         other_carry = lax.ppermute(carry, "space", SWAP)
-        ready[name] = (query, parts, other_parts, carry, other_carry)
-
-    partial = partial_call(core, loaded, ready["a"], w_out, frames)
-    blocks = latent_call(
-        core, partial, ready["b"], w_out, w_latent, frames, columns, tiles
-    )
+        ready[name] = (query, parts, other, carry, other_carry)
+
+    partial = partial_call(place, near, ready["a"], w_out, frames)
+    blocks = latent_call(place, partial, ready["b"], w_out, w_latent, frames, columns, tiles)
     blocks = lax.all_to_all(blocks, "tm", 0, 0, tiled=True)
-    return decode(core, blocks, conv_weight, conv_bias, frames, grid_rows, own, tiles)
-
-
-def decode(core, blocks, conv_weight, conv_bias, frames, grid_rows, own, tiles):
+    return decode(place, blocks, conv_weight, conv_bias, frames, grid_rows, own, tiles)
+
+
+def decode(place, blocks, conv_weight, conv_bias, frames, grid_rows, own, tiles):
     channels = conv_weight.shape[2]
     width = conv_weight.shape[3]
     group = frames * own
@@ -400,7 +484,7 @@
     def edge(r):
         return jnp.concatenate([blocks[:, r * group : (r + 1) * group], sides[:, :, r]], axis=1)
 
-    mine = jnp.where(core[0] == 0, edge(grid_rows - 1), edge(0))
+    mine = jnp.where(place[0] == 0, edge(grid_rows - 1), edge(0))
     beside = lax.ppermute(mine, "space", SWAP)
     total = tiles * group
     return pl.pallas_call(
@@ -415,7 +499,7 @@
         ],
         name="decode",
         compiler_params=params(36),
-    )(core, blocks, beside, conv_weight, conv_bias.reshape(1, width))
+    )(place, blocks, beside, conv_weight, conv_bias.reshape(1, width))
 
 
 def solution(mesh):

time: 73.2 us -> 75.6 us (1.033)
  other arithmetic: 5.5 us -> 0.1 us
  Pallas kernels: 28.9 us -> 33.6 us
  waiting for transfers between devices: 17.3 us -> 19.2 us
  starting transfers between devices: 20.5 us -> 22.1 us
    convert_element_type x8 -> x0, other arithmetic: 5.48 us -> none  [the longest x6 5.4 us: prefix_rounds(): sent = total.astype(BF16)]
    pallas_call x2 -> x10, Pallas kernels: 13.3 us -> 17.5 us  [the longest x1 9.23 us: first_states(): pl.pallas_call(functools.partial(states_kernel, frames, 0, heads, later,...]
    ppermute x10 -> x8, waiting for transfers between devices: 5.17 us -> 7.01 us  [the longest x6 7 us: prefix_rounds(): got = lax.ppermute(sent, 'tm', pairs)]
    ppermute x10 -> x8, starting transfers between devices: 13.3 us -> 15 us  [the longest x6 14.3 us: prefix_rounds(): got = lax.ppermute(sent, 'tm', pairs)]
  transfers between devices with their start and end apart: 14 -> 12, of which waited for: 5 -> 6; matrix products, arithmetic and copies ran while one was open for 8% -> 0% of each run, Pallas kernels for 16% -> 21%
where the time goes in v1:
time: 75.6 us; the launch traced here: 75.3 us
  Pallas kernels  33.6 us (44%)
  starting transfers between devices  22.1 us (29%)
  waiting for transfers between devices  19.2 us (25%)
    ppermute x6, starting transfers between devices, prefix_rounds(): got = lax.ppermute(sent, 'tm', pairs)  14.3 us
    all_to_all x1, waiting for transfers between devices, body(): blocks = lax.all_to_all(blocks, 'tm', 0, 0, tiled=True)  10.9 us
    pallas_call x1, Pallas kernels, first_states(): pl.pallas_call(functools.partial(states_kernel, frames, 0, heads, later,...  9.23 us
    ppermute x6, waiting for transfers between devices, prefix_rounds(): got = lax.ppermute(sent, 'tm', pairs)  7 us
    all_to_all x1, starting transfers between devices, body(): blocks = lax.all_to_all(blocks, 'tm', 0, 0, tiled=True)  6.9 us
    pallas_call x1, Pallas kernels, latent_call(): pl.pallas_call(functools.partial(latent_kernel, frames, columns, tiles),...  4.85 us
    pallas_call x2, Pallas kernels, query_call(): pl.pallas_call(kernel, out_shape=shape((video.shape[0], width), BF16), in...  3.93 us
    pallas_call x1, Pallas kernels, decode(): pl.pallas_call(functools.partial(decode_kernel, frames, tiles, grid_rows,...  3.89 us
  transfers between devices with their start and end apart: 12, of which 6 were waited for; matrix products, arithmetic and copies ran while one was open for 0% of the time, Pallas kernels for 21%

profile of v1, /device:TPU:0, one launch (start us, length us, event | category | flops | bytes accessed | tf_op | source)
XLA Modules:
  0.0 75.3 jit_solution(525901328206937017)
XLA Ops:
  0.0 0.1 pad_add_fusion.place
  0.1 9.2 %states.2 = (bf16[2,6,128,128]{3,2,1,0:T(8,128)(2,1)S(1)}, bf16[1024,1152]{1,0:T(8,128)(2,1)S(1)}, bf16[1152,384]{1,0:T(8,128)(2,1)S(1)}, bf16[1152,384]{1,0:T(8,128)(2,1)S(1)}) custom-call(s32[2]{0:T(128)S(1)} %pad_add_fusion.place, bf16[1024,1152]{1,0:T(8,128)(2,1)} %bitcast.11, bf16[1152,1152]{1,0:T(8,128)(2,1)} %wk_hbm.1, bf16[1152,1152]{1,0:T(8,128)(2,1)} %wv_hbm.1), custom_call_target="tpu_custom_call" | custom-call | tf_op jit(solution)/shard_map/states/pallas_call | solution.py:132
  9.3 0.6 collective-permute-start
  9.9 3.5 %states.3 = (bf16[2,3,128,128]{3,2,1,0:T(8,128)(2,1)S(1)}, bf16[1152,1152]{1,0:T(8,128)(2,1)S(1)}) custom-call(s32[2]{0:T(128)S(1)} %pad_add_fusion.place, bf16[1024,1152]{1,0:T(8,128)(2,1)S(1)} %get-tuple-element.27.video_in.video, bf16[1152,384]{1,0:T(8,128)(2,1)S(1)} %get-tuple-element.28.wk_hbm, bf16[1152,384]{1,0:T(8,128)(2,1)S(1)} %get-tuple-element.29.wv_hbm, ...), custom_call_target="tpu_custom_call" | custom-call | tf_op jit(solution)/shard_map/states/pallas_call | solution.py:160
  13.4 0.1 collective-permute-start.5
  13.5 0.6 total.2
  14.2 3.0 %collective-permute-start.1 = (bf16[6,64,128]{2,1,0:T(8,128)(2,1)S(1)}, bf16[6,64,128]{2,1,0:T(8,128)(2,1)S(1)}, u32[]{:S(2)}, u32[]{:S(2)}) collective-permute-start(bf16[6,64,128]{2,1,0:T(8,128)(2,1)S(1)} %get-tuple-element.32), channel_id=1, source_target_pairs={{0,2},{2,0},{4,6},{6,4},{8,10},{10,8},{12,14},{14,12},{1,3},{3,1},... | collective-permute-start | bytes 294920 | tf_op jit(solution)/shard_map/ppermute | solution.py:435
  17.2 3.0 %collective-permute-done.1.got = bf16[6,64,128]{2,1,0:T(8,128)(2,1)S(1)} collective-permute-done((bf16[6,64,128]{2,1,0:T(8,128)(2,1)S(1)}, bf16[6,64,128]{2,1,0:T(8,128)(2,1)S(1)}, u32[]{:S(2)}, u32[]{:S(2)}) %collective-permute-start.1) | collective-permute-done | bytes 98336 | tf_op jit(solution)/shard_map/ppermute | solution.py:435
  20.2 0.6 round.6
  20.8 1.9 %collective-permute-start.2 = (bf16[6,64,128]{2,1,0:T(8,128)(2,1)S(1)}, bf16[6,64,128]{2,1,0:T(8,128)(2,1)S(1)}, u32[]{:S(2)}, u32[]{:S(2)}) collective-permute-start(bf16[6,64,128]{2,1,0:T(8,128)(2,1)S(1)} %get-tuple-element.34), channel_id=1, source_target_pairs={{0,4},{2,6},{4,0},{6,2},{8,12},{10,14},{12,8},{14,10},{1,5},{3,7},... | collective-permute-start | bytes 294920 | tf_op jit(solution)/shard_map/ppermute | solution.py:435
  22.7 0.6 total.3
  23.3 1.6 %collective-permute-start.6 = (bf16[3,64,128]{2,1,0:T(8,128)(2,1)S(1)}, bf16[3,64,128]{2,1,0:T(8,128)(2,1)S(1)}, u32[]{:S(2)}, u32[]{:S(2)}) collective-permute-start(bf16[3,64,128]{2,1,0:T(8,128)(2,1)S(1)} %get-tuple-element.41), channel_id=1, source_target_pairs={{0,2},{2,0},{4,6},{6,4},{8,10},{10,8},{12,14},{14,12},{1,3},{3,1},... | collective-permute-start | bytes 147464 | tf_op jit(solution)/shard_map/ppermute | solution.py:435
  24.8 0.6 collective-permute-done.2.got
  25.5 0.6 round.7
  26.1 4.7 %collective-permute-start.3 = (bf16[6,64,128]{2,1,0:T(8,128)(2,1)S(1)}, bf16[6,64,128]{2,1,0:T(8,128)(2,1)S(1)}, u32[]{:S(2)}, u32[]{:S(2)}) collective-permute-start(bf16[6,64,128]{2,1,0:T(8,128)(2,1)S(1)} %get-tuple-element.37), channel_id=1, source_target_pairs={{0,8},{2,10},{4,12},{6,14},{1,9},{3,11},{5,13},{7,15},{16,24},{18,... | collective-permute-start | bytes 294920 | tf_op jit(solution)/shard_map/ppermute | solution.py:435
  30.8 0.6 round.9
  31.4 1.6 %collective-permute-start.7 = (bf16[3,64,128]{2,1,0:T(8,128)(2,1)S(1)}, bf16[3,64,128]{2,1,0:T(8,128)(2,1)S(1)}, u32[]{:S(2)}, u32[]{:S(2)}) collective-permute-start(bf16[3,64,128]{2,1,0:T(8,128)(2,1)S(1)} %get-tuple-element.43), channel_id=1, source_target_pairs={{0,4},{2,6},{4,0},{6,2},{8,12},{10,14},{12,8},{14,10},{1,5},{3,7},... | collective-permute-start | bytes 147464 | tf_op jit(solution)/shard_map/ppermute | solution.py:435
  33.0 2.5 %collective-permute-done.7.got = bf16[3,64,128]{2,1,0:T(8,128)(2,1)S(1)} collective-permute-done((bf16[3,64,128]{2,1,0:T(8,128)(2,1)S(1)}, bf16[3,64,128]{2,1,0:T(8,128)(2,1)S(1)}, u32[]{:S(2)}, u32[]{:S(2)}) %collective-permute-start.7) | collective-permute-done | bytes 49184 | tf_op jit(solution)/shard_map/ppermute | solution.py:435
  35.5 0.6 round.10
  36.1 1.5 %collective-permute-start.8 = (bf16[3,64,128]{2,1,0:T(8,128)(2,1)S(1)}, bf16[3,64,128]{2,1,0:T(8,128)(2,1)S(1)}, u32[]{:S(2)}, u32[]{:S(2)}) collective-permute-start(bf16[3,64,128]{2,1,0:T(8,128)(2,1)S(1)} %get-tuple-element.46), channel_id=1, source_target_pairs={{0,8},{2,10},{4,12},{6,14},{1,9},{3,11},{5,13},{7,15},{16,24},{18,... | collective-permute-start | bytes 147464 | tf_op jit(solution)/shard_map/ppermute | solution.py:435
  37.6 0.6 round.8.carry
  38.3 0.9 %collective-permute-done.8.got = bf16[3,64,128]{2,1,0:T(8,128)(2,1)S(1)} collective-permute-done((bf16[3,64,128]{2,1,0:T(8,128)(2,1)S(1)}, bf16[3,64,128]{2,1,0:T(8,128)(2,1)S(1)}, u32[]{:S(2)}, u32[]{:S(2)}) %collective-permute-start.8) | collective-permute-done | bytes 49184 | tf_op jit(solution)/shard_map/ppermute | solution.py:435
  39.1 0.6 round.11.carry
  39.8 1.6 %query.3 = bf16[1024,384]{1,0:T(8,128)(2,1)S(1)} custom-call(bf16[1024,1152]{1,0:T(8,128)(2,1)S(1)} %get-tuple-element.27.video_in.video, bf16[1152,1152]{1,0:T(8,128)(2,1)S(1)} %get-tuple-element.30.w), custom_call_target="tpu_custom_call" | custom-call | tf_op jit(solution)/shard_map/query/pallas_call | solution.py:208
  41.4 2.4 %query.2 = bf16[1024,768]{1,0:T(8,128)(2,1)S(1)} custom-call(bf16[1024,1152]{1,0:T(8,128)(2,1)S(1)} %get-tuple-element.27.video_in.video, bf16[1152,1152]{1,0:T(8,128)(2,1)S(1)} %get-tuple-element.30.w), custom_call_target="tpu_custom_call" | custom-call | tf_op jit(solution)/shard_map/query/pallas_call | solution.py:208
  43.8 3.5 %partial.1 = f32[1024,1152]{1,0:T(8,128)S(1)} custom-call(s32[2]{0:T(128)S(1)} %pad_add_fusion.place, bf16[1024,1152]{1,0:T(8,128)(2,1)S(1)} %get-tuple-element.27.video_in.video, bf16[1024,768]{1,0:T(8,128)(2,1)S(1)} %query.2, bf16[2,6,128,128]{3,2,1,0:T(8,128)(2,1)S(1)} %get-tuple-element.31.parts, ...), custom_call_target="tpu_custom_call" | custom-call | tf_op jit(solution)/shard_map/partial/pallas_call | solution.py:265
  47.3 4.9 %latent.1 = bf16[8,160,128]{2,1,0:T(8,128)(2,1)} custom-call(s32[2]{0:T(128)S(1)} %pad_add_fusion.place, f32[1024,1152]{1,0:T(8,128)S(1)} %partial.1, bf16[1024,384]{1,0:T(8,128)(2,1)S(1)} %query.3, bf16[2,3,128,128]{3,2,1,0:T(8,128)(2,1)S(1)} %get-tuple-element.40.parts, bf16[2,3,128,128]{3,2,1,0:T(8,128)(2,1)S(1)} %collective-permute-done.5.other_parts, ...), custom_call_target="tpu_custom_call" | custom-call | tf_op jit(solution)/shard_map/latent/pallas_call | solution.py:316
  52.2 6.9 %all-to-all-start = ((bf16[8,160,128]{2,1,0:T(8,128)(2,1)}), bf16[8,160,128]{2,1,0:T(8,128)(2,1)S(1)}, u32[]{:S(2)}, u32[]{:S(2)}) async-start(bf16[8,160,128]{2,1,0:T(8,128)(2,1)} %latent.1), calls=%async_computation | async-start | bytes 655360 | tf_op jit(solution)/shard_map/all_to_all | solution.py:473
  59.1 10.9 %all-to-all-done.blocks = bf16[8,160,128]{2,1,0:T(8,128)(2,1)S(1)} async-done(((bf16[8,160,128]{2,1,0:T(8,128)(2,1)}), bf16[8,160,128]{2,1,0:T(8,128)(2,1)S(1)}, u32[]{:S(2)}, u32[]{:S(2)}) %all-to-all-start) | async-done | bytes 327712 | tf_op jit(solution)/shard_map/all_to_all | solution.py:473
  70.1 0.1 collective-permute-start.10
  70.2 1.2 %collective-permute-done.10.edge = bf16[8,20,128]{2,1,0:T(8,128)(2,1)S(1)} collective-permute-done((bf16[8,20,128]{2,1,0:T(8,128)(2,1)S(1)}, bf16[8,20,128]{2,1,0:T(8,128)(2,1)S(1)}, u32[]{:S(2)}, u32[]{:S(2)}) %collective-permute-start.10) | collective-permute-done | bytes 40992 | tf_op jit(solution)/shard_map/ppermute | solution.py:488
  71.4 3.9 %decode.1 = bf16[16,16,16,256]{3,2,1,0:T(8,128)(2,1)} custom-call(s32[2]{0:T(128)S(1)} %pad_add_fusion.place, bf16[8,160,128]{2,1,0:T(8,128)(2,1)S(1)} %all-to-all-done.blocks, bf16[8,20,128]{2,1,0:T(8,128)(2,1)S(1)} %collective-permute-done.10.edge, bf16[3,3,128,256]{3,2,1,0:T(8,128)(2,1)S(1)} %copy-done.1, f32[1,256]{1,0:T(1,128)S(1)} %bitcast.10), custom_call_target="tpu_custom_call" | custom-call | tf_op jit(solution)/shard_map/decode/pallas_call | solution.py:490
  (21 shorter events, 0.3 us)
Async XLA Ops:
  9.3 4.2 %collective-permute-start = (bf16[2,6,128,128]{3,2,1,0:T(8,128)(2,1)S(1)}, bf16[2,6,128,128]{3,2,1,0:T(8,128)(2,1)S(1)}, u32[]{:S(2)}, u32[]{:S(2)}) collective-permute-start(bf16[2,6,128,128]{3,2,1,0:T(8,128)(2,1)S(1)} %get-tuple-element.31.parts), channel_id=1, source_target_pairs={{0,1},{1,0},{2,3},{3,2},{4,5},{5,4},{6,7},{7,6},{8,9},{9,8},{10,11... | collective-permute-start | bytes 1179656 | tf_op jit(solution)/shard_map/ppermute | solution.py:458
  13.4 9.2 %collective-permute-start.5 = (bf16[2,3,128,128]{3,2,1,0:T(8,128)(2,1)S(1)}, bf16[2,3,128,128]{3,2,1,0:T(8,128)(2,1)S(1)}, u32[]{:S(2)}, u32[]{:S(2)}) collective-permute-start(bf16[2,3,128,128]{3,2,1,0:T(8,128)(2,1)S(1)} %get-tuple-element.40.parts), channel_id=1, source_target_pairs={{0,1},{1,0},{2,3},{3,2},{4,5},{5,4},{6,7},{7,6},{8,9},{9,8},{10,11... | collective-permute-start | bytes 589832 | tf_op jit(solution)/shard_map/ppermute | solution.py:460
  14.2 6.0 %collective-permute-start.1 = (bf16[6,64,128]{2,1,0:T(8,128)(2,1)S(1)}, bf16[6,64,128]{2,1,0:T(8,128)(2,1)S(1)}, u32[]{:S(2)}, u32[]{:S(2)}) collective-permute-start(bf16[6,64,128]{2,1,0:T(8,128)(2,1)S(1)} %get-tuple-element.32), channel_id=1, source_target_pairs={{0,2},{2,0},{4,6},{6,4},{8,10},{10,8},{12,14},{14,12},{1,3},{3,1},... | collective-permute-start | bytes 294920 | tf_op jit(solution)/shard_map/ppermute | solution.py:435
  20.8 4.7 %collective-permute-start.2 = (bf16[6,64,128]{2,1,0:T(8,128)(2,1)S(1)}, bf16[6,64,128]{2,1,0:T(8,128)(2,1)S(1)}, u32[]{:S(2)}, u32[]{:S(2)}) collective-permute-start(bf16[6,64,128]{2,1,0:T(8,128)(2,1)S(1)} %get-tuple-element.34), channel_id=1, source_target_pairs={{0,4},{2,6},{4,0},{6,2},{8,12},{10,14},{12,8},{14,10},{1,5},{3,7},... | collective-permute-start | bytes 294920 | tf_op jit(solution)/shard_map/ppermute | solution.py:435
  23.3 7.5 %collective-permute-start.6 = (bf16[3,64,128]{2,1,0:T(8,128)(2,1)S(1)}, bf16[3,64,128]{2,1,0:T(8,128)(2,1)S(1)}, u32[]{:S(2)}, u32[]{:S(2)}) collective-permute-start(bf16[3,64,128]{2,1,0:T(8,128)(2,1)S(1)} %get-tuple-element.41), channel_id=1, source_target_pairs={{0,2},{2,0},{4,6},{6,4},{8,10},{10,8},{12,14},{14,12},{1,3},{3,1},... | collective-permute-start | bytes 147464 | tf_op jit(solution)/shard_map/ppermute | solution.py:435
  26.1 11.5 %collective-permute-start.3 = (bf16[6,64,128]{2,1,0:T(8,128)(2,1)S(1)}, bf16[6,64,128]{2,1,0:T(8,128)(2,1)S(1)}, u32[]{:S(2)}, u32[]{:S(2)}) collective-permute-start(bf16[6,64,128]{2,1,0:T(8,128)(2,1)S(1)} %get-tuple-element.37), channel_id=1, source_target_pairs={{0,8},{2,10},{4,12},{6,14},{1,9},{3,11},{5,13},{7,15},{16,24},{18,... | collective-permute-start | bytes 294920 | tf_op jit(solution)/shard_map/ppermute | solution.py:435
  31.4 4.2 %collective-permute-start.7 = (bf16[3,64,128]{2,1,0:T(8,128)(2,1)S(1)}, bf16[3,64,128]{2,1,0:T(8,128)(2,1)S(1)}, u32[]{:S(2)}, u32[]{:S(2)}) collective-permute-start(bf16[3,64,128]{2,1,0:T(8,128)(2,1)S(1)} %get-tuple-element.43), channel_id=1, source_target_pairs={{0,4},{2,6},{4,0},{6,2},{8,12},{10,14},{12,8},{14,10},{1,5},{3,7},... | collective-permute-start | bytes 147464 | tf_op jit(solution)/shard_map/ppermute | solution.py:435
  36.1 3.0 %collective-permute-start.8 = (bf16[3,64,128]{2,1,0:T(8,128)(2,1)S(1)}, bf16[3,64,128]{2,1,0:T(8,128)(2,1)S(1)}, u32[]{:S(2)}, u32[]{:S(2)}) collective-permute-start(bf16[3,64,128]{2,1,0:T(8,128)(2,1)S(1)} %get-tuple-element.46), channel_id=1, source_target_pairs={{0,8},{2,10},{4,12},{6,14},{1,9},{3,11},{5,13},{7,15},{16,24},{18,... | collective-permute-start | bytes 147464 | tf_op jit(solution)/shard_map/ppermute | solution.py:435
  38.2 5.6 %collective-permute-start.4 = (bf16[6,64,128]{2,1,0:T(8,128)(2,1)S(1)}, bf16[6,64,128]{2,1,0:T(8,128)(2,1)S(1)}, u32[]{:S(2)}, u32[]{:S(2)}) collective-permute-start(bf16[6,64,128]{2,1,0:T(8,128)(2,1)S(1)} %round.8.carry), channel_id=1, source_target_pairs={{0,1},{1,0},{2,3},{3,2},{4,5},{5,4},{6,7},{7,6},{8,9},{9,8},{10,11... | collective-permute-start | bytes 294920 | tf_op jit(solution)/shard_map/ppermute | solution.py:468
  39.7 7.6 %collective-permute-start.9 = (bf16[3,64,128]{2,1,0:T(8,128)(2,1)S(1)}, bf16[3,64,128]{2,1,0:T(8,128)(2,1)S(1)}, u32[]{:S(2)}, u32[]{:S(2)}) collective-permute-start(bf16[3,64,128]{2,1,0:T(8,128)(2,1)S(1)} %round.11.carry), channel_id=1, source_target_pairs={{0,1},{1,0},{2,3},{3,2},{4,5},{5,4},{6,7},{7,6},{8,9},{9,8},{10,11... | collective-permute-start | bytes 147464 | tf_op jit(solution)/shard_map/ppermute | solution.py:468
  41.3 2.4 %copy-start = (bf16[1152,1152]{1,0:T(8,128)(2,1)S(1)}, bf16[1152,1152]{1,0:T(8,128)(2,1)}, u32[]{:S(2)}) copy-start(bf16[1152,1152]{1,0:T(8,128)(2,1)} %w_out.3) | copy-start | bytes 7962628
  43.7 3.6 %copy-start.2 = (bf16[1152,128]{1,0:T(8,128)(2,1)S(1)}, bf16[1152,128]{1,0:T(8,128)(2,1)}, u32[]{:S(2)}) copy-start(bf16[1152,128]{1,0:T(8,128)(2,1)} %w_latent.1) | copy-start | bytes 884740
  47.3 24.1 %copy-start.1 = (bf16[3,3,128,256]{3,2,1,0:T(8,128)(2,1)S(1)}, bf16[3,3,128,256]{3,2,1,0:T(8,128)(2,1)}, u32[]{:S(2)}) copy-start(bf16[3,3,128,256]{3,2,1,0:T(8,128)(2,1)} %weight.1) | copy-start | bytes 1769476
  47.3 24.1 %copy-start.3 = (f32[256]{0:T(256)S(1)}, f32[256]{0:T(256)}, u32[]{:S(2)}) copy-start(f32[256]{0:T(256)} %param.15) | copy-start | bytes 3076
  52.2 17.8 %all-to-all-start = ((bf16[8,160,128]{2,1,0:T(8,128)(2,1)}), bf16[8,160,128]{2,1,0:T(8,128)(2,1)S(1)}, u32[]{:S(2)}, u32[]{:S(2)}) async-start(bf16[8,160,128]{2,1,0:T(8,128)(2,1)} %latent.1), calls=%async_computation | async-start | bytes 655360 | tf_op jit(solution)/shard_map/all_to_all | solution.py:473
  70.1 1.3 %collective-permute-start.10 = (bf16[8,20,128]{2,1,0:T(8,128)(2,1)S(1)}, bf16[8,20,128]{2,1,0:T(8,128)(2,1)S(1)}, u32[]{:S(2)}, u32[]{:S(2)}) collective-permute-start(bf16[8,20,128]{2,1,0:T(8,128)(2,1)S(1)} %maximum_select_fusion), channel_id=1, source_target_pairs={{0,1},{1,0},{2,3},{3,2},{4,5},{5,4},{6,7},{7,6},{8,9},{9,8},{10,11... | collective-permute-start | bytes 122888 | tf_op jit(solution)/shard_map/ppermute | solution.py:488

commit v2 on v1

--- a/solution.py
+++ b/solution.py
@@ -16,7 +16,6 @@
 
 IN_HBM = pl.BlockSpec(memory_space=pltpu.HBM)
 IN_VMEM = pl.BlockSpec(memory_space=pltpu.VMEM)
-IN_SMEM = pl.BlockSpec(memory_space=pltpu.SMEM)
 
 
 def shape(dims, dtype):
@@ -31,10 +30,6 @@
     return pltpu.with_memory_space_constraint(x, pltpu.HBM)
 
 
-def in_vmem(x):
-    return pltpu.with_memory_space_constraint(x, pltpu.VMEM)
-
-
 def matmul(a, b):
     return jnp.dot(a, b, preferred_element_type=F32)
 
@@ -43,7 +38,7 @@
     return jnp.where(x > 0.0, x + 1.0, jnp.exp(jnp.minimum(x, 0.0)))
 
 
-def states_kernel(frames, first, heads, later, fetched, place, video_in, wk_hbm, wv_hbm, *refs):
+def states_kernel(frames, first, heads, later, fetched, video_in, wk_hbm, wv_hbm, *refs):
     refs = list(refs)
     wq_hbm = refs.pop(0) if fetched else None
     parts_out = refs.pop(0)
@@ -126,7 +121,7 @@
         c.wait()
 
 
-def first_states(place, video, wk, wv, frames, heads, later):
+def first_states(video, wk, wv, frames, heads, later):
     tokens, d = video.shape
     width = heads * HEAD
     return pl.pallas_call(
@@ -137,7 +132,7 @@
             shape((d, later * HEAD), BF16),
             shape((d, later * HEAD), BF16),
         ],
-        in_specs=[IN_SMEM] + [IN_HBM] * 3,
+        in_specs=[IN_HBM] * 3,
         out_specs=[IN_VMEM] * 4,
         scratch_shapes=[
             pltpu.VMEM((d, width), BF16),
@@ -151,10 +146,10 @@
         ],
         name="states",
         compiler_params=params(20),
-    )(place, in_hbm(video), in_hbm(wk), in_hbm(wv))
-
-
-def second_states(place, video, wk, wv, wq, frames):
+    )(in_hbm(video), in_hbm(wk), in_hbm(wv))
+
+
+def second_states(video, wk, wv, wq, frames):
     tokens, _ = video.shape
     heads = wk.shape[1] // HEAD
     return pl.pallas_call(
@@ -163,7 +158,7 @@
             shape((frames, heads, HEAD, HEAD), BF16),
             shape(wq.shape, BF16),
         ],
-        in_specs=[IN_SMEM] + [IN_VMEM] * 3 + [IN_HBM],
+        in_specs=[IN_VMEM] * 3 + [IN_HBM],
         out_specs=[IN_VMEM] * 2,
         scratch_shapes=[
             pltpu.VMEM((heads, tokens, HEAD), BF16),
@@ -172,15 +167,15 @@
         ],
         name="states",
         compiler_params=params(20),
-    )(place, video, wk, wv, in_hbm(wq))
-
-
-def total_call(place, parts, other_parts):
+    )(video, wk, wv, in_hbm(wq))
+
+
+def total_call(parts, other_parts):
     frames, heads = parts.shape[:2]
     half = HEAD // 2
 
-    def kernel(place, parts, other_parts, out, sent):
-        low = place[0] == 0
+    def kernel(parts, other_parts, out, sent):
+        low = lax.axis_index("space") == 0
         for h in range(heads):
             total = None
             for f in range(frames):
@@ -194,11 +189,11 @@
     return pl.pallas_call(
         kernel,
         out_shape=[shape(dims, F32), shape(dims, BF16)],
-        in_specs=[IN_SMEM] + [IN_VMEM] * 2,
+        in_specs=[IN_VMEM] * 2,
         out_specs=[IN_VMEM] * 2,
         name="total",
         compiler_params=params(4),
-    )(place, in_vmem(parts), in_vmem(other_parts))
+    )(parts, other_parts)
 
 
 def query_call(video, w, first, width):
@@ -215,10 +210,10 @@
     )(video, w)
 
 
-def attend(frames, place, query, parts, other_parts, carry, other_carry, used, head_out):
+def attend(frames, query, parts, other_parts, carry, other_carry, used, head_out):
     heads = carry.shape[0]
     per = query.shape[0] // frames
-    low = place[0] == 0
+    low = lax.axis_index("space") == 0
     used[...] = jnp.zeros_like(used)
     for h in range(heads):
         mine, theirs = carry[h].astype(F32), other_carry[h].astype(F32)
@@ -248,13 +243,13 @@
     return pltpu.VMEM((frames, pl.cdiv(heads, 2), 2 * HEAD, 2 * HEAD), BF16)
 
 
-def partial_call(place, video, chunk, w_out, frames):
+def partial_call(video, chunk, w_out, frames):
     tokens, d = video.shape
     heads = chunk[3].shape[0]
 
-    def kernel(place, video, query, parts, other_parts, carry, other_carry, w_out, out,
+    def kernel(video, query, parts, other_parts, carry, other_carry, w_out, out,
                used, head_out):
-        attend(frames, place, query, parts, other_parts, carry, other_carry, used, head_out)
+        attend(frames, query, parts, other_parts, carry, other_carry, used, head_out)
         per = tokens // frames
         for f in range(frames):
             rows = slice(f * per, (f + 1) * per)
@@ -265,22 +260,22 @@
     return pl.pallas_call(
         kernel,
         out_shape=shape((tokens, d), F32),
-        in_specs=[IN_SMEM] + [IN_VMEM] * 7,
+        in_specs=[IN_VMEM] * 7,
         out_specs=IN_VMEM,
         scratch_shapes=[used_shape(frames, heads), pltpu.VMEM((tokens, heads * HEAD), BF16)],
         name="partial",
         compiler_params=params(20),
-    )(place, video, *chunk, w_out)
+    )(video, *chunk, w_out)
 
 
 def latent_kernel(
-    frames, columns, tiles, place, partial, query, parts, other_parts, carry, other_carry,
+    frames, columns, tiles, partial, query, parts, other_parts, carry, other_carry,
     w_out, w_latent, out, used, head_out, latent,
 ):
     tokens, d = partial.shape
     per = tokens // frames
     width = head_out.shape[1]
-    attend(frames, place, query, parts, other_parts, carry, other_carry, used, head_out)
+    attend(frames, query, parts, other_parts, carry, other_carry, used, head_out)
     for f in range(frames):
         rows = slice(f * per, (f + 1) * per)
         summed = partial[rows, :] + matmul(head_out[rows, :], w_out[d - width :, :])
@@ -308,7 +303,7 @@
         out[t, main:, :] = jnp.concatenate(sides, axis=0).astype(BF16)
 
 
-def latent_call(place, partial, chunk, w_out, w_latent, frames, columns, tiles):
+def latent_call(partial, chunk, w_out, w_latent, frames, columns, tiles):
     tokens, _ = partial.shape
     channels = w_latent.shape[1]
     heads = chunk[3].shape[0]
@@ -316,7 +311,7 @@
     return pl.pallas_call(
         functools.partial(latent_kernel, frames, columns, tiles),
         out_shape=shape((tiles, rows, channels), BF16),
-        in_specs=[IN_SMEM] + [IN_VMEM] * 8,
+        in_specs=[IN_VMEM] * 8,
         out_specs=IN_VMEM,
         scratch_shapes=[
             used_shape(frames, heads),
@@ -325,15 +320,16 @@
         ],
         name="latent",
         compiler_params=params(20),
-    )(place, partial, *chunk, w_out, w_latent)
+    )(partial, *chunk, w_out, w_latent)
 
 
 def decode_kernel(
-    frames, tiles, grid_rows, own, place, blocks, edge, weight, bias,
+    frames, tiles, grid_rows, own, blocks, edge, weight, bias,
     out, left, middle, right, taps, wide,
 ):
     group = frames * own
     main = grid_rows * group
+    tile = lax.axis_index("space")
     column = lax.broadcasted_iota(jnp.int32, (group, 1), 0) % own
     channels = weight.shape[2]
 
@@ -362,7 +358,7 @@
             ]
             lay(r + 1, t, body, jnp.concatenate(sides, axis=0))
         beside = edge[t].astype(F32)
-        for row, present in ((0, place[0] == 1), (grid_rows + 1, place[0] == 0)):
+        for row, present in ((0, tile == 1), (grid_rows + 1, tile == 0)):
             there = jnp.where(present, beside, 0.0)
             lay(row, t, there[:group], there[group:])
 
@@ -394,9 +390,9 @@
                 out[:, 2 * r + a, :, n * 128 : (n + 1) * 128] = shaped[r].astype(BF16)
 
 
-def round_call(place, step, last, got, total, carry):
-    def kernel(place, got, total, *refs):
-        upper = (place[1] // step) % 2 == 1
+def round_call(step, last, got, total, carry):
+    def kernel(got, total, *refs):
+        upper = (lax.axis_index("tm") // step) % 2 == 1
         received = got[...].astype(F32)
         before = jnp.where(upper, received, 0.0)
         if carry is not None:
@@ -416,14 +412,14 @@
     return pl.pallas_call(
         kernel,
         out_shape=[shape(total.shape, kind) for kind in kinds],
-        in_specs=[IN_SMEM] + [IN_VMEM] * len(near),
+        in_specs=[IN_VMEM] * len(near),
         out_specs=[IN_VMEM] * len(kinds),
         name="round",
         compiler_params=params(4),
-    )(place, *near)
-
-
-def prefix_rounds(place, total, sent, tiles):
+    )(*near)
+
+
+def prefix_rounds(total, sent, tiles):
     carry = None
     step, number = 1, 0
     while step < tiles:
@@ -433,7 +429,7 @@
         else:
             pairs = [(i, i ^ step) for i in range(tiles)]
         got = lax.ppermute(sent, "tm", pairs)
-        out = round_call(place, step, last, got, total, carry)
+        out = round_call(step, last, got, total, carry)
         if last:
             return out[0]
         carry, total, sent = out
@@ -450,31 +446,32 @@
     tiles = lax.axis_size("tm")
     own = columns // tiles
     flat = video.reshape(-1, d)
-    place = jnp.stack([lax.axis_index("space"), lax.axis_index("tm")]).astype(jnp.int32)
     heads = d // HEAD
     split = heads // 3 * 2
     rest = heads - split
-    parts_a, near, wk_b, wv_b = first_states(place, flat, w_key, w_value, frames, split, rest)
+    parts_a, near, wk_b, wv_b = first_states(flat, w_key, w_value, frames, split, rest)
     other_a = lax.ppermute(parts_a, "space", SWAP)
-    parts_b, near_query = second_states(place, near, wk_b, wv_b, w_query, frames)
+    parts_b, near_query = second_states(near, wk_b, wv_b, w_query, frames)
     other_b = lax.ppermute(parts_b, "space", SWAP)
 
     ready = {}
     for name, first, parts, other in (("a", 0, parts_a, other_a), ("b", split, parts_b, other_b)):
         count = parts.shape[1]
-        total, sent = total_call(place, parts, other)
+        total, sent = total_call(parts, other)
         query = query_call(near, near_query, first * HEAD, count * HEAD)
-        carry = prefix_rounds(place, total, sent, tiles)
+        carry = prefix_rounds(total, sent, tiles)
         other_carry = lax.ppermute(carry, "space", SWAP)
         ready[name] = (query, parts, other, carry, other_carry)
 
-    partial = partial_call(place, near, ready["a"], w_out, frames)
-    blocks = latent_call(place, partial, ready["b"], w_out, w_latent, frames, columns, tiles)
+    partial = partial_call(near, ready["a"], w_out, frames)
+    blocks = latent_call(
+        partial, ready["b"], w_out, w_latent, frames, columns, tiles
+    )
     blocks = lax.all_to_all(blocks, "tm", 0, 0, tiled=True)
-    return decode(place, blocks, conv_weight, conv_bias, frames, grid_rows, own, tiles)
-
-
-def decode(place, blocks, conv_weight, conv_bias, frames, grid_rows, own, tiles):
+    return decode(blocks, conv_weight, conv_bias, frames, grid_rows, own, tiles)
+
+
+def decode(blocks, conv_weight, conv_bias, frames, grid_rows, own, tiles):
     channels = conv_weight.shape[2]
     width = conv_weight.shape[3]
     group = frames * own
@@ -484,13 +481,13 @@
     def edge(r):
         return jnp.concatenate([blocks[:, r * group : (r + 1) * group], sides[:, :, r]], axis=1)
 
-    mine = jnp.where(place[0] == 0, edge(grid_rows - 1), edge(0))
+    mine = jnp.where(lax.axis_index("space") == 0, edge(grid_rows - 1), edge(0))
     beside = lax.ppermute(mine, "space", SWAP)
     total = tiles * group
     return pl.pallas_call(
         functools.partial(decode_kernel, frames, tiles, grid_rows, own),
         out_shape=shape((tiles * frames, 2 * grid_rows, 2 * own, width), BF16),
-        in_specs=[IN_SMEM] + [IN_VMEM] * 4,
+        in_specs=[IN_VMEM] * 4,
         out_specs=IN_VMEM,
         scratch_shapes=[pltpu.VMEM((grid_rows + 2, total, channels), BF16)] * 3
         + [
@@ -499,7 +496,7 @@
         ],
         name="decode",
         compiler_params=params(36),
-    )(place, blocks, beside, conv_weight, conv_bias.reshape(1, width))
+    )(blocks, beside, conv_weight, conv_bias.reshape(1, width))
 
 
 def solution(mesh):

time: 75.6 us -> 69.2 us (0.915)
  Pallas kernels: 33.6 us -> 26.2 us
  waiting for transfers between devices: 19.2 us -> 20.2 us
    pallas_call x6, Pallas kernels: 3.44 us -> 0.2 us  [round_call(): pl.pallas_call(kernel, out_shape=[shape(total.shape, kind) for kind in ki...]
    ppermute x6, waiting for transfers between devices: 7 us -> 8.09 us  [prefix_rounds(): got = lax.ppermute(sent, 'tm', pairs)]
    pallas_call x2, Pallas kernels: 1.24 us -> 0.16 us  [total_call(): pl.pallas_call(kernel, out_shape=[shape(dims, F32), shape(dims, BF16)], i...]
  transfers between devices with their start and end apart: 12 -> 12, of which waited for: 6 -> 6; matrix products, arithmetic and copies ran while one was open for 0% -> 0% of each run, Pallas kernels for 21% -> 15%
where the time goes in v2:
time: 69.2 us; the launch traced here: 68.9 us
  Pallas kernels  26.2 us (38%)
  starting transfers between devices  22.1 us (32%)
  waiting for transfers between devices  20.2 us (29%)
    ppermute x6, starting transfers between devices, prefix_rounds(): got = lax.ppermute(sent, 'tm', pairs)  14.3 us
    all_to_all x1, waiting for transfers between devices, body(): blocks = lax.all_to_all(blocks, 'tm', 0, 0, tiled=True)  10.9 us
    pallas_call x1, Pallas kernels, first_states(): pl.pallas_call(functools.partial(states_kernel, frames, 0, heads, later,...  8.68 us
    ppermute x6, waiting for transfers between devices, prefix_rounds(): got = lax.ppermute(sent, 'tm', pairs)  8.09 us
    all_to_all x1, starting transfers between devices, body(): blocks = lax.all_to_all(blocks, 'tm', 0, 0, tiled=True)  6.91 us
    pallas_call x1, Pallas kernels, latent_call(): pl.pallas_call(functools.partial(latent_kernel, frames, columns, tiles),...  4.1 us
    pallas_call x2, Pallas kernels, query_call(): pl.pallas_call(kernel, out_shape=shape((video.shape[0], width), BF16), in...  3.93 us
    pallas_call x1, Pallas kernels, decode(): pl.pallas_call(functools.partial(decode_kernel, frames, tiles, grid_rows,...  3.37 us
  transfers between devices with their start and end apart: 12, of which 6 were waited for; matrix products, arithmetic and copies ran while one was open for 0% of the time, Pallas kernels for 15%

profile of v2, /device:TPU:0, one launch (start us, length us, event | category | flops | bytes accessed | tf_op | source)
XLA Modules:
  0.0 68.9 jit_solution(16072040631607565006)
XLA Ops:
  0.0 8.7 %states.2 = (bf16[2,6,128,128]{3,2,1,0:T(8,128)(2,1)S(1)}, bf16[1024,1152]{1,0:T(8,128)(2,1)S(1)}, bf16[1152,384]{1,0:T(8,128)(2,1)S(1)}, bf16[1152,384]{1,0:T(8,128)(2,1)S(1)}) custom-call(bf16[1024,1152]{1,0:T(8,128)(2,1)} %bitcast.9, bf16[1152,1152]{1,0:T(8,128)(2,1)} %wk_hbm.1, bf16[1152,1152]{1,0:T(8,128)(2,1)} %wv_hbm.1), custom_call_target="tpu_custom_call" | custom-call | tf_op jit(solution)/shard_map/states/pallas_call | solution.py:127
  8.7 0.6 collective-permute-start
  9.2 3.0 %states.3 = (bf16[2,3,128,128]{3,2,1,0:T(8,128)(2,1)S(1)}, bf16[1152,1152]{1,0:T(8,128)(2,1)S(1)}) custom-call(bf16[1024,1152]{1,0:T(8,128)(2,1)S(1)} %get-tuple-element.27.video_in.video, bf16[1152,384]{1,0:T(8,128)(2,1)S(1)} %get-tuple-element.28.wk_hbm, bf16[1152,384]{1,0:T(8,128)(2,1)S(1)} %get-tuple-element.29.wv_hbm, bf16[1152,1152]{1,0:T(8,128)(2,1)} %refs_0_.1), custom_call_target="tpu_custom_call" | custom-call | tf_op jit(solution)/shard_map/states/pallas_call | solution.py:155
  12.3 0.1 collective-permute-start.5
  12.4 0.1 total.2
  12.5 3.0 %collective-permute-start.1 = (bf16[6,64,128]{2,1,0:T(8,128)(2,1)S(1)}, bf16[6,64,128]{2,1,0:T(8,128)(2,1)S(1)}, u32[]{:S(2)}, u32[]{:S(2)}) collective-permute-start(bf16[6,64,128]{2,1,0:T(8,128)(2,1)S(1)} %get-tuple-element.32), channel_id=1, source_target_pairs={{0,2},{2,0},{4,6},{6,4},{8,10},{10,8},{12,14},{14,12},{1,3},{3,1},... | collective-permute-start | bytes 294920 | tf_op jit(solution)/shard_map/ppermute | solution.py:431
  15.5 3.0 %collective-permute-done.1.got = bf16[6,64,128]{2,1,0:T(8,128)(2,1)S(1)} collective-permute-done((bf16[6,64,128]{2,1,0:T(8,128)(2,1)S(1)}, bf16[6,64,128]{2,1,0:T(8,128)(2,1)S(1)}, u32[]{:S(2)}, u32[]{:S(2)}) %collective-permute-start.1) | collective-permute-done | bytes 98336 | tf_op jit(solution)/shard_map/ppermute | solution.py:431
  18.5 1.9 %collective-permute-start.2 = (bf16[6,64,128]{2,1,0:T(8,128)(2,1)S(1)}, bf16[6,64,128]{2,1,0:T(8,128)(2,1)S(1)}, u32[]{:S(2)}, u32[]{:S(2)}) collective-permute-start(bf16[6,64,128]{2,1,0:T(8,128)(2,1)S(1)} %get-tuple-element.34), channel_id=1, source_target_pairs={{0,4},{2,6},{4,0},{6,2},{8,12},{10,14},{12,8},{14,10},{1,5},{3,7},... | collective-permute-start | bytes 294920 | tf_op jit(solution)/shard_map/ppermute | solution.py:431
  20.4 0.0 collective-permute-done.5.other_parts
  20.4 0.1 total.3
  20.5 1.6 %collective-permute-start.6 = (bf16[3,64,128]{2,1,0:T(8,128)(2,1)S(1)}, bf16[3,64,128]{2,1,0:T(8,128)(2,1)S(1)}, u32[]{:S(2)}, u32[]{:S(2)}) collective-permute-start(bf16[3,64,128]{2,1,0:T(8,128)(2,1)S(1)} %get-tuple-element.41), channel_id=1, source_target_pairs={{0,2},{2,0},{4,6},{6,4},{8,10},{10,8},{12,14},{14,12},{1,3},{3,1},... | collective-permute-start | bytes 147464 | tf_op jit(solution)/shard_map/ppermute | solution.py:431
  22.1 1.2 %collective-permute-done.2.got = bf16[6,64,128]{2,1,0:T(8,128)(2,1)S(1)} collective-permute-done((bf16[6,64,128]{2,1,0:T(8,128)(2,1)S(1)}, bf16[6,64,128]{2,1,0:T(8,128)(2,1)S(1)}, u32[]{:S(2)}, u32[]{:S(2)}) %collective-permute-start.2) | collective-permute-done | bytes 98336 | tf_op jit(solution)/shard_map/ppermute | solution.py:431
  23.3 4.7 %collective-permute-start.3 = (bf16[6,64,128]{2,1,0:T(8,128)(2,1)S(1)}, bf16[6,64,128]{2,1,0:T(8,128)(2,1)S(1)}, u32[]{:S(2)}, u32[]{:S(2)}) collective-permute-start(bf16[6,64,128]{2,1,0:T(8,128)(2,1)S(1)} %get-tuple-element.37), channel_id=1, source_target_pairs={{0,8},{2,10},{4,12},{6,14},{1,9},{3,11},{5,13},{7,15},{16,24},{18,... | collective-permute-start | bytes 294920 | tf_op jit(solution)/shard_map/ppermute | solution.py:431
  28.0 1.6 %collective-permute-start.7 = (bf16[3,64,128]{2,1,0:T(8,128)(2,1)S(1)}, bf16[3,64,128]{2,1,0:T(8,128)(2,1)S(1)}, u32[]{:S(2)}, u32[]{:S(2)}) collective-permute-start(bf16[3,64,128]{2,1,0:T(8,128)(2,1)S(1)} %get-tuple-element.43), channel_id=1, source_target_pairs={{0,4},{2,6},{4,0},{6,2},{8,12},{10,14},{12,8},{14,10},{1,5},{3,7},... | collective-permute-start | bytes 147464 | tf_op jit(solution)/shard_map/ppermute | solution.py:431
  29.7 2.5 %collective-permute-done.7.got = bf16[3,64,128]{2,1,0:T(8,128)(2,1)S(1)} collective-permute-done((bf16[3,64,128]{2,1,0:T(8,128)(2,1)S(1)}, bf16[3,64,128]{2,1,0:T(8,128)(2,1)S(1)}, u32[]{:S(2)}, u32[]{:S(2)}) %collective-permute-start.7) | collective-permute-done | bytes 49184 | tf_op jit(solution)/shard_map/ppermute | solution.py:431
  32.2 1.5 %collective-permute-start.8 = (bf16[3,64,128]{2,1,0:T(8,128)(2,1)S(1)}, bf16[3,64,128]{2,1,0:T(8,128)(2,1)S(1)}, u32[]{:S(2)}, u32[]{:S(2)}) collective-permute-start(bf16[3,64,128]{2,1,0:T(8,128)(2,1)S(1)} %get-tuple-element.46), channel_id=1, source_target_pairs={{0,8},{2,10},{4,12},{6,14},{1,9},{3,11},{5,13},{7,15},{16,24},{18,... | collective-permute-start | bytes 147464 | tf_op jit(solution)/shard_map/ppermute | solution.py:431
  33.8 0.1 collective-permute-start.4
  33.9 1.4 %collective-permute-done.8.got = bf16[3,64,128]{2,1,0:T(8,128)(2,1)S(1)} collective-permute-done((bf16[3,64,128]{2,1,0:T(8,128)(2,1)S(1)}, bf16[3,64,128]{2,1,0:T(8,128)(2,1)S(1)}, u32[]{:S(2)}, u32[]{:S(2)}) %collective-permute-start.8) | collective-permute-done | bytes 49184 | tf_op jit(solution)/shard_map/ppermute | solution.py:431
  35.3 0.1 collective-permute-start.9
  35.4 1.6 %query.3 = bf16[1024,384]{1,0:T(8,128)(2,1)S(1)} custom-call(bf16[1024,1152]{1,0:T(8,128)(2,1)S(1)} %get-tuple-element.27.video_in.video, bf16[1152,1152]{1,0:T(8,128)(2,1)S(1)} %get-tuple-element.30.w), custom_call_target="tpu_custom_call" | custom-call | tf_op jit(solution)/shard_map/query/pallas_call | solution.py:203
  36.9 0.0 copy-start
  36.9 2.4 %query.2 = bf16[1024,768]{1,0:T(8,128)(2,1)S(1)} custom-call(bf16[1024,1152]{1,0:T(8,128)(2,1)S(1)} %get-tuple-element.27.video_in.video, bf16[1152,1152]{1,0:T(8,128)(2,1)S(1)} %get-tuple-element.30.w), custom_call_target="tpu_custom_call" | custom-call | tf_op jit(solution)/shard_map/query/pallas_call | solution.py:203
  39.3 0.0 copy-start.2
  39.4 2.8 %partial.1 = f32[1024,1152]{1,0:T(8,128)S(1)} custom-call(bf16[1024,1152]{1,0:T(8,128)(2,1)S(1)} %get-tuple-element.27.video_in.video, bf16[1024,768]{1,0:T(8,128)(2,1)S(1)} %query.2, bf16[2,6,128,128]{3,2,1,0:T(8,128)(2,1)S(1)} %get-tuple-element.31.parts, bf16[2,6,128,128]{3,2,1,0:T(8,128)(2,1)S(1)} %collective-permute-done.other_parts, ...), custom_call_target="tpu_custom_call" | custom-call | tf_op jit(solution)/shard_map/partial/pallas_call | solution.py:260
  42.2 0.0 copy-start.1
  42.2 0.0 copy-start.3
  42.2 4.1 %latent.1 = bf16[8,160,128]{2,1,0:T(8,128)(2,1)} custom-call(f32[1024,1152]{1,0:T(8,128)S(1)} %partial.1, bf16[1024,384]{1,0:T(8,128)(2,1)S(1)} %query.3, bf16[2,3,128,128]{3,2,1,0:T(8,128)(2,1)S(1)} %get-tuple-element.40.parts, bf16[2,3,128,128]{3,2,1,0:T(8,128)(2,1)S(1)} %collective-permute-done.5.other_parts, bf16[3,64,128]{2,1,0:T(8,128)(2,1)S(1)} %round.11.carry, ...), custom_call_target="tpu_custom_call" | custom-call | tf_op jit(solution)/shard_map/latent/pallas_call | solution.py:311
  46.3 6.9 %all-to-all-start = ((bf16[8,160,128]{2,1,0:T(8,128)(2,1)}), bf16[8,160,128]{2,1,0:T(8,128)(2,1)S(1)}, u32[]{:S(2)}, u32[]{:S(2)}) async-start(bf16[8,160,128]{2,1,0:T(8,128)(2,1)} %latent.1), calls=%async_computation | async-start | bytes 655360 | tf_op jit(solution)/shard_map/all_to_all | solution.py:470
  53.2 10.9 %all-to-all-done.blocks = bf16[8,160,128]{2,1,0:T(8,128)(2,1)S(1)} async-done(((bf16[8,160,128]{2,1,0:T(8,128)(2,1)}), bf16[8,160,128]{2,1,0:T(8,128)(2,1)S(1)}, u32[]{:S(2)}, u32[]{:S(2)}) %all-to-all-start) | async-done | bytes 327712 | tf_op jit(solution)/shard_map/all_to_all | solution.py:470
  64.2 0.1 collective-permute-start.10
  64.3 1.2 %collective-permute-done.10.edge = bf16[8,20,128]{2,1,0:T(8,128)(2,1)S(1)} collective-permute-done((bf16[8,20,128]{2,1,0:T(8,128)(2,1)S(1)}, bf16[8,20,128]{2,1,0:T(8,128)(2,1)S(1)}, u32[]{:S(2)}, u32[]{:S(2)}) %collective-permute-start.10) | collective-permute-done | bytes 40992 | tf_op jit(solution)/shard_map/ppermute | solution.py:485
  65.6 3.4 %decode.1 = bf16[16,16,16,256]{3,2,1,0:T(8,128)(2,1)} custom-call(bf16[8,160,128]{2,1,0:T(8,128)(2,1)S(1)} %all-to-all-done.blocks, bf16[8,20,128]{2,1,0:T(8,128)(2,1)S(1)} %collective-permute-done.10.edge, bf16[3,3,128,256]{3,2,1,0:T(8,128)(2,1)S(1)} %copy-done.1, f32[1,256]{1,0:T(1,128)S(1)} %bitcast.8), custom_call_target="tpu_custom_call" | custom-call | tf_op jit(solution)/shard_map/decode/pallas_call | solution.py:487
  (20 shorter events, 0.3 us)
Async XLA Ops:
  8.7 3.7 %collective-permute-start = (bf16[2,6,128,128]{3,2,1,0:T(8,128)(2,1)S(1)}, bf16[2,6,128,128]{3,2,1,0:T(8,128)(2,1)S(1)}, u32[]{:S(2)}, u32[]{:S(2)}) collective-permute-start(bf16[2,6,128,128]{3,2,1,0:T(8,128)(2,1)S(1)} %get-tuple-element.31.parts), channel_id=1, source_target_pairs={{0,1},{1,0},{2,3},{3,2},{4,5},{5,4},{6,7},{7,6},{8,9},{9,8},{10,11... | collective-permute-start | bytes 1179656 | tf_op jit(solution)/shard_map/ppermute | solution.py:453
  12.3 8.2 %collective-permute-start.5 = (bf16[2,3,128,128]{3,2,1,0:T(8,128)(2,1)S(1)}, bf16[2,3,128,128]{3,2,1,0:T(8,128)(2,1)S(1)}, u32[]{:S(2)}, u32[]{:S(2)}) collective-permute-start(bf16[2,3,128,128]{3,2,1,0:T(8,128)(2,1)S(1)} %get-tuple-element.40.parts), channel_id=1, source_target_pairs={{0,1},{1,0},{2,3},{3,2},{4,5},{5,4},{6,7},{7,6},{8,9},{9,8},{10,11... | collective-permute-start | bytes 589832 | tf_op jit(solution)/shard_map/ppermute | solution.py:455
  12.5 6.0 %collective-permute-start.1 = (bf16[6,64,128]{2,1,0:T(8,128)(2,1)S(1)}, bf16[6,64,128]{2,1,0:T(8,128)(2,1)S(1)}, u32[]{:S(2)}, u32[]{:S(2)}) collective-permute-start(bf16[6,64,128]{2,1,0:T(8,128)(2,1)S(1)} %get-tuple-element.32), channel_id=1, source_target_pairs={{0,2},{2,0},{4,6},{6,4},{8,10},{10,8},{12,14},{14,12},{1,3},{3,1},... | collective-permute-start | bytes 294920 | tf_op jit(solution)/shard_map/ppermute | solution.py:431
  18.5 4.7 %collective-permute-start.2 = (bf16[6,64,128]{2,1,0:T(8,128)(2,1)S(1)}, bf16[6,64,128]{2,1,0:T(8,128)(2,1)S(1)}, u32[]{:S(2)}, u32[]{:S(2)}) collective-permute-start(bf16[6,64,128]{2,1,0:T(8,128)(2,1)S(1)} %get-tuple-element.34), channel_id=1, source_target_pairs={{0,4},{2,6},{4,0},{6,2},{8,12},{10,14},{12,8},{14,10},{1,5},{3,7},... | collective-permute-start | bytes 294920 | tf_op jit(solution)/shard_map/ppermute | solution.py:431
  20.5 7.5 %collective-permute-start.6 = (bf16[3,64,128]{2,1,0:T(8,128)(2,1)S(1)}, bf16[3,64,128]{2,1,0:T(8,128)(2,1)S(1)}, u32[]{:S(2)}, u32[]{:S(2)}) collective-permute-start(bf16[3,64,128]{2,1,0:T(8,128)(2,1)S(1)} %get-tuple-element.41), channel_id=1, source_target_pairs={{0,2},{2,0},{4,6},{6,4},{8,10},{10,8},{12,14},{14,12},{1,3},{3,1},... | collective-permute-start | bytes 147464 | tf_op jit(solution)/shard_map/ppermute | solution.py:431
  23.3 10.4 %collective-permute-start.3 = (bf16[6,64,128]{2,1,0:T(8,128)(2,1)S(1)}, bf16[6,64,128]{2,1,0:T(8,128)(2,1)S(1)}, u32[]{:S(2)}, u32[]{:S(2)}) collective-permute-start(bf16[6,64,128]{2,1,0:T(8,128)(2,1)S(1)} %get-tuple-element.37), channel_id=1, source_target_pairs={{0,8},{2,10},{4,12},{6,14},{1,9},{3,11},{5,13},{7,15},{16,24},{18,... | collective-permute-start | bytes 294920 | tf_op jit(solution)/shard_map/ppermute | solution.py:431
  28.0 4.2 %collective-permute-start.7 = (bf16[3,64,128]{2,1,0:T(8,128)(2,1)S(1)}, bf16[3,64,128]{2,1,0:T(8,128)(2,1)S(1)}, u32[]{:S(2)}, u32[]{:S(2)}) collective-permute-start(bf16[3,64,128]{2,1,0:T(8,128)(2,1)S(1)} %get-tuple-element.43), channel_id=1, source_target_pairs={{0,4},{2,6},{4,0},{6,2},{8,12},{10,14},{12,8},{14,10},{1,5},{3,7},... | collective-permute-start | bytes 147464 | tf_op jit(solution)/shard_map/ppermute | solution.py:431
  32.2 3.0 %collective-permute-start.8 = (bf16[3,64,128]{2,1,0:T(8,128)(2,1)S(1)}, bf16[3,64,128]{2,1,0:T(8,128)(2,1)S(1)}, u32[]{:S(2)}, u32[]{:S(2)}) collective-permute-start(bf16[3,64,128]{2,1,0:T(8,128)(2,1)S(1)} %get-tuple-element.46), channel_id=1, source_target_pairs={{0,8},{2,10},{4,12},{6,14},{1,9},{3,11},{5,13},{7,15},{16,24},{18,... | collective-permute-start | bytes 147464 | tf_op jit(solution)/shard_map/ppermute | solution.py:431
  33.8 5.6 %collective-permute-start.4 = (bf16[6,64,128]{2,1,0:T(8,128)(2,1)S(1)}, bf16[6,64,128]{2,1,0:T(8,128)(2,1)S(1)}, u32[]{:S(2)}, u32[]{:S(2)}) collective-permute-start(bf16[6,64,128]{2,1,0:T(8,128)(2,1)S(1)} %round.8.carry), channel_id=1, source_target_pairs={{0,1},{1,0},{2,3},{3,2},{4,5},{5,4},{6,7},{7,6},{8,9},{9,8},{10,11... | collective-permute-start | bytes 294920 | tf_op jit(solution)/shard_map/ppermute | solution.py:463
  35.3 6.9 %collective-permute-start.9 = (bf16[3,64,128]{2,1,0:T(8,128)(2,1)S(1)}, bf16[3,64,128]{2,1,0:T(8,128)(2,1)S(1)}, u32[]{:S(2)}, u32[]{:S(2)}) collective-permute-start(bf16[3,64,128]{2,1,0:T(8,128)(2,1)S(1)} %round.11.carry), channel_id=1, source_target_pairs={{0,1},{1,0},{2,3},{3,2},{4,5},{5,4},{6,7},{7,6},{8,9},{9,8},{10,11... | collective-permute-start | bytes 147464 | tf_op jit(solution)/shard_map/ppermute | solution.py:463
  36.9 2.4 %copy-start = (bf16[1152,1152]{1,0:T(8,128)(2,1)S(1)}, bf16[1152,1152]{1,0:T(8,128)(2,1)}, u32[]{:S(2)}) copy-start(bf16[1152,1152]{1,0:T(8,128)(2,1)} %w_out.3) | copy-start | bytes 7962628
  39.3 2.9 %copy-start.2 = (bf16[1152,128]{1,0:T(8,128)(2,1)S(1)}, bf16[1152,128]{1,0:T(8,128)(2,1)}, u32[]{:S(2)}) copy-start(bf16[1152,128]{1,0:T(8,128)(2,1)} %w_latent.1) | copy-start | bytes 884740
  42.2 23.4 %copy-start.1 = (bf16[3,3,128,256]{3,2,1,0:T(8,128)(2,1)S(1)}, bf16[3,3,128,256]{3,2,1,0:T(8,128)(2,1)}, u32[]{:S(2)}) copy-start(bf16[3,3,128,256]{3,2,1,0:T(8,128)(2,1)} %weight.1) | copy-start | bytes 1769476
  42.2 23.4 %copy-start.3 = (f32[256]{0:T(256)S(1)}, f32[256]{0:T(256)}, u32[]{:S(2)}) copy-start(f32[256]{0:T(256)} %param.15) | copy-start | bytes 3076
  46.3 17.8 %all-to-all-start = ((bf16[8,160,128]{2,1,0:T(8,128)(2,1)}), bf16[8,160,128]{2,1,0:T(8,128)(2,1)S(1)}, u32[]{:S(2)}, u32[]{:S(2)}) async-start(bf16[8,160,128]{2,1,0:T(8,128)(2,1)} %latent.1), calls=%async_computation | async-start | bytes 655360 | tf_op jit(solution)/shard_map/all_to_all | solution.py:470
  64.2 1.3 %collective-permute-start.10 = (bf16[8,20,128]{2,1,0:T(8,128)(2,1)S(1)}, bf16[8,20,128]{2,1,0:T(8,128)(2,1)S(1)}, u32[]{:S(2)}, u32[]{:S(2)}) collective-permute-start(bf16[8,20,128]{2,1,0:T(8,128)(2,1)S(1)} %maximum_select_fusion), channel_id=1, source_target_pairs={{0,1},{1,0},{2,3},{3,2},{4,5},{5,4},{6,7},{7,6},{8,9},{9,8},{10,11... | collective-permute-start | bytes 122888 | tf_op jit(solution)/shard_map/ppermute | solution.py:485

commit v3 on v2

--- a/solution.py
+++ b/solution.py
@@ -38,76 +38,63 @@
     return jnp.where(x > 0.0, x + 1.0, jnp.exp(jnp.minimum(x, 0.0)))
 
 
-def states_kernel(frames, first, heads, later, fetched, video_in, wk_hbm, wv_hbm, *refs):
-    refs = list(refs)
-    wq_hbm = refs.pop(0) if fetched else None
-    parts_out = refs.pop(0)
+def states_kernel(frames, heads, fetched, video_in, wk_hbm, wv_hbm, *refs):
     if fetched:
-        wq_out, key, value, wq_sem = refs
+        parts_out, key, value = refs
         video, wk, wv = video_in, wk_hbm, wv_hbm
+        late = []
     else:
-        video, wk_out, wv_out, wk, wv, key, value, wk_sem, wv_sem, video_sem, late_sem = refs
+        (wq_hbm, parts_out, video, wk_out, wv_out, wq_out, wk, wv, key, value,
+         wk_sem, wv_sem, video_sem, late_sem) = refs
+        rest = wk_out.shape[1]
+        source = pl.ds(heads * HEAD, rest)
+        late = [
+            pltpu.make_async_copy(wq_hbm, wq_out, late_sem.at[0]),
+            pltpu.make_async_copy(wk_hbm.at[:, source], wk_out, late_sem.at[1]),
+            pltpu.make_async_copy(wv_hbm.at[:, source], wv_out, late_sem.at[2]),
+        ]
     per = video.shape[0] // frames
-    blocks = 2 * frames
-    rows_of = video.shape[0] // blocks
 
     def weight_copies(h):
-        source = pl.ds(pl.multiple_of((first + h) * HEAD, HEAD), HEAD)
         cols = pl.ds(pl.multiple_of(h * HEAD, HEAD), HEAD)
         return (
-            pltpu.make_async_copy(wk_hbm.at[:, source], wk.at[:, cols], wk_sem.at[h]),
-            pltpu.make_async_copy(wv_hbm.at[:, source], wv.at[:, cols], wv_sem.at[h]),
+            pltpu.make_async_copy(wk_hbm.at[:, cols], wk.at[:, cols], wk_sem.at[h]),
+            pltpu.make_async_copy(wv_hbm.at[:, cols], wv.at[:, cols], wv_sem.at[h]),
         )
 
-    def video_copy(i):
-        rows = pl.ds(i * rows_of, rows_of)
-        return pltpu.make_async_copy(video_in.at[rows], video.at[rows], video_sem.at[i])
-
-    def project(h, rows, both):
-        kv = matmul(video[rows, :], both)
-        key[h, rows, :] = features(kv[:, :HEAD]).astype(BF16)
-        value[h, rows, :] = kv[:, HEAD:].astype(BF16)
-
-    def weights(h):
-        cols = pl.ds(pl.multiple_of(h * HEAD, HEAD), HEAD)
-        return jnp.concatenate([wk[:, cols], wv[:, cols]], axis=1)
+    def video_copy(f):
+        rows = pl.ds(f * per, per)
+        return pltpu.make_async_copy(video_in.at[rows], video.at[rows], video_sem.at[f])
+
+    if not fetched:
+        soon = min(2, heads)
+        for h in range(soon):
+            for c in weight_copies(h):
+                c.start()
+        for f in range(frames):
+            video_copy(f).start()
+        for f in range(frames):
+            video_copy(f).wait()
+        for h in range(soon, heads):
+            for c in weight_copies(h):
+                c.start()
+        for c in late:
+            c.start()
 
     def one_head(h, carry):
         if not fetched:
             for c in weight_copies(h):
                 c.wait()
-        both = weights(h)
-        for f in range(frames):
-            project(h, slice(f * per, (f + 1) * per), both)
+        cols = pl.ds(pl.multiple_of(h * HEAD, HEAD), HEAD)
+        both = jnp.concatenate([wk[:, cols], wv[:, cols]], axis=1)
+        for f in range(frames):
+            rows = slice(f * per, (f + 1) * per)
+            kv = matmul(video[rows, :], both)
+            key[h, rows, :] = features(kv[:, :HEAD]).astype(BF16)
+            value[h, rows, :] = kv[:, HEAD:].astype(BF16)
         return carry
 
-    if fetched:
-        late = [pltpu.make_async_copy(wq_hbm, wq_out, wq_sem)]
-        late[0].start()
-        lax.fori_loop(0, heads, one_head, 0)
-    else:
-        for c in weight_copies(0):
-            c.start()
-        for i in range(blocks):
-            video_copy(i).start()
-        for c in weight_copies(0):
-            c.wait()
-        both = weights(0)
-        for i in range(blocks):
-            video_copy(i).wait()
-            if i == 0:
-                for h in range(1, heads):
-                    for c in weight_copies(h):
-                        c.start()
-            project(0, slice(i * rows_of, (i + 1) * rows_of), both)
-        source = pl.ds((first + heads) * HEAD, later * HEAD)
-        late = [
-            pltpu.make_async_copy(wk_hbm.at[:, source], wk_out, late_sem.at[0]),
-            pltpu.make_async_copy(wv_hbm.at[:, source], wv_out, late_sem.at[1]),
-        ]
-        for c in late:
-            c.start()
-        lax.fori_loop(1, heads, one_head, 0)
+    lax.fori_loop(0, heads, one_head, 0)
 
     for h in range(heads):
         for f in range(frames):
@@ -121,19 +108,20 @@
         c.wait()
 
 
-def first_states(video, wk, wv, frames, heads, later):
+def first_states(video, wk, wv, wq, frames, heads):
     tokens, d = video.shape
     width = heads * HEAD
     return pl.pallas_call(
-        functools.partial(states_kernel, frames, 0, heads, later, False),
+        functools.partial(states_kernel, frames, heads, False),
         out_shape=[
             shape((frames, heads, HEAD, HEAD), BF16),
             shape((tokens, d), BF16),
-            shape((d, later * HEAD), BF16),
-            shape((d, later * HEAD), BF16),
+            shape((d, d - width), BF16),
+            shape((d, d - width), BF16),
+            shape((d, d), BF16),
         ],
-        in_specs=[IN_HBM] * 3,
-        out_specs=[IN_VMEM] * 4,
+        in_specs=[IN_HBM] * 4,
+        out_specs=[IN_VMEM] * 5,
         scratch_shapes=[
             pltpu.VMEM((d, width), BF16),
             pltpu.VMEM((d, width), BF16),
@@ -141,33 +129,29 @@
             pltpu.VMEM((heads, tokens, HEAD), BF16),
             pltpu.SemaphoreType.DMA((heads,)),
             pltpu.SemaphoreType.DMA((heads,)),
-            pltpu.SemaphoreType.DMA((2 * frames,)),
-            pltpu.SemaphoreType.DMA((2,)),
+            pltpu.SemaphoreType.DMA((frames,)),
+            pltpu.SemaphoreType.DMA((3,)),
         ],
         name="states",
         compiler_params=params(20),
-    )(in_hbm(video), in_hbm(wk), in_hbm(wv))
-
-
-def second_states(video, wk, wv, wq, frames):
+    )(in_hbm(video), in_hbm(wk), in_hbm(wv), in_hbm(wq))
+
+
+def second_states(video, wk, wv, frames):
     tokens, _ = video.shape
     heads = wk.shape[1] // HEAD
     return pl.pallas_call(
-        functools.partial(states_kernel, frames, 0, heads, 0, True),
-        out_shape=[
-            shape((frames, heads, HEAD, HEAD), BF16),
-            shape(wq.shape, BF16),
-        ],
-        in_specs=[IN_VMEM] * 3 + [IN_HBM],
-        out_specs=[IN_VMEM] * 2,
+        functools.partial(states_kernel, frames, heads, True),
+        out_shape=shape((frames, heads, HEAD, HEAD), BF16),
+        in_specs=[IN_VMEM] * 3,
+        out_specs=IN_VMEM,
         scratch_shapes=[
             pltpu.VMEM((heads, tokens, HEAD), BF16),
             pltpu.VMEM((heads, tokens, HEAD), BF16),
-            pltpu.SemaphoreType.DMA,
         ],
         name="states",
         compiler_params=params(20),
-    )(video, wk, wv, in_hbm(wq))
+    )(video, wk, wv)
 
 
 def total_call(parts, other_parts):
@@ -447,15 +431,18 @@
     own = columns // tiles
     flat = video.reshape(-1, d)
     heads = d // HEAD
-    split = heads // 3 * 2
-    rest = heads - split
-    parts_a, near, wk_b, wv_b = first_states(flat, w_key, w_value, frames, split, rest)
+    split = heads - heads // 2
+    parts_a, near, wk_b, wv_b, near_query = first_states(
+        flat, w_key, w_value, w_query, frames, split
+    )
     other_a = lax.ppermute(parts_a, "space", SWAP)
-    parts_b, near_query = second_states(near, wk_b, wv_b, w_query, frames)
+    parts_b = second_states(near, wk_b, wv_b, frames)
     other_b = lax.ppermute(parts_b, "space", SWAP)
 
     ready = {}
-    for name, first, parts, other in (("a", 0, parts_a, other_a), ("b", split, parts_b, other_b)):
+    for name, first, parts, other in (
+        ("a", 0, parts_a, other_a), ("b", split, parts_b, other_b),
+    ):
         count = parts.shape[1]
         total, sent = total_call(parts, other)
         query = query_call(near, near_query, first * HEAD, count * HEAD)
@@ -464,9 +451,7 @@
         ready[name] = (query, parts, other, carry, other_carry)
 
     partial = partial_call(near, ready["a"], w_out, frames)
-    blocks = latent_call(
-        partial, ready["b"], w_out, w_latent, frames, columns, tiles
-    )
+    blocks = latent_call(partial, ready["b"], w_out, w_latent, frames, columns, tiles)
     blocks = lax.all_to_all(blocks, "tm", 0, 0, tiled=True)
     return decode(blocks, conv_weight, conv_bias, frames, grid_rows, own, tiles)
 

time: 69.2 us -> 65.5 us (0.947)
  waiting for transfers between devices: 20.2 us -> 17.1 us
  Pallas kernels: 26.2 us -> 25.4 us
    ppermute x6, waiting for transfers between devices: 8.09 us -> 4.89 us  [prefix_rounds(): got = lax.ppermute(sent, 'tm', pairs)]
    all_to_all x1, starting transfers between devices: 6.91 us -> 8.19 us  [body(): blocks = lax.all_to_all(blocks, 'tm', 0, 0, tiled=True)]
    ppermute x6, starting transfers between devices: 14.3 us -> 13.5 us  [prefix_rounds(): got = lax.ppermute(sent, 'tm', pairs)]
    pallas_call x2, Pallas kernels: 11.7 us -> 10.9 us  [the longest x1 7.03 us: first_states(): pl.pallas_call(functools.partial(states_kernel, frames, heads, False), ou...]
  transfers between devices with their start and end apart: 12 -> 12, of which waited for: 6 -> 6; matrix products, arithmetic and copies ran while one was open for 0% -> 0% of each run, Pallas kernels for 15% -> 16%
where the time goes in v3:
time: 65.5 us; the launch traced here: 65.3 us
  Pallas kernels  25.4 us (39%)
  starting transfers between devices  22.5 us (34%)
  waiting for transfers between devices  17.1 us (26%)
    ppermute x6, starting transfers between devices, prefix_rounds(): got = lax.ppermute(sent, 'tm', pairs)  13.5 us
    all_to_all x1, waiting for transfers between devices, body(): blocks = lax.all_to_all(blocks, 'tm', 0, 0, tiled=True)  10.9 us
    all_to_all x1, starting transfers between devices, body(): blocks = lax.all_to_all(blocks, 'tm', 0, 0, tiled=True)  8.19 us
    pallas_call x1, Pallas kernels, first_states(): pl.pallas_call(functools.partial(states_kernel, frames, heads, False), ou...  7.03 us
    ppermute x6, waiting for transfers between devices, prefix_rounds(): got = lax.ppermute(sent, 'tm', pairs)  4.89 us
    pallas_call x1, Pallas kernels, latent_call(): pl.pallas_call(functools.partial(latent_kernel, frames, columns, tiles),...  4.23 us
    pallas_call x1, Pallas kernels, second_states(): pl.pallas_call(functools.partial(states_kernel, frames, heads, True), out...  3.92 us
    pallas_call x2, Pallas kernels, query_call(): pl.pallas_call(kernel, out_shape=shape((video.shape[0], width), BF16), in...  3.83 us
  transfers between devices with their start and end apart: 12, of which 6 were waited for; matrix products, arithmetic and copies ran while one was open for 0% of the time, Pallas kernels for 16%

profile of v3, /device:TPU:0, one launch (start us, length us, event | category | flops | bytes accessed | tf_op | source)
XLA Modules:
  0.0 65.3 jit_solution(14703621950966995548)
XLA Ops:
  0.0 7.0 %states.2 = (bf16[2,5,128,128]{3,2,1,0:T(8,128)(2,1)S(1)}, bf16[1024,1152]{1,0:T(8,128)(2,1)S(1)}, bf16[1152,512]{1,0:T(8,128)(2,1)S(1)}, bf16[1152,512]{1,0:T(8,128)(2,1)S(1)}, bf16[1152,1152]{1,0:T(8,128)(2,1)S(1)}) custom-call(bf16[1024,1152]{1,0:T(8,128)(2,1)} %bitcast.9, bf16[1152,1152]{1,0:T(8,128)(2,1)} %wk_hbm.1, bf16[1152,1152]{1,0:T(8,128)(2,1)} %wv_hbm.1, ...), custom_call_target="tpu_custom_call" | custom-call | tf_op jit(solution)/shard_map/states/pallas_call | solution.py:114
  7.0 0.6 collective-permute-start
  7.6 3.9 %states.3.parts = bf16[2,4,128,128]{3,2,1,0:T(8,128)(2,1)S(1)} custom-call(bf16[1024,1152]{1,0:T(8,128)(2,1)S(1)} %get-tuple-element.26.video.video_in, bf16[1152,512]{1,0:T(8,128)(2,1)S(1)} %get-tuple-element.37.wk_hbm, bf16[1152,512]{1,0:T(8,128)(2,1)S(1)} %get-tuple-element.38.wv_hbm), custom_call_target="tpu_custom_call" | custom-call | tf_op jit(solution)/shard_map/states/pallas_call | solution.py:143
  11.5 0.1 collective-permute-start.5
  11.6 0.1 total.2
  11.7 3.0 %collective-permute-start.1 = (bf16[5,64,128]{2,1,0:T(8,128)(2,1)S(1)}, bf16[5,64,128]{2,1,0:T(8,128)(2,1)S(1)}, u32[]{:S(2)}, u32[]{:S(2)}) collective-permute-start(bf16[5,64,128]{2,1,0:T(8,128)(2,1)S(1)} %get-tuple-element.29), channel_id=1, source_target_pairs={{0,2},{2,0},{4,6},{6,4},{8,10},{10,8},{12,14},{14,12},{1,3},{3,1},... | collective-permute-start | bytes 245768 | tf_op jit(solution)/shard_map/ppermute | solution.py:415
  14.8 0.1 total.3
  14.8 1.1 %collective-permute-start.6 = (bf16[4,64,128]{2,1,0:T(8,128)(2,1)S(1)}, bf16[4,64,128]{2,1,0:T(8,128)(2,1)S(1)}, u32[]{:S(2)}, u32[]{:S(2)}) collective-permute-start(bf16[4,64,128]{2,1,0:T(8,128)(2,1)S(1)} %get-tuple-element.39), channel_id=1, source_target_pairs={{0,2},{2,0},{4,6},{6,4},{8,10},{10,8},{12,14},{14,12},{1,3},{3,1},... | collective-permute-start | bytes 196616 | tf_op jit(solution)/shard_map/ppermute | solution.py:415
  15.9 1.6 %collective-permute-done.1.got = bf16[5,64,128]{2,1,0:T(8,128)(2,1)S(1)} collective-permute-done((bf16[5,64,128]{2,1,0:T(8,128)(2,1)S(1)}, bf16[5,64,128]{2,1,0:T(8,128)(2,1)S(1)}, u32[]{:S(2)}, u32[]{:S(2)}) %collective-permute-start.1) | collective-permute-done | bytes 81952 | tf_op jit(solution)/shard_map/ppermute | solution.py:415
  17.6 2.1 %collective-permute-start.2 = (bf16[5,64,128]{2,1,0:T(8,128)(2,1)S(1)}, bf16[5,64,128]{2,1,0:T(8,128)(2,1)S(1)}, u32[]{:S(2)}, u32[]{:S(2)}) collective-permute-start(bf16[5,64,128]{2,1,0:T(8,128)(2,1)S(1)} %get-tuple-element.31), channel_id=1, source_target_pairs={{0,4},{2,6},{4,0},{6,2},{8,12},{10,14},{12,8},{14,10},{1,5},{3,7},... | collective-permute-start | bytes 245768 | tf_op jit(solution)/shard_map/ppermute | solution.py:415
  19.7 1.1 %collective-permute-start.7 = (bf16[4,64,128]{2,1,0:T(8,128)(2,1)S(1)}, bf16[4,64,128]{2,1,0:T(8,128)(2,1)S(1)}, u32[]{:S(2)}, u32[]{:S(2)}) collective-permute-start(bf16[4,64,128]{2,1,0:T(8,128)(2,1)S(1)} %get-tuple-element.41), channel_id=1, source_target_pairs={{0,4},{2,6},{4,0},{6,2},{8,12},{10,14},{12,8},{14,10},{1,5},{3,7},... | collective-permute-start | bytes 196616 | tf_op jit(solution)/shard_map/ppermute | solution.py:415
  20.8 1.5 %collective-permute-done.2.got = bf16[5,64,128]{2,1,0:T(8,128)(2,1)S(1)} collective-permute-done((bf16[5,64,128]{2,1,0:T(8,128)(2,1)S(1)}, bf16[5,64,128]{2,1,0:T(8,128)(2,1)S(1)}, u32[]{:S(2)}, u32[]{:S(2)}) %collective-permute-start.2) | collective-permute-done | bytes 81952 | tf_op jit(solution)/shard_map/ppermute | solution.py:415
  22.3 4.7 %collective-permute-start.3 = (bf16[5,64,128]{2,1,0:T(8,128)(2,1)S(1)}, bf16[5,64,128]{2,1,0:T(8,128)(2,1)S(1)}, u32[]{:S(2)}, u32[]{:S(2)}) collective-permute-start(bf16[5,64,128]{2,1,0:T(8,128)(2,1)S(1)} %get-tuple-element.34), channel_id=1, source_target_pairs={{0,8},{2,10},{4,12},{6,14},{1,9},{3,11},{5,13},{7,15},{16,24},{18,... | collective-permute-start | bytes 245768 | tf_op jit(solution)/shard_map/ppermute | solution.py:415
  27.1 0.0 collective-permute-done.7.got
  27.1 1.4 %collective-permute-start.8 = (bf16[4,64,128]{2,1,0:T(8,128)(2,1)S(1)}, bf16[4,64,128]{2,1,0:T(8,128)(2,1)S(1)}, u32[]{:S(2)}, u32[]{:S(2)}) collective-permute-start(bf16[4,64,128]{2,1,0:T(8,128)(2,1)S(1)} %get-tuple-element.44), channel_id=1, source_target_pairs={{0,8},{2,10},{4,12},{6,14},{1,9},{3,11},{5,13},{7,15},{16,24},{18,... | collective-permute-start | bytes 196616 | tf_op jit(solution)/shard_map/ppermute | solution.py:415
  28.6 0.5 collective-permute-done.3.got
  29.2 0.1 collective-permute-start.4
  29.2 1.2 %collective-permute-done.8.got = bf16[4,64,128]{2,1,0:T(8,128)(2,1)S(1)} collective-permute-done((bf16[4,64,128]{2,1,0:T(8,128)(2,1)S(1)}, bf16[4,64,128]{2,1,0:T(8,128)(2,1)S(1)}, u32[]{:S(2)}, u32[]{:S(2)}) %collective-permute-start.8) | collective-permute-done | bytes 65568 | tf_op jit(solution)/shard_map/ppermute | solution.py:415
  30.5 0.1 collective-permute-start.9
  30.6 1.7 %query.3 = bf16[1024,512]{1,0:T(8,128)(2,1)S(1)} custom-call(bf16[1024,1152]{1,0:T(8,128)(2,1)S(1)} %get-tuple-element.26.video.video_in, bf16[1152,1152]{1,0:T(8,128)(2,1)S(1)} %get-tuple-element.27.w), custom_call_target="tpu_custom_call" | custom-call | tf_op jit(solution)/shard_map/query/pallas_call | solution.py:187
  32.3 0.0 copy-start
  32.3 2.1 %query.2 = bf16[1024,640]{1,0:T(8,128)(2,1)S(1)} custom-call(bf16[1024,1152]{1,0:T(8,128)(2,1)S(1)} %get-tuple-element.26.video.video_in, bf16[1152,1152]{1,0:T(8,128)(2,1)S(1)} %get-tuple-element.27.w), custom_call_target="tpu_custom_call" | custom-call | tf_op jit(solution)/shard_map/query/pallas_call | solution.py:187
  34.4 0.0 copy-start.2
  34.5 2.6 %partial.1 = f32[1024,1152]{1,0:T(8,128)S(1)} custom-call(bf16[1024,1152]{1,0:T(8,128)(2,1)S(1)} %get-tuple-element.26.video.video_in, bf16[1024,640]{1,0:T(8,128)(2,1)S(1)} %query.2, bf16[2,5,128,128]{3,2,1,0:T(8,128)(2,1)S(1)} %get-tuple-element.28.parts, bf16[2,5,128,128]{3,2,1,0:T(8,128)(2,1)S(1)} %collective-permute-done.other_parts, ...), custom_call_target="tpu_custom_call" | custom-call | tf_op jit(solution)/shard_map/partial/pallas_call | solution.py:244
  37.1 0.0 copy-start.1
  37.1 0.0 copy-start.3
  37.2 4.2 %latent.1 = bf16[8,160,128]{2,1,0:T(8,128)(2,1)} custom-call(f32[1024,1152]{1,0:T(8,128)S(1)} %partial.1, bf16[1024,512]{1,0:T(8,128)(2,1)S(1)} %query.3, bf16[2,4,128,128]{3,2,1,0:T(8,128)(2,1)S(1)} %states.3.parts, bf16[2,4,128,128]{3,2,1,0:T(8,128)(2,1)S(1)} %collective-permute-done.5.other_parts, bf16[4,64,128]{2,1,0:T(8,128)(2,1)S(1)} %round.11.carry, ...), custom_call_target="tpu_custom_call" | custom-call | tf_op jit(solution)/shard_map/latent/pallas_call | solution.py:295
  41.4 8.2 %all-to-all-start = ((bf16[8,160,128]{2,1,0:T(8,128)(2,1)}), bf16[8,160,128]{2,1,0:T(8,128)(2,1)S(1)}, u32[]{:S(2)}, u32[]{:S(2)}) async-start(bf16[8,160,128]{2,1,0:T(8,128)(2,1)} %latent.1), calls=%async_computation | async-start | bytes 655360 | tf_op jit(solution)/shard_map/all_to_all | solution.py:455
  49.6 10.9 %all-to-all-done.blocks = bf16[8,160,128]{2,1,0:T(8,128)(2,1)S(1)} async-done(((bf16[8,160,128]{2,1,0:T(8,128)(2,1)}), bf16[8,160,128]{2,1,0:T(8,128)(2,1)S(1)}, u32[]{:S(2)}, u32[]{:S(2)}) %all-to-all-start) | async-done | bytes 327712 | tf_op jit(solution)/shard_map/all_to_all | solution.py:455
  60.6 0.1 collective-permute-start.10
  60.7 1.2 %collective-permute-done.10.edge = bf16[8,20,128]{2,1,0:T(8,128)(2,1)S(1)} collective-permute-done((bf16[8,20,128]{2,1,0:T(8,128)(2,1)S(1)}, bf16[8,20,128]{2,1,0:T(8,128)(2,1)S(1)}, u32[]{:S(2)}, u32[]{:S(2)}) %collective-permute-start.10) | collective-permute-done | bytes 40992 | tf_op jit(solution)/shard_map/ppermute | solution.py:470
  61.9 3.4 %decode.1 = bf16[16,16,16,256]{3,2,1,0:T(8,128)(2,1)} custom-call(bf16[8,160,128]{2,1,0:T(8,128)(2,1)S(1)} %all-to-all-done.blocks, bf16[8,20,128]{2,1,0:T(8,128)(2,1)S(1)} %collective-permute-done.10.edge, bf16[3,3,128,256]{3,2,1,0:T(8,128)(2,1)S(1)} %copy-done.1, f32[1,256]{1,0:T(1,128)S(1)} %bitcast.8), custom_call_target="tpu_custom_call" | custom-call | tf_op jit(solution)/shard_map/decode/pallas_call | solution.py:472
  (20 shorter events, 0.3 us)
Async XLA Ops:
  7.0 4.6 %collective-permute-start = (bf16[2,5,128,128]{3,2,1,0:T(8,128)(2,1)S(1)}, bf16[2,5,128,128]{3,2,1,0:T(8,128)(2,1)S(1)}, u32[]{:S(2)}, u32[]{:S(2)}) collective-permute-start(bf16[2,5,128,128]{3,2,1,0:T(8,128)(2,1)S(1)} %get-tuple-element.28.parts), channel_id=1, source_target_pairs={{0,1},{1,0},{2,3},{3,2},{4,5},{5,4},{6,7},{7,6},{8,9},{9,8},{10,11... | collective-permute-start | bytes 983048 | tf_op jit(solution)/shard_map/ppermute | solution.py:438
  11.5 3.2 %collective-permute-start.5 = (bf16[2,4,128,128]{3,2,1,0:T(8,128)(2,1)S(1)}, bf16[2,4,128,128]{3,2,1,0:T(8,128)(2,1)S(1)}, u32[]{:S(2)}, u32[]{:S(2)}) collective-permute-start(bf16[2,4,128,128]{3,2,1,0:T(8,128)(2,1)S(1)} %states.3.parts), channel_id=1, source_target_pairs={{0,1},{1,0},{2,3},{3,2},{4,5},{5,4},{6,7},{7,6},{8,9},{9,8},{10,11... | collective-permute-start | bytes 786440 | tf_op jit(solution)/shard_map/ppermute | solution.py:440
  11.7 5.8 %collective-permute-start.1 = (bf16[5,64,128]{2,1,0:T(8,128)(2,1)S(1)}, bf16[5,64,128]{2,1,0:T(8,128)(2,1)S(1)}, u32[]{:S(2)}, u32[]{:S(2)}) collective-permute-start(bf16[5,64,128]{2,1,0:T(8,128)(2,1)S(1)} %get-tuple-element.29), channel_id=1, source_target_pairs={{0,2},{2,0},{4,6},{6,4},{8,10},{10,8},{12,14},{14,12},{1,3},{3,1},... | collective-permute-start | bytes 245768 | tf_op jit(solution)/shard_map/ppermute | solution.py:415
  14.8 4.9 %collective-permute-start.6 = (bf16[4,64,128]{2,1,0:T(8,128)(2,1)S(1)}, bf16[4,64,128]{2,1,0:T(8,128)(2,1)S(1)}, u32[]{:S(2)}, u32[]{:S(2)}) collective-permute-start(bf16[4,64,128]{2,1,0:T(8,128)(2,1)S(1)} %get-tuple-element.39), channel_id=1, source_target_pairs={{0,2},{2,0},{4,6},{6,4},{8,10},{10,8},{12,14},{14,12},{1,3},{3,1},... | collective-permute-start | bytes 196616 | tf_op jit(solution)/shard_map/ppermute | solution.py:415
  17.6 4.7 %collective-permute-start.2 = (bf16[5,64,128]{2,1,0:T(8,128)(2,1)S(1)}, bf16[5,64,128]{2,1,0:T(8,128)(2,1)S(1)}, u32[]{:S(2)}, u32[]{:S(2)}) collective-permute-start(bf16[5,64,128]{2,1,0:T(8,128)(2,1)S(1)} %get-tuple-element.31), channel_id=1, source_target_pairs={{0,4},{2,6},{4,0},{6,2},{8,12},{10,14},{12,8},{14,10},{1,5},{3,7},... | collective-permute-start | bytes 245768 | tf_op jit(solution)/shard_map/ppermute | solution.py:415
  19.7 7.4 %collective-permute-start.7 = (bf16[4,64,128]{2,1,0:T(8,128)(2,1)S(1)}, bf16[4,64,128]{2,1,0:T(8,128)(2,1)S(1)}, u32[]{:S(2)}, u32[]{:S(2)}) collective-permute-start(bf16[4,64,128]{2,1,0:T(8,128)(2,1)S(1)} %get-tuple-element.41), channel_id=1, source_target_pairs={{0,4},{2,6},{4,0},{6,2},{8,12},{10,14},{12,8},{14,10},{1,5},{3,7},... | collective-permute-start | bytes 196616 | tf_op jit(solution)/shard_map/ppermute | solution.py:415
  22.3 6.8 %collective-permute-start.3 = (bf16[5,64,128]{2,1,0:T(8,128)(2,1)S(1)}, bf16[5,64,128]{2,1,0:T(8,128)(2,1)S(1)}, u32[]{:S(2)}, u32[]{:S(2)}) collective-permute-start(bf16[5,64,128]{2,1,0:T(8,128)(2,1)S(1)} %get-tuple-element.34), channel_id=1, source_target_pairs={{0,8},{2,10},{4,12},{6,14},{1,9},{3,11},{5,13},{7,15},{16,24},{18,... | collective-permute-start | bytes 245768 | tf_op jit(solution)/shard_map/ppermute | solution.py:415
  27.1 3.3 %collective-permute-start.8 = (bf16[4,64,128]{2,1,0:T(8,128)(2,1)S(1)}, bf16[4,64,128]{2,1,0:T(8,128)(2,1)S(1)}, u32[]{:S(2)}, u32[]{:S(2)}) collective-permute-start(bf16[4,64,128]{2,1,0:T(8,128)(2,1)S(1)} %get-tuple-element.44), channel_id=1, source_target_pairs={{0,8},{2,10},{4,12},{6,14},{1,9},{3,11},{5,13},{7,15},{16,24},{18,... | collective-permute-start | bytes 196616 | tf_op jit(solution)/shard_map/ppermute | solution.py:415
  29.2 5.3 %collective-permute-start.4 = (bf16[5,64,128]{2,1,0:T(8,128)(2,1)S(1)}, bf16[5,64,128]{2,1,0:T(8,128)(2,1)S(1)}, u32[]{:S(2)}, u32[]{:S(2)}) collective-permute-start(bf16[5,64,128]{2,1,0:T(8,128)(2,1)S(1)} %round.8.carry), channel_id=1, source_target_pairs={{0,1},{1,0},{2,3},{3,2},{4,5},{5,4},{6,7},{7,6},{8,9},{9,8},{10,11... | collective-permute-start | bytes 245768 | tf_op jit(solution)/shard_map/ppermute | solution.py:450
  30.5 6.6 %collective-permute-start.9 = (bf16[4,64,128]{2,1,0:T(8,128)(2,1)S(1)}, bf16[4,64,128]{2,1,0:T(8,128)(2,1)S(1)}, u32[]{:S(2)}, u32[]{:S(2)}) collective-permute-start(bf16[4,64,128]{2,1,0:T(8,128)(2,1)S(1)} %round.11.carry), channel_id=1, source_target_pairs={{0,1},{1,0},{2,3},{3,2},{4,5},{5,4},{6,7},{7,6},{8,9},{9,8},{10,11... | collective-permute-start | bytes 196616 | tf_op jit(solution)/shard_map/ppermute | solution.py:450
  32.3 2.2 %copy-start = (bf16[1152,1152]{1,0:T(8,128)(2,1)S(1)}, bf16[1152,1152]{1,0:T(8,128)(2,1)}, u32[]{:S(2)}) copy-start(bf16[1152,1152]{1,0:T(8,128)(2,1)} %w_out.3) | copy-start | bytes 7962628
  34.4 2.7 %copy-start.2 = (bf16[1152,128]{1,0:T(8,128)(2,1)S(1)}, bf16[1152,128]{1,0:T(8,128)(2,1)}, u32[]{:S(2)}) copy-start(bf16[1152,128]{1,0:T(8,128)(2,1)} %w_latent.1) | copy-start | bytes 884740
  37.1 24.8 %copy-start.1 = (bf16[3,3,128,256]{3,2,1,0:T(8,128)(2,1)S(1)}, bf16[3,3,128,256]{3,2,1,0:T(8,128)(2,1)}, u32[]{:S(2)}) copy-start(bf16[3,3,128,256]{3,2,1,0:T(8,128)(2,1)} %weight.1) | copy-start | bytes 1769476
  37.1 24.8 %copy-start.3 = (f32[256]{0:T(256)S(1)}, f32[256]{0:T(256)}, u32[]{:S(2)}) copy-start(f32[256]{0:T(256)} %param.15) | copy-start | bytes 3076
  41.4 19.1 %all-to-all-start = ((bf16[8,160,128]{2,1,0:T(8,128)(2,1)}), bf16[8,160,128]{2,1,0:T(8,128)(2,1)S(1)}, u32[]{:S(2)}, u32[]{:S(2)}) async-start(bf16[8,160,128]{2,1,0:T(8,128)(2,1)} %latent.1), calls=%async_computation | async-start | bytes 655360 | tf_op jit(solution)/shard_map/all_to_all | solution.py:455
  60.6 1.3 %collective-permute-start.10 = (bf16[8,20,128]{2,1,0:T(8,128)(2,1)S(1)}, bf16[8,20,128]{2,1,0:T(8,128)(2,1)S(1)}, u32[]{:S(2)}, u32[]{:S(2)}) collective-permute-start(bf16[8,20,128]{2,1,0:T(8,128)(2,1)S(1)} %maximum_select_fusion), channel_id=1, source_target_pairs={{0,1},{1,0},{2,3},{3,2},{4,5},{5,4},{6,7},{7,6},{8,9},{9,8},{10,11... | collective-permute-start | bytes 122888 | tf_op jit(solution)/shard_map/ppermute | solution.py:470

commit v4 on v3

--- a/solution.py
+++ b/solution.py
@@ -264,7 +264,7 @@
         rows = slice(f * per, (f + 1) * per)
         summed = partial[rows, :] + matmul(head_out[rows, :], w_out[d - width :, :])
         scale = lax.rsqrt(jnp.mean(summed * summed, axis=1, keepdims=True) + EPS)
-        latent[rows, :] = matmul((summed * scale).astype(BF16), w_latent[...])
+        latent[rows, :] = matmul(summed.astype(BF16), w_latent[...]) * scale
 
     own = columns // tiles
     grid_rows = per // columns
@@ -308,8 +308,8 @@
 
 
 def decode_kernel(
-    frames, tiles, grid_rows, own, blocks, edge, weight, bias,
-    out, left, middle, right, taps, wide,
+    frames, tiles, grid_rows, own, chunk, blocks, edge, weight, bias,
+    out, left, middle, right, taps, wide, staged, sem,
 ):
     group = frames * own
     main = grid_rows * group
@@ -354,24 +354,37 @@
                 for j, cols in enumerate(row_sets[b]):
                     tap = sum(w[r, c] for r in rows for c in cols)
                     at = (2 * i + j) * channels
-                    taps[2 * a + b, at : at + channels, :] = tap.astype(BF16)
+                    taps[2 * a + b, at : at + channels, :] = (0.5 * tap).astype(BF16)
 
     views = ((left, middle), (middle, right))
     total = tiles * group
-    for a in range(2):
-        for b in range(2):
-            lhs = jnp.concatenate(
-                [v[a + i : a + i + grid_rows].reshape(grid_rows * total, channels)
-                 for i in range(2) for v in views[b]], axis=1
-            )
-            mapped = matmul(lhs, taps[2 * a + b]) + bias[...]
-            value = 0.5 * mapped * (1.0 + jnp.tanh(0.5 * mapped))
-            for n in range(wide.shape[0]):
-                wide[n, pl.ds(b, grid_rows * total, stride=2), :] = value[:, n * 128 : (n + 1) * 128]
-        for n in range(wide.shape[0]):
-            shaped = wide[n].reshape(grid_rows, tiles * frames, 2 * own, 128)
-            for r in range(grid_rows):
-                out[:, 2 * r + a, :, n * 128 : (n + 1) * 128] = shaped[r].astype(BF16)
+    half_bias = 0.5 * bias[...]
+    lanes = wide.shape[-1]
+    copies = []
+    for i in range(grid_rows // chunk):
+        for a in range(2):
+            for b in range(2):
+                lhs = jnp.concatenate(
+                    [v[i * chunk + a + k : i * chunk + a + k + chunk].reshape(
+                        chunk * total, channels) for k in range(2) for v in views[b]], axis=1
+                )
+                h = matmul(lhs, taps[2 * a + b]) + half_bias
+                value = h + h * jnp.tanh(h)
+                for n in range(wide.shape[1]):
+                    wide[a, n, pl.ds(b, chunk * total, stride=2), :] = (
+                        value[:, n * lanes : (n + 1) * lanes]
+                    )
+            for n in range(wide.shape[1]):
+                shaped = wide[a, n].reshape(chunk, tiles * frames, 2 * own, lanes)
+                for r in range(chunk):
+                    staged[:, 2 * (i * chunk + r) + a, :, n * lanes : (n + 1) * lanes] = (
+                        shaped[r].astype(BF16)
+                    )
+        rows = pl.ds(2 * i * chunk, 2 * chunk)
+        copies.append(pltpu.make_async_copy(staged.at[:, rows], out.at[:, rows], sem.at[i]))
+        copies[-1].start()
+    for c in copies:
+        c.wait()
 
 
 def round_call(step, last, got, total, carry):
@@ -440,9 +453,7 @@
     other_b = lax.ppermute(parts_b, "space", SWAP)
 
     ready = {}
-    for name, first, parts, other in (
-        ("a", 0, parts_a, other_a), ("b", split, parts_b, other_b),
-    ):
+    for name, first, parts, other in (("a", 0, parts_a, other_a), ("b", split, parts_b, other_b)):
         count = parts.shape[1]
         total, sent = total_call(parts, other)
         query = query_call(near, near_query, first * HEAD, count * HEAD)
@@ -451,7 +462,9 @@
         ready[name] = (query, parts, other, carry, other_carry)
 
     partial = partial_call(near, ready["a"], w_out, frames)
-    blocks = latent_call(partial, ready["b"], w_out, w_latent, frames, columns, tiles)
+    blocks = latent_call(
+        partial, ready["b"], w_out, w_latent, frames, columns, tiles
+    )
     blocks = lax.all_to_all(blocks, "tm", 0, 0, tiled=True)
     return decode(blocks, conv_weight, conv_bias, frames, grid_rows, own, tiles)
 
@@ -469,15 +482,19 @@
     mine = jnp.where(lax.axis_index("space") == 0, edge(grid_rows - 1), edge(0))
     beside = lax.ppermute(mine, "space", SWAP)
     total = tiles * group
-    return pl.pallas_call(
-        functools.partial(decode_kernel, frames, tiles, grid_rows, own),
-        out_shape=shape((tiles * frames, 2 * grid_rows, 2 * own, width), BF16),
+    chunk = 1 if grid_rows % 1 == 0 else grid_rows
+    dims = (tiles * frames, 2 * grid_rows, 2 * own, width)
+    return pl.pallas_call(
+        functools.partial(decode_kernel, frames, tiles, grid_rows, own, chunk),
+        out_shape=shape(dims, BF16),
         in_specs=[IN_VMEM] * 4,
-        out_specs=IN_VMEM,
+        out_specs=IN_HBM,
         scratch_shapes=[pltpu.VMEM((grid_rows + 2, total, channels), BF16)] * 3
         + [
             pltpu.VMEM((4, 4 * channels, width), BF16),
-            pltpu.VMEM((width // 128, 2 * grid_rows * total, 128), F32),
+            pltpu.VMEM((2, width // HEAD, 2 * chunk * total, HEAD), F32),
+            pltpu.VMEM(dims, BF16),
+            pltpu.SemaphoreType.DMA((grid_rows // chunk,)),
         ],
         name="decode",
         compiler_params=params(36),

time: 65.5 us -> 64.1 us (0.979)
  Pallas kernels: 25.4 us -> 23.9 us
    pallas_call x1, Pallas kernels: 4.23 us -> 3.48 us  [latent_call(): pl.pallas_call(functools.partial(latent_kernel, frames, columns, tiles),...]
    pallas_call x1, Pallas kernels: 3.37 us -> 2.67 us  [decode(): pl.pallas_call(functools.partial(decode_kernel, frames, tiles, grid_rows,...]
  transfers between devices with their start and end apart: 12 -> 12, of which waited for: 6 -> 6; matrix products, arithmetic and copies ran while one was open for 0% -> 0% of each run, Pallas kernels for 16% -> 17%
where the time goes in v4:
time: 64.1 us; the launch traced here: 63.8 us
  Pallas kernels  23.9 us (37%)
  starting transfers between devices  22.6 us (35%)
  waiting for transfers between devices  17 us (27%)
    ppermute x6, starting transfers between devices, prefix_rounds(): got = lax.ppermute(sent, 'tm', pairs)  13.5 us
    all_to_all x1, waiting for transfers between devices, body(): blocks = lax.all_to_all(blocks, 'tm', 0, 0, tiled=True)  10.9 us
    all_to_all x1, starting transfers between devices, body(): blocks = lax.all_to_all(blocks, 'tm', 0, 0, tiled=True)  8.19 us
    pallas_call x1, Pallas kernels, first_states(): pl.pallas_call(functools.partial(states_kernel, frames, heads, False), ou...  7.03 us
    ppermute x6, waiting for transfers between devices, prefix_rounds(): got = lax.ppermute(sent, 'tm', pairs)  4.89 us
    pallas_call x1, Pallas kernels, second_states(): pl.pallas_call(functools.partial(states_kernel, frames, heads, True), out...  3.92 us
    pallas_call x2, Pallas kernels, query_call(): pl.pallas_call(kernel, out_shape=shape((video.shape[0], width), BF16), in...  3.83 us
    pallas_call x1, Pallas kernels, latent_call(): pl.pallas_call(functools.partial(latent_kernel, frames, columns, tiles),...  3.48 us
  transfers between devices with their start and end apart: 12, of which 6 were waited for; matrix products, arithmetic and copies ran while one was open for 0% of the time, Pallas kernels for 17%

profile of v4, /device:TPU:0, one launch (start us, length us, event | category | flops | bytes accessed | tf_op | source)
XLA Modules:
  0.0 63.8 jit_solution(6357884803728511962)
XLA Ops:
  0.0 7.0 %states.2 = (bf16[2,5,128,128]{3,2,1,0:T(8,128)(2,1)S(1)}, bf16[1024,1152]{1,0:T(8,128)(2,1)S(1)}, bf16[1152,512]{1,0:T(8,128)(2,1)S(1)}, bf16[1152,512]{1,0:T(8,128)(2,1)S(1)}, bf16[1152,1152]{1,0:T(8,128)(2,1)S(1)}) custom-call(bf16[1024,1152]{1,0:T(8,128)(2,1)} %bitcast.9, bf16[1152,1152]{1,0:T(8,128)(2,1)} %wk_hbm.1, bf16[1152,1152]{1,0:T(8,128)(2,1)} %wv_hbm.1, ...), custom_call_target="tpu_custom_call" | custom-call | tf_op jit(solution)/shard_map/states/pallas_call | solution.py:114
  7.0 0.6 collective-permute-start
  7.6 3.9 %states.3.parts = bf16[2,4,128,128]{3,2,1,0:T(8,128)(2,1)S(1)} custom-call(bf16[1024,1152]{1,0:T(8,128)(2,1)S(1)} %get-tuple-element.26.video.video_in, bf16[1152,512]{1,0:T(8,128)(2,1)S(1)} %get-tuple-element.37.wk_hbm, bf16[1152,512]{1,0:T(8,128)(2,1)S(1)} %get-tuple-element.38.wv_hbm), custom_call_target="tpu_custom_call" | custom-call | tf_op jit(solution)/shard_map/states/pallas_call | solution.py:143
  11.5 0.1 collective-permute-start.5
  11.6 0.1 total.2
  11.7 3.0 %collective-permute-start.1 = (bf16[5,64,128]{2,1,0:T(8,128)(2,1)S(1)}, bf16[5,64,128]{2,1,0:T(8,128)(2,1)S(1)}, u32[]{:S(2)}, u32[]{:S(2)}) collective-permute-start(bf16[5,64,128]{2,1,0:T(8,128)(2,1)S(1)} %get-tuple-element.29), channel_id=1, source_target_pairs={{0,2},{2,0},{4,6},{6,4},{8,10},{10,8},{12,14},{14,12},{1,3},{3,1},... | collective-permute-start | bytes 245768 | tf_op jit(solution)/shard_map/ppermute | solution.py:428
  14.8 0.1 total.3
  14.8 1.1 %collective-permute-start.6 = (bf16[4,64,128]{2,1,0:T(8,128)(2,1)S(1)}, bf16[4,64,128]{2,1,0:T(8,128)(2,1)S(1)}, u32[]{:S(2)}, u32[]{:S(2)}) collective-permute-start(bf16[4,64,128]{2,1,0:T(8,128)(2,1)S(1)} %get-tuple-element.39), channel_id=1, source_target_pairs={{0,2},{2,0},{4,6},{6,4},{8,10},{10,8},{12,14},{14,12},{1,3},{3,1},... | collective-permute-start | bytes 196616 | tf_op jit(solution)/shard_map/ppermute | solution.py:428
  15.9 1.6 %collective-permute-done.1.got = bf16[5,64,128]{2,1,0:T(8,128)(2,1)S(1)} collective-permute-done((bf16[5,64,128]{2,1,0:T(8,128)(2,1)S(1)}, bf16[5,64,128]{2,1,0:T(8,128)(2,1)S(1)}, u32[]{:S(2)}, u32[]{:S(2)}) %collective-permute-start.1) | collective-permute-done | bytes 81952 | tf_op jit(solution)/shard_map/ppermute | solution.py:428
  17.6 2.1 %collective-permute-start.2 = (bf16[5,64,128]{2,1,0:T(8,128)(2,1)S(1)}, bf16[5,64,128]{2,1,0:T(8,128)(2,1)S(1)}, u32[]{:S(2)}, u32[]{:S(2)}) collective-permute-start(bf16[5,64,128]{2,1,0:T(8,128)(2,1)S(1)} %get-tuple-element.31), channel_id=1, source_target_pairs={{0,4},{2,6},{4,0},{6,2},{8,12},{10,14},{12,8},{14,10},{1,5},{3,7},... | collective-permute-start | bytes 245768 | tf_op jit(solution)/shard_map/ppermute | solution.py:428
  19.7 1.1 %collective-permute-start.7 = (bf16[4,64,128]{2,1,0:T(8,128)(2,1)S(1)}, bf16[4,64,128]{2,1,0:T(8,128)(2,1)S(1)}, u32[]{:S(2)}, u32[]{:S(2)}) collective-permute-start(bf16[4,64,128]{2,1,0:T(8,128)(2,1)S(1)} %get-tuple-element.41), channel_id=1, source_target_pairs={{0,4},{2,6},{4,0},{6,2},{8,12},{10,14},{12,8},{14,10},{1,5},{3,7},... | collective-permute-start | bytes 196616 | tf_op jit(solution)/shard_map/ppermute | solution.py:428
  20.8 1.5 %collective-permute-done.2.got = bf16[5,64,128]{2,1,0:T(8,128)(2,1)S(1)} collective-permute-done((bf16[5,64,128]{2,1,0:T(8,128)(2,1)S(1)}, bf16[5,64,128]{2,1,0:T(8,128)(2,1)S(1)}, u32[]{:S(2)}, u32[]{:S(2)}) %collective-permute-start.2) | collective-permute-done | bytes 81952 | tf_op jit(solution)/shard_map/ppermute | solution.py:428
  22.3 4.7 %collective-permute-start.3 = (bf16[5,64,128]{2,1,0:T(8,128)(2,1)S(1)}, bf16[5,64,128]{2,1,0:T(8,128)(2,1)S(1)}, u32[]{:S(2)}, u32[]{:S(2)}) collective-permute-start(bf16[5,64,128]{2,1,0:T(8,128)(2,1)S(1)} %get-tuple-element.34), channel_id=1, source_target_pairs={{0,8},{2,10},{4,12},{6,14},{1,9},{3,11},{5,13},{7,15},{16,24},{18,... | collective-permute-start | bytes 245768 | tf_op jit(solution)/shard_map/ppermute | solution.py:428
  27.1 0.0 collective-permute-done.7.got
  27.1 1.4 %collective-permute-start.8 = (bf16[4,64,128]{2,1,0:T(8,128)(2,1)S(1)}, bf16[4,64,128]{2,1,0:T(8,128)(2,1)S(1)}, u32[]{:S(2)}, u32[]{:S(2)}) collective-permute-start(bf16[4,64,128]{2,1,0:T(8,128)(2,1)S(1)} %get-tuple-element.44), channel_id=1, source_target_pairs={{0,8},{2,10},{4,12},{6,14},{1,9},{3,11},{5,13},{7,15},{16,24},{18,... | collective-permute-start | bytes 196616 | tf_op jit(solution)/shard_map/ppermute | solution.py:428
  28.6 0.5 collective-permute-done.3.got
  29.2 0.1 collective-permute-start.4
  29.2 1.2 %collective-permute-done.8.got = bf16[4,64,128]{2,1,0:T(8,128)(2,1)S(1)} collective-permute-done((bf16[4,64,128]{2,1,0:T(8,128)(2,1)S(1)}, bf16[4,64,128]{2,1,0:T(8,128)(2,1)S(1)}, u32[]{:S(2)}, u32[]{:S(2)}) %collective-permute-start.8) | collective-permute-done | bytes 65568 | tf_op jit(solution)/shard_map/ppermute | solution.py:428
  30.5 0.1 collective-permute-start.9
  30.6 1.7 %query.3 = bf16[1024,512]{1,0:T(8,128)(2,1)S(1)} custom-call(bf16[1024,1152]{1,0:T(8,128)(2,1)S(1)} %get-tuple-element.26.video.video_in, bf16[1152,1152]{1,0:T(8,128)(2,1)S(1)} %get-tuple-element.27.w), custom_call_target="tpu_custom_call" | custom-call | tf_op jit(solution)/shard_map/query/pallas_call | solution.py:187
  32.3 0.0 copy-start
  32.3 2.1 %query.2 = bf16[1024,640]{1,0:T(8,128)(2,1)S(1)} custom-call(bf16[1024,1152]{1,0:T(8,128)(2,1)S(1)} %get-tuple-element.26.video.video_in, bf16[1152,1152]{1,0:T(8,128)(2,1)S(1)} %get-tuple-element.27.w), custom_call_target="tpu_custom_call" | custom-call | tf_op jit(solution)/shard_map/query/pallas_call | solution.py:187
  34.4 0.0 copy-start.2
  34.5 2.6 %partial.1 = f32[1024,1152]{1,0:T(8,128)S(1)} custom-call(bf16[1024,1152]{1,0:T(8,128)(2,1)S(1)} %get-tuple-element.26.video.video_in, bf16[1024,640]{1,0:T(8,128)(2,1)S(1)} %query.2, bf16[2,5,128,128]{3,2,1,0:T(8,128)(2,1)S(1)} %get-tuple-element.28.parts, bf16[2,5,128,128]{3,2,1,0:T(8,128)(2,1)S(1)} %collective-permute-done.other_parts, ...), custom_call_target="tpu_custom_call" | custom-call | tf_op jit(solution)/shard_map/partial/pallas_call | solution.py:244
  37.1 0.0 copy-start.1
  37.1 0.0 copy-start.3
  37.2 3.5 %latent.1 = bf16[8,160,128]{2,1,0:T(8,128)(2,1)} custom-call(f32[1024,1152]{1,0:T(8,128)S(1)} %partial.1, bf16[1024,512]{1,0:T(8,128)(2,1)S(1)} %query.3, bf16[2,4,128,128]{3,2,1,0:T(8,128)(2,1)S(1)} %states.3.parts, bf16[2,4,128,128]{3,2,1,0:T(8,128)(2,1)S(1)} %collective-permute-done.5.other_parts, bf16[4,64,128]{2,1,0:T(8,128)(2,1)S(1)} %round.11.carry, ...), custom_call_target="tpu_custom_call" | custom-call | tf_op jit(solution)/shard_map/latent/pallas_call | solution.py:295
  40.6 8.2 %all-to-all-start = ((bf16[8,160,128]{2,1,0:T(8,128)(2,1)}), bf16[8,160,128]{2,1,0:T(8,128)(2,1)S(1)}, u32[]{:S(2)}, u32[]{:S(2)}) async-start(bf16[8,160,128]{2,1,0:T(8,128)(2,1)} %latent.1), calls=%async_computation | async-start | bytes 655360 | tf_op jit(solution)/shard_map/all_to_all | solution.py:468
  48.8 10.9 %all-to-all-done.blocks = bf16[8,160,128]{2,1,0:T(8,128)(2,1)S(1)} async-done(((bf16[8,160,128]{2,1,0:T(8,128)(2,1)}), bf16[8,160,128]{2,1,0:T(8,128)(2,1)S(1)}, u32[]{:S(2)}, u32[]{:S(2)}) %all-to-all-start) | async-done | bytes 327712 | tf_op jit(solution)/shard_map/all_to_all | solution.py:468
  59.9 0.1 collective-permute-start.10
  59.9 1.2 %collective-permute-done.10.edge = bf16[8,20,128]{2,1,0:T(8,128)(2,1)S(1)} collective-permute-done((bf16[8,20,128]{2,1,0:T(8,128)(2,1)S(1)}, bf16[8,20,128]{2,1,0:T(8,128)(2,1)S(1)}, u32[]{:S(2)}, u32[]{:S(2)}) %collective-permute-start.10) | collective-permute-done | bytes 40992 | tf_op jit(solution)/shard_map/ppermute | solution.py:483
  61.2 2.7 %decode.1 = bf16[16,16,16,256]{3,2,1,0:T(8,128)(2,1)} custom-call(bf16[8,160,128]{2,1,0:T(8,128)(2,1)S(1)} %all-to-all-done.blocks, bf16[8,20,128]{2,1,0:T(8,128)(2,1)S(1)} %collective-permute-done.10.edge, bf16[3,3,128,256]{3,2,1,0:T(8,128)(2,1)S(1)} %copy-done.1, f32[1,256]{1,0:T(1,128)S(1)} %bitcast.8), custom_call_target="tpu_custom_call" | custom-call | tf_op jit(solution)/shard_map/decode/pallas_call | solution.py:487
  (20 shorter events, 0.3 us)
Async XLA Ops:
  7.0 4.6 %collective-permute-start = (bf16[2,5,128,128]{3,2,1,0:T(8,128)(2,1)S(1)}, bf16[2,5,128,128]{3,2,1,0:T(8,128)(2,1)S(1)}, u32[]{:S(2)}, u32[]{:S(2)}) collective-permute-start(bf16[2,5,128,128]{3,2,1,0:T(8,128)(2,1)S(1)} %get-tuple-element.28.parts), channel_id=1, source_target_pairs={{0,1},{1,0},{2,3},{3,2},{4,5},{5,4},{6,7},{7,6},{8,9},{9,8},{10,11... | collective-permute-start | bytes 983048 | tf_op jit(solution)/shard_map/ppermute | solution.py:451
  11.5 3.2 %collective-permute-start.5 = (bf16[2,4,128,128]{3,2,1,0:T(8,128)(2,1)S(1)}, bf16[2,4,128,128]{3,2,1,0:T(8,128)(2,1)S(1)}, u32[]{:S(2)}, u32[]{:S(2)}) collective-permute-start(bf16[2,4,128,128]{3,2,1,0:T(8,128)(2,1)S(1)} %states.3.parts), channel_id=1, source_target_pairs={{0,1},{1,0},{2,3},{3,2},{4,5},{5,4},{6,7},{7,6},{8,9},{9,8},{10,11... | collective-permute-start | bytes 786440 | tf_op jit(solution)/shard_map/ppermute | solution.py:453
  11.7 5.8 %collective-permute-start.1 = (bf16[5,64,128]{2,1,0:T(8,128)(2,1)S(1)}, bf16[5,64,128]{2,1,0:T(8,128)(2,1)S(1)}, u32[]{:S(2)}, u32[]{:S(2)}) collective-permute-start(bf16[5,64,128]{2,1,0:T(8,128)(2,1)S(1)} %get-tuple-element.29), channel_id=1, source_target_pairs={{0,2},{2,0},{4,6},{6,4},{8,10},{10,8},{12,14},{14,12},{1,3},{3,1},... | collective-permute-start | bytes 245768 | tf_op jit(solution)/shard_map/ppermute | solution.py:428
  14.8 4.9 %collective-permute-start.6 = (bf16[4,64,128]{2,1,0:T(8,128)(2,1)S(1)}, bf16[4,64,128]{2,1,0:T(8,128)(2,1)S(1)}, u32[]{:S(2)}, u32[]{:S(2)}) collective-permute-start(bf16[4,64,128]{2,1,0:T(8,128)(2,1)S(1)} %get-tuple-element.39), channel_id=1, source_target_pairs={{0,2},{2,0},{4,6},{6,4},{8,10},{10,8},{12,14},{14,12},{1,3},{3,1},... | collective-permute-start | bytes 196616 | tf_op jit(solution)/shard_map/ppermute | solution.py:428
  17.6 4.7 %collective-permute-start.2 = (bf16[5,64,128]{2,1,0:T(8,128)(2,1)S(1)}, bf16[5,64,128]{2,1,0:T(8,128)(2,1)S(1)}, u32[]{:S(2)}, u32[]{:S(2)}) collective-permute-start(bf16[5,64,128]{2,1,0:T(8,128)(2,1)S(1)} %get-tuple-element.31), channel_id=1, source_target_pairs={{0,4},{2,6},{4,0},{6,2},{8,12},{10,14},{12,8},{14,10},{1,5},{3,7},... | collective-permute-start | bytes 245768 | tf_op jit(solution)/shard_map/ppermute | solution.py:428
  19.7 7.4 %collective-permute-start.7 = (bf16[4,64,128]{2,1,0:T(8,128)(2,1)S(1)}, bf16[4,64,128]{2,1,0:T(8,128)(2,1)S(1)}, u32[]{:S(2)}, u32[]{:S(2)}) collective-permute-start(bf16[4,64,128]{2,1,0:T(8,128)(2,1)S(1)} %get-tuple-element.41), channel_id=1, source_target_pairs={{0,4},{2,6},{4,0},{6,2},{8,12},{10,14},{12,8},{14,10},{1,5},{3,7},... | collective-permute-start | bytes 196616 | tf_op jit(solution)/shard_map/ppermute | solution.py:428
  22.3 6.8 %collective-permute-start.3 = (bf16[5,64,128]{2,1,0:T(8,128)(2,1)S(1)}, bf16[5,64,128]{2,1,0:T(8,128)(2,1)S(1)}, u32[]{:S(2)}, u32[]{:S(2)}) collective-permute-start(bf16[5,64,128]{2,1,0:T(8,128)(2,1)S(1)} %get-tuple-element.34), channel_id=1, source_target_pairs={{0,8},{2,10},{4,12},{6,14},{1,9},{3,11},{5,13},{7,15},{16,24},{18,... | collective-permute-start | bytes 245768 | tf_op jit(solution)/shard_map/ppermute | solution.py:428
  27.1 3.3 %collective-permute-start.8 = (bf16[4,64,128]{2,1,0:T(8,128)(2,1)S(1)}, bf16[4,64,128]{2,1,0:T(8,128)(2,1)S(1)}, u32[]{:S(2)}, u32[]{:S(2)}) collective-permute-start(bf16[4,64,128]{2,1,0:T(8,128)(2,1)S(1)} %get-tuple-element.44), channel_id=1, source_target_pairs={{0,8},{2,10},{4,12},{6,14},{1,9},{3,11},{5,13},{7,15},{16,24},{18,... | collective-permute-start | bytes 196616 | tf_op jit(solution)/shard_map/ppermute | solution.py:428
  29.2 5.3 %collective-permute-start.4 = (bf16[5,64,128]{2,1,0:T(8,128)(2,1)S(1)}, bf16[5,64,128]{2,1,0:T(8,128)(2,1)S(1)}, u32[]{:S(2)}, u32[]{:S(2)}) collective-permute-start(bf16[5,64,128]{2,1,0:T(8,128)(2,1)S(1)} %round.8.carry), channel_id=1, source_target_pairs={{0,1},{1,0},{2,3},{3,2},{4,5},{5,4},{6,7},{7,6},{8,9},{9,8},{10,11... | collective-permute-start | bytes 245768 | tf_op jit(solution)/shard_map/ppermute | solution.py:461
  30.5 6.6 %collective-permute-start.9 = (bf16[4,64,128]{2,1,0:T(8,128)(2,1)S(1)}, bf16[4,64,128]{2,1,0:T(8,128)(2,1)S(1)}, u32[]{:S(2)}, u32[]{:S(2)}) collective-permute-start(bf16[4,64,128]{2,1,0:T(8,128)(2,1)S(1)} %round.11.carry), channel_id=1, source_target_pairs={{0,1},{1,0},{2,3},{3,2},{4,5},{5,4},{6,7},{7,6},{8,9},{9,8},{10,11... | collective-permute-start | bytes 196616 | tf_op jit(solution)/shard_map/ppermute | solution.py:461
  32.3 2.2 %copy-start = (bf16[1152,1152]{1,0:T(8,128)(2,1)S(1)}, bf16[1152,1152]{1,0:T(8,128)(2,1)}, u32[]{:S(2)}) copy-start(bf16[1152,1152]{1,0:T(8,128)(2,1)} %w_out.3) | copy-start | bytes 7962628
  34.4 2.7 %copy-start.2 = (bf16[1152,128]{1,0:T(8,128)(2,1)S(1)}, bf16[1152,128]{1,0:T(8,128)(2,1)}, u32[]{:S(2)}) copy-start(bf16[1152,128]{1,0:T(8,128)(2,1)} %w_latent.1) | copy-start | bytes 884740
  37.1 24.0 %copy-start.1 = (bf16[3,3,128,256]{3,2,1,0:T(8,128)(2,1)S(1)}, bf16[3,3,128,256]{3,2,1,0:T(8,128)(2,1)}, u32[]{:S(2)}) copy-start(bf16[3,3,128,256]{3,2,1,0:T(8,128)(2,1)} %weight.1) | copy-start | bytes 1769476
  37.1 24.0 %copy-start.3 = (f32[256]{0:T(256)S(1)}, f32[256]{0:T(256)}, u32[]{:S(2)}) copy-start(f32[256]{0:T(256)} %param.15) | copy-start | bytes 3076
  40.6 19.1 %all-to-all-start = ((bf16[8,160,128]{2,1,0:T(8,128)(2,1)}), bf16[8,160,128]{2,1,0:T(8,128)(2,1)S(1)}, u32[]{:S(2)}, u32[]{:S(2)}) async-start(bf16[8,160,128]{2,1,0:T(8,128)(2,1)} %latent.1), calls=%async_computation | async-start | bytes 655360 | tf_op jit(solution)/shard_map/all_to_all | solution.py:468
  59.9 1.3 %collective-permute-start.10 = (bf16[8,20,128]{2,1,0:T(8,128)(2,1)S(1)}, bf16[8,20,128]{2,1,0:T(8,128)(2,1)S(1)}, u32[]{:S(2)}, u32[]{:S(2)}) collective-permute-start(bf16[8,20,128]{2,1,0:T(8,128)(2,1)S(1)} %maximum_select_fusion), channel_id=1, source_target_pairs={{0,1},{1,0},{2,3},{3,2},{4,5},{5,4},{6,7},{7,6},{8,9},{9,8},{10,11... | collective-permute-start | bytes 122888 | tf_op jit(solution)/shard_map/ppermute | solution.py:483

commit v5 on v4

--- a/solution.py
+++ b/solution.py
@@ -421,11 +421,7 @@
     step, number = 1, 0
     while step < tiles:
         last = 2 * step >= tiles
-        if last:
-            pairs = [(i, i + step) for i in range(step)]
-        else:
-            pairs = [(i, i ^ step) for i in range(tiles)]
-        got = lax.ppermute(sent, "tm", pairs)
+        got = lax.ppermute(sent, "tm", [(i, i ^ step) for i in range(tiles)])
         out = round_call(step, last, got, total, carry)
         if last:
             return out[0]

time: 64.1 us -> 62.2 us (0.970)
  starting transfers between devices: 22.6 us -> 18.9 us
  waiting for transfers between devices: 17 us -> 18.9 us
    all_to_all x1, starting transfers between devices: 8.19 us -> 6.3 us  [body(): blocks = lax.all_to_all(blocks, 'tm', 0, 0, tiled=True)]
    ppermute x6, waiting for transfers between devices: 4.89 us -> 6.72 us  [prefix_rounds(): got = lax.ppermute(sent, 'tm', [(i, i ^ step) for i in range(tiles)])]
    ppermute x6, starting transfers between devices: 13.5 us -> 11.8 us  [prefix_rounds(): got = lax.ppermute(sent, 'tm', [(i, i ^ step) for i in range(tiles)])]
where the time goes in v5:
time: 62.2 us; the launch traced here: 62 us
  Pallas kernels  23.9 us (38%)
  starting transfers between devices  18.9 us (30%)
  waiting for transfers between devices  18.9 us (30%)
    ppermute x6, starting transfers between devices, prefix_rounds(): got = lax.ppermute(sent, 'tm', [(i, i ^ step) for i in range(tiles)])  11.8 us
    all_to_all x1, waiting for transfers between devices, body(): blocks = lax.all_to_all(blocks, 'tm', 0, 0, tiled=True)  10.9 us
    pallas_call x1, Pallas kernels, first_states(): pl.pallas_call(functools.partial(states_kernel, frames, heads, False), ou...  7.03 us
    ppermute x6, waiting for transfers between devices, prefix_rounds(): got = lax.ppermute(sent, 'tm', [(i, i ^ step) for i in range(tiles)])  6.72 us
    all_to_all x1, starting transfers between devices, body(): blocks = lax.all_to_all(blocks, 'tm', 0, 0, tiled=True)  6.3 us
    pallas_call x1, Pallas kernels, second_states(): pl.pallas_call(functools.partial(states_kernel, frames, heads, True), out...  3.92 us
    pallas_call x2, Pallas kernels, query_call(): pl.pallas_call(kernel, out_shape=shape((video.shape[0], width), BF16), in...  3.83 us
    pallas_call x1, Pallas kernels, latent_call(): pl.pallas_call(functools.partial(latent_kernel, frames, columns, tiles),...  3.48 us
  transfers between devices with their start and end apart: 12, of which 6 were waited for; matrix products, arithmetic and copies ran while one was open for 0% of the time, Pallas kernels for 17%

profile of v5, /device:TPU:0, one launch (start us, length us, event | category | flops | bytes accessed | tf_op | source)
XLA Modules:
  0.0 62.0 jit_solution(10139796484341842289)
XLA Ops:
  0.0 7.0 %states.2 = (bf16[2,5,128,128]{3,2,1,0:T(8,128)(2,1)S(1)}, bf16[1024,1152]{1,0:T(8,128)(2,1)S(1)}, bf16[1152,512]{1,0:T(8,128)(2,1)S(1)}, bf16[1152,512]{1,0:T(8,128)(2,1)S(1)}, bf16[1152,1152]{1,0:T(8,128)(2,1)S(1)}) custom-call(bf16[1024,1152]{1,0:T(8,128)(2,1)} %bitcast.9, bf16[1152,1152]{1,0:T(8,128)(2,1)} %wk_hbm.1, bf16[1152,1152]{1,0:T(8,128)(2,1)} %wv_hbm.1, ...), custom_call_target="tpu_custom_call" | custom-call | tf_op jit(solution)/shard_map/states/pallas_call | solution.py:114
  7.0 0.6 collective-permute-start
  7.6 3.9 %states.3.parts = bf16[2,4,128,128]{3,2,1,0:T(8,128)(2,1)S(1)} custom-call(bf16[1024,1152]{1,0:T(8,128)(2,1)S(1)} %get-tuple-element.26.video.video_in, bf16[1152,512]{1,0:T(8,128)(2,1)S(1)} %get-tuple-element.37.wk_hbm, bf16[1152,512]{1,0:T(8,128)(2,1)S(1)} %get-tuple-element.38.wv_hbm), custom_call_target="tpu_custom_call" | custom-call | tf_op jit(solution)/shard_map/states/pallas_call | solution.py:143
  11.5 0.1 collective-permute-start.5
  11.6 0.1 total.2
  11.7 3.0 %collective-permute-start.1 = (bf16[5,64,128]{2,1,0:T(8,128)(2,1)S(1)}, bf16[5,64,128]{2,1,0:T(8,128)(2,1)S(1)}, u32[]{:S(2)}, u32[]{:S(2)}) collective-permute-start(bf16[5,64,128]{2,1,0:T(8,128)(2,1)S(1)} %get-tuple-element.29), channel_id=1, source_target_pairs={{0,2},{2,0},{4,6},{6,4},{8,10},{10,8},{12,14},{14,12},{1,3},{3,1},... | collective-permute-start | bytes 245768 | tf_op jit(solution)/shard_map/ppermute | solution.py:424
  14.8 0.1 total.3
  14.8 1.1 %collective-permute-start.6 = (bf16[4,64,128]{2,1,0:T(8,128)(2,1)S(1)}, bf16[4,64,128]{2,1,0:T(8,128)(2,1)S(1)}, u32[]{:S(2)}, u32[]{:S(2)}) collective-permute-start(bf16[4,64,128]{2,1,0:T(8,128)(2,1)S(1)} %get-tuple-element.39), channel_id=1, source_target_pairs={{0,2},{2,0},{4,6},{6,4},{8,10},{10,8},{12,14},{14,12},{1,3},{3,1},... | collective-permute-start | bytes 196616 | tf_op jit(solution)/shard_map/ppermute | solution.py:424
  15.9 1.6 %collective-permute-done.1.got = bf16[5,64,128]{2,1,0:T(8,128)(2,1)S(1)} collective-permute-done((bf16[5,64,128]{2,1,0:T(8,128)(2,1)S(1)}, bf16[5,64,128]{2,1,0:T(8,128)(2,1)S(1)}, u32[]{:S(2)}, u32[]{:S(2)}) %collective-permute-start.1) | collective-permute-done | bytes 81952 | tf_op jit(solution)/shard_map/ppermute | solution.py:424
  17.6 2.1 %collective-permute-start.2 = (bf16[5,64,128]{2,1,0:T(8,128)(2,1)S(1)}, bf16[5,64,128]{2,1,0:T(8,128)(2,1)S(1)}, u32[]{:S(2)}, u32[]{:S(2)}) collective-permute-start(bf16[5,64,128]{2,1,0:T(8,128)(2,1)S(1)} %get-tuple-element.31), channel_id=1, source_target_pairs={{0,4},{2,6},{4,0},{6,2},{8,12},{10,14},{12,8},{14,10},{1,5},{3,7},... | collective-permute-start | bytes 245768 | tf_op jit(solution)/shard_map/ppermute | solution.py:424
  19.7 1.1 %collective-permute-start.7 = (bf16[4,64,128]{2,1,0:T(8,128)(2,1)S(1)}, bf16[4,64,128]{2,1,0:T(8,128)(2,1)S(1)}, u32[]{:S(2)}, u32[]{:S(2)}) collective-permute-start(bf16[4,64,128]{2,1,0:T(8,128)(2,1)S(1)} %get-tuple-element.41), channel_id=1, source_target_pairs={{0,4},{2,6},{4,0},{6,2},{8,12},{10,14},{12,8},{14,10},{1,5},{3,7},... | collective-permute-start | bytes 196616 | tf_op jit(solution)/shard_map/ppermute | solution.py:424
  20.8 1.5 %collective-permute-done.2.got = bf16[5,64,128]{2,1,0:T(8,128)(2,1)S(1)} collective-permute-done((bf16[5,64,128]{2,1,0:T(8,128)(2,1)S(1)}, bf16[5,64,128]{2,1,0:T(8,128)(2,1)S(1)}, u32[]{:S(2)}, u32[]{:S(2)}) %collective-permute-start.2) | collective-permute-done | bytes 81952 | tf_op jit(solution)/shard_map/ppermute | solution.py:424
  22.3 2.9 %collective-permute-start.3 = (bf16[5,64,128]{2,1,0:T(8,128)(2,1)S(1)}, bf16[5,64,128]{2,1,0:T(8,128)(2,1)S(1)}, u32[]{:S(2)}, u32[]{:S(2)}) collective-permute-start(bf16[5,64,128]{2,1,0:T(8,128)(2,1)S(1)} %get-tuple-element.34), channel_id=1, source_target_pairs={{0,8},{2,10},{4,12},{6,14},{8,0},{10,2},{12,4},{14,6},{1,9},{3,11}... | collective-permute-start | bytes 245768 | tf_op jit(solution)/shard_map/ppermute | solution.py:424
  25.3 1.5 %collective-permute-start.8 = (bf16[4,64,128]{2,1,0:T(8,128)(2,1)S(1)}, bf16[4,64,128]{2,1,0:T(8,128)(2,1)S(1)}, u32[]{:S(2)}, u32[]{:S(2)}) collective-permute-start(bf16[4,64,128]{2,1,0:T(8,128)(2,1)S(1)} %get-tuple-element.44), channel_id=1, source_target_pairs={{0,8},{2,10},{4,12},{6,14},{8,0},{10,2},{12,4},{14,6},{1,9},{3,11}... | collective-permute-start | bytes 196616 | tf_op jit(solution)/shard_map/ppermute | solution.py:424
  26.8 2.5 %collective-permute-done.3.got = bf16[5,64,128]{2,1,0:T(8,128)(2,1)S(1)} collective-permute-done((bf16[5,64,128]{2,1,0:T(8,128)(2,1)S(1)}, bf16[5,64,128]{2,1,0:T(8,128)(2,1)S(1)}, u32[]{:S(2)}, u32[]{:S(2)}) %collective-permute-start.3) | collective-permute-done | bytes 81952 | tf_op jit(solution)/shard_map/ppermute | solution.py:424
  29.4 0.1 collective-permute-start.4
  29.4 1.1 %collective-permute-done.8.got = bf16[4,64,128]{2,1,0:T(8,128)(2,1)S(1)} collective-permute-done((bf16[4,64,128]{2,1,0:T(8,128)(2,1)S(1)}, bf16[4,64,128]{2,1,0:T(8,128)(2,1)S(1)}, u32[]{:S(2)}, u32[]{:S(2)}) %collective-permute-start.8) | collective-permute-done | bytes 65568 | tf_op jit(solution)/shard_map/ppermute | solution.py:424
  30.6 0.1 collective-permute-start.9
  30.6 1.7 %query.3 = bf16[1024,512]{1,0:T(8,128)(2,1)S(1)} custom-call(bf16[1024,1152]{1,0:T(8,128)(2,1)S(1)} %get-tuple-element.26.video.video_in, bf16[1152,1152]{1,0:T(8,128)(2,1)S(1)} %get-tuple-element.27.w), custom_call_target="tpu_custom_call" | custom-call | tf_op jit(solution)/shard_map/query/pallas_call | solution.py:187
  32.3 0.0 copy-start
  32.3 2.1 %query.2 = bf16[1024,640]{1,0:T(8,128)(2,1)S(1)} custom-call(bf16[1024,1152]{1,0:T(8,128)(2,1)S(1)} %get-tuple-element.26.video.video_in, bf16[1152,1152]{1,0:T(8,128)(2,1)S(1)} %get-tuple-element.27.w), custom_call_target="tpu_custom_call" | custom-call | tf_op jit(solution)/shard_map/query/pallas_call | solution.py:187
  34.5 0.0 copy-start.2
  34.5 0.0 collective-permute-done.4.other_carry
  34.5 2.6 %partial.1 = f32[1024,1152]{1,0:T(8,128)S(1)} custom-call(bf16[1024,1152]{1,0:T(8,128)(2,1)S(1)} %get-tuple-element.26.video.video_in, bf16[1024,640]{1,0:T(8,128)(2,1)S(1)} %query.2, bf16[2,5,128,128]{3,2,1,0:T(8,128)(2,1)S(1)} %get-tuple-element.28.parts, bf16[2,5,128,128]{3,2,1,0:T(8,128)(2,1)S(1)} %collective-permute-done.other_parts, ...), custom_call_target="tpu_custom_call" | custom-call | tf_op jit(solution)/shard_map/partial/pallas_call | solution.py:244
  37.2 0.0 copy-start.1
  37.2 0.0 copy-start.3
  37.2 3.5 %latent.1 = bf16[8,160,128]{2,1,0:T(8,128)(2,1)} custom-call(f32[1024,1152]{1,0:T(8,128)S(1)} %partial.1, bf16[1024,512]{1,0:T(8,128)(2,1)S(1)} %query.3, bf16[2,4,128,128]{3,2,1,0:T(8,128)(2,1)S(1)} %states.3.parts, bf16[2,4,128,128]{3,2,1,0:T(8,128)(2,1)S(1)} %collective-permute-done.5.other_parts, bf16[4,64,128]{2,1,0:T(8,128)(2,1)S(1)} %round.11.carry, ...), custom_call_target="tpu_custom_call" | custom-call | tf_op jit(solution)/shard_map/latent/pallas_call | solution.py:295
  40.7 6.3 %all-to-all-start = ((bf16[8,160,128]{2,1,0:T(8,128)(2,1)}), bf16[8,160,128]{2,1,0:T(8,128)(2,1)S(1)}, u32[]{:S(2)}, u32[]{:S(2)}) async-start(bf16[8,160,128]{2,1,0:T(8,128)(2,1)} %latent.1), calls=%async_computation | async-start | bytes 655360 | tf_op jit(solution)/shard_map/all_to_all | solution.py:464
  47.0 10.9 %all-to-all-done.blocks = bf16[8,160,128]{2,1,0:T(8,128)(2,1)S(1)} async-done(((bf16[8,160,128]{2,1,0:T(8,128)(2,1)}), bf16[8,160,128]{2,1,0:T(8,128)(2,1)S(1)}, u32[]{:S(2)}, u32[]{:S(2)}) %all-to-all-start) | async-done | bytes 327712 | tf_op jit(solution)/shard_map/all_to_all | solution.py:464
  58.0 0.1 collective-permute-start.10
  58.1 1.2 %collective-permute-done.10.edge = bf16[8,20,128]{2,1,0:T(8,128)(2,1)S(1)} collective-permute-done((bf16[8,20,128]{2,1,0:T(8,128)(2,1)S(1)}, bf16[8,20,128]{2,1,0:T(8,128)(2,1)S(1)}, u32[]{:S(2)}, u32[]{:S(2)}) %collective-permute-start.10) | collective-permute-done | bytes 40992 | tf_op jit(solution)/shard_map/ppermute | solution.py:479
  59.3 2.7 %decode.1 = bf16[16,16,16,256]{3,2,1,0:T(8,128)(2,1)} custom-call(bf16[8,160,128]{2,1,0:T(8,128)(2,1)S(1)} %all-to-all-done.blocks, bf16[8,20,128]{2,1,0:T(8,128)(2,1)S(1)} %collective-permute-done.10.edge, bf16[3,3,128,256]{3,2,1,0:T(8,128)(2,1)S(1)} %copy-done.1, f32[1,256]{1,0:T(1,128)S(1)} %bitcast.8), custom_call_target="tpu_custom_call" | custom-call | tf_op jit(solution)/shard_map/decode/pallas_call | solution.py:483
  (20 shorter events, 0.3 us)
Async XLA Ops:
  7.0 4.6 %collective-permute-start = (bf16[2,5,128,128]{3,2,1,0:T(8,128)(2,1)S(1)}, bf16[2,5,128,128]{3,2,1,0:T(8,128)(2,1)S(1)}, u32[]{:S(2)}, u32[]{:S(2)}) collective-permute-start(bf16[2,5,128,128]{3,2,1,0:T(8,128)(2,1)S(1)} %get-tuple-element.28.parts), channel_id=1, source_target_pairs={{0,1},{1,0},{2,3},{3,2},{4,5},{5,4},{6,7},{7,6},{8,9},{9,8},{10,11... | collective-permute-start | bytes 983048 | tf_op jit(solution)/shard_map/ppermute | solution.py:447
  11.5 3.2 %collective-permute-start.5 = (bf16[2,4,128,128]{3,2,1,0:T(8,128)(2,1)S(1)}, bf16[2,4,128,128]{3,2,1,0:T(8,128)(2,1)S(1)}, u32[]{:S(2)}, u32[]{:S(2)}) collective-permute-start(bf16[2,4,128,128]{3,2,1,0:T(8,128)(2,1)S(1)} %states.3.parts), channel_id=1, source_target_pairs={{0,1},{1,0},{2,3},{3,2},{4,5},{5,4},{6,7},{7,6},{8,9},{9,8},{10,11... | collective-permute-start | bytes 786440 | tf_op jit(solution)/shard_map/ppermute | solution.py:449
  11.7 5.8 %collective-permute-start.1 = (bf16[5,64,128]{2,1,0:T(8,128)(2,1)S(1)}, bf16[5,64,128]{2,1,0:T(8,128)(2,1)S(1)}, u32[]{:S(2)}, u32[]{:S(2)}) collective-permute-start(bf16[5,64,128]{2,1,0:T(8,128)(2,1)S(1)} %get-tuple-element.29), channel_id=1, source_target_pairs={{0,2},{2,0},{4,6},{6,4},{8,10},{10,8},{12,14},{14,12},{1,3},{3,1},... | collective-permute-start | bytes 245768 | tf_op jit(solution)/shard_map/ppermute | solution.py:424
  14.8 4.9 %collective-permute-start.6 = (bf16[4,64,128]{2,1,0:T(8,128)(2,1)S(1)}, bf16[4,64,128]{2,1,0:T(8,128)(2,1)S(1)}, u32[]{:S(2)}, u32[]{:S(2)}) collective-permute-start(bf16[4,64,128]{2,1,0:T(8,128)(2,1)S(1)} %get-tuple-element.39), channel_id=1, source_target_pairs={{0,2},{2,0},{4,6},{6,4},{8,10},{10,8},{12,14},{14,12},{1,3},{3,1},... | collective-permute-start | bytes 196616 | tf_op jit(solution)/shard_map/ppermute | solution.py:424
  17.6 4.7 %collective-permute-start.2 = (bf16[5,64,128]{2,1,0:T(8,128)(2,1)S(1)}, bf16[5,64,128]{2,1,0:T(8,128)(2,1)S(1)}, u32[]{:S(2)}, u32[]{:S(2)}) collective-permute-start(bf16[5,64,128]{2,1,0:T(8,128)(2,1)S(1)} %get-tuple-element.31), channel_id=1, source_target_pairs={{0,4},{2,6},{4,0},{6,2},{8,12},{10,14},{12,8},{14,10},{1,5},{3,7},... | collective-permute-start | bytes 245768 | tf_op jit(solution)/shard_map/ppermute | solution.py:424
  19.7 5.5 %collective-permute-start.7 = (bf16[4,64,128]{2,1,0:T(8,128)(2,1)S(1)}, bf16[4,64,128]{2,1,0:T(8,128)(2,1)S(1)}, u32[]{:S(2)}, u32[]{:S(2)}) collective-permute-start(bf16[4,64,128]{2,1,0:T(8,128)(2,1)S(1)} %get-tuple-element.41), channel_id=1, source_target_pairs={{0,4},{2,6},{4,0},{6,2},{8,12},{10,14},{12,8},{14,10},{1,5},{3,7},... | collective-permute-start | bytes 196616 | tf_op jit(solution)/shard_map/ppermute | solution.py:424
  22.3 7.0 %collective-permute-start.3 = (bf16[5,64,128]{2,1,0:T(8,128)(2,1)S(1)}, bf16[5,64,128]{2,1,0:T(8,128)(2,1)S(1)}, u32[]{:S(2)}, u32[]{:S(2)}) collective-permute-start(bf16[5,64,128]{2,1,0:T(8,128)(2,1)S(1)} %get-tuple-element.34), channel_id=1, source_target_pairs={{0,8},{2,10},{4,12},{6,14},{8,0},{10,2},{12,4},{14,6},{1,9},{3,11}... | collective-permute-start | bytes 245768 | tf_op jit(solution)/shard_map/ppermute | solution.py:424
  25.3 5.2 %collective-permute-start.8 = (bf16[4,64,128]{2,1,0:T(8,128)(2,1)S(1)}, bf16[4,64,128]{2,1,0:T(8,128)(2,1)S(1)}, u32[]{:S(2)}, u32[]{:S(2)}) collective-permute-start(bf16[4,64,128]{2,1,0:T(8,128)(2,1)S(1)} %get-tuple-element.44), channel_id=1, source_target_pairs={{0,8},{2,10},{4,12},{6,14},{8,0},{10,2},{12,4},{14,6},{1,9},{3,11}... | collective-permute-start | bytes 196616 | tf_op jit(solution)/shard_map/ppermute | solution.py:424
  29.4 5.2 %collective-permute-start.4 = (bf16[5,64,128]{2,1,0:T(8,128)(2,1)S(1)}, bf16[5,64,128]{2,1,0:T(8,128)(2,1)S(1)}, u32[]{:S(2)}, u32[]{:S(2)}) collective-permute-start(bf16[5,64,128]{2,1,0:T(8,128)(2,1)S(1)} %round.8.carry), channel_id=1, source_target_pairs={{0,1},{1,0},{2,3},{3,2},{4,5},{5,4},{6,7},{7,6},{8,9},{9,8},{10,11... | collective-permute-start | bytes 245768 | tf_op jit(solution)/shard_map/ppermute | solution.py:457
  30.6 6.6 %collective-permute-start.9 = (bf16[4,64,128]{2,1,0:T(8,128)(2,1)S(1)}, bf16[4,64,128]{2,1,0:T(8,128)(2,1)S(1)}, u32[]{:S(2)}, u32[]{:S(2)}) collective-permute-start(bf16[4,64,128]{2,1,0:T(8,128)(2,1)S(1)} %round.11.carry), channel_id=1, source_target_pairs={{0,1},{1,0},{2,3},{3,2},{4,5},{5,4},{6,7},{7,6},{8,9},{9,8},{10,11... | collective-permute-start | bytes 196616 | tf_op jit(solution)/shard_map/ppermute | solution.py:457
  32.3 2.2 %copy-start = (bf16[1152,1152]{1,0:T(8,128)(2,1)S(1)}, bf16[1152,1152]{1,0:T(8,128)(2,1)}, u32[]{:S(2)}) copy-start(bf16[1152,1152]{1,0:T(8,128)(2,1)} %w_out.3) | copy-start | bytes 7962628
  34.5 2.7 %copy-start.2 = (bf16[1152,128]{1,0:T(8,128)(2,1)S(1)}, bf16[1152,128]{1,0:T(8,128)(2,1)}, u32[]{:S(2)}) copy-start(bf16[1152,128]{1,0:T(8,128)(2,1)} %w_latent.1) | copy-start | bytes 884740
  37.2 22.2 %copy-start.1 = (bf16[3,3,128,256]{3,2,1,0:T(8,128)(2,1)S(1)}, bf16[3,3,128,256]{3,2,1,0:T(8,128)(2,1)}, u32[]{:S(2)}) copy-start(bf16[3,3,128,256]{3,2,1,0:T(8,128)(2,1)} %weight.1) | copy-start | bytes 1769476
  37.2 22.1 %copy-start.3 = (f32[256]{0:T(256)S(1)}, f32[256]{0:T(256)}, u32[]{:S(2)}) copy-start(f32[256]{0:T(256)} %param.15) | copy-start | bytes 3076
  40.7 17.2 %all-to-all-start = ((bf16[8,160,128]{2,1,0:T(8,128)(2,1)}), bf16[8,160,128]{2,1,0:T(8,128)(2,1)S(1)}, u32[]{:S(2)}, u32[]{:S(2)}) async-start(bf16[8,160,128]{2,1,0:T(8,128)(2,1)} %latent.1), calls=%async_computation | async-start | bytes 655360 | tf_op jit(solution)/shard_map/all_to_all | solution.py:464
  58.0 1.3 %collective-permute-start.10 = (bf16[8,20,128]{2,1,0:T(8,128)(2,1)S(1)}, bf16[8,20,128]{2,1,0:T(8,128)(2,1)S(1)}, u32[]{:S(2)}, u32[]{:S(2)}) collective-permute-start(bf16[8,20,128]{2,1,0:T(8,128)(2,1)S(1)} %maximum_select_fusion), channel_id=1, source_target_pairs={{0,1},{1,0},{2,3},{3,2},{4,5},{5,4},{6,7},{7,6},{8,9},{9,8},{10,11... | collective-permute-start | bytes 122888 | tf_op jit(solution)/shard_map/ppermute | solution.py:479

commit v6 on v5

--- a/solution.py
+++ b/solution.py
@@ -194,9 +194,9 @@
     )(video, w)
 
 
-def attend(frames, query, parts, other_parts, carry, other_carry, used, head_out):
+def attend(frames, queries, parts, other_parts, carry, other_carry, used, head_out):
     heads = carry.shape[0]
-    per = query.shape[0] // frames
+    per = head_out.shape[0] // frames
     low = lax.axis_index("space") == 0
     used[...] = jnp.zeros_like(used)
     for h in range(heads):
@@ -213,9 +213,12 @@
         for p in range(pl.cdiv(heads, 2)):
             width = min(2, heads - 2 * p) * HEAD
             first = 2 * p * HEAD
-            attended = matmul(
-                query[rows, first : first + width], used[f, p, :width, :width]
-            )
+            query, at = queries[0], first
+            for piece in queries[1:]:
+                if at < query.shape[1]:
+                    break
+                query, at = piece, at - query.shape[1]
+            attended = matmul(query[rows, at : at + width], used[f, p, :width, :width])
             for h in range(width // HEAD):
                 one = attended[:, h * HEAD : (h + 1) * HEAD]
                 scale = lax.rsqrt(jnp.mean(one * one, axis=1, keepdims=True) + EPS)
@@ -231,9 +234,12 @@
     tokens, d = video.shape
     heads = chunk[3].shape[0]
 
-    def kernel(video, query, parts, other_parts, carry, other_carry, w_out, out,
-               used, head_out):
-        attend(frames, query, parts, other_parts, carry, other_carry, used, head_out)
+    queries, chunk = chunk[0], chunk[1:]
+    n = len(queries)
+
+    def kernel(video, *refs):
+        parts, other_parts, carry, other_carry, w_out, out, used, head_out = refs[n:]
+        attend(frames, refs[:n], parts, other_parts, carry, other_carry, used, head_out)
         per = tokens // frames
         for f in range(frames):
             rows = slice(f * per, (f + 1) * per)
@@ -244,12 +250,12 @@
     return pl.pallas_call(
         kernel,
         out_shape=shape((tokens, d), F32),
-        in_specs=[IN_VMEM] * 7,
+        in_specs=[IN_VMEM] * (n + 6),
         out_specs=IN_VMEM,
         scratch_shapes=[used_shape(frames, heads), pltpu.VMEM((tokens, heads * HEAD), BF16)],
         name="partial",
         compiler_params=params(20),
-    )(video, *chunk, w_out)
+    )(video, *queries, *chunk, w_out)
 
 
 def latent_kernel(
@@ -259,7 +265,7 @@
     tokens, d = partial.shape
     per = tokens // frames
     width = head_out.shape[1]
-    attend(frames, query, parts, other_parts, carry, other_carry, used, head_out)
+    attend(frames, [query], parts, other_parts, carry, other_carry, used, head_out)
     for f in range(frames):
         rows = slice(f * per, (f + 1) * per)
         summed = partial[rows, :] + matmul(head_out[rows, :], w_out[d - width :, :])
@@ -304,7 +310,7 @@
         ],
         name="latent",
         compiler_params=params(20),
-    )(partial, *chunk, w_out, w_latent)
+    )(partial, *chunk[0], *chunk[1:], w_out, w_latent)
 
 
 def decode_kernel(
@@ -452,10 +458,15 @@
     for name, first, parts, other in (("a", 0, parts_a, other_a), ("b", split, parts_b, other_b)):
         count = parts.shape[1]
         total, sent = total_call(parts, other)
-        query = query_call(near, near_query, first * HEAD, count * HEAD)
+        cuts = [first, first + 2, first + count] if name == "a" else [first, first + count]
+        queries = []
+        for low, high in zip(cuts, cuts[1:]):
+            queries.append(
+                query_call(near, near_query, low * HEAD, (high - low) * HEAD)
+            )
         carry = prefix_rounds(total, sent, tiles)
         other_carry = lax.ppermute(carry, "space", SWAP)
-        ready[name] = (query, parts, other, carry, other_carry)
+        ready[name] = (queries, parts, other, carry, other_carry)
 
     partial = partial_call(near, ready["a"], w_out, frames)
     blocks = latent_call(

time: 62.2 us -> 62.5 us (level)
    pallas_call x2 -> x3, Pallas kernels: 3.83 us -> 4.1 us  [query_call(): pl.pallas_call(kernel, out_shape=shape((video.shape[0], width), BF16), in...]
  transfers between devices with their start and end apart: 12 -> 12, of which waited for: 6 -> 6; matrix products, arithmetic and copies ran while one was open for 0% -> 0% of each run, Pallas kernels for 17% -> 18%
where the time goes in v6:
time: 62.5 us; the launch traced here: 62.3 us
  Pallas kernels  24.2 us (39%)
  starting transfers between devices  18.9 us (30%)
  waiting for transfers between devices  18.9 us (30%)
    ppermute x6, starting transfers between devices, prefix_rounds(): got = lax.ppermute(sent, 'tm', [(i, i ^ step) for i in range(tiles)])  11.8 us
    all_to_all x1, waiting for transfers between devices, body(): blocks = lax.all_to_all(blocks, 'tm', 0, 0, tiled=True)  10.9 us
    pallas_call x1, Pallas kernels, first_states(): pl.pallas_call(functools.partial(states_kernel, frames, heads, False), ou...  7.03 us
    ppermute x6, waiting for transfers between devices, prefix_rounds(): got = lax.ppermute(sent, 'tm', [(i, i ^ step) for i in range(tiles)])  6.72 us
    all_to_all x1, starting transfers between devices, body(): blocks = lax.all_to_all(blocks, 'tm', 0, 0, tiled=True)  6.3 us
    pallas_call x3, Pallas kernels, query_call(): pl.pallas_call(kernel, out_shape=shape((video.shape[0], width), BF16), in...  4.1 us
    pallas_call x1, Pallas kernels, second_states(): pl.pallas_call(functools.partial(states_kernel, frames, heads, True), out...  3.92 us
    pallas_call x1, Pallas kernels, latent_call(): pl.pallas_call(functools.partial(latent_kernel, frames, columns, tiles),...  3.48 us
  transfers between devices with their start and end apart: 12, of which 6 were waited for; matrix products, arithmetic and copies ran while one was open for 0% of the time, Pallas kernels for 18%

profile of v6, /device:TPU:0, one launch (start us, length us, event | category | flops | bytes accessed | tf_op | source)
XLA Modules:
  0.0 62.3 jit_solution(17952460371375216654)
XLA Ops:
  0.0 7.0 %states.2 = (bf16[2,5,128,128]{3,2,1,0:T(8,128)(2,1)S(1)}, bf16[1024,1152]{1,0:T(8,128)(2,1)S(1)}, bf16[1152,512]{1,0:T(8,128)(2,1)S(1)}, bf16[1152,512]{1,0:T(8,128)(2,1)S(1)}, bf16[1152,1152]{1,0:T(8,128)(2,1)S(1)}) custom-call(bf16[1024,1152]{1,0:T(8,128)(2,1)} %bitcast.9, bf16[1152,1152]{1,0:T(8,128)(2,1)} %wk_hbm.1, bf16[1152,1152]{1,0:T(8,128)(2,1)} %wv_hbm.1, ...), custom_call_target="tpu_custom_call" | custom-call | tf_op jit(solution)/shard_map/states/pallas_call | solution.py:114
  7.0 0.6 collective-permute-start
  7.6 3.9 %states.3.parts = bf16[2,4,128,128]{3,2,1,0:T(8,128)(2,1)S(1)} custom-call(bf16[1024,1152]{1,0:T(8,128)(2,1)S(1)} %get-tuple-element.26.video.video_in, bf16[1152,512]{1,0:T(8,128)(2,1)S(1)} %get-tuple-element.37.wk_hbm, bf16[1152,512]{1,0:T(8,128)(2,1)S(1)} %get-tuple-element.38.wv_hbm), custom_call_target="tpu_custom_call" | custom-call | tf_op jit(solution)/shard_map/states/pallas_call | solution.py:143
  11.5 0.1 collective-permute-start.5
  11.6 0.1 total.2
  11.7 3.0 %collective-permute-start.1 = (bf16[5,64,128]{2,1,0:T(8,128)(2,1)S(1)}, bf16[5,64,128]{2,1,0:T(8,128)(2,1)S(1)}, u32[]{:S(2)}, u32[]{:S(2)}) collective-permute-start(bf16[5,64,128]{2,1,0:T(8,128)(2,1)S(1)} %get-tuple-element.29), channel_id=1, source_target_pairs={{0,2},{2,0},{4,6},{6,4},{8,10},{10,8},{12,14},{14,12},{1,3},{3,1},... | collective-permute-start | bytes 245768 | tf_op jit(solution)/shard_map/ppermute | solution.py:430
  14.8 0.1 total.3
  14.8 1.1 %collective-permute-start.6 = (bf16[4,64,128]{2,1,0:T(8,128)(2,1)S(1)}, bf16[4,64,128]{2,1,0:T(8,128)(2,1)S(1)}, u32[]{:S(2)}, u32[]{:S(2)}) collective-permute-start(bf16[4,64,128]{2,1,0:T(8,128)(2,1)S(1)} %get-tuple-element.39), channel_id=1, source_target_pairs={{0,2},{2,0},{4,6},{6,4},{8,10},{10,8},{12,14},{14,12},{1,3},{3,1},... | collective-permute-start | bytes 196616 | tf_op jit(solution)/shard_map/ppermute | solution.py:430
  15.9 1.6 %collective-permute-done.1.got = bf16[5,64,128]{2,1,0:T(8,128)(2,1)S(1)} collective-permute-done((bf16[5,64,128]{2,1,0:T(8,128)(2,1)S(1)}, bf16[5,64,128]{2,1,0:T(8,128)(2,1)S(1)}, u32[]{:S(2)}, u32[]{:S(2)}) %collective-permute-start.1) | collective-permute-done | bytes 81952 | tf_op jit(solution)/shard_map/ppermute | solution.py:430
  17.6 2.1 %collective-permute-start.2 = (bf16[5,64,128]{2,1,0:T(8,128)(2,1)S(1)}, bf16[5,64,128]{2,1,0:T(8,128)(2,1)S(1)}, u32[]{:S(2)}, u32[]{:S(2)}) collective-permute-start(bf16[5,64,128]{2,1,0:T(8,128)(2,1)S(1)} %get-tuple-element.31), channel_id=1, source_target_pairs={{0,4},{2,6},{4,0},{6,2},{8,12},{10,14},{12,8},{14,10},{1,5},{3,7},... | collective-permute-start | bytes 245768 | tf_op jit(solution)/shard_map/ppermute | solution.py:430
  19.7 1.1 %collective-permute-start.7 = (bf16[4,64,128]{2,1,0:T(8,128)(2,1)S(1)}, bf16[4,64,128]{2,1,0:T(8,128)(2,1)S(1)}, u32[]{:S(2)}, u32[]{:S(2)}) collective-permute-start(bf16[4,64,128]{2,1,0:T(8,128)(2,1)S(1)} %get-tuple-element.41), channel_id=1, source_target_pairs={{0,4},{2,6},{4,0},{6,2},{8,12},{10,14},{12,8},{14,10},{1,5},{3,7},... | collective-permute-start | bytes 196616 | tf_op jit(solution)/shard_map/ppermute | solution.py:430
  20.8 1.5 %collective-permute-done.2.got = bf16[5,64,128]{2,1,0:T(8,128)(2,1)S(1)} collective-permute-done((bf16[5,64,128]{2,1,0:T(8,128)(2,1)S(1)}, bf16[5,64,128]{2,1,0:T(8,128)(2,1)S(1)}, u32[]{:S(2)}, u32[]{:S(2)}) %collective-permute-start.2) | collective-permute-done | bytes 81952 | tf_op jit(solution)/shard_map/ppermute | solution.py:430
  22.3 2.9 %collective-permute-start.3 = (bf16[5,64,128]{2,1,0:T(8,128)(2,1)S(1)}, bf16[5,64,128]{2,1,0:T(8,128)(2,1)S(1)}, u32[]{:S(2)}, u32[]{:S(2)}) collective-permute-start(bf16[5,64,128]{2,1,0:T(8,128)(2,1)S(1)} %get-tuple-element.34), channel_id=1, source_target_pairs={{0,8},{2,10},{4,12},{6,14},{8,0},{10,2},{12,4},{14,6},{1,9},{3,11}... | collective-permute-start | bytes 245768 | tf_op jit(solution)/shard_map/ppermute | solution.py:430
  25.3 1.5 %collective-permute-start.8 = (bf16[4,64,128]{2,1,0:T(8,128)(2,1)S(1)}, bf16[4,64,128]{2,1,0:T(8,128)(2,1)S(1)}, u32[]{:S(2)}, u32[]{:S(2)}) collective-permute-start(bf16[4,64,128]{2,1,0:T(8,128)(2,1)S(1)} %get-tuple-element.44), channel_id=1, source_target_pairs={{0,8},{2,10},{4,12},{6,14},{8,0},{10,2},{12,4},{14,6},{1,9},{3,11}... | collective-permute-start | bytes 196616 | tf_op jit(solution)/shard_map/ppermute | solution.py:430
  26.8 2.5 %collective-permute-done.3.got = bf16[5,64,128]{2,1,0:T(8,128)(2,1)S(1)} collective-permute-done((bf16[5,64,128]{2,1,0:T(8,128)(2,1)S(1)}, bf16[5,64,128]{2,1,0:T(8,128)(2,1)S(1)}, u32[]{:S(2)}, u32[]{:S(2)}) %collective-permute-start.3) | collective-permute-done | bytes 81952 | tf_op jit(solution)/shard_map/ppermute | solution.py:430
  29.4 0.1 collective-permute-start.4
  29.4 1.1 %collective-permute-done.8.got = bf16[4,64,128]{2,1,0:T(8,128)(2,1)S(1)} collective-permute-done((bf16[4,64,128]{2,1,0:T(8,128)(2,1)S(1)}, bf16[4,64,128]{2,1,0:T(8,128)(2,1)S(1)}, u32[]{:S(2)}, u32[]{:S(2)}) %collective-permute-start.8) | collective-permute-done | bytes 65568 | tf_op jit(solution)/shard_map/ppermute | solution.py:430
  30.6 0.1 collective-permute-start.9
  30.6 0.9 %query.3.refs_0_ = bf16[1024,256]{1,0:T(8,128)(2,1)S(1)} custom-call(bf16[1024,1152]{1,0:T(8,128)(2,1)S(1)} %get-tuple-element.26.video.video_in, bf16[1152,1152]{1,0:T(8,128)(2,1)S(1)} %get-tuple-element.27.w), custom_call_target="tpu_custom_call" | custom-call | tf_op jit(solution)/shard_map/query/pallas_call | solution.py:187
  31.5 1.6 %query.4.refs_1_ = bf16[1024,384]{1,0:T(8,128)(2,1)S(1)} custom-call(bf16[1024,1152]{1,0:T(8,128)(2,1)S(1)} %get-tuple-element.26.video.video_in, bf16[1152,1152]{1,0:T(8,128)(2,1)S(1)} %get-tuple-element.27.w), custom_call_target="tpu_custom_call" | custom-call | tf_op jit(solution)/shard_map/query/pallas_call | solution.py:187
  33.1 0.0 copy-start
  33.1 1.7 %query.5 = bf16[1024,512]{1,0:T(8,128)(2,1)S(1)} custom-call(bf16[1024,1152]{1,0:T(8,128)(2,1)S(1)} %get-tuple-element.26.video.video_in, bf16[1152,1152]{1,0:T(8,128)(2,1)S(1)} %get-tuple-element.27.w), custom_call_target="tpu_custom_call" | custom-call | tf_op jit(solution)/shard_map/query/pallas_call | solution.py:187
  34.8 0.0 copy-start.2
  34.8 0.0 copy-done
  34.8 2.6 %partial.1 = f32[1024,1152]{1,0:T(8,128)S(1)} custom-call(bf16[1024,1152]{1,0:T(8,128)(2,1)S(1)} %get-tuple-element.26.video.video_in, bf16[1024,256]{1,0:T(8,128)(2,1)S(1)} %query.3.refs_0_, bf16[1024,384]{1,0:T(8,128)(2,1)S(1)} %query.4.refs_1_, bf16[2,5,128,128]{3,2,1,0:T(8,128)(2,1)S(1)} %get-tuple-element.28.parts.refs_2_, ...), custom_call_target="tpu_custom_call" | custom-call | tf_op jit(solution)/shard_map/partial/pallas_call | solution.py:250
  37.5 0.0 copy-start.1
  37.5 3.5 %latent.1 = bf16[8,160,128]{2,1,0:T(8,128)(2,1)} custom-call(f32[1024,1152]{1,0:T(8,128)S(1)} %partial.1, bf16[1024,512]{1,0:T(8,128)(2,1)S(1)} %query.5, bf16[2,4,128,128]{3,2,1,0:T(8,128)(2,1)S(1)} %states.3.parts, bf16[2,4,128,128]{3,2,1,0:T(8,128)(2,1)S(1)} %collective-permute-done.5.other_parts, bf16[4,64,128]{2,1,0:T(8,128)(2,1)S(1)} %round.11.carry, ...), custom_call_target="tpu_custom_call" | custom-call | tf_op jit(solution)/shard_map/latent/pallas_call | solution.py:301
  41.0 6.3 %all-to-all-start = ((bf16[8,160,128]{2,1,0:T(8,128)(2,1)}), bf16[8,160,128]{2,1,0:T(8,128)(2,1)S(1)}, u32[]{:S(2)}, u32[]{:S(2)}) async-start(bf16[8,160,128]{2,1,0:T(8,128)(2,1)} %latent.1), calls=%async_computation | async-start | bytes 655360 | tf_op jit(solution)/shard_map/all_to_all | solution.py:475
  47.3 10.9 %all-to-all-done.blocks = bf16[8,160,128]{2,1,0:T(8,128)(2,1)S(1)} async-done(((bf16[8,160,128]{2,1,0:T(8,128)(2,1)}), bf16[8,160,128]{2,1,0:T(8,128)(2,1)S(1)}, u32[]{:S(2)}, u32[]{:S(2)}) %all-to-all-start) | async-done | bytes 327712 | tf_op jit(solution)/shard_map/all_to_all | solution.py:475
  58.3 0.1 collective-permute-start.10
  58.4 1.2 %collective-permute-done.10.edge = bf16[8,20,128]{2,1,0:T(8,128)(2,1)S(1)} collective-permute-done((bf16[8,20,128]{2,1,0:T(8,128)(2,1)S(1)}, bf16[8,20,128]{2,1,0:T(8,128)(2,1)S(1)}, u32[]{:S(2)}, u32[]{:S(2)}) %collective-permute-start.10) | collective-permute-done | bytes 40992 | tf_op jit(solution)/shard_map/ppermute | solution.py:490
  59.6 2.7 %decode.1 = bf16[16,16,16,256]{3,2,1,0:T(8,128)(2,1)} custom-call(bf16[8,160,128]{2,1,0:T(8,128)(2,1)S(1)} %all-to-all-done.blocks, bf16[8,20,128]{2,1,0:T(8,128)(2,1)S(1)} %collective-permute-done.10.edge, bf16[3,3,128,256]{3,2,1,0:T(8,128)(2,1)S(1)} %copy-done.1, f32[1,256]{1,0:T(1,128)S(1)} %bitcast.8), custom_call_target="tpu_custom_call" | custom-call | tf_op jit(solution)/shard_map/decode/pallas_call | solution.py:494
  (21 shorter events, 0.3 us)
Async XLA Ops:
  7.0 4.6 %collective-permute-start = (bf16[2,5,128,128]{3,2,1,0:T(8,128)(2,1)S(1)}, bf16[2,5,128,128]{3,2,1,0:T(8,128)(2,1)S(1)}, u32[]{:S(2)}, u32[]{:S(2)}) collective-permute-start(bf16[2,5,128,128]{3,2,1,0:T(8,128)(2,1)S(1)} %get-tuple-element.28.parts.refs_2_), channel_id=1, source_target_pairs={{0,1},{1,0},{2,3},{3,2},{4,5},{5,4},{6,7},{7,6},{8,9},{9,8},{10,11... | collective-permute-start | bytes 983048 | tf_op jit(solution)/shard_map/ppermute | solution.py:453
  11.5 3.2 %collective-permute-start.5 = (bf16[2,4,128,128]{3,2,1,0:T(8,128)(2,1)S(1)}, bf16[2,4,128,128]{3,2,1,0:T(8,128)(2,1)S(1)}, u32[]{:S(2)}, u32[]{:S(2)}) collective-permute-start(bf16[2,4,128,128]{3,2,1,0:T(8,128)(2,1)S(1)} %states.3.parts), channel_id=1, source_target_pairs={{0,1},{1,0},{2,3},{3,2},{4,5},{5,4},{6,7},{7,6},{8,9},{9,8},{10,11... | collective-permute-start | bytes 786440 | tf_op jit(solution)/shard_map/ppermute | solution.py:455
  11.7 5.8 %collective-permute-start.1 = (bf16[5,64,128]{2,1,0:T(8,128)(2,1)S(1)}, bf16[5,64,128]{2,1,0:T(8,128)(2,1)S(1)}, u32[]{:S(2)}, u32[]{:S(2)}) collective-permute-start(bf16[5,64,128]{2,1,0:T(8,128)(2,1)S(1)} %get-tuple-element.29), channel_id=1, source_target_pairs={{0,2},{2,0},{4,6},{6,4},{8,10},{10,8},{12,14},{14,12},{1,3},{3,1},... | collective-permute-start | bytes 245768 | tf_op jit(solution)/shard_map/ppermute | solution.py:430
  14.8 4.9 %collective-permute-start.6 = (bf16[4,64,128]{2,1,0:T(8,128)(2,1)S(1)}, bf16[4,64,128]{2,1,0:T(8,128)(2,1)S(1)}, u32[]{:S(2)}, u32[]{:S(2)}) collective-permute-start(bf16[4,64,128]{2,1,0:T(8,128)(2,1)S(1)} %get-tuple-element.39), channel_id=1, source_target_pairs={{0,2},{2,0},{4,6},{6,4},{8,10},{10,8},{12,14},{14,12},{1,3},{3,1},... | collective-permute-start | bytes 196616 | tf_op jit(solution)/shard_map/ppermute | solution.py:430
  17.6 4.7 %collective-permute-start.2 = (bf16[5,64,128]{2,1,0:T(8,128)(2,1)S(1)}, bf16[5,64,128]{2,1,0:T(8,128)(2,1)S(1)}, u32[]{:S(2)}, u32[]{:S(2)}) collective-permute-start(bf16[5,64,128]{2,1,0:T(8,128)(2,1)S(1)} %get-tuple-element.31), channel_id=1, source_target_pairs={{0,4},{2,6},{4,0},{6,2},{8,12},{10,14},{12,8},{14,10},{1,5},{3,7},... | collective-permute-start | bytes 245768 | tf_op jit(solution)/shard_map/ppermute | solution.py:430
  19.7 5.5 %collective-permute-start.7 = (bf16[4,64,128]{2,1,0:T(8,128)(2,1)S(1)}, bf16[4,64,128]{2,1,0:T(8,128)(2,1)S(1)}, u32[]{:S(2)}, u32[]{:S(2)}) collective-permute-start(bf16[4,64,128]{2,1,0:T(8,128)(2,1)S(1)} %get-tuple-element.41), channel_id=1, source_target_pairs={{0,4},{2,6},{4,0},{6,2},{8,12},{10,14},{12,8},{14,10},{1,5},{3,7},... | collective-permute-start | bytes 196616 | tf_op jit(solution)/shard_map/ppermute | solution.py:430
  22.3 7.0 %collective-permute-start.3 = (bf16[5,64,128]{2,1,0:T(8,128)(2,1)S(1)}, bf16[5,64,128]{2,1,0:T(8,128)(2,1)S(1)}, u32[]{:S(2)}, u32[]{:S(2)}) collective-permute-start(bf16[5,64,128]{2,1,0:T(8,128)(2,1)S(1)} %get-tuple-element.34), channel_id=1, source_target_pairs={{0,8},{2,10},{4,12},{6,14},{8,0},{10,2},{12,4},{14,6},{1,9},{3,11}... | collective-permute-start | bytes 245768 | tf_op jit(solution)/shard_map/ppermute | solution.py:430
  25.3 5.2 %collective-permute-start.8 = (bf16[4,64,128]{2,1,0:T(8,128)(2,1)S(1)}, bf16[4,64,128]{2,1,0:T(8,128)(2,1)S(1)}, u32[]{:S(2)}, u32[]{:S(2)}) collective-permute-start(bf16[4,64,128]{2,1,0:T(8,128)(2,1)S(1)} %get-tuple-element.44), channel_id=1, source_target_pairs={{0,8},{2,10},{4,12},{6,14},{8,0},{10,2},{12,4},{14,6},{1,9},{3,11}... | collective-permute-start | bytes 196616 | tf_op jit(solution)/shard_map/ppermute | solution.py:430
  29.4 5.4 %collective-permute-start.4 = (bf16[5,64,128]{2,1,0:T(8,128)(2,1)S(1)}, bf16[5,64,128]{2,1,0:T(8,128)(2,1)S(1)}, u32[]{:S(2)}, u32[]{:S(2)}) collective-permute-start(bf16[5,64,128]{2,1,0:T(8,128)(2,1)S(1)} %round.8.refs_4_), channel_id=1, source_target_pairs={{0,1},{1,0},{2,3},{3,2},{4,5},{5,4},{6,7},{7,6},{8,9},{9,8},{10,11... | collective-permute-start | bytes 245768 | tf_op jit(solution)/shard_map/ppermute | solution.py:468
  30.6 6.9 %collective-permute-start.9 = (bf16[4,64,128]{2,1,0:T(8,128)(2,1)S(1)}, bf16[4,64,128]{2,1,0:T(8,128)(2,1)S(1)}, u32[]{:S(2)}, u32[]{:S(2)}) collective-permute-start(bf16[4,64,128]{2,1,0:T(8,128)(2,1)S(1)} %round.11.carry), channel_id=1, source_target_pairs={{0,1},{1,0},{2,3},{3,2},{4,5},{5,4},{6,7},{7,6},{8,9},{9,8},{10,11... | collective-permute-start | bytes 196616 | tf_op jit(solution)/shard_map/ppermute | solution.py:468
  33.1 1.8 %copy-start = (bf16[1152,1152]{1,0:T(8,128)(2,1)S(1)}, bf16[1152,1152]{1,0:T(8,128)(2,1)}, u32[]{:S(2)}) copy-start(bf16[1152,1152]{1,0:T(8,128)(2,1)} %w_out.1) | copy-start | bytes 7962628
  34.8 2.7 %copy-start.2 = (bf16[1152,128]{1,0:T(8,128)(2,1)S(1)}, bf16[1152,128]{1,0:T(8,128)(2,1)}, u32[]{:S(2)}) copy-start(bf16[1152,128]{1,0:T(8,128)(2,1)} %w_latent.1) | copy-start | bytes 884740
  37.5 22.1 %copy-start.1 = (bf16[3,3,128,256]{3,2,1,0:T(8,128)(2,1)S(1)}, bf16[3,3,128,256]{3,2,1,0:T(8,128)(2,1)}, u32[]{:S(2)}) copy-start(bf16[3,3,128,256]{3,2,1,0:T(8,128)(2,1)} %weight.1) | copy-start | bytes 1769476
  37.5 22.1 %copy-start.3 = (f32[256]{0:T(256)S(1)}, f32[256]{0:T(256)}, u32[]{:S(2)}) copy-start(f32[256]{0:T(256)} %param.15) | copy-start | bytes 3076
  41.0 17.2 %all-to-all-start = ((bf16[8,160,128]{2,1,0:T(8,128)(2,1)}), bf16[8,160,128]{2,1,0:T(8,128)(2,1)S(1)}, u32[]{:S(2)}, u32[]{:S(2)}) async-start(bf16[8,160,128]{2,1,0:T(8,128)(2,1)} %latent.1), calls=%async_computation | async-start | bytes 655360 | tf_op jit(solution)/shard_map/all_to_all | solution.py:475
  58.3 1.3 %collective-permute-start.10 = (bf16[8,20,128]{2,1,0:T(8,128)(2,1)S(1)}, bf16[8,20,128]{2,1,0:T(8,128)(2,1)S(1)}, u32[]{:S(2)}, u32[]{:S(2)}) collective-permute-start(bf16[8,20,128]{2,1,0:T(8,128)(2,1)S(1)} %maximum_select_fusion), channel_id=1, source_target_pairs={{0,1},{1,0},{2,3},{3,2},{4,5},{5,4},{6,7},{7,6},{8,9},{9,8},{10,11... | collective-permute-start | bytes 122888 | tf_op jit(solution)/shard_map/ppermute | solution.py:490

commit v7 on v6

--- a/solution.py
+++ b/solution.py
@@ -481,12 +481,35 @@
     width = conv_weight.shape[3]
     group = frames * own
     main = grid_rows * group
-    sides = blocks[:, main:].reshape(tiles, 2 * frames, grid_rows, channels)
-
-    def edge(r):
-        return jnp.concatenate([blocks[:, r * group : (r + 1) * group], sides[:, :, r]], axis=1)
-
-    mine = jnp.where(lax.axis_index("space") == 0, edge(grid_rows - 1), edge(0))
+
+    def edge_kernel(blocks, out):
+        def take(r):
+            for t in range(tiles):
+                out[t, :group] = blocks[t, r * group : (r + 1) * group]
+                sides = blocks[t, main:].astype(F32)
+                out[t, group:] = jnp.concatenate(
+                    [sides[k * grid_rows + r : k * grid_rows + r + 1] for k in range(2 * frames)],
+                    axis=0,
+                ).astype(BF16)
+
+        upper = lax.axis_index("space") == 0
+
+        @pl.when(upper)
+        def _():
+            take(grid_rows - 1)
+
+        @pl.when(jnp.logical_not(upper))
+        def _():
+            take(0)
+
+    mine = pl.pallas_call(
+        edge_kernel,
+        out_shape=shape((tiles, group + 2 * frames, channels), BF16),
+        in_specs=[IN_VMEM],
+        out_specs=IN_VMEM,
+        name="edge",
+        compiler_params=params(4),
+    )(blocks)
     beside = lax.ppermute(mine, "space", SWAP)
     total = tiles * group
     chunk = 1 if grid_rows % 1 == 0 else grid_rows

time: 62.5 us -> 62.1 us (level)
  blocking collectives: 0 us -> 17.7 us
  waiting for transfers between devices: 18.9 us -> 7.95 us
  starting transfers between devices: 18.9 us -> 12.6 us
  Pallas kernels: 24.2 us -> 23.5 us
    all_to_all x0 -> x1, blocking collectives: none -> 17.7 us  [body(): blocks = lax.all_to_all(blocks, 'tm', 0, 0, tiled=True)]
    all_to_all x1 -> x0, waiting for transfers between devices: 10.9 us -> none  [body(): blocks = lax.all_to_all(blocks, 'tm', 0, 0, tiled=True)]
    all_to_all x1 -> x0, starting transfers between devices: 6.3 us -> none  [body(): blocks = lax.all_to_all(blocks, 'tm', 0, 0, tiled=True)]
    pallas_call x1, Pallas kernels: 3.48 us -> 2.76 us  [latent_call(): pl.pallas_call(functools.partial(latent_kernel, frames, columns, tiles),...]
  transfers between devices with their start and end apart: 12 -> 11, of which waited for: 6 -> 5; matrix products, arithmetic and copies ran while one was open for 0% -> 0% of each run, Pallas kernels for 18% -> 18%
where the time goes in v7:
time: 62.1 us; the launch traced here: 61.9 us
  Pallas kernels  23.5 us (38%)
  blocking collectives  17.7 us (29%)
  starting transfers between devices  12.6 us (20%)
  waiting for transfers between devices  7.95 us (13%)
    all_to_all x1, blocking collectives, body(): blocks = lax.all_to_all(blocks, 'tm', 0, 0, tiled=True)  17.7 us
    ppermute x6, starting transfers between devices, prefix_rounds(): got = lax.ppermute(sent, 'tm', [(i, i ^ step) for i in range(tiles)])  11.8 us
    pallas_call x1, Pallas kernels, first_states(): pl.pallas_call(functools.partial(states_kernel, frames, heads, False), ou...  7.03 us
    ppermute x6, waiting for transfers between devices, prefix_rounds(): got = lax.ppermute(sent, 'tm', [(i, i ^ step) for i in range(tiles)])  6.72 us
    pallas_call x3, Pallas kernels, query_call(): pl.pallas_call(kernel, out_shape=shape((video.shape[0], width), BF16), in...  4.1 us
    pallas_call x1, Pallas kernels, second_states(): pl.pallas_call(functools.partial(states_kernel, frames, heads, True), out...  3.92 us
    pallas_call x1, Pallas kernels, latent_call(): pl.pallas_call(functools.partial(latent_kernel, frames, columns, tiles),...  2.76 us
    pallas_call x1, Pallas kernels, decode(): pl.pallas_call(functools.partial(decode_kernel, frames, tiles, grid_rows,...  2.67 us
  transfers between devices with their start and end apart: 11, of which 5 were waited for; matrix products, arithmetic and copies ran while one was open for 0% of the time, Pallas kernels for 18%

profile of v7, /device:TPU:0, one launch (start us, length us, event | category | flops | bytes accessed | tf_op | source)
XLA Modules:
  0.0 61.9 jit_solution(14050084844535228812)
XLA Ops:
  0.0 7.0 %states.2 = (bf16[2,5,128,128]{3,2,1,0:T(8,128)(2,1)S(1)}, bf16[1024,1152]{1,0:T(8,128)(2,1)S(1)}, bf16[1152,512]{1,0:T(8,128)(2,1)S(1)}, bf16[1152,512]{1,0:T(8,128)(2,1)S(1)}, bf16[1152,1152]{1,0:T(8,128)(2,1)S(1)}) custom-call(bf16[1024,1152]{1,0:T(8,128)(2,1)} %bitcast.3, bf16[1152,1152]{1,0:T(8,128)(2,1)} %wk_hbm.1, bf16[1152,1152]{1,0:T(8,128)(2,1)} %wv_hbm.1, ...), custom_call_target="tpu_custom_call" | custom-call | tf_op jit(solution)/shard_map/states/pallas_call | solution.py:114
  7.0 0.6 collective-permute-start
  7.6 3.9 %states.3.parts = bf16[2,4,128,128]{3,2,1,0:T(8,128)(2,1)S(1)} custom-call(bf16[1024,1152]{1,0:T(8,128)(2,1)S(1)} %get-tuple-element.26.video.video_in, bf16[1152,512]{1,0:T(8,128)(2,1)S(1)} %get-tuple-element.37.wk_hbm, bf16[1152,512]{1,0:T(8,128)(2,1)S(1)} %get-tuple-element.38.wv_hbm), custom_call_target="tpu_custom_call" | custom-call | tf_op jit(solution)/shard_map/states/pallas_call | solution.py:143
  11.5 0.1 collective-permute-start.5
  11.6 0.1 total.2
  11.7 3.0 %collective-permute-start.1 = (bf16[5,64,128]{2,1,0:T(8,128)(2,1)S(1)}, bf16[5,64,128]{2,1,0:T(8,128)(2,1)S(1)}, u32[]{:S(2)}, u32[]{:S(2)}) collective-permute-start(bf16[5,64,128]{2,1,0:T(8,128)(2,1)S(1)} %get-tuple-element.29), channel_id=1, source_target_pairs={{0,2},{2,0},{4,6},{6,4},{8,10},{10,8},{12,14},{14,12},{1,3},{3,1},... | collective-permute-start | bytes 245768 | tf_op jit(solution)/shard_map/ppermute | solution.py:430
  14.8 0.1 total.3
  14.8 1.1 %collective-permute-start.6 = (bf16[4,64,128]{2,1,0:T(8,128)(2,1)S(1)}, bf16[4,64,128]{2,1,0:T(8,128)(2,1)S(1)}, u32[]{:S(2)}, u32[]{:S(2)}) collective-permute-start(bf16[4,64,128]{2,1,0:T(8,128)(2,1)S(1)} %get-tuple-element.39), channel_id=1, source_target_pairs={{0,2},{2,0},{4,6},{6,4},{8,10},{10,8},{12,14},{14,12},{1,3},{3,1},... | collective-permute-start | bytes 196616 | tf_op jit(solution)/shard_map/ppermute | solution.py:430
  15.9 1.6 %collective-permute-done.1.got = bf16[5,64,128]{2,1,0:T(8,128)(2,1)S(1)} collective-permute-done((bf16[5,64,128]{2,1,0:T(8,128)(2,1)S(1)}, bf16[5,64,128]{2,1,0:T(8,128)(2,1)S(1)}, u32[]{:S(2)}, u32[]{:S(2)}) %collective-permute-start.1) | collective-permute-done | bytes 81952 | tf_op jit(solution)/shard_map/ppermute | solution.py:430
  17.6 2.1 %collective-permute-start.2 = (bf16[5,64,128]{2,1,0:T(8,128)(2,1)S(1)}, bf16[5,64,128]{2,1,0:T(8,128)(2,1)S(1)}, u32[]{:S(2)}, u32[]{:S(2)}) collective-permute-start(bf16[5,64,128]{2,1,0:T(8,128)(2,1)S(1)} %get-tuple-element.31), channel_id=1, source_target_pairs={{0,4},{2,6},{4,0},{6,2},{8,12},{10,14},{12,8},{14,10},{1,5},{3,7},... | collective-permute-start | bytes 245768 | tf_op jit(solution)/shard_map/ppermute | solution.py:430
  19.7 1.1 %collective-permute-start.7 = (bf16[4,64,128]{2,1,0:T(8,128)(2,1)S(1)}, bf16[4,64,128]{2,1,0:T(8,128)(2,1)S(1)}, u32[]{:S(2)}, u32[]{:S(2)}) collective-permute-start(bf16[4,64,128]{2,1,0:T(8,128)(2,1)S(1)} %get-tuple-element.41), channel_id=1, source_target_pairs={{0,4},{2,6},{4,0},{6,2},{8,12},{10,14},{12,8},{14,10},{1,5},{3,7},... | collective-permute-start | bytes 196616 | tf_op jit(solution)/shard_map/ppermute | solution.py:430
  20.8 1.5 %collective-permute-done.2.got = bf16[5,64,128]{2,1,0:T(8,128)(2,1)S(1)} collective-permute-done((bf16[5,64,128]{2,1,0:T(8,128)(2,1)S(1)}, bf16[5,64,128]{2,1,0:T(8,128)(2,1)S(1)}, u32[]{:S(2)}, u32[]{:S(2)}) %collective-permute-start.2) | collective-permute-done | bytes 81952 | tf_op jit(solution)/shard_map/ppermute | solution.py:430
  22.3 2.9 %collective-permute-start.3 = (bf16[5,64,128]{2,1,0:T(8,128)(2,1)S(1)}, bf16[5,64,128]{2,1,0:T(8,128)(2,1)S(1)}, u32[]{:S(2)}, u32[]{:S(2)}) collective-permute-start(bf16[5,64,128]{2,1,0:T(8,128)(2,1)S(1)} %get-tuple-element.34), channel_id=1, source_target_pairs={{0,8},{2,10},{4,12},{6,14},{8,0},{10,2},{12,4},{14,6},{1,9},{3,11}... | collective-permute-start | bytes 245768 | tf_op jit(solution)/shard_map/ppermute | solution.py:430
  25.3 1.5 %collective-permute-start.8 = (bf16[4,64,128]{2,1,0:T(8,128)(2,1)S(1)}, bf16[4,64,128]{2,1,0:T(8,128)(2,1)S(1)}, u32[]{:S(2)}, u32[]{:S(2)}) collective-permute-start(bf16[4,64,128]{2,1,0:T(8,128)(2,1)S(1)} %get-tuple-element.44), channel_id=1, source_target_pairs={{0,8},{2,10},{4,12},{6,14},{8,0},{10,2},{12,4},{14,6},{1,9},{3,11}... | collective-permute-start | bytes 196616 | tf_op jit(solution)/shard_map/ppermute | solution.py:430
  26.8 2.5 %collective-permute-done.3.got = bf16[5,64,128]{2,1,0:T(8,128)(2,1)S(1)} collective-permute-done((bf16[5,64,128]{2,1,0:T(8,128)(2,1)S(1)}, bf16[5,64,128]{2,1,0:T(8,128)(2,1)S(1)}, u32[]{:S(2)}, u32[]{:S(2)}) %collective-permute-start.3) | collective-permute-done | bytes 81952 | tf_op jit(solution)/shard_map/ppermute | solution.py:430
  29.4 0.1 collective-permute-start.4
  29.4 1.1 %collective-permute-done.8.got = bf16[4,64,128]{2,1,0:T(8,128)(2,1)S(1)} collective-permute-done((bf16[4,64,128]{2,1,0:T(8,128)(2,1)S(1)}, bf16[4,64,128]{2,1,0:T(8,128)(2,1)S(1)}, u32[]{:S(2)}, u32[]{:S(2)}) %collective-permute-start.8) | collective-permute-done | bytes 65568 | tf_op jit(solution)/shard_map/ppermute | solution.py:430
  30.6 0.1 collective-permute-start.9
  30.6 0.9 %query.3.refs_0_ = bf16[1024,256]{1,0:T(8,128)(2,1)S(1)} custom-call(bf16[1024,1152]{1,0:T(8,128)(2,1)S(1)} %get-tuple-element.26.video.video_in, bf16[1152,1152]{1,0:T(8,128)(2,1)S(1)} %get-tuple-element.27.w), custom_call_target="tpu_custom_call" | custom-call | tf_op jit(solution)/shard_map/query/pallas_call | solution.py:187
  31.5 1.6 %query.4.refs_1_ = bf16[1024,384]{1,0:T(8,128)(2,1)S(1)} custom-call(bf16[1024,1152]{1,0:T(8,128)(2,1)S(1)} %get-tuple-element.26.video.video_in, bf16[1152,1152]{1,0:T(8,128)(2,1)S(1)} %get-tuple-element.27.w), custom_call_target="tpu_custom_call" | custom-call | tf_op jit(solution)/shard_map/query/pallas_call | solution.py:187
  33.1 0.0 copy-start
  33.1 1.7 %query.5 = bf16[1024,512]{1,0:T(8,128)(2,1)S(1)} custom-call(bf16[1024,1152]{1,0:T(8,128)(2,1)S(1)} %get-tuple-element.26.video.video_in, bf16[1152,1152]{1,0:T(8,128)(2,1)S(1)} %get-tuple-element.27.w), custom_call_target="tpu_custom_call" | custom-call | tf_op jit(solution)/shard_map/query/pallas_call | solution.py:187
  34.8 0.0 copy-start.2
  34.8 0.0 copy-done
  34.8 2.6 %partial.1 = f32[1024,1152]{1,0:T(8,128)S(1)} custom-call(bf16[1024,1152]{1,0:T(8,128)(2,1)S(1)} %get-tuple-element.26.video.video_in, bf16[1024,256]{1,0:T(8,128)(2,1)S(1)} %query.3.refs_0_, bf16[1024,384]{1,0:T(8,128)(2,1)S(1)} %query.4.refs_1_, bf16[2,5,128,128]{3,2,1,0:T(8,128)(2,1)S(1)} %get-tuple-element.28.parts.refs_2_, ...), custom_call_target="tpu_custom_call" | custom-call | tf_op jit(solution)/shard_map/partial/pallas_call | solution.py:250
  37.5 0.0 copy-start.1
  37.5 0.0 copy-start.3
  37.5 2.8 %latent.1 = bf16[8,160,128]{2,1,0:T(8,128)(2,1)S(1)} custom-call(f32[1024,1152]{1,0:T(8,128)S(1)} %partial.1, bf16[1024,512]{1,0:T(8,128)(2,1)S(1)} %query.5, bf16[2,4,128,128]{3,2,1,0:T(8,128)(2,1)S(1)} %states.3.parts, bf16[2,4,128,128]{3,2,1,0:T(8,128)(2,1)S(1)} %collective-permute-done.5.other_parts, bf16[4,64,128]{2,1,0:T(8,128)(2,1)S(1)} %round.11.carry, ...), custom_call_target="tpu_custom_call" | custom-call | tf_op jit(solution)/shard_map/latent/pallas_call | solution.py:301
  40.3 17.7 %all_to_all.5.blocks = bf16[8,160,128]{2,1,0:T(8,128)(2,1)S(1)} all-to-all(bf16[8,160,128]{2,1,0:T(8,128)(2,1)S(1)} %latent.1), channel_id=1, replica_groups=mesh['groups'=2,'tm'=8,'space'=2] {'tm'}, dimensions={0} | all-to-all | bytes 655360 | tf_op jit(solution)/shard_map/all_to_all | solution.py:475
  58.0 0.1 collective-permute-start.10
  58.0 1.2 %collective-permute-done.10.edge = bf16[8,20,128]{2,1,0:T(8,128)(2,1)S(1)} collective-permute-done((bf16[8,20,128]{2,1,0:T(8,128)(2,1)S(1)}, bf16[8,20,128]{2,1,0:T(8,128)(2,1)S(1)}, u32[]{:S(2)}, u32[]{:S(2)}) %collective-permute-start.10) | collective-permute-done | bytes 40992 | tf_op jit(solution)/shard_map/ppermute | solution.py:513
  59.3 2.7 %decode.1 = bf16[16,16,16,256]{3,2,1,0:T(8,128)(2,1)} custom-call(bf16[8,160,128]{2,1,0:T(8,128)(2,1)S(1)} %all_to_all.5.blocks, bf16[8,20,128]{2,1,0:T(8,128)(2,1)S(1)} %collective-permute-done.10.edge, bf16[3,3,128,256]{3,2,1,0:T(8,128)(2,1)S(1)} %copy-done.1, f32[1,256]{1,0:T(1,128)S(1)} %bitcast.2), custom_call_target="tpu_custom_call" | custom-call | tf_op jit(solution)/shard_map/decode/pallas_call | solution.py:517
  (16 shorter events, 0.2 us)
Async XLA Ops:
  7.0 4.6 %collective-permute-start = (bf16[2,5,128,128]{3,2,1,0:T(8,128)(2,1)S(1)}, bf16[2,5,128,128]{3,2,1,0:T(8,128)(2,1)S(1)}, u32[]{:S(2)}, u32[]{:S(2)}) collective-permute-start(bf16[2,5,128,128]{3,2,1,0:T(8,128)(2,1)S(1)} %get-tuple-element.28.parts.refs_2_), channel_id=1, source_target_pairs={{0,1},{1,0},{2,3},{3,2},{4,5},{5,4},{6,7},{7,6},{8,9},{9,8},{10,11... | collective-permute-start | bytes 983048 | tf_op jit(solution)/shard_map/ppermute | solution.py:453
  11.5 3.2 %collective-permute-start.5 = (bf16[2,4,128,128]{3,2,1,0:T(8,128)(2,1)S(1)}, bf16[2,4,128,128]{3,2,1,0:T(8,128)(2,1)S(1)}, u32[]{:S(2)}, u32[]{:S(2)}) collective-permute-start(bf16[2,4,128,128]{3,2,1,0:T(8,128)(2,1)S(1)} %states.3.parts), channel_id=1, source_target_pairs={{0,1},{1,0},{2,3},{3,2},{4,5},{5,4},{6,7},{7,6},{8,9},{9,8},{10,11... | collective-permute-start | bytes 786440 | tf_op jit(solution)/shard_map/ppermute | solution.py:455
  11.7 5.8 %collective-permute-start.1 = (bf16[5,64,128]{2,1,0:T(8,128)(2,1)S(1)}, bf16[5,64,128]{2,1,0:T(8,128)(2,1)S(1)}, u32[]{:S(2)}, u32[]{:S(2)}) collective-permute-start(bf16[5,64,128]{2,1,0:T(8,128)(2,1)S(1)} %get-tuple-element.29), channel_id=1, source_target_pairs={{0,2},{2,0},{4,6},{6,4},{8,10},{10,8},{12,14},{14,12},{1,3},{3,1},... | collective-permute-start | bytes 245768 | tf_op jit(solution)/shard_map/ppermute | solution.py:430
  14.8 4.9 %collective-permute-start.6 = (bf16[4,64,128]{2,1,0:T(8,128)(2,1)S(1)}, bf16[4,64,128]{2,1,0:T(8,128)(2,1)S(1)}, u32[]{:S(2)}, u32[]{:S(2)}) collective-permute-start(bf16[4,64,128]{2,1,0:T(8,128)(2,1)S(1)} %get-tuple-element.39), channel_id=1, source_target_pairs={{0,2},{2,0},{4,6},{6,4},{8,10},{10,8},{12,14},{14,12},{1,3},{3,1},... | collective-permute-start | bytes 196616 | tf_op jit(solution)/shard_map/ppermute | solution.py:430
  17.6 4.7 %collective-permute-start.2 = (bf16[5,64,128]{2,1,0:T(8,128)(2,1)S(1)}, bf16[5,64,128]{2,1,0:T(8,128)(2,1)S(1)}, u32[]{:S(2)}, u32[]{:S(2)}) collective-permute-start(bf16[5,64,128]{2,1,0:T(8,128)(2,1)S(1)} %get-tuple-element.31), channel_id=1, source_target_pairs={{0,4},{2,6},{4,0},{6,2},{8,12},{10,14},{12,8},{14,10},{1,5},{3,7},... | collective-permute-start | bytes 245768 | tf_op jit(solution)/shard_map/ppermute | solution.py:430
  19.7 5.5 %collective-permute-start.7 = (bf16[4,64,128]{2,1,0:T(8,128)(2,1)S(1)}, bf16[4,64,128]{2,1,0:T(8,128)(2,1)S(1)}, u32[]{:S(2)}, u32[]{:S(2)}) collective-permute-start(bf16[4,64,128]{2,1,0:T(8,128)(2,1)S(1)} %get-tuple-element.41), channel_id=1, source_target_pairs={{0,4},{2,6},{4,0},{6,2},{8,12},{10,14},{12,8},{14,10},{1,5},{3,7},... | collective-permute-start | bytes 196616 | tf_op jit(solution)/shard_map/ppermute | solution.py:430
  22.3 7.0 %collective-permute-start.3 = (bf16[5,64,128]{2,1,0:T(8,128)(2,1)S(1)}, bf16[5,64,128]{2,1,0:T(8,128)(2,1)S(1)}, u32[]{:S(2)}, u32[]{:S(2)}) collective-permute-start(bf16[5,64,128]{2,1,0:T(8,128)(2,1)S(1)} %get-tuple-element.34), channel_id=1, source_target_pairs={{0,8},{2,10},{4,12},{6,14},{8,0},{10,2},{12,4},{14,6},{1,9},{3,11}... | collective-permute-start | bytes 245768 | tf_op jit(solution)/shard_map/ppermute | solution.py:430
  25.3 5.2 %collective-permute-start.8 = (bf16[4,64,128]{2,1,0:T(8,128)(2,1)S(1)}, bf16[4,64,128]{2,1,0:T(8,128)(2,1)S(1)}, u32[]{:S(2)}, u32[]{:S(2)}) collective-permute-start(bf16[4,64,128]{2,1,0:T(8,128)(2,1)S(1)} %get-tuple-element.44), channel_id=1, source_target_pairs={{0,8},{2,10},{4,12},{6,14},{8,0},{10,2},{12,4},{14,6},{1,9},{3,11}... | collective-permute-start | bytes 196616 | tf_op jit(solution)/shard_map/ppermute | solution.py:430
  29.4 5.4 %collective-permute-start.4 = (bf16[5,64,128]{2,1,0:T(8,128)(2,1)S(1)}, bf16[5,64,128]{2,1,0:T(8,128)(2,1)S(1)}, u32[]{:S(2)}, u32[]{:S(2)}) collective-permute-start(bf16[5,64,128]{2,1,0:T(8,128)(2,1)S(1)} %round.8.refs_4_), channel_id=1, source_target_pairs={{0,1},{1,0},{2,3},{3,2},{4,5},{5,4},{6,7},{7,6},{8,9},{9,8},{10,11... | collective-permute-start | bytes 245768 | tf_op jit(solution)/shard_map/ppermute | solution.py:468
  30.6 6.9 %collective-permute-start.9 = (bf16[4,64,128]{2,1,0:T(8,128)(2,1)S(1)}, bf16[4,64,128]{2,1,0:T(8,128)(2,1)S(1)}, u32[]{:S(2)}, u32[]{:S(2)}) collective-permute-start(bf16[4,64,128]{2,1,0:T(8,128)(2,1)S(1)} %round.11.carry), channel_id=1, source_target_pairs={{0,1},{1,0},{2,3},{3,2},{4,5},{5,4},{6,7},{7,6},{8,9},{9,8},{10,11... | collective-permute-start | bytes 196616 | tf_op jit(solution)/shard_map/ppermute | solution.py:468
  33.1 1.8 %copy-start = (bf16[1152,1152]{1,0:T(8,128)(2,1)S(1)}, bf16[1152,1152]{1,0:T(8,128)(2,1)}, u32[]{:S(2)}) copy-start(bf16[1152,1152]{1,0:T(8,128)(2,1)} %w_out.1) | copy-start | bytes 7962628
  34.8 2.7 %copy-start.2 = (bf16[1152,128]{1,0:T(8,128)(2,1)S(1)}, bf16[1152,128]{1,0:T(8,128)(2,1)}, u32[]{:S(2)}) copy-start(bf16[1152,128]{1,0:T(8,128)(2,1)} %w_latent.1) | copy-start | bytes 884740
  37.5 21.8 %copy-start.1 = (bf16[3,3,128,256]{3,2,1,0:T(8,128)(2,1)S(1)}, bf16[3,3,128,256]{3,2,1,0:T(8,128)(2,1)}, u32[]{:S(2)}) copy-start(bf16[3,3,128,256]{3,2,1,0:T(8,128)(2,1)} %weight.1) | copy-start | bytes 1769476
  37.5 21.8 %copy-start.3 = (f32[256]{0:T(256)S(1)}, f32[256]{0:T(256)}, u32[]{:S(2)}) copy-start(f32[256]{0:T(256)} %param.15) | copy-start | bytes 3076
  58.0 1.3 %collective-permute-start.10 = (bf16[8,20,128]{2,1,0:T(8,128)(2,1)S(1)}, bf16[8,20,128]{2,1,0:T(8,128)(2,1)S(1)}, u32[]{:S(2)}, u32[]{:S(2)}) collective-permute-start(bf16[8,20,128]{2,1,0:T(8,128)(2,1)S(1)} %edge.1), channel_id=1, source_target_pairs={{0,1},{1,0},{2,3},{3,2},{4,5},{5,4},{6,7},{7,6},{8,9},{9,8},{10,11... | collective-permute-start | bytes 122888 | tf_op jit(solution)/shard_map/ppermute | solution.py:513

commit v8 on v7

--- a/solution.py
+++ b/solution.py
@@ -68,11 +68,11 @@
 
     if not fetched:
         soon = min(2, heads)
+        for f in range(frames):
+            video_copy(f).start()
         for h in range(soon):
             for c in weight_copies(h):
                 c.start()
-        for f in range(frames):
-            video_copy(f).start()
         for f in range(frames):
             video_copy(f).wait()
         for h in range(soon, heads):
@@ -313,46 +313,47 @@
     )(partial, *chunk[0], *chunk[1:], w_out, w_latent)
 
 
-def decode_kernel(
-    frames, tiles, grid_rows, own, chunk, blocks, edge, weight, bias,
-    out, left, middle, right, taps, wide, staged, sem,
-):
+def lay_rows(frames, tiles, grid_rows, own, rows, blocks, edge, left, middle, right):
     group = frames * own
     main = grid_rows * group
-    tile = lax.axis_index("space")
+    channels = left.shape[-1]
     column = lax.broadcasted_iota(jnp.int32, (group, 1), 0) % own
-    channels = weight.shape[2]
-
-    def lay(row, t, body, sides):
+
+    def lay(index, t, body, sides):
         at = slice(t * group, (t + 1) * group)
-        first = jnp.concatenate(
-            [jnp.broadcast_to(sides[f : f + 1], (own, channels)) for f in range(frames)], axis=0
-        )
-        last = jnp.concatenate(
-            [jnp.broadcast_to(sides[frames + f : frames + f + 1], (own, channels))
-             for f in range(frames)], axis=0
+        first, last = (
+            jnp.concatenate(
+                [jnp.broadcast_to(sides[k : k + 1], (own, channels))
+                 for k in range(side * frames, (side + 1) * frames)], axis=0
+            )
+            for side in range(2)
         )
         down = pltpu.roll(body, 1, 0)
         up = pltpu.roll(body, group - 1, 0)
-        left[row, at, :] = jnp.where(column == 0, first, down).astype(BF16)
-        middle[row, at, :] = body.astype(BF16)
-        right[row, at, :] = jnp.where(column == own - 1, last, up).astype(BF16)
+        left[index, at, :] = jnp.where(column == 0, first, down).astype(BF16)
+        middle[index, at, :] = body.astype(BF16)
+        right[index, at, :] = jnp.where(column == own - 1, last, up).astype(BF16)
 
     for t in range(tiles):
         everything = blocks[t].astype(F32)
-        for r in range(grid_rows):
-            body = everything[r * group : (r + 1) * group]
-            sides = [
-                everything[main + s * grid_rows + r : main + s * grid_rows + r + 1]
-                for s in range(2 * frames)
-            ]
-            lay(r + 1, t, body, jnp.concatenate(sides, axis=0))
-        beside = edge[t].astype(F32)
-        for row, present in ((0, tile == 1), (grid_rows + 1, tile == 0)):
-            there = jnp.where(present, beside, 0.0)
-            lay(row, t, there[:group], there[group:])
-
+        beside = None if edge is None else edge[t].astype(F32)
+        for index, row in enumerate(rows):
+            if 0 <= row < grid_rows:
+                sides = [
+                    everything[main + k * grid_rows + row : main + k * grid_rows + row + 1]
+                    for k in range(2 * frames)
+                ]
+                lay(index, t, everything[row * group : (row + 1) * group],
+                    jnp.concatenate(sides, axis=0))
+            else:
+                present = lax.axis_index("space") == (1 if row < 0 else 0)
+                there = jnp.where(present, beside, 0.0)
+                lay(index, t, there[:group], there[group:])
+
+
+def lay_taps(weight, taps):
     w = weight[...].astype(F32)
+    channels = weight.shape[2]
     row_sets = (((0,), (1, 2)), ((0, 1), (2,)))
     for a in range(2):
         for b in range(2):
@@ -362,35 +363,92 @@
                     at = (2 * i + j) * channels
                     taps[2 * a + b, at : at + channels, :] = (0.5 * tap).astype(BF16)
 
+
+def decode_row(own, index, bias, left, middle, right, taps, wide, staged, first):
     views = ((left, middle), (middle, right))
-    total = tiles * group
     half_bias = 0.5 * bias[...]
     lanes = wide.shape[-1]
-    copies = []
-    for i in range(grid_rows // chunk):
-        for a in range(2):
-            for b in range(2):
-                lhs = jnp.concatenate(
-                    [v[i * chunk + a + k : i * chunk + a + k + chunk].reshape(
-                        chunk * total, channels) for k in range(2) for v in views[b]], axis=1
+    total = left.shape[1]
+    for a in range(2):
+        for b in range(2):
+            lhs = jnp.concatenate(
+                [v[index + a + k] for k in range(2) for v in views[b]], axis=1
+            )
+            h = matmul(lhs, taps[2 * a + b]) + half_bias
+            value = h + h * jnp.tanh(h)
+            for n in range(wide.shape[1]):
+                wide[a, n, pl.ds(b, total, stride=2), :] = value[:, n * lanes : (n + 1) * lanes]
+        for n in range(wide.shape[1]):
+            shaped = wide[a, n].reshape(total // own, 2 * own, lanes)
+            staged[:, first + a, :, n * lanes : (n + 1) * lanes] = shaped.astype(BF16)
+
+
+def decode_scratch(rows, total, channels, width):
+    return [pltpu.VMEM((rows, total, channels), BF16)] * 3 + [
+        pltpu.VMEM((2, width // HEAD, 2 * total, HEAD), F32)
+    ]
+
+
+def interior_call(blocks, weight, bias, frames, tiles, grid_rows, own):
+    channels, width = weight.shape[2:]
+    total = tiles * frames * own
+
+    def kernel(blocks, weight, bias, out, taps, left, middle, right, wide):
+        lay_taps(weight, taps)
+        lay_rows(frames, tiles, grid_rows, own, range(grid_rows), blocks, None,
+                 left, middle, right)
+        for r in range(1, grid_rows - 1):
+            decode_row(own, r - 1, bias, left, middle, right, taps, wide, out, 2 * (r - 1))
+
+    return pl.pallas_call(
+        kernel,
+        out_shape=[
+            shape((tiles * frames, 2 * (grid_rows - 2), 2 * own, width), BF16),
+            shape((4, 4 * channels, width), BF16),
+        ],
+        in_specs=[IN_VMEM] * 3,
+        out_specs=[IN_VMEM] * 2,
+        scratch_shapes=decode_scratch(grid_rows, total, channels, width),
+        name="interior",
+        compiler_params=params(24),
+    )(blocks, weight, bias)
+
+
+def border_call(blocks, edge, interior, taps, bias, frames, tiles, grid_rows, own):
+    channels = blocks.shape[2]
+    width = taps.shape[2]
+    total = tiles * frames * own
+    last = 2 * (grid_rows - 1)
+
+    def kernel(blocks, edge, interior, taps, bias, out, left, middle, right, wide, staged, sem):
+        copies = [pltpu.make_async_copy(interior, out.at[:, pl.ds(2, last - 2)], sem.at[2])]
+        copies[0].start()
+        rows = [-1, 0, 1, grid_rows - 2, grid_rows - 1, grid_rows]
+        lay_rows(frames, tiles, grid_rows, own, rows, blocks, edge, left, middle, right)
+        for i, (index, row) in enumerate(((0, 0), (3, last))):
+            decode_row(own, index, bias, left, middle, right, taps, wide, staged, 2 * i)
+            copies.append(
+                pltpu.make_async_copy(
+                    staged.at[:, pl.ds(2 * i, 2)], out.at[:, pl.ds(row, 2)], sem.at[i]
                 )
-                h = matmul(lhs, taps[2 * a + b]) + half_bias
-                value = h + h * jnp.tanh(h)
-                for n in range(wide.shape[1]):
-                    wide[a, n, pl.ds(b, chunk * total, stride=2), :] = (
-                        value[:, n * lanes : (n + 1) * lanes]
-                    )
-            for n in range(wide.shape[1]):
-                shaped = wide[a, n].reshape(chunk, tiles * frames, 2 * own, lanes)
-                for r in range(chunk):
-                    staged[:, 2 * (i * chunk + r) + a, :, n * lanes : (n + 1) * lanes] = (
-                        shaped[r].astype(BF16)
-                    )
-        rows = pl.ds(2 * i * chunk, 2 * chunk)
-        copies.append(pltpu.make_async_copy(staged.at[:, rows], out.at[:, rows], sem.at[i]))
-        copies[-1].start()
-    for c in copies:
-        c.wait()
+            )
+            copies[-1].start()
+        for c in copies:
+            c.wait()
+
+    return pl.pallas_call(
+        kernel,
+        out_shape=shape((tiles * frames, 2 * grid_rows, 2 * own, width), BF16),
+        in_specs=[IN_VMEM] * 5,
+        out_specs=IN_HBM,
+        scratch_shapes=decode_scratch(6, total, channels, width)
+        + [
+            pltpu.VMEM((tiles * frames, 4, 2 * own, width), BF16),
+            pltpu.SemaphoreType.DMA((3,)),
+        ],
+        name="border",
+        compiler_params=params(24),
+    )(blocks, edge, interior, taps, bias)
 
 
 def round_call(step, last, got, total, carry):
@@ -511,24 +569,11 @@
         compiler_params=params(4),
     )(blocks)
     beside = lax.ppermute(mine, "space", SWAP)
-    total = tiles * group
-    chunk = 1 if grid_rows % 1 == 0 else grid_rows
-    dims = (tiles * frames, 2 * grid_rows, 2 * own, width)
-    return pl.pallas_call(
-        functools.partial(decode_kernel, frames, tiles, grid_rows, own, chunk),
-        out_shape=shape(dims, BF16),
-        in_specs=[IN_VMEM] * 4,
-        out_specs=IN_HBM,
-        scratch_shapes=[pltpu.VMEM((grid_rows + 2, total, channels), BF16)] * 3
-        + [
-            pltpu.VMEM((4, 4 * channels, width), BF16),
-            pltpu.VMEM((2, width // HEAD, 2 * chunk * total, HEAD), F32),
-            pltpu.VMEM(dims, BF16),
-            pltpu.SemaphoreType.DMA((grid_rows // chunk,)),
-        ],
-        name="decode",
-        compiler_params=params(36),
-    )(blocks, beside, conv_weight, conv_bias.reshape(1, width))
+    bias = conv_bias.reshape(1, width)
+    interior, taps = interior_call(
+        blocks, conv_weight, bias, frames, tiles, grid_rows, own
+    )
+    return border_call(blocks, beside, interior, taps, bias, frames, tiles, grid_rows, own)
 
 
 def solution(mesh):

time: 62.1 us -> 61.4 us (0.989)
  waiting for transfers between devices: 7.95 us -> 6.73 us
    ppermute x1, waiting for transfers between devices: 1.22 us -> 0.01 us  [decode(): beside = lax.ppermute(mine, 'space', SWAP)]
    pallas_call x1 -> x2, Pallas kernels: 2.67 us -> 3.31 us  [the longest x1 1.71 us: border_call(): pl.pallas_call(kernel, out_shape=shape((tiles * frames, 2 * grid_rows, 2...]
  transfers between devices with their start and end apart: 11 -> 11, of which waited for: 5 -> 4; matrix products, arithmetic and copies ran while one was open for 0% -> 0% of each run, Pallas kernels for 18% -> 21%
where the time goes in v8:
time: 61.4 us; the launch traced here: 61.2 us
  Pallas kernels  23.9 us (39%)
  blocking collectives  17.7 us (29%)
  starting transfers between devices  12.6 us (21%)
  waiting for transfers between devices  6.73 us (11%)
    all_to_all x1, blocking collectives, body(): blocks = lax.all_to_all(blocks, 'tm', 0, 0, tiled=True)  17.7 us
    ppermute x6, starting transfers between devices, prefix_rounds(): got = lax.ppermute(sent, 'tm', [(i, i ^ step) for i in range(tiles)])  11.8 us
    pallas_call x1, Pallas kernels, first_states(): pl.pallas_call(functools.partial(states_kernel, frames, heads, False), ou...  6.82 us
    ppermute x6, waiting for transfers between devices, prefix_rounds(): got = lax.ppermute(sent, 'tm', [(i, i ^ step) for i in range(tiles)])  6.72 us
    pallas_call x3, Pallas kernels, query_call(): pl.pallas_call(kernel, out_shape=shape((video.shape[0], width), BF16), in...  4.1 us
    pallas_call x1, Pallas kernels, second_states(): pl.pallas_call(functools.partial(states_kernel, frames, heads, True), out...  3.92 us
    pallas_call x1, Pallas kernels, latent_call(): pl.pallas_call(functools.partial(latent_kernel, frames, columns, tiles),...  2.76 us
    pallas_call x1, Pallas kernels, partial_call(): pl.pallas_call(kernel, out_shape=shape((tokens, d), F32), in_specs=[IN_VM...  2.64 us
  transfers between devices with their start and end apart: 11, of which 4 were waited for; matrix products, arithmetic and copies ran while one was open for 0% of the time, Pallas kernels for 21%

profile of v8, /device:TPU:0, one launch (start us, length us, event | category | flops | bytes accessed | tf_op | source)
XLA Modules:
  0.0 61.2 jit_solution(15580121313234597824)
XLA Ops:
  0.0 6.8 %states.2 = (bf16[2,5,128,128]{3,2,1,0:T(8,128)(2,1)S(1)}, bf16[1024,1152]{1,0:T(8,128)(2,1)S(1)}, bf16[1152,512]{1,0:T(8,128)(2,1)S(1)}, bf16[1152,512]{1,0:T(8,128)(2,1)S(1)}, bf16[1152,1152]{1,0:T(8,128)(2,1)S(1)}) custom-call(bf16[1024,1152]{1,0:T(8,128)(2,1)} %bitcast.4, bf16[1152,1152]{1,0:T(8,128)(2,1)} %wk_hbm.1, bf16[1152,1152]{1,0:T(8,128)(2,1)} %wv_hbm.1, ...), custom_call_target="tpu_custom_call" | custom-call | tf_op jit(solution)/shard_map/states/pallas_call | solution.py:114
  6.8 0.6 collective-permute-start
  7.4 3.9 %states.3.parts = bf16[2,4,128,128]{3,2,1,0:T(8,128)(2,1)S(1)} custom-call(bf16[1024,1152]{1,0:T(8,128)(2,1)S(1)} %get-tuple-element.28.video.video_in, bf16[1152,512]{1,0:T(8,128)(2,1)S(1)} %get-tuple-element.39.wk_hbm, bf16[1152,512]{1,0:T(8,128)(2,1)S(1)} %get-tuple-element.40.wv_hbm), custom_call_target="tpu_custom_call" | custom-call | tf_op jit(solution)/shard_map/states/pallas_call | solution.py:143
  11.3 0.1 collective-permute-start.5
  11.4 0.1 total.2
  11.5 3.1 %collective-permute-start.1 = (bf16[5,64,128]{2,1,0:T(8,128)(2,1)S(1)}, bf16[5,64,128]{2,1,0:T(8,128)(2,1)S(1)}, u32[]{:S(2)}, u32[]{:S(2)}) collective-permute-start(bf16[5,64,128]{2,1,0:T(8,128)(2,1)S(1)} %get-tuple-element.31), channel_id=1, source_target_pairs={{0,2},{2,0},{4,6},{6,4},{8,10},{10,8},{12,14},{14,12},{1,3},{3,1},... | collective-permute-start | bytes 245768 | tf_op jit(solution)/shard_map/ppermute | solution.py:488
  14.5 0.1 total.3
  14.6 1.1 %collective-permute-start.6 = (bf16[4,64,128]{2,1,0:T(8,128)(2,1)S(1)}, bf16[4,64,128]{2,1,0:T(8,128)(2,1)S(1)}, u32[]{:S(2)}, u32[]{:S(2)}) collective-permute-start(bf16[4,64,128]{2,1,0:T(8,128)(2,1)S(1)} %get-tuple-element.41), channel_id=1, source_target_pairs={{0,2},{2,0},{4,6},{6,4},{8,10},{10,8},{12,14},{14,12},{1,3},{3,1},... | collective-permute-start | bytes 196616 | tf_op jit(solution)/shard_map/ppermute | solution.py:488
  15.7 1.6 %collective-permute-done.1.got = bf16[5,64,128]{2,1,0:T(8,128)(2,1)S(1)} collective-permute-done((bf16[5,64,128]{2,1,0:T(8,128)(2,1)S(1)}, bf16[5,64,128]{2,1,0:T(8,128)(2,1)S(1)}, u32[]{:S(2)}, u32[]{:S(2)}) %collective-permute-start.1) | collective-permute-done | bytes 81952 | tf_op jit(solution)/shard_map/ppermute | solution.py:488
  17.4 2.1 %collective-permute-start.2 = (bf16[5,64,128]{2,1,0:T(8,128)(2,1)S(1)}, bf16[5,64,128]{2,1,0:T(8,128)(2,1)S(1)}, u32[]{:S(2)}, u32[]{:S(2)}) collective-permute-start(bf16[5,64,128]{2,1,0:T(8,128)(2,1)S(1)} %get-tuple-element.33), channel_id=1, source_target_pairs={{0,4},{2,6},{4,0},{6,2},{8,12},{10,14},{12,8},{14,10},{1,5},{3,7},... | collective-permute-start | bytes 245768 | tf_op jit(solution)/shard_map/ppermute | solution.py:488
  19.5 1.1 %collective-permute-start.7 = (bf16[4,64,128]{2,1,0:T(8,128)(2,1)S(1)}, bf16[4,64,128]{2,1,0:T(8,128)(2,1)S(1)}, u32[]{:S(2)}, u32[]{:S(2)}) collective-permute-start(bf16[4,64,128]{2,1,0:T(8,128)(2,1)S(1)} %get-tuple-element.43), channel_id=1, source_target_pairs={{0,4},{2,6},{4,0},{6,2},{8,12},{10,14},{12,8},{14,10},{1,5},{3,7},... | collective-permute-start | bytes 196616 | tf_op jit(solution)/shard_map/ppermute | solution.py:488
  20.6 1.5 %collective-permute-done.2.got = bf16[5,64,128]{2,1,0:T(8,128)(2,1)S(1)} collective-permute-done((bf16[5,64,128]{2,1,0:T(8,128)(2,1)S(1)}, bf16[5,64,128]{2,1,0:T(8,128)(2,1)S(1)}, u32[]{:S(2)}, u32[]{:S(2)}) %collective-permute-start.2) | collective-permute-done | bytes 81952 | tf_op jit(solution)/shard_map/ppermute | solution.py:488
  22.1 2.9 %collective-permute-start.3 = (bf16[5,64,128]{2,1,0:T(8,128)(2,1)S(1)}, bf16[5,64,128]{2,1,0:T(8,128)(2,1)S(1)}, u32[]{:S(2)}, u32[]{:S(2)}) collective-permute-start(bf16[5,64,128]{2,1,0:T(8,128)(2,1)S(1)} %get-tuple-element.36), channel_id=1, source_target_pairs={{0,8},{2,10},{4,12},{6,14},{8,0},{10,2},{12,4},{14,6},{1,9},{3,11}... | collective-permute-start | bytes 245768 | tf_op jit(solution)/shard_map/ppermute | solution.py:488
  25.1 1.5 %collective-permute-start.8 = (bf16[4,64,128]{2,1,0:T(8,128)(2,1)S(1)}, bf16[4,64,128]{2,1,0:T(8,128)(2,1)S(1)}, u32[]{:S(2)}, u32[]{:S(2)}) collective-permute-start(bf16[4,64,128]{2,1,0:T(8,128)(2,1)S(1)} %get-tuple-element.46), channel_id=1, source_target_pairs={{0,8},{2,10},{4,12},{6,14},{8,0},{10,2},{12,4},{14,6},{1,9},{3,11}... | collective-permute-start | bytes 196616 | tf_op jit(solution)/shard_map/ppermute | solution.py:488
  26.6 2.5 %collective-permute-done.3.got = bf16[5,64,128]{2,1,0:T(8,128)(2,1)S(1)} collective-permute-done((bf16[5,64,128]{2,1,0:T(8,128)(2,1)S(1)}, bf16[5,64,128]{2,1,0:T(8,128)(2,1)S(1)}, u32[]{:S(2)}, u32[]{:S(2)}) %collective-permute-start.3) | collective-permute-done | bytes 81952 | tf_op jit(solution)/shard_map/ppermute | solution.py:488
  29.1 0.1 collective-permute-start.4
  29.2 1.1 %collective-permute-done.8.got = bf16[4,64,128]{2,1,0:T(8,128)(2,1)S(1)} collective-permute-done((bf16[4,64,128]{2,1,0:T(8,128)(2,1)S(1)}, bf16[4,64,128]{2,1,0:T(8,128)(2,1)S(1)}, u32[]{:S(2)}, u32[]{:S(2)}) %collective-permute-start.8) | collective-permute-done | bytes 65568 | tf_op jit(solution)/shard_map/ppermute | solution.py:488
  30.4 0.1 collective-permute-start.9
  30.4 0.9 %query.3.refs_0_ = bf16[1024,256]{1,0:T(8,128)(2,1)S(1)} custom-call(bf16[1024,1152]{1,0:T(8,128)(2,1)S(1)} %get-tuple-element.28.video.video_in, bf16[1152,1152]{1,0:T(8,128)(2,1)S(1)} %get-tuple-element.29.w), custom_call_target="tpu_custom_call" | custom-call | tf_op jit(solution)/shard_map/query/pallas_call | solution.py:187
  31.3 1.6 %query.4.refs_1_ = bf16[1024,384]{1,0:T(8,128)(2,1)S(1)} custom-call(bf16[1024,1152]{1,0:T(8,128)(2,1)S(1)} %get-tuple-element.28.video.video_in, bf16[1152,1152]{1,0:T(8,128)(2,1)S(1)} %get-tuple-element.29.w), custom_call_target="tpu_custom_call" | custom-call | tf_op jit(solution)/shard_map/query/pallas_call | solution.py:187
  32.9 0.0 copy-start
  32.9 1.7 %query.5 = bf16[1024,512]{1,0:T(8,128)(2,1)S(1)} custom-call(bf16[1024,1152]{1,0:T(8,128)(2,1)S(1)} %get-tuple-element.28.video.video_in, bf16[1152,1152]{1,0:T(8,128)(2,1)S(1)} %get-tuple-element.29.w), custom_call_target="tpu_custom_call" | custom-call | tf_op jit(solution)/shard_map/query/pallas_call | solution.py:187
  34.6 0.0 copy-start.2
  34.6 0.0 copy-done
  34.6 2.6 %partial.1 = f32[1024,1152]{1,0:T(8,128)S(1)} custom-call(bf16[1024,1152]{1,0:T(8,128)(2,1)S(1)} %get-tuple-element.28.video.video_in, bf16[1024,256]{1,0:T(8,128)(2,1)S(1)} %query.3.refs_0_, bf16[1024,384]{1,0:T(8,128)(2,1)S(1)} %query.4.refs_1_, bf16[2,5,128,128]{3,2,1,0:T(8,128)(2,1)S(1)} %get-tuple-element.30.parts.refs_2_, ...), custom_call_target="tpu_custom_call" | custom-call | tf_op jit(solution)/shard_map/partial/pallas_call | solution.py:250
  37.3 0.0 copy-start.1
  37.3 0.0 copy-start.3
  37.3 2.8 %latent.1 = bf16[8,160,128]{2,1,0:T(8,128)(2,1)S(1)} custom-call(f32[1024,1152]{1,0:T(8,128)S(1)} %partial.1, bf16[1024,512]{1,0:T(8,128)(2,1)S(1)} %query.5, bf16[2,4,128,128]{3,2,1,0:T(8,128)(2,1)S(1)} %states.3.parts, bf16[2,4,128,128]{3,2,1,0:T(8,128)(2,1)S(1)} %collective-permute-done.5.other_parts, bf16[4,64,128]{2,1,0:T(8,128)(2,1)S(1)} %round.11.carry, ...), custom_call_target="tpu_custom_call" | custom-call | tf_op jit(solution)/shard_map/latent/pallas_call | solution.py:301
  40.1 17.7 %all_to_all.5.blocks = bf16[8,160,128]{2,1,0:T(8,128)(2,1)S(1)} all-to-all(bf16[8,160,128]{2,1,0:T(8,128)(2,1)S(1)} %latent.1), channel_id=1, replica_groups=mesh['groups'=2,'tm'=8,'space'=2] {'tm'}, dimensions={0} | all-to-all | bytes 655360 | tf_op jit(solution)/shard_map/all_to_all | solution.py:533
  57.7 0.1 collective-permute-start.10
  57.8 1.6 %interior.1 = (bf16[16,12,16,256]{3,2,1,0:T(8,128)(2,1)S(1)}, bf16[4,512,256]{2,1,0:T(8,128)(2,1)S(1)}) custom-call(bf16[8,160,128]{2,1,0:T(8,128)(2,1)S(1)} %all_to_all.5.blocks, bf16[3,3,128,256]{3,2,1,0:T(8,128)(2,1)S(1)} %copy-done.1, f32[1,256]{1,0:T(1,128)S(1)} %bitcast.2), custom_call_target="tpu_custom_call" | custom-call | tf_op jit(solution)/shard_map/interior/pallas_call | solution.py:403
  59.5 1.7 %border.1 = bf16[16,16,16,256]{3,2,1,0:T(8,128)(2,1)} custom-call(bf16[8,160,128]{2,1,0:T(8,128)(2,1)S(1)} %all_to_all.5.blocks, bf16[8,20,128]{2,1,0:T(8,128)(2,1)S(1)} %collective-permute-done.10.edge, bf16[16,12,16,256]{3,2,1,0:T(8,128)(2,1)S(1)} %get-tuple-element.49.interior, bf16[4,512,256]{2,1,0:T(8,128)(2,1)S(1)} %get-tuple-element.50.taps, ...), custom_call_target="tpu_custom_call" | custom-call | tf_op jit(solution)/shard_map/border/pallas_call | solution.py:439
  (17 shorter events, 0.2 us)
Async XLA Ops:
  6.8 4.6 %collective-permute-start = (bf16[2,5,128,128]{3,2,1,0:T(8,128)(2,1)S(1)}, bf16[2,5,128,128]{3,2,1,0:T(8,128)(2,1)S(1)}, u32[]{:S(2)}, u32[]{:S(2)}) collective-permute-start(bf16[2,5,128,128]{3,2,1,0:T(8,128)(2,1)S(1)} %get-tuple-element.30.parts.refs_2_), channel_id=1, source_target_pairs={{0,1},{1,0},{2,3},{3,2},{4,5},{5,4},{6,7},{7,6},{8,9},{9,8},{10,11... | collective-permute-start | bytes 983048 | tf_op jit(solution)/shard_map/ppermute | solution.py:511
  11.3 3.2 %collective-permute-start.5 = (bf16[2,4,128,128]{3,2,1,0:T(8,128)(2,1)S(1)}, bf16[2,4,128,128]{3,2,1,0:T(8,128)(2,1)S(1)}, u32[]{:S(2)}, u32[]{:S(2)}) collective-permute-start(bf16[2,4,128,128]{3,2,1,0:T(8,128)(2,1)S(1)} %states.3.parts), channel_id=1, source_target_pairs={{0,1},{1,0},{2,3},{3,2},{4,5},{5,4},{6,7},{7,6},{8,9},{9,8},{10,11... | collective-permute-start | bytes 786440 | tf_op jit(solution)/shard_map/ppermute | solution.py:513
  11.5 5.8 %collective-permute-start.1 = (bf16[5,64,128]{2,1,0:T(8,128)(2,1)S(1)}, bf16[5,64,128]{2,1,0:T(8,128)(2,1)S(1)}, u32[]{:S(2)}, u32[]{:S(2)}) collective-permute-start(bf16[5,64,128]{2,1,0:T(8,128)(2,1)S(1)} %get-tuple-element.31), channel_id=1, source_target_pairs={{0,2},{2,0},{4,6},{6,4},{8,10},{10,8},{12,14},{14,12},{1,3},{3,1},... | collective-permute-start | bytes 245768 | tf_op jit(solution)/shard_map/ppermute | solution.py:488
  14.6 4.8 %collective-permute-start.6 = (bf16[4,64,128]{2,1,0:T(8,128)(2,1)S(1)}, bf16[4,64,128]{2,1,0:T(8,128)(2,1)S(1)}, u32[]{:S(2)}, u32[]{:S(2)}) collective-permute-start(bf16[4,64,128]{2,1,0:T(8,128)(2,1)S(1)} %get-tuple-element.41), channel_id=1, source_target_pairs={{0,2},{2,0},{4,6},{6,4},{8,10},{10,8},{12,14},{14,12},{1,3},{3,1},... | collective-permute-start | bytes 196616 | tf_op jit(solution)/shard_map/ppermute | solution.py:488
  17.4 4.7 %collective-permute-start.2 = (bf16[5,64,128]{2,1,0:T(8,128)(2,1)S(1)}, bf16[5,64,128]{2,1,0:T(8,128)(2,1)S(1)}, u32[]{:S(2)}, u32[]{:S(2)}) collective-permute-start(bf16[5,64,128]{2,1,0:T(8,128)(2,1)S(1)} %get-tuple-element.33), channel_id=1, source_target_pairs={{0,4},{2,6},{4,0},{6,2},{8,12},{10,14},{12,8},{14,10},{1,5},{3,7},... | collective-permute-start | bytes 245768 | tf_op jit(solution)/shard_map/ppermute | solution.py:488
  19.5 5.6 %collective-permute-start.7 = (bf16[4,64,128]{2,1,0:T(8,128)(2,1)S(1)}, bf16[4,64,128]{2,1,0:T(8,128)(2,1)S(1)}, u32[]{:S(2)}, u32[]{:S(2)}) collective-permute-start(bf16[4,64,128]{2,1,0:T(8,128)(2,1)S(1)} %get-tuple-element.43), channel_id=1, source_target_pairs={{0,4},{2,6},{4,0},{6,2},{8,12},{10,14},{12,8},{14,10},{1,5},{3,7},... | collective-permute-start | bytes 196616 | tf_op jit(solution)/shard_map/ppermute | solution.py:488
  22.1 7.0 %collective-permute-start.3 = (bf16[5,64,128]{2,1,0:T(8,128)(2,1)S(1)}, bf16[5,64,128]{2,1,0:T(8,128)(2,1)S(1)}, u32[]{:S(2)}, u32[]{:S(2)}) collective-permute-start(bf16[5,64,128]{2,1,0:T(8,128)(2,1)S(1)} %get-tuple-element.36), channel_id=1, source_target_pairs={{0,8},{2,10},{4,12},{6,14},{8,0},{10,2},{12,4},{14,6},{1,9},{3,11}... | collective-permute-start | bytes 245768 | tf_op jit(solution)/shard_map/ppermute | solution.py:488
  25.1 5.2 %collective-permute-start.8 = (bf16[4,64,128]{2,1,0:T(8,128)(2,1)S(1)}, bf16[4,64,128]{2,1,0:T(8,128)(2,1)S(1)}, u32[]{:S(2)}, u32[]{:S(2)}) collective-permute-start(bf16[4,64,128]{2,1,0:T(8,128)(2,1)S(1)} %get-tuple-element.46), channel_id=1, source_target_pairs={{0,8},{2,10},{4,12},{6,14},{8,0},{10,2},{12,4},{14,6},{1,9},{3,11}... | collective-permute-start | bytes 196616 | tf_op jit(solution)/shard_map/ppermute | solution.py:488
  29.1 5.4 %collective-permute-start.4 = (bf16[5,64,128]{2,1,0:T(8,128)(2,1)S(1)}, bf16[5,64,128]{2,1,0:T(8,128)(2,1)S(1)}, u32[]{:S(2)}, u32[]{:S(2)}) collective-permute-start(bf16[5,64,128]{2,1,0:T(8,128)(2,1)S(1)} %round.8.refs_4_), channel_id=1, source_target_pairs={{0,1},{1,0},{2,3},{3,2},{4,5},{5,4},{6,7},{7,6},{8,9},{9,8},{10,11... | collective-permute-start | bytes 245768 | tf_op jit(solution)/shard_map/ppermute | solution.py:526
  30.4 6.9 %collective-permute-start.9 = (bf16[4,64,128]{2,1,0:T(8,128)(2,1)S(1)}, bf16[4,64,128]{2,1,0:T(8,128)(2,1)S(1)}, u32[]{:S(2)}, u32[]{:S(2)}) collective-permute-start(bf16[4,64,128]{2,1,0:T(8,128)(2,1)S(1)} %round.11.carry), channel_id=1, source_target_pairs={{0,1},{1,0},{2,3},{3,2},{4,5},{5,4},{6,7},{7,6},{8,9},{9,8},{10,11... | collective-permute-start | bytes 196616 | tf_op jit(solution)/shard_map/ppermute | solution.py:526
  32.9 1.8 %copy-start = (bf16[1152,1152]{1,0:T(8,128)(2,1)S(1)}, bf16[1152,1152]{1,0:T(8,128)(2,1)}, u32[]{:S(2)}) copy-start(bf16[1152,1152]{1,0:T(8,128)(2,1)} %w_out.1) | copy-start | bytes 7962628
  34.6 2.7 %copy-start.2 = (bf16[1152,128]{1,0:T(8,128)(2,1)S(1)}, bf16[1152,128]{1,0:T(8,128)(2,1)}, u32[]{:S(2)}) copy-start(bf16[1152,128]{1,0:T(8,128)(2,1)} %w_latent.1) | copy-start | bytes 884740
  37.3 20.6 %copy-start.1 = (bf16[3,3,128,256]{3,2,1,0:T(8,128)(2,1)S(1)}, bf16[3,3,128,256]{3,2,1,0:T(8,128)(2,1)}, u32[]{:S(2)}) copy-start(bf16[3,3,128,256]{3,2,1,0:T(8,128)(2,1)} %weight.1) | copy-start | bytes 1769476
  37.3 20.6 %copy-start.3 = (f32[256]{0:T(256)S(1)}, f32[256]{0:T(256)}, u32[]{:S(2)}) copy-start(f32[256]{0:T(256)} %param.15) | copy-start | bytes 3076
  57.7 1.7 %collective-permute-start.10 = (bf16[8,20,128]{2,1,0:T(8,128)(2,1)S(1)}, bf16[8,20,128]{2,1,0:T(8,128)(2,1)S(1)}, u32[]{:S(2)}, u32[]{:S(2)}) collective-permute-start(bf16[8,20,128]{2,1,0:T(8,128)(2,1)S(1)} %edge.1), channel_id=1, source_target_pairs={{0,1},{1,0},{2,3},{3,2},{4,5},{5,4},{6,7},{7,6},{8,9},{9,8},{10,11... | collective-permute-start | bytes 122888 | tf_op jit(solution)/shard_map/ppermute | solution.py:571

commit v9 on v8

--- a/solution.py
+++ b/solution.py
@@ -40,7 +40,7 @@
 
 def states_kernel(frames, heads, fetched, video_in, wk_hbm, wv_hbm, *refs):
     if fetched:
-        parts_out, key, value = refs
+        parts_out, mine_out, theirs_out, key, value = refs
         video, wk, wv = video_in, wk_hbm, wv_hbm
         late = []
     else:
@@ -96,7 +96,9 @@
 
     lax.fori_loop(0, heads, one_head, 0)
 
+    totals = []
     for h in range(heads):
+        total = None
         for f in range(frames):
             rows = slice(f * per, (f + 1) * per)
             state = lax.dot_general(
@@ -104,6 +106,14 @@
                 preferred_element_type=F32,
             )
             parts_out[f, h] = state.astype(BF16)
+            total = state if total is None else total + state
+        totals.append(total)
+    if fetched:
+        lower = lax.axis_index("space") == 0
+        half = heads // 2
+        for h in range(half):
+            mine_out[h] = jnp.where(lower, totals[h], totals[half + h])
+            theirs_out[h] = jnp.where(lower, totals[half + h], totals[h]).astype(BF16)
     for c in late:
         c.wait()
 
@@ -142,9 +152,13 @@
     heads = wk.shape[1] // HEAD
     return pl.pallas_call(
         functools.partial(states_kernel, frames, heads, True),
-        out_shape=shape((frames, heads, HEAD, HEAD), BF16),
+        out_shape=[
+            shape((frames, heads, HEAD, HEAD), BF16),
+            shape((heads // 2, HEAD, HEAD), F32),
+            shape((heads // 2, HEAD, HEAD), BF16),
+        ],
         in_specs=[IN_VMEM] * 3,
-        out_specs=IN_VMEM,
+        out_specs=[IN_VMEM] * 3,
         scratch_shapes=[
             pltpu.VMEM((heads, tokens, HEAD), BF16),
             pltpu.VMEM((heads, tokens, HEAD), BF16),
@@ -178,6 +192,22 @@
         name="total",
         compiler_params=params(4),
     )(parts, other_parts)
+
+
+def add_call(mine, got):
+    def kernel(mine, got, out, sent):
+        total = mine[...] + got[...].astype(F32)
+        out[...] = total
+        sent[...] = total.astype(BF16)
+
+    return pl.pallas_call(
+        kernel,
+        out_shape=[shape(mine.shape, F32), shape(mine.shape, BF16)],
+        in_specs=[IN_VMEM] * 2,
+        out_specs=[IN_VMEM] * 2,
+        name="add",
+        compiler_params=params(4),
+    )(mine, got)
 
 
 def query_call(video, w, first, width):
@@ -258,17 +288,74 @@
     )(video, *queries, *chunk, w_out)
 
 
+def attend_half(frames, half, query, parts, other_parts, carry, used, head_out):
+    heads = carry.shape[0]
+    per = head_out.shape[0] // frames
+    used[...] = jnp.zeros_like(used)
+    for h in range(heads):
+        running = carry[h].astype(F32)
+        at = (h % 2) * HEAD
+        for f in range(frames):
+            own = half * heads + h
+            running = running + parts[f, own].astype(F32) + other_parts[f, own].astype(F32)
+            used[f, h // 2, at : at + HEAD, at : at + HEAD] = running.astype(BF16)
+    for f in range(frames):
+        rows = slice(f * per, (f + 1) * per)
+        for p in range(pl.cdiv(heads, 2)):
+            width = min(2, heads - 2 * p) * HEAD
+            first = 2 * p * HEAD
+            cols = pl.ds(pl.multiple_of(half * heads * HEAD + first, HEAD), width)
+            attended = matmul(query[rows, cols], used[f, p, :width, :width])
+            for h in range(width // HEAD):
+                one = attended[:, h * HEAD : (h + 1) * HEAD]
+                scale = lax.rsqrt(jnp.mean(one * one, axis=1, keepdims=True) + EPS)
+                at = first + h * HEAD
+                head_out[rows, at : at + HEAD] = (one * scale).astype(BF16)
+
+
+def half_rows(w_out, half, width):
+    first = w_out.shape[0] - 2 * width
+    return w_out[pl.ds(pl.multiple_of(first + half * width, HEAD), width), :]
+
+
+def own_call(partial, chunk, w_out, frames):
+    query, parts, other_parts, carry, _ = chunk
+    tokens, d = partial.shape
+    heads = carry.shape[0]
+    width = heads * HEAD
+
+    def kernel(partial, query, parts, other_parts, carry, w_out, out, used, head_out):
+        half = lax.axis_index("space")
+        attend_half(frames, half, query, parts, other_parts, carry, used, head_out)
+        w = half_rows(w_out, half, width)
+        per = tokens // frames
+        for f in range(frames):
+            rows = slice(f * per, (f + 1) * per)
+            out[rows, :] = partial[rows, :] + matmul(head_out[rows, :], w)
+
+    return pl.pallas_call(
+        kernel,
+        out_shape=shape((tokens, d), F32),
+        in_specs=[IN_VMEM] * 6,
+        out_specs=IN_VMEM,
+        scratch_shapes=[used_shape(frames, heads), pltpu.VMEM((tokens, width), BF16)],
+        name="own",
+        compiler_params=params(20),
+    )(partial, query, parts, other_parts, carry, w_out)
+
+
 def latent_kernel(
-    frames, columns, tiles, partial, query, parts, other_parts, carry, other_carry,
+    frames, columns, tiles, partial, query, parts, other_parts, carry,
     w_out, w_latent, out, used, head_out, latent,
 ):
-    tokens, d = partial.shape
+    tokens, _ = partial.shape
     per = tokens // frames
-    width = head_out.shape[1]
-    attend(frames, [query], parts, other_parts, carry, other_carry, used, head_out)
+    half = 1 - lax.axis_index("space")
+    attend_half(frames, half, query, parts, other_parts, carry, used, head_out)
+    w = half_rows(w_out, half, head_out.shape[1])
     for f in range(frames):
         rows = slice(f * per, (f + 1) * per)
-        summed = partial[rows, :] + matmul(head_out[rows, :], w_out[d - width :, :])
+        summed = partial[rows, :] + matmul(head_out[rows, :], w)
         scale = lax.rsqrt(jnp.mean(summed * summed, axis=1, keepdims=True) + EPS)
         latent[rows, :] = matmul(summed.astype(BF16), w_latent[...]) * scale
 
@@ -294,14 +381,15 @@
 
 
 def latent_call(partial, chunk, w_out, w_latent, frames, columns, tiles):
+    query, parts, other_parts, _, other_carry = chunk
     tokens, _ = partial.shape
     channels = w_latent.shape[1]
-    heads = chunk[3].shape[0]
+    heads = other_carry.shape[0]
     rows = tokens // columns * (columns // tiles + 2)
     return pl.pallas_call(
         functools.partial(latent_kernel, frames, columns, tiles),
         out_shape=shape((tiles, rows, channels), BF16),
-        in_specs=[IN_VMEM] * 8,
+        in_specs=[IN_VMEM] * 7,
         out_specs=IN_VMEM,
         scratch_shapes=[
             used_shape(frames, heads),
@@ -310,7 +398,7 @@
         ],
         name="latent",
         compiler_params=params(20),
-    )(partial, *chunk[0], *chunk[1:], w_out, w_latent)
+    )(partial, query, parts, other_parts, other_carry, w_out, w_latent)
 
 
 def lay_rows(frames, tiles, grid_rows, own, rows, blocks, edge, left, middle, right):
@@ -504,18 +592,22 @@
     own = columns // tiles
     flat = video.reshape(-1, d)
     heads = d // HEAD
-    split = heads - heads // 2
+    split = heads - heads // 4 * 2
     parts_a, near, wk_b, wv_b, near_query = first_states(
         flat, w_key, w_value, w_query, frames, split
     )
     other_a = lax.ppermute(parts_a, "space", SWAP)
-    parts_b = second_states(near, wk_b, wv_b, frames)
+    parts_b, mine_b, theirs_b = second_states(near, wk_b, wv_b, frames)
+    got_b = lax.ppermute(theirs_b, "space", SWAP)
     other_b = lax.ppermute(parts_b, "space", SWAP)
+    total_a = total_call(parts_a, other_a)
+    total_b = add_call(mine_b, got_b)
 
     ready = {}
-    for name, first, parts, other in (("a", 0, parts_a, other_a), ("b", split, parts_b, other_b)):
+    for name, first, parts, other, (total, sent) in (
+        ("a", 0, parts_a, other_a, total_a), ("b", split, parts_b, other_b, total_b),
+    ):
         count = parts.shape[1]
-        total, sent = total_call(parts, other)
         cuts = [first, first + 2, first + count] if name == "a" else [first, first + count]
         queries = []
         for low, high in zip(cuts, cuts[1:]):
@@ -527,9 +619,9 @@
         ready[name] = (queries, parts, other, carry, other_carry)
 
     partial = partial_call(near, ready["a"], w_out, frames)
-    blocks = latent_call(
-        partial, ready["b"], w_out, w_latent, frames, columns, tiles
-    )
+    chunk_b = (ready["b"][0][0],) + ready["b"][1:]
+    partial = own_call(partial, chunk_b, w_out, frames)
+    blocks = latent_call(partial, chunk_b, w_out, w_latent, frames, columns, tiles)
     blocks = lax.all_to_all(blocks, "tm", 0, 0, tiled=True)
     return decode(blocks, conv_weight, conv_bias, frames, grid_rows, own, tiles)
 

time: 61.4 us -> 61.5 us (level)
    pallas_call x0 -> x2, Pallas kernels: none -> 1.16 us  [the longest x1 1.15 us: own_call(): pl.pallas_call(kernel, out_shape=shape((tokens, d), F32), in_specs=[IN_VM...]
    ppermute x0 -> x1, waiting for transfers between devices: none -> 1.04 us  [body(): got_b = lax.ppermute(theirs_b, 'space', SWAP)]
    ppermute x6, waiting for transfers between devices: 6.72 us -> 5.76 us  [prefix_rounds(): got = lax.ppermute(sent, 'tm', [(i, i ^ step) for i in range(tiles)])]
    pallas_call x1, Pallas kernels: 2.76 us -> 2.01 us  [latent_call(): pl.pallas_call(functools.partial(latent_kernel, frames, columns, tiles),...]
  transfers between devices with their start and end apart: 11 -> 12, of which waited for: 4 -> 6; matrix products, arithmetic and copies ran while one was open for 0% -> 0% of each run, Pallas kernels for 21% -> 22%
where the time goes in v9:
time: 61.5 us; the launch traced here: 61.3 us
  Pallas kernels  24.2 us (39%)
  blocking collectives  17.3 us (28%)
  starting transfers between devices  12.6 us (20%)
  waiting for transfers between devices  6.81 us (11%)
    all_to_all x1, blocking collectives, body(): blocks = lax.all_to_all(blocks, 'tm', 0, 0, tiled=True)  17.3 us
    ppermute x6, starting transfers between devices, prefix_rounds(): got = lax.ppermute(sent, 'tm', [(i, i ^ step) for i in range(tiles)])  11.6 us
    pallas_call x1, Pallas kernels, first_states(): pl.pallas_call(functools.partial(states_kernel, frames, heads, False), ou...  6.82 us
    ppermute x6, waiting for transfers between devices, prefix_rounds(): got = lax.ppermute(sent, 'tm', [(i, i ^ step) for i in range(tiles)])  5.76 us
    pallas_call x3, Pallas kernels, query_call(): pl.pallas_call(kernel, out_shape=shape((video.shape[0], width), BF16), in...  4.1 us
    pallas_call x1, Pallas kernels, second_states(): pl.pallas_call(functools.partial(states_kernel, frames, heads, True), out...  3.92 us
    pallas_call x1, Pallas kernels, partial_call(): pl.pallas_call(kernel, out_shape=shape((tokens, d), F32), in_specs=[IN_VM...  2.64 us
    pallas_call x1, Pallas kernels, latent_call(): pl.pallas_call(functools.partial(latent_kernel, frames, columns, tiles),...  2.01 us
  transfers between devices with their start and end apart: 12, of which 6 were waited for; matrix products, arithmetic and copies ran while one was open for 0% of the time, Pallas kernels for 22%

profile of v9, /device:TPU:0, one launch (start us, length us, event | category | flops | bytes accessed | tf_op | source)
XLA Modules:
  0.0 61.3 jit_solution(2738716272985022658)
XLA Ops:
  0.0 6.8 %states.2 = (bf16[2,5,128,128]{3,2,1,0:T(8,128)(2,1)S(1)}, bf16[1024,1152]{1,0:T(8,128)(2,1)S(1)}, bf16[1152,512]{1,0:T(8,128)(2,1)S(1)}, bf16[1152,512]{1,0:T(8,128)(2,1)S(1)}, bf16[1152,1152]{1,0:T(8,128)(2,1)S(1)}) custom-call(bf16[1024,1152]{1,0:T(8,128)(2,1)} %bitcast.4, bf16[1152,1152]{1,0:T(8,128)(2,1)} %wk_hbm.1, bf16[1152,1152]{1,0:T(8,128)(2,1)} %wv_hbm.1, ...), custom_call_target="tpu_custom_call" | custom-call | tf_op jit(solution)/shard_map/states/pallas_call | solution.py:124
  6.8 0.6 collective-permute-start
  7.4 3.9 %states.3 = (bf16[2,4,128,128]{3,2,1,0:T(8,128)(2,1)S(1)}, f32[2,128,128]{2,1,0:T(8,128)S(1)}, bf16[2,128,128]{2,1,0:T(8,128)(2,1)S(1)}) custom-call(bf16[1024,1152]{1,0:T(8,128)(2,1)S(1)} %get-tuple-element.31.video.video_in, bf16[1152,512]{1,0:T(8,128)(2,1)S(1)} %get-tuple-element.42.wk_hbm, bf16[1152,512]{1,0:T(8,128)(2,1)S(1)} %get-tuple-element.43.wv_hbm), custom_call_target="tpu_custom_call" | custom-call | tf_op jit(solution)/shard_map/states/pallas_call | solution.py:153
  11.3 0.1 total.1
  11.4 2.6 %collective-permute-start.1 = (bf16[5,64,128]{2,1,0:T(8,128)(2,1)S(1)}, bf16[5,64,128]{2,1,0:T(8,128)(2,1)S(1)}, u32[]{:S(2)}, u32[]{:S(2)}) collective-permute-start(bf16[5,64,128]{2,1,0:T(8,128)(2,1)S(1)} %get-tuple-element.34), channel_id=1, source_target_pairs={{0,2},{2,0},{4,6},{6,4},{8,10},{10,8},{12,14},{14,12},{1,3},{3,1},... | collective-permute-start | bytes 245768 | tf_op jit(solution)/shard_map/ppermute | solution.py:576
  14.0 0.2 collective-permute-start.6
  14.2 1.0 %collective-permute-done.6.got = bf16[2,128,128]{2,1,0:T(8,128)(2,1)S(1)} collective-permute-done((bf16[2,128,128]{2,1,0:T(8,128)(2,1)S(1)}, bf16[2,128,128]{2,1,0:T(8,128)(2,1)S(1)}, u32[]{:S(2)}, u32[]{:S(2)}) %collective-permute-start.6) | collective-permute-done | bytes 65568 | tf_op jit(solution)/shard_map/ppermute | solution.py:601
  15.3 0.3 collective-permute-start.7
  15.6 0.1 collective-permute-start.5
  15.6 1.5 %collective-permute-done.1.got = bf16[5,64,128]{2,1,0:T(8,128)(2,1)S(1)} collective-permute-done((bf16[5,64,128]{2,1,0:T(8,128)(2,1)S(1)}, bf16[5,64,128]{2,1,0:T(8,128)(2,1)S(1)}, u32[]{:S(2)}, u32[]{:S(2)}) %collective-permute-start.1) | collective-permute-done | bytes 81952 | tf_op jit(solution)/shard_map/ppermute | solution.py:576
  17.1 1.9 %collective-permute-start.2 = (bf16[5,64,128]{2,1,0:T(8,128)(2,1)S(1)}, bf16[5,64,128]{2,1,0:T(8,128)(2,1)S(1)}, u32[]{:S(2)}, u32[]{:S(2)}) collective-permute-start(bf16[5,64,128]{2,1,0:T(8,128)(2,1)S(1)} %get-tuple-element.36), channel_id=1, source_target_pairs={{0,4},{2,6},{4,0},{6,2},{8,12},{10,14},{12,8},{14,10},{1,5},{3,7},... | collective-permute-start | bytes 245768 | tf_op jit(solution)/shard_map/ppermute | solution.py:576
  19.0 0.6 collective-permute-done.7.got
  19.6 1.6 %collective-permute-start.8 = (bf16[2,128,128]{2,1,0:T(8,128)(2,1)S(1)}, bf16[2,128,128]{2,1,0:T(8,128)(2,1)S(1)}, u32[]{:S(2)}, u32[]{:S(2)}) collective-permute-start(bf16[2,128,128]{2,1,0:T(8,128)(2,1)S(1)} %get-tuple-element.49), channel_id=1, source_target_pairs={{0,4},{2,6},{4,0},{6,2},{8,12},{10,14},{12,8},{14,10},{1,5},{3,7},... | collective-permute-start | bytes 196616 | tf_op jit(solution)/shard_map/ppermute | solution.py:576
  21.3 0.6 %collective-permute-done.2.got = bf16[5,64,128]{2,1,0:T(8,128)(2,1)S(1)} collective-permute-done((bf16[5,64,128]{2,1,0:T(8,128)(2,1)S(1)}, bf16[5,64,128]{2,1,0:T(8,128)(2,1)S(1)}, u32[]{:S(2)}, u32[]{:S(2)}) %collective-permute-start.2) | collective-permute-done | bytes 81952 | tf_op jit(solution)/shard_map/ppermute | solution.py:576
  22.0 3.1 %collective-permute-start.3 = (bf16[5,64,128]{2,1,0:T(8,128)(2,1)S(1)}, bf16[5,64,128]{2,1,0:T(8,128)(2,1)S(1)}, u32[]{:S(2)}, u32[]{:S(2)}) collective-permute-start(bf16[5,64,128]{2,1,0:T(8,128)(2,1)S(1)} %get-tuple-element.39), channel_id=1, source_target_pairs={{0,8},{2,10},{4,12},{6,14},{8,0},{10,2},{12,4},{14,6},{1,9},{3,11}... | collective-permute-start | bytes 245768 | tf_op jit(solution)/shard_map/ppermute | solution.py:576
  25.1 2.1 %collective-permute-start.9 = (bf16[2,128,128]{2,1,0:T(8,128)(2,1)S(1)}, bf16[2,128,128]{2,1,0:T(8,128)(2,1)S(1)}, u32[]{:S(2)}, u32[]{:S(2)}) collective-permute-start(bf16[2,128,128]{2,1,0:T(8,128)(2,1)S(1)} %get-tuple-element.52), channel_id=1, source_target_pairs={{0,8},{2,10},{4,12},{6,14},{8,0},{10,2},{12,4},{14,6},{1,9},{3,11}... | collective-permute-start | bytes 196616 | tf_op jit(solution)/shard_map/ppermute | solution.py:576
  27.2 2.3 %collective-permute-done.3.got = bf16[5,64,128]{2,1,0:T(8,128)(2,1)S(1)} collective-permute-done((bf16[5,64,128]{2,1,0:T(8,128)(2,1)S(1)}, bf16[5,64,128]{2,1,0:T(8,128)(2,1)S(1)}, u32[]{:S(2)}, u32[]{:S(2)}) %collective-permute-start.3) | collective-permute-done | bytes 81952 | tf_op jit(solution)/shard_map/ppermute | solution.py:576
  29.6 0.1 collective-permute-start.4
  29.6 0.7 %collective-permute-done.9.got = bf16[2,128,128]{2,1,0:T(8,128)(2,1)S(1)} collective-permute-done((bf16[2,128,128]{2,1,0:T(8,128)(2,1)S(1)}, bf16[2,128,128]{2,1,0:T(8,128)(2,1)S(1)}, u32[]{:S(2)}, u32[]{:S(2)}) %collective-permute-start.9) | collective-permute-done | bytes 65568 | tf_op jit(solution)/shard_map/ppermute | solution.py:576
  30.4 0.1 collective-permute-start.10
  30.5 0.9 %query.3.refs_0_ = bf16[1024,256]{1,0:T(8,128)(2,1)S(1)} custom-call(bf16[1024,1152]{1,0:T(8,128)(2,1)S(1)} %get-tuple-element.31.video.video_in, bf16[1152,1152]{1,0:T(8,128)(2,1)S(1)} %get-tuple-element.32.w), custom_call_target="tpu_custom_call" | custom-call | tf_op jit(solution)/shard_map/query/pallas_call | solution.py:217
  31.3 1.6 %query.4.refs_1_ = bf16[1024,384]{1,0:T(8,128)(2,1)S(1)} custom-call(bf16[1024,1152]{1,0:T(8,128)(2,1)S(1)} %get-tuple-element.31.video.video_in, bf16[1152,1152]{1,0:T(8,128)(2,1)S(1)} %get-tuple-element.32.w), custom_call_target="tpu_custom_call" | custom-call | tf_op jit(solution)/shard_map/query/pallas_call | solution.py:217
  32.9 0.0 copy-start
  32.9 1.7 %query.5 = bf16[1024,512]{1,0:T(8,128)(2,1)S(1)} custom-call(bf16[1024,1152]{1,0:T(8,128)(2,1)S(1)} %get-tuple-element.31.video.video_in, bf16[1152,1152]{1,0:T(8,128)(2,1)S(1)} %get-tuple-element.32.w), custom_call_target="tpu_custom_call" | custom-call | tf_op jit(solution)/shard_map/query/pallas_call | solution.py:217
  34.6 0.0 copy-done
  34.6 2.6 %partial.1 = f32[1024,1152]{1,0:T(8,128)S(1)} custom-call(bf16[1024,1152]{1,0:T(8,128)(2,1)S(1)} %get-tuple-element.31.video.video_in, bf16[1024,256]{1,0:T(8,128)(2,1)S(1)} %query.3.refs_0_, bf16[1024,384]{1,0:T(8,128)(2,1)S(1)} %query.4.refs_1_, bf16[2,5,128,128]{3,2,1,0:T(8,128)(2,1)S(1)} %get-tuple-element.33.parts.refs_2_, ...), custom_call_target="tpu_custom_call" | custom-call | tf_op jit(solution)/shard_map/partial/pallas_call | solution.py:280
  37.3 1.1 %own.1.partial = f32[1024,1152]{1,0:T(8,128)S(1)} custom-call(f32[1024,1152]{1,0:T(8,128)S(1)} %partial.1, bf16[1024,512]{1,0:T(8,128)(2,1)S(1)} %query.5, bf16[2,4,128,128]{3,2,1,0:T(8,128)(2,1)S(1)} %get-tuple-element.44.parts, bf16[2,4,128,128]{3,2,1,0:T(8,128)(2,1)S(1)} %collective-permute-done.5.other_parts, bf16[2,128,128]{2,1,0:T(8,128)(2,1)S(1)} %round.11.carry, ...), custom_call_target="tpu_custom_call" | custom-call | tf_op jit(solution)/shard_map/own/pallas_call | solution.py:336
  38.5 2.0 %latent.1 = bf16[8,160,128]{2,1,0:T(8,128)(2,1)S(1)} custom-call(f32[1024,1152]{1,0:T(8,128)S(1)} %own.1.partial, bf16[1024,512]{1,0:T(8,128)(2,1)S(1)} %query.5, bf16[2,4,128,128]{3,2,1,0:T(8,128)(2,1)S(1)} %get-tuple-element.44.parts, bf16[2,4,128,128]{3,2,1,0:T(8,128)(2,1)S(1)} %collective-permute-done.5.other_parts, ...), custom_call_target="tpu_custom_call" | custom-call | tf_op jit(solution)/shard_map/latent/pallas_call | solution.py:389
  40.5 17.3 %all_to_all.5.blocks = bf16[8,160,128]{2,1,0:T(8,128)(2,1)S(1)} all-to-all(bf16[8,160,128]{2,1,0:T(8,128)(2,1)S(1)} %latent.1), channel_id=1, replica_groups=mesh['groups'=2,'tm'=8,'space'=2] {'tm'}, dimensions={0} | all-to-all | bytes 655360 | tf_op jit(solution)/shard_map/all_to_all | solution.py:625
  57.8 0.1 collective-permute-start.11
  57.9 1.6 %interior.1 = (bf16[16,12,16,256]{3,2,1,0:T(8,128)(2,1)S(1)}, bf16[4,512,256]{2,1,0:T(8,128)(2,1)S(1)}) custom-call(bf16[8,160,128]{2,1,0:T(8,128)(2,1)S(1)} %all_to_all.5.blocks, bf16[3,3,128,256]{3,2,1,0:T(8,128)(2,1)S(1)} %copy-done.1, f32[1,256]{1,0:T(1,128)S(1)} %bitcast.2), custom_call_target="tpu_custom_call" | custom-call | tf_op jit(solution)/shard_map/interior/pallas_call | solution.py:491
  59.6 1.7 %border.1 = bf16[16,16,16,256]{3,2,1,0:T(8,128)(2,1)} custom-call(bf16[8,160,128]{2,1,0:T(8,128)(2,1)S(1)} %all_to_all.5.blocks, bf16[8,20,128]{2,1,0:T(8,128)(2,1)S(1)} %collective-permute-done.11.edge, bf16[16,12,16,256]{3,2,1,0:T(8,128)(2,1)S(1)} %get-tuple-element.55.interior, bf16[4,512,256]{2,1,0:T(8,128)(2,1)S(1)} %get-tuple-element.56.taps, ...), custom_call_target="tpu_custom_call" | custom-call | tf_op jit(solution)/shard_map/border/pallas_call | solution.py:527
  (20 shorter events, 0.2 us)
Async XLA Ops:
  6.8 4.5 %collective-permute-start = (bf16[2,5,128,128]{3,2,1,0:T(8,128)(2,1)S(1)}, bf16[2,5,128,128]{3,2,1,0:T(8,128)(2,1)S(1)}, u32[]{:S(2)}, u32[]{:S(2)}) collective-permute-start(bf16[2,5,128,128]{3,2,1,0:T(8,128)(2,1)S(1)} %get-tuple-element.33.parts.refs_2_), channel_id=1, source_target_pairs={{0,1},{1,0},{2,3},{3,2},{4,5},{5,4},{6,7},{7,6},{8,9},{9,8},{10,11... | collective-permute-start | bytes 983048 | tf_op jit(solution)/shard_map/ppermute | solution.py:599
  11.4 5.7 %collective-permute-start.1 = (bf16[5,64,128]{2,1,0:T(8,128)(2,1)S(1)}, bf16[5,64,128]{2,1,0:T(8,128)(2,1)S(1)}, u32[]{:S(2)}, u32[]{:S(2)}) collective-permute-start(bf16[5,64,128]{2,1,0:T(8,128)(2,1)S(1)} %get-tuple-element.34), channel_id=1, source_target_pairs={{0,2},{2,0},{4,6},{6,4},{8,10},{10,8},{12,14},{14,12},{1,3},{3,1},... | collective-permute-start | bytes 245768 | tf_op jit(solution)/shard_map/ppermute | solution.py:576
  14.0 1.3 %collective-permute-start.6 = (bf16[2,128,128]{2,1,0:T(8,128)(2,1)S(1)}, bf16[2,128,128]{2,1,0:T(8,128)(2,1)S(1)}, u32[]{:S(2)}, u32[]{:S(2)}) collective-permute-start(bf16[2,128,128]{2,1,0:T(8,128)(2,1)S(1)} %get-tuple-element.46), channel_id=1, source_target_pairs={{0,1},{1,0},{2,3},{3,2},{4,5},{5,4},{6,7},{7,6},{8,9},{9,8},{10,11... | collective-permute-start | bytes 196616 | tf_op jit(solution)/shard_map/ppermute | solution.py:601
  15.3 4.3 %collective-permute-start.7 = (bf16[2,128,128]{2,1,0:T(8,128)(2,1)S(1)}, bf16[2,128,128]{2,1,0:T(8,128)(2,1)S(1)}, u32[]{:S(2)}, u32[]{:S(2)}) collective-permute-start(bf16[2,128,128]{2,1,0:T(8,128)(2,1)S(1)} %get-tuple-element.47), channel_id=1, source_target_pairs={{0,2},{2,0},{4,6},{6,4},{8,10},{10,8},{12,14},{14,12},{1,3},{3,1},... | collective-permute-start | bytes 196616 | tf_op jit(solution)/shard_map/ppermute | solution.py:576
  15.6 21.7 %collective-permute-start.5 = (bf16[2,4,128,128]{3,2,1,0:T(8,128)(2,1)S(1)}, bf16[2,4,128,128]{3,2,1,0:T(8,128)(2,1)S(1)}, u32[]{:S(2)}, u32[]{:S(2)}) collective-permute-start(bf16[2,4,128,128]{3,2,1,0:T(8,128)(2,1)S(1)} %get-tuple-element.44.parts), channel_id=1, source_target_pairs={{0,1},{1,0},{2,3},{3,2},{4,5},{5,4},{6,7},{7,6},{8,9},{9,8},{10,11... | collective-permute-start | bytes 786440 | tf_op jit(solution)/shard_map/ppermute | solution.py:602
  17.1 4.8 %collective-permute-start.2 = (bf16[5,64,128]{2,1,0:T(8,128)(2,1)S(1)}, bf16[5,64,128]{2,1,0:T(8,128)(2,1)S(1)}, u32[]{:S(2)}, u32[]{:S(2)}) collective-permute-start(bf16[5,64,128]{2,1,0:T(8,128)(2,1)S(1)} %get-tuple-element.36), channel_id=1, source_target_pairs={{0,4},{2,6},{4,0},{6,2},{8,12},{10,14},{12,8},{14,10},{1,5},{3,7},... | collective-permute-start | bytes 245768 | tf_op jit(solution)/shard_map/ppermute | solution.py:576
  19.6 5.4 %collective-permute-start.8 = (bf16[2,128,128]{2,1,0:T(8,128)(2,1)S(1)}, bf16[2,128,128]{2,1,0:T(8,128)(2,1)S(1)}, u32[]{:S(2)}, u32[]{:S(2)}) collective-permute-start(bf16[2,128,128]{2,1,0:T(8,128)(2,1)S(1)} %get-tuple-element.49), channel_id=1, source_target_pairs={{0,4},{2,6},{4,0},{6,2},{8,12},{10,14},{12,8},{14,10},{1,5},{3,7},... | collective-permute-start | bytes 196616 | tf_op jit(solution)/shard_map/ppermute | solution.py:576
  22.0 7.6 %collective-permute-start.3 = (bf16[5,64,128]{2,1,0:T(8,128)(2,1)S(1)}, bf16[5,64,128]{2,1,0:T(8,128)(2,1)S(1)}, u32[]{:S(2)}, u32[]{:S(2)}) collective-permute-start(bf16[5,64,128]{2,1,0:T(8,128)(2,1)S(1)} %get-tuple-element.39), channel_id=1, source_target_pairs={{0,8},{2,10},{4,12},{6,14},{8,0},{10,2},{12,4},{14,6},{1,9},{3,11}... | collective-permute-start | bytes 245768 | tf_op jit(solution)/shard_map/ppermute | solution.py:576
  25.1 5.2 %collective-permute-start.9 = (bf16[2,128,128]{2,1,0:T(8,128)(2,1)S(1)}, bf16[2,128,128]{2,1,0:T(8,128)(2,1)S(1)}, u32[]{:S(2)}, u32[]{:S(2)}) collective-permute-start(bf16[2,128,128]{2,1,0:T(8,128)(2,1)S(1)} %get-tuple-element.52), channel_id=1, source_target_pairs={{0,8},{2,10},{4,12},{6,14},{8,0},{10,2},{12,4},{14,6},{1,9},{3,11}... | collective-permute-start | bytes 196616 | tf_op jit(solution)/shard_map/ppermute | solution.py:576
  29.6 5.0 %collective-permute-start.4 = (bf16[5,64,128]{2,1,0:T(8,128)(2,1)S(1)}, bf16[5,64,128]{2,1,0:T(8,128)(2,1)S(1)}, u32[]{:S(2)}, u32[]{:S(2)}) collective-permute-start(bf16[5,64,128]{2,1,0:T(8,128)(2,1)S(1)} %round.8.refs_4_), channel_id=1, source_target_pairs={{0,1},{1,0},{2,3},{3,2},{4,5},{5,4},{6,7},{7,6},{8,9},{9,8},{10,11... | collective-permute-start | bytes 245768 | tf_op jit(solution)/shard_map/ppermute | solution.py:618
  30.4 8.1 %collective-permute-start.10 = (bf16[2,128,128]{2,1,0:T(8,128)(2,1)S(1)}, bf16[2,128,128]{2,1,0:T(8,128)(2,1)S(1)}, u32[]{:S(2)}, u32[]{:S(2)}) collective-permute-start(bf16[2,128,128]{2,1,0:T(8,128)(2,1)S(1)} %round.11.carry), channel_id=1, source_target_pairs={{0,1},{1,0},{2,3},{3,2},{4,5},{5,4},{6,7},{7,6},{8,9},{9,8},{10,11... | collective-permute-start | bytes 196616 | tf_op jit(solution)/shard_map/ppermute | solution.py:618
  32.9 1.8 %copy-start = (bf16[1152,1152]{1,0:T(8,128)(2,1)S(1)}, bf16[1152,1152]{1,0:T(8,128)(2,1)}, u32[]{:S(2)}) copy-start(bf16[1152,1152]{1,0:T(8,128)(2,1)} %w_out.3) | copy-start | bytes 7962628
  37.3 1.2 %copy-start.2 = (bf16[1152,128]{1,0:T(8,128)(2,1)S(1)}, bf16[1152,128]{1,0:T(8,128)(2,1)}, u32[]{:S(2)}) copy-start(bf16[1152,128]{1,0:T(8,128)(2,1)} %w_latent.1) | copy-start | bytes 884740
  38.4 19.5 %copy-start.1 = (bf16[3,3,128,256]{3,2,1,0:T(8,128)(2,1)S(1)}, bf16[3,3,128,256]{3,2,1,0:T(8,128)(2,1)}, u32[]{:S(2)}) copy-start(bf16[3,3,128,256]{3,2,1,0:T(8,128)(2,1)} %weight.1) | copy-start | bytes 1769476
  38.5 19.5 %copy-start.3 = (f32[256]{0:T(256)S(1)}, f32[256]{0:T(256)}, u32[]{:S(2)}) copy-start(f32[256]{0:T(256)} %param.15) | copy-start | bytes 3076
  57.8 1.7 %collective-permute-start.11 = (bf16[8,20,128]{2,1,0:T(8,128)(2,1)S(1)}, bf16[8,20,128]{2,1,0:T(8,128)(2,1)S(1)}, u32[]{:S(2)}, u32[]{:S(2)}) collective-permute-start(bf16[8,20,128]{2,1,0:T(8,128)(2,1)S(1)} %edge.1), channel_id=1, source_target_pairs={{0,1},{1,0},{2,3},{3,2},{4,5},{5,4},{6,7},{7,6},{8,9},{9,8},{10,11... | collective-permute-start | bytes 122888 | tf_op jit(solution)/shard_map/ppermute | solution.py:663

commit v10 on v9

--- a/solution.py
+++ b/solution.py
@@ -452,41 +452,47 @@
                     taps[2 * a + b, at : at + channels, :] = (0.5 * tap).astype(BF16)
 
 
-def decode_row(own, index, bias, left, middle, right, taps, wide, staged, first):
+def decode_rows(own, index, count, bias, left, middle, right, taps, wide, staged, first):
     views = ((left, middle), (middle, right))
     half_bias = 0.5 * bias[...]
     lanes = wide.shape[-1]
-    total = left.shape[1]
+    total, channels = left.shape[1:]
+    size = count * total
     for a in range(2):
         for b in range(2):
             lhs = jnp.concatenate(
-                [v[index + a + k] for k in range(2) for v in views[b]], axis=1
+                [v[index + a + k : index + a + k + count].reshape(size, channels)
+                 for k in range(2) for v in views[b]], axis=1
             )
             h = matmul(lhs, taps[2 * a + b]) + half_bias
             value = h + h * jnp.tanh(h)
             for n in range(wide.shape[1]):
-                wide[a, n, pl.ds(b, total, stride=2), :] = value[:, n * lanes : (n + 1) * lanes]
+                wide[a, n, pl.ds(b, size, stride=2), :] = value[:, n * lanes : (n + 1) * lanes]
         for n in range(wide.shape[1]):
-            shaped = wide[a, n].reshape(total // own, 2 * own, lanes)
-            staged[:, first + a, :, n * lanes : (n + 1) * lanes] = shaped.astype(BF16)
-
-
-def decode_scratch(rows, total, channels, width):
+            shaped = wide[a, n].reshape(count, total // own, 2 * own, lanes)
+            for r in range(count):
+                staged[:, first + 2 * r + a, :, n * lanes : (n + 1) * lanes] = (
+                    shaped[r].astype(BF16)
+                )
+
+
+def decode_scratch(rows, count, total, channels, width):
     return [pltpu.VMEM((rows, total, channels), BF16)] * 3 + [
-        pltpu.VMEM((2, width // HEAD, 2 * total, HEAD), F32)
+        pltpu.VMEM((2, width // HEAD, 2 * count * total, HEAD), F32)
     ]
 
 
 def interior_call(blocks, weight, bias, frames, tiles, grid_rows, own):
     channels, width = weight.shape[2:]
     total = tiles * frames * own
+    count = 3 if (grid_rows - 2) % 3 == 0 else 1
 
     def kernel(blocks, weight, bias, out, taps, left, middle, right, wide):
         lay_taps(weight, taps)
         lay_rows(frames, tiles, grid_rows, own, range(grid_rows), blocks, None,
                  left, middle, right)
-        for r in range(1, grid_rows - 1):
-            decode_row(own, r - 1, bias, left, middle, right, taps, wide, out, 2 * (r - 1))
+        for i in range(0, grid_rows - 2, count):
+            decode_rows(own, i, count, bias, left, middle, right, taps, wide, out, 2 * i)
 
     return pl.pallas_call(
         kernel,
@@ -496,7 +502,7 @@
         ],
         in_specs=[IN_VMEM] * 3,
         out_specs=[IN_VMEM] * 2,
-        scratch_shapes=decode_scratch(grid_rows, total, channels, width),
+        scratch_shapes=decode_scratch(grid_rows, count, total, channels, width),
         name="interior",
         compiler_params=params(24),
     )(blocks, weight, bias)
@@ -514,7 +520,7 @@
         rows = [-1, 0, 1, grid_rows - 2, grid_rows - 1, grid_rows]
         lay_rows(frames, tiles, grid_rows, own, rows, blocks, edge, left, middle, right)
         for i, (index, row) in enumerate(((0, 0), (3, last))):
-            decode_row(own, index, bias, left, middle, right, taps, wide, staged, 2 * i)
+            decode_rows(own, index, 1, bias, left, middle, right, taps, wide, staged, 2 * i)
             copies.append(
                 pltpu.make_async_copy(
                     staged.at[:, pl.ds(2 * i, 2)], out.at[:, pl.ds(row, 2)], sem.at[i]
@@ -529,7 +535,7 @@
         out_shape=shape((tiles * frames, 2 * grid_rows, 2 * own, width), BF16),
         in_specs=[IN_VMEM] * 5,
         out_specs=IN_HBM,
-        scratch_shapes=decode_scratch(6, total, channels, width)
+        scratch_shapes=decode_scratch(6, 1, total, channels, width)
         + [
             pltpu.VMEM((tiles * frames, 4, 2 * own, width), BF16),
             pltpu.SemaphoreType.DMA((3,)),

time: 61.5 us -> 61.3 us (level)
  no operation moved by 1% of the time
where the time goes in v10:
time: 61.3 us; the launch traced here: 61.1 us
  Pallas kernels  24.1 us (39%)
  blocking collectives  17.3 us (28%)
  starting transfers between devices  12.6 us (21%)
  waiting for transfers between devices  6.81 us (11%)
    all_to_all x1, blocking collectives, body(): blocks = lax.all_to_all(blocks, 'tm', 0, 0, tiled=True)  17.3 us
    ppermute x6, starting transfers between devices, prefix_rounds(): got = lax.ppermute(sent, 'tm', [(i, i ^ step) for i in range(tiles)])  11.6 us
    pallas_call x1, Pallas kernels, first_states(): pl.pallas_call(functools.partial(states_kernel, frames, heads, False), ou...  6.82 us
    ppermute x6, waiting for transfers between devices, prefix_rounds(): got = lax.ppermute(sent, 'tm', [(i, i ^ step) for i in range(tiles)])  5.76 us
    pallas_call x3, Pallas kernels, query_call(): pl.pallas_call(kernel, out_shape=shape((video.shape[0], width), BF16), in...  4.1 us
    pallas_call x1, Pallas kernels, second_states(): pl.pallas_call(functools.partial(states_kernel, frames, heads, True), out...  3.92 us
    pallas_call x1, Pallas kernels, partial_call(): pl.pallas_call(kernel, out_shape=shape((tokens, d), F32), in_specs=[IN_VM...  2.64 us
    pallas_call x1, Pallas kernels, latent_call(): pl.pallas_call(functools.partial(latent_kernel, frames, columns, tiles),...  2.01 us
  transfers between devices with their start and end apart: 12, of which 6 were waited for; matrix products, arithmetic and copies ran while one was open for 0% of the time, Pallas kernels for 22%

profile of v10, /device:TPU:0, one launch (start us, length us, event | category | flops | bytes accessed | tf_op | source)
XLA Modules:
  0.0 61.1 jit_solution(7242835492935374643)
XLA Ops:
  0.0 6.8 %states.2 = (bf16[2,5,128,128]{3,2,1,0:T(8,128)(2,1)S(1)}, bf16[1024,1152]{1,0:T(8,128)(2,1)S(1)}, bf16[1152,512]{1,0:T(8,128)(2,1)S(1)}, bf16[1152,512]{1,0:T(8,128)(2,1)S(1)}, bf16[1152,1152]{1,0:T(8,128)(2,1)S(1)}) custom-call(bf16[1024,1152]{1,0:T(8,128)(2,1)} %bitcast.4, bf16[1152,1152]{1,0:T(8,128)(2,1)} %wk_hbm.1, bf16[1152,1152]{1,0:T(8,128)(2,1)} %wv_hbm.1, ...), custom_call_target="tpu_custom_call" | custom-call | tf_op jit(solution)/shard_map/states/pallas_call | solution.py:124
  6.8 0.6 collective-permute-start
  7.4 3.9 %states.3 = (bf16[2,4,128,128]{3,2,1,0:T(8,128)(2,1)S(1)}, f32[2,128,128]{2,1,0:T(8,128)S(1)}, bf16[2,128,128]{2,1,0:T(8,128)(2,1)S(1)}) custom-call(bf16[1024,1152]{1,0:T(8,128)(2,1)S(1)} %get-tuple-element.31.video.video_in, bf16[1152,512]{1,0:T(8,128)(2,1)S(1)} %get-tuple-element.42.wk_hbm, bf16[1152,512]{1,0:T(8,128)(2,1)S(1)} %get-tuple-element.43.wv_hbm), custom_call_target="tpu_custom_call" | custom-call | tf_op jit(solution)/shard_map/states/pallas_call | solution.py:153
  11.3 0.1 total.1
  11.4 2.6 %collective-permute-start.1 = (bf16[5,64,128]{2,1,0:T(8,128)(2,1)S(1)}, bf16[5,64,128]{2,1,0:T(8,128)(2,1)S(1)}, u32[]{:S(2)}, u32[]{:S(2)}) collective-permute-start(bf16[5,64,128]{2,1,0:T(8,128)(2,1)S(1)} %get-tuple-element.34), channel_id=1, source_target_pairs={{0,2},{2,0},{4,6},{6,4},{8,10},{10,8},{12,14},{14,12},{1,3},{3,1},... | collective-permute-start | bytes 245768 | tf_op jit(solution)/shard_map/ppermute | solution.py:582
  14.0 0.2 collective-permute-start.6
  14.2 1.0 %collective-permute-done.6.got = bf16[2,128,128]{2,1,0:T(8,128)(2,1)S(1)} collective-permute-done((bf16[2,128,128]{2,1,0:T(8,128)(2,1)S(1)}, bf16[2,128,128]{2,1,0:T(8,128)(2,1)S(1)}, u32[]{:S(2)}, u32[]{:S(2)}) %collective-permute-start.6) | collective-permute-done | bytes 65568 | tf_op jit(solution)/shard_map/ppermute | solution.py:607
  15.3 0.3 collective-permute-start.7
  15.6 0.1 collective-permute-start.5
  15.6 1.5 %collective-permute-done.1.got = bf16[5,64,128]{2,1,0:T(8,128)(2,1)S(1)} collective-permute-done((bf16[5,64,128]{2,1,0:T(8,128)(2,1)S(1)}, bf16[5,64,128]{2,1,0:T(8,128)(2,1)S(1)}, u32[]{:S(2)}, u32[]{:S(2)}) %collective-permute-start.1) | collective-permute-done | bytes 81952 | tf_op jit(solution)/shard_map/ppermute | solution.py:582
  17.1 1.9 %collective-permute-start.2 = (bf16[5,64,128]{2,1,0:T(8,128)(2,1)S(1)}, bf16[5,64,128]{2,1,0:T(8,128)(2,1)S(1)}, u32[]{:S(2)}, u32[]{:S(2)}) collective-permute-start(bf16[5,64,128]{2,1,0:T(8,128)(2,1)S(1)} %get-tuple-element.36), channel_id=1, source_target_pairs={{0,4},{2,6},{4,0},{6,2},{8,12},{10,14},{12,8},{14,10},{1,5},{3,7},... | collective-permute-start | bytes 245768 | tf_op jit(solution)/shard_map/ppermute | solution.py:582
  19.0 0.6 %collective-permute-done.7.got = bf16[2,128,128]{2,1,0:T(8,128)(2,1)S(1)} collective-permute-done((bf16[2,128,128]{2,1,0:T(8,128)(2,1)S(1)}, bf16[2,128,128]{2,1,0:T(8,128)(2,1)S(1)}, u32[]{:S(2)}, u32[]{:S(2)}) %collective-permute-start.7) | collective-permute-done | bytes 65568 | tf_op jit(solution)/shard_map/ppermute | solution.py:582
  19.6 1.6 %collective-permute-start.8 = (bf16[2,128,128]{2,1,0:T(8,128)(2,1)S(1)}, bf16[2,128,128]{2,1,0:T(8,128)(2,1)S(1)}, u32[]{:S(2)}, u32[]{:S(2)}) collective-permute-start(bf16[2,128,128]{2,1,0:T(8,128)(2,1)S(1)} %get-tuple-element.49), channel_id=1, source_target_pairs={{0,4},{2,6},{4,0},{6,2},{8,12},{10,14},{12,8},{14,10},{1,5},{3,7},... | collective-permute-start | bytes 196616 | tf_op jit(solution)/shard_map/ppermute | solution.py:582
  21.3 0.6 %collective-permute-done.2.got = bf16[5,64,128]{2,1,0:T(8,128)(2,1)S(1)} collective-permute-done((bf16[5,64,128]{2,1,0:T(8,128)(2,1)S(1)}, bf16[5,64,128]{2,1,0:T(8,128)(2,1)S(1)}, u32[]{:S(2)}, u32[]{:S(2)}) %collective-permute-start.2) | collective-permute-done | bytes 81952 | tf_op jit(solution)/shard_map/ppermute | solution.py:582
  22.0 3.1 %collective-permute-start.3 = (bf16[5,64,128]{2,1,0:T(8,128)(2,1)S(1)}, bf16[5,64,128]{2,1,0:T(8,128)(2,1)S(1)}, u32[]{:S(2)}, u32[]{:S(2)}) collective-permute-start(bf16[5,64,128]{2,1,0:T(8,128)(2,1)S(1)} %get-tuple-element.39), channel_id=1, source_target_pairs={{0,8},{2,10},{4,12},{6,14},{8,0},{10,2},{12,4},{14,6},{1,9},{3,11}... | collective-permute-start | bytes 245768 | tf_op jit(solution)/shard_map/ppermute | solution.py:582
  25.1 2.1 %collective-permute-start.9 = (bf16[2,128,128]{2,1,0:T(8,128)(2,1)S(1)}, bf16[2,128,128]{2,1,0:T(8,128)(2,1)S(1)}, u32[]{:S(2)}, u32[]{:S(2)}) collective-permute-start(bf16[2,128,128]{2,1,0:T(8,128)(2,1)S(1)} %get-tuple-element.52), channel_id=1, source_target_pairs={{0,8},{2,10},{4,12},{6,14},{8,0},{10,2},{12,4},{14,6},{1,9},{3,11}... | collective-permute-start | bytes 196616 | tf_op jit(solution)/shard_map/ppermute | solution.py:582
  27.2 2.3 %collective-permute-done.3.got = bf16[5,64,128]{2,1,0:T(8,128)(2,1)S(1)} collective-permute-done((bf16[5,64,128]{2,1,0:T(8,128)(2,1)S(1)}, bf16[5,64,128]{2,1,0:T(8,128)(2,1)S(1)}, u32[]{:S(2)}, u32[]{:S(2)}) %collective-permute-start.3) | collective-permute-done | bytes 81952 | tf_op jit(solution)/shard_map/ppermute | solution.py:582
  29.6 0.1 collective-permute-start.4
  29.6 0.7 %collective-permute-done.9.got = bf16[2,128,128]{2,1,0:T(8,128)(2,1)S(1)} collective-permute-done((bf16[2,128,128]{2,1,0:T(8,128)(2,1)S(1)}, bf16[2,128,128]{2,1,0:T(8,128)(2,1)S(1)}, u32[]{:S(2)}, u32[]{:S(2)}) %collective-permute-start.9) | collective-permute-done | bytes 65568 | tf_op jit(solution)/shard_map/ppermute | solution.py:582
  30.4 0.1 collective-permute-start.10
  30.5 0.9 %query.3.refs_0_ = bf16[1024,256]{1,0:T(8,128)(2,1)S(1)} custom-call(bf16[1024,1152]{1,0:T(8,128)(2,1)S(1)} %get-tuple-element.31.video.video_in, bf16[1152,1152]{1,0:T(8,128)(2,1)S(1)} %get-tuple-element.32.w), custom_call_target="tpu_custom_call" | custom-call | tf_op jit(solution)/shard_map/query/pallas_call | solution.py:217
  31.3 1.6 %query.4.refs_1_ = bf16[1024,384]{1,0:T(8,128)(2,1)S(1)} custom-call(bf16[1024,1152]{1,0:T(8,128)(2,1)S(1)} %get-tuple-element.31.video.video_in, bf16[1152,1152]{1,0:T(8,128)(2,1)S(1)} %get-tuple-element.32.w), custom_call_target="tpu_custom_call" | custom-call | tf_op jit(solution)/shard_map/query/pallas_call | solution.py:217
  32.9 0.0 copy-start
  32.9 1.7 %query.5 = bf16[1024,512]{1,0:T(8,128)(2,1)S(1)} custom-call(bf16[1024,1152]{1,0:T(8,128)(2,1)S(1)} %get-tuple-element.31.video.video_in, bf16[1152,1152]{1,0:T(8,128)(2,1)S(1)} %get-tuple-element.32.w), custom_call_target="tpu_custom_call" | custom-call | tf_op jit(solution)/shard_map/query/pallas_call | solution.py:217
  34.6 0.0 copy-done
  34.6 2.6 %partial.1 = f32[1024,1152]{1,0:T(8,128)S(1)} custom-call(bf16[1024,1152]{1,0:T(8,128)(2,1)S(1)} %get-tuple-element.31.video.video_in, bf16[1024,256]{1,0:T(8,128)(2,1)S(1)} %query.3.refs_0_, bf16[1024,384]{1,0:T(8,128)(2,1)S(1)} %query.4.refs_1_, bf16[2,5,128,128]{3,2,1,0:T(8,128)(2,1)S(1)} %get-tuple-element.33.parts.refs_2_, ...), custom_call_target="tpu_custom_call" | custom-call | tf_op jit(solution)/shard_map/partial/pallas_call | solution.py:280
  37.3 1.1 %own.1.partial = f32[1024,1152]{1,0:T(8,128)S(1)} custom-call(f32[1024,1152]{1,0:T(8,128)S(1)} %partial.1, bf16[1024,512]{1,0:T(8,128)(2,1)S(1)} %query.5, bf16[2,4,128,128]{3,2,1,0:T(8,128)(2,1)S(1)} %get-tuple-element.44.parts, bf16[2,4,128,128]{3,2,1,0:T(8,128)(2,1)S(1)} %collective-permute-done.5.other_parts, bf16[2,128,128]{2,1,0:T(8,128)(2,1)S(1)} %round.11.carry, ...), custom_call_target="tpu_custom_call" | custom-call | tf_op jit(solution)/shard_map/own/pallas_call | solution.py:336
  38.5 2.0 %latent.1 = bf16[8,160,128]{2,1,0:T(8,128)(2,1)S(1)} custom-call(f32[1024,1152]{1,0:T(8,128)S(1)} %own.1.partial, bf16[1024,512]{1,0:T(8,128)(2,1)S(1)} %query.5, bf16[2,4,128,128]{3,2,1,0:T(8,128)(2,1)S(1)} %get-tuple-element.44.parts, bf16[2,4,128,128]{3,2,1,0:T(8,128)(2,1)S(1)} %collective-permute-done.5.other_parts, ...), custom_call_target="tpu_custom_call" | custom-call | tf_op jit(solution)/shard_map/latent/pallas_call | solution.py:389
  40.5 17.3 %all_to_all.5.blocks = bf16[8,160,128]{2,1,0:T(8,128)(2,1)S(1)} all-to-all(bf16[8,160,128]{2,1,0:T(8,128)(2,1)S(1)} %latent.1), channel_id=1, replica_groups=mesh['groups'=2,'tm'=8,'space'=2] {'tm'}, dimensions={0} | all-to-all | bytes 655360 | tf_op jit(solution)/shard_map/all_to_all | solution.py:631
  57.8 0.1 collective-permute-start.11
  57.9 1.4 %interior.1 = (bf16[16,12,16,256]{3,2,1,0:T(8,128)(2,1)S(1)}, bf16[4,512,256]{2,1,0:T(8,128)(2,1)S(1)}) custom-call(bf16[8,160,128]{2,1,0:T(8,128)(2,1)S(1)} %all_to_all.5.blocks, bf16[3,3,128,256]{3,2,1,0:T(8,128)(2,1)S(1)} %copy-done.1, f32[1,256]{1,0:T(1,128)S(1)} %bitcast.2), custom_call_target="tpu_custom_call" | custom-call | tf_op jit(solution)/shard_map/interior/pallas_call | solution.py:497
  59.4 1.7 %border.1 = bf16[16,16,16,256]{3,2,1,0:T(8,128)(2,1)} custom-call(bf16[8,160,128]{2,1,0:T(8,128)(2,1)S(1)} %all_to_all.5.blocks, bf16[8,20,128]{2,1,0:T(8,128)(2,1)S(1)} %collective-permute-done.11.edge, bf16[16,12,16,256]{3,2,1,0:T(8,128)(2,1)S(1)} %get-tuple-element.55.interior, bf16[4,512,256]{2,1,0:T(8,128)(2,1)S(1)} %get-tuple-element.56.taps, ...), custom_call_target="tpu_custom_call" | custom-call | tf_op jit(solution)/shard_map/border/pallas_call | solution.py:533
  (20 shorter events, 0.2 us)
Async XLA Ops:
  6.8 4.5 %collective-permute-start = (bf16[2,5,128,128]{3,2,1,0:T(8,128)(2,1)S(1)}, bf16[2,5,128,128]{3,2,1,0:T(8,128)(2,1)S(1)}, u32[]{:S(2)}, u32[]{:S(2)}) collective-permute-start(bf16[2,5,128,128]{3,2,1,0:T(8,128)(2,1)S(1)} %get-tuple-element.33.parts.refs_2_), channel_id=1, source_target_pairs={{0,1},{1,0},{2,3},{3,2},{4,5},{5,4},{6,7},{7,6},{8,9},{9,8},{10,11... | collective-permute-start | bytes 983048 | tf_op jit(solution)/shard_map/ppermute | solution.py:605
  11.4 5.7 %collective-permute-start.1 = (bf16[5,64,128]{2,1,0:T(8,128)(2,1)S(1)}, bf16[5,64,128]{2,1,0:T(8,128)(2,1)S(1)}, u32[]{:S(2)}, u32[]{:S(2)}) collective-permute-start(bf16[5,64,128]{2,1,0:T(8,128)(2,1)S(1)} %get-tuple-element.34), channel_id=1, source_target_pairs={{0,2},{2,0},{4,6},{6,4},{8,10},{10,8},{12,14},{14,12},{1,3},{3,1},... | collective-permute-start | bytes 245768 | tf_op jit(solution)/shard_map/ppermute | solution.py:582
  14.0 1.3 %collective-permute-start.6 = (bf16[2,128,128]{2,1,0:T(8,128)(2,1)S(1)}, bf16[2,128,128]{2,1,0:T(8,128)(2,1)S(1)}, u32[]{:S(2)}, u32[]{:S(2)}) collective-permute-start(bf16[2,128,128]{2,1,0:T(8,128)(2,1)S(1)} %get-tuple-element.46), channel_id=1, source_target_pairs={{0,1},{1,0},{2,3},{3,2},{4,5},{5,4},{6,7},{7,6},{8,9},{9,8},{10,11... | collective-permute-start | bytes 196616 | tf_op jit(solution)/shard_map/ppermute | solution.py:607
  15.3 4.3 %collective-permute-start.7 = (bf16[2,128,128]{2,1,0:T(8,128)(2,1)S(1)}, bf16[2,128,128]{2,1,0:T(8,128)(2,1)S(1)}, u32[]{:S(2)}, u32[]{:S(2)}) collective-permute-start(bf16[2,128,128]{2,1,0:T(8,128)(2,1)S(1)} %get-tuple-element.47), channel_id=1, source_target_pairs={{0,2},{2,0},{4,6},{6,4},{8,10},{10,8},{12,14},{14,12},{1,3},{3,1},... | collective-permute-start | bytes 196616 | tf_op jit(solution)/shard_map/ppermute | solution.py:582
  15.6 21.7 %collective-permute-start.5 = (bf16[2,4,128,128]{3,2,1,0:T(8,128)(2,1)S(1)}, bf16[2,4,128,128]{3,2,1,0:T(8,128)(2,1)S(1)}, u32[]{:S(2)}, u32[]{:S(2)}) collective-permute-start(bf16[2,4,128,128]{3,2,1,0:T(8,128)(2,1)S(1)} %get-tuple-element.44.parts), channel_id=1, source_target_pairs={{0,1},{1,0},{2,3},{3,2},{4,5},{5,4},{6,7},{7,6},{8,9},{9,8},{10,11... | collective-permute-start | bytes 786440 | tf_op jit(solution)/shard_map/ppermute | solution.py:608
  17.1 4.8 %collective-permute-start.2 = (bf16[5,64,128]{2,1,0:T(8,128)(2,1)S(1)}, bf16[5,64,128]{2,1,0:T(8,128)(2,1)S(1)}, u32[]{:S(2)}, u32[]{:S(2)}) collective-permute-start(bf16[5,64,128]{2,1,0:T(8,128)(2,1)S(1)} %get-tuple-element.36), channel_id=1, source_target_pairs={{0,4},{2,6},{4,0},{6,2},{8,12},{10,14},{12,8},{14,10},{1,5},{3,7},... | collective-permute-start | bytes 245768 | tf_op jit(solution)/shard_map/ppermute | solution.py:582
  19.6 5.4 %collective-permute-start.8 = (bf16[2,128,128]{2,1,0:T(8,128)(2,1)S(1)}, bf16[2,128,128]{2,1,0:T(8,128)(2,1)S(1)}, u32[]{:S(2)}, u32[]{:S(2)}) collective-permute-start(bf16[2,128,128]{2,1,0:T(8,128)(2,1)S(1)} %get-tuple-element.49), channel_id=1, source_target_pairs={{0,4},{2,6},{4,0},{6,2},{8,12},{10,14},{12,8},{14,10},{1,5},{3,7},... | collective-permute-start | bytes 196616 | tf_op jit(solution)/shard_map/ppermute | solution.py:582
  22.0 7.6 %collective-permute-start.3 = (bf16[5,64,128]{2,1,0:T(8,128)(2,1)S(1)}, bf16[5,64,128]{2,1,0:T(8,128)(2,1)S(1)}, u32[]{:S(2)}, u32[]{:S(2)}) collective-permute-start(bf16[5,64,128]{2,1,0:T(8,128)(2,1)S(1)} %get-tuple-element.39), channel_id=1, source_target_pairs={{0,8},{2,10},{4,12},{6,14},{8,0},{10,2},{12,4},{14,6},{1,9},{3,11}... | collective-permute-start | bytes 245768 | tf_op jit(solution)/shard_map/ppermute | solution.py:582
  25.1 5.2 %collective-permute-start.9 = (bf16[2,128,128]{2,1,0:T(8,128)(2,1)S(1)}, bf16[2,128,128]{2,1,0:T(8,128)(2,1)S(1)}, u32[]{:S(2)}, u32[]{:S(2)}) collective-permute-start(bf16[2,128,128]{2,1,0:T(8,128)(2,1)S(1)} %get-tuple-element.52), channel_id=1, source_target_pairs={{0,8},{2,10},{4,12},{6,14},{8,0},{10,2},{12,4},{14,6},{1,9},{3,11}... | collective-permute-start | bytes 196616 | tf_op jit(solution)/shard_map/ppermute | solution.py:582
  29.6 5.0 %collective-permute-start.4 = (bf16[5,64,128]{2,1,0:T(8,128)(2,1)S(1)}, bf16[5,64,128]{2,1,0:T(8,128)(2,1)S(1)}, u32[]{:S(2)}, u32[]{:S(2)}) collective-permute-start(bf16[5,64,128]{2,1,0:T(8,128)(2,1)S(1)} %round.8.refs_4_), channel_id=1, source_target_pairs={{0,1},{1,0},{2,3},{3,2},{4,5},{5,4},{6,7},{7,6},{8,9},{9,8},{10,11... | collective-permute-start | bytes 245768 | tf_op jit(solution)/shard_map/ppermute | solution.py:624
  30.4 8.1 %collective-permute-start.10 = (bf16[2,128,128]{2,1,0:T(8,128)(2,1)S(1)}, bf16[2,128,128]{2,1,0:T(8,128)(2,1)S(1)}, u32[]{:S(2)}, u32[]{:S(2)}) collective-permute-start(bf16[2,128,128]{2,1,0:T(8,128)(2,1)S(1)} %round.11.carry), channel_id=1, source_target_pairs={{0,1},{1,0},{2,3},{3,2},{4,5},{5,4},{6,7},{7,6},{8,9},{9,8},{10,11... | collective-permute-start | bytes 196616 | tf_op jit(solution)/shard_map/ppermute | solution.py:624
  32.9 1.8 %copy-start = (bf16[1152,1152]{1,0:T(8,128)(2,1)S(1)}, bf16[1152,1152]{1,0:T(8,128)(2,1)}, u32[]{:S(2)}) copy-start(bf16[1152,1152]{1,0:T(8,128)(2,1)} %w_out.3) | copy-start | bytes 7962628
  37.3 1.2 %copy-start.2 = (bf16[1152,128]{1,0:T(8,128)(2,1)S(1)}, bf16[1152,128]{1,0:T(8,128)(2,1)}, u32[]{:S(2)}) copy-start(bf16[1152,128]{1,0:T(8,128)(2,1)} %w_latent.1) | copy-start | bytes 884740
  38.4 19.5 %copy-start.1 = (bf16[3,3,128,256]{3,2,1,0:T(8,128)(2,1)S(1)}, bf16[3,3,128,256]{3,2,1,0:T(8,128)(2,1)}, u32[]{:S(2)}) copy-start(bf16[3,3,128,256]{3,2,1,0:T(8,128)(2,1)} %weight.1) | copy-start | bytes 1769476
  38.5 19.5 %copy-start.3 = (f32[256]{0:T(256)S(1)}, f32[256]{0:T(256)}, u32[]{:S(2)}) copy-start(f32[256]{0:T(256)} %param.15) | copy-start | bytes 3076
  57.8 1.6 %collective-permute-start.11 = (bf16[8,20,128]{2,1,0:T(8,128)(2,1)S(1)}, bf16[8,20,128]{2,1,0:T(8,128)(2,1)S(1)}, u32[]{:S(2)}, u32[]{:S(2)}) collective-permute-start(bf16[8,20,128]{2,1,0:T(8,128)(2,1)S(1)} %edge.1), channel_id=1, source_target_pairs={{0,1},{1,0},{2,3},{3,2},{4,5},{5,4},{6,7},{7,6},{8,9},{9,8},{10,11... | collective-permute-start | bytes 122888 | tf_op jit(solution)/shard_map/ppermute | solution.py:669

commit v11 on v10

--- a/solution.py
+++ b/solution.py
@@ -49,9 +49,9 @@
         rest = wk_out.shape[1]
         source = pl.ds(heads * HEAD, rest)
         late = [
-            pltpu.make_async_copy(wq_hbm, wq_out, late_sem.at[0]),
             pltpu.make_async_copy(wk_hbm.at[:, source], wk_out, late_sem.at[1]),
             pltpu.make_async_copy(wv_hbm.at[:, source], wv_out, late_sem.at[2]),
+            pltpu.make_async_copy(wq_hbm, wq_out, late_sem.at[0]),
         ]
     per = video.shape[0] // frames
 
@@ -94,7 +94,7 @@
             value[h, rows, :] = kv[:, HEAD:].astype(BF16)
         return carry
 
-    lax.fori_loop(0, heads, one_head, 0)
+    lax.fori_loop(0, heads, one_head, 0, unroll=2 if heads % 2 == 0 else 1)
 
     totals = []
     for h in range(heads):
@@ -353,8 +353,9 @@
     half = 1 - lax.axis_index("space")
     attend_half(frames, half, query, parts, other_parts, carry, used, head_out)
     w = half_rows(w_out, half, head_out.shape[1])
-    for f in range(frames):
-        rows = slice(f * per, (f + 1) * per)
+    piece = per // 2
+    for i in range(2 * frames):
+        rows = slice(i * piece, (i + 1) * piece)
         summed = partial[rows, :] + matmul(head_out[rows, :], w)
         scale = lax.rsqrt(jnp.mean(summed * summed, axis=1, keepdims=True) + EPS)
         latent[rows, :] = matmul(summed.astype(BF16), w_latent[...]) * scale

time: 61.3 us -> 60.8 us (level)
  no operation moved by 1% of the time
where the time goes in v11:
time: 60.8 us; the launch traced here: 60.6 us
  Pallas kernels  23.6 us (39%)
  blocking collectives  17.3 us (28%)
  starting transfers between devices  12.6 us (21%)
  waiting for transfers between devices  6.81 us (11%)
    all_to_all x1, blocking collectives, body(): blocks = lax.all_to_all(blocks, 'tm', 0, 0, tiled=True)  17.3 us
    ppermute x6, starting transfers between devices, prefix_rounds(): got = lax.ppermute(sent, 'tm', [(i, i ^ step) for i in range(tiles)])  11.6 us
    pallas_call x1, Pallas kernels, first_states(): pl.pallas_call(functools.partial(states_kernel, frames, heads, False), ou...  6.82 us
    ppermute x6, waiting for transfers between devices, prefix_rounds(): got = lax.ppermute(sent, 'tm', [(i, i ^ step) for i in range(tiles)])  5.75 us
    pallas_call x3, Pallas kernels, query_call(): pl.pallas_call(kernel, out_shape=shape((video.shape[0], width), BF16), in...  4.1 us
    pallas_call x1, Pallas kernels, second_states(): pl.pallas_call(functools.partial(states_kernel, frames, heads, True), out...  3.57 us
    pallas_call x1, Pallas kernels, partial_call(): pl.pallas_call(kernel, out_shape=shape((tokens, d), F32), in_specs=[IN_VM...  2.64 us
    pallas_call x1, Pallas kernels, latent_call(): pl.pallas_call(functools.partial(latent_kernel, frames, columns, tiles),...  1.89 us
  transfers between devices with their start and end apart: 12, of which 6 were waited for; matrix products, arithmetic and copies ran while one was open for 0% of the time, Pallas kernels for 22%

profile of v11, /device:TPU:0, one launch (start us, length us, event | category | flops | bytes accessed | tf_op | source)
XLA Modules:
  0.0 60.6 jit_solution(15127306046187325680)
XLA Ops:
  0.0 6.8 %states.2 = (bf16[2,5,128,128]{3,2,1,0:T(8,128)(2,1)S(1)}, bf16[1024,1152]{1,0:T(8,128)(2,1)S(1)}, bf16[1152,512]{1,0:T(8,128)(2,1)S(1)}, bf16[1152,512]{1,0:T(8,128)(2,1)S(1)}, bf16[1152,1152]{1,0:T(8,128)(2,1)S(1)}) custom-call(bf16[1024,1152]{1,0:T(8,128)(2,1)} %bitcast.4, bf16[1152,1152]{1,0:T(8,128)(2,1)} %wk_hbm.1, bf16[1152,1152]{1,0:T(8,128)(2,1)} %wv_hbm.1, ...), custom_call_target="tpu_custom_call" | custom-call | tf_op jit(solution)/shard_map/states/pallas_call | solution.py:124
  6.8 0.6 collective-permute-start
  7.4 3.6 %states.3 = (bf16[2,4,128,128]{3,2,1,0:T(8,128)(2,1)S(1)}, f32[2,128,128]{2,1,0:T(8,128)S(1)}, bf16[2,128,128]{2,1,0:T(8,128)(2,1)S(1)}) custom-call(bf16[1024,1152]{1,0:T(8,128)(2,1)S(1)} %get-tuple-element.31.video.video_in, bf16[1152,512]{1,0:T(8,128)(2,1)S(1)} %get-tuple-element.42.wk_hbm, bf16[1152,512]{1,0:T(8,128)(2,1)S(1)} %get-tuple-element.43.wv_hbm), custom_call_target="tpu_custom_call" | custom-call | tf_op jit(solution)/shard_map/states/pallas_call | solution.py:153
  11.0 0.1 total.1
  11.1 2.6 %collective-permute-start.1 = (bf16[5,64,128]{2,1,0:T(8,128)(2,1)S(1)}, bf16[5,64,128]{2,1,0:T(8,128)(2,1)S(1)}, u32[]{:S(2)}, u32[]{:S(2)}) collective-permute-start(bf16[5,64,128]{2,1,0:T(8,128)(2,1)S(1)} %get-tuple-element.34), channel_id=1, source_target_pairs={{0,2},{2,0},{4,6},{6,4},{8,10},{10,8},{12,14},{14,12},{1,3},{3,1},... | collective-permute-start | bytes 245768 | tf_op jit(solution)/shard_map/ppermute | solution.py:583
  13.6 0.2 collective-permute-start.6
  13.9 1.0 %collective-permute-done.6.got = bf16[2,128,128]{2,1,0:T(8,128)(2,1)S(1)} collective-permute-done((bf16[2,128,128]{2,1,0:T(8,128)(2,1)S(1)}, bf16[2,128,128]{2,1,0:T(8,128)(2,1)S(1)}, u32[]{:S(2)}, u32[]{:S(2)}) %collective-permute-start.6) | collective-permute-done | bytes 65568 | tf_op jit(solution)/shard_map/ppermute | solution.py:608
  14.9 0.3 collective-permute-start.7
  15.2 0.1 collective-permute-start.5
  15.3 1.5 %collective-permute-done.1.got = bf16[5,64,128]{2,1,0:T(8,128)(2,1)S(1)} collective-permute-done((bf16[5,64,128]{2,1,0:T(8,128)(2,1)S(1)}, bf16[5,64,128]{2,1,0:T(8,128)(2,1)S(1)}, u32[]{:S(2)}, u32[]{:S(2)}) %collective-permute-start.1) | collective-permute-done | bytes 81952 | tf_op jit(solution)/shard_map/ppermute | solution.py:583
  16.8 1.9 %collective-permute-start.2 = (bf16[5,64,128]{2,1,0:T(8,128)(2,1)S(1)}, bf16[5,64,128]{2,1,0:T(8,128)(2,1)S(1)}, u32[]{:S(2)}, u32[]{:S(2)}) collective-permute-start(bf16[5,64,128]{2,1,0:T(8,128)(2,1)S(1)} %get-tuple-element.36), channel_id=1, source_target_pairs={{0,4},{2,6},{4,0},{6,2},{8,12},{10,14},{12,8},{14,10},{1,5},{3,7},... | collective-permute-start | bytes 245768 | tf_op jit(solution)/shard_map/ppermute | solution.py:583
  18.6 0.6 %collective-permute-done.7.got = bf16[2,128,128]{2,1,0:T(8,128)(2,1)S(1)} collective-permute-done((bf16[2,128,128]{2,1,0:T(8,128)(2,1)S(1)}, bf16[2,128,128]{2,1,0:T(8,128)(2,1)S(1)}, u32[]{:S(2)}, u32[]{:S(2)}) %collective-permute-start.7) | collective-permute-done | bytes 65568 | tf_op jit(solution)/shard_map/ppermute | solution.py:583
  19.3 1.6 %collective-permute-start.8 = (bf16[2,128,128]{2,1,0:T(8,128)(2,1)S(1)}, bf16[2,128,128]{2,1,0:T(8,128)(2,1)S(1)}, u32[]{:S(2)}, u32[]{:S(2)}) collective-permute-start(bf16[2,128,128]{2,1,0:T(8,128)(2,1)S(1)} %get-tuple-element.49), channel_id=1, source_target_pairs={{0,4},{2,6},{4,0},{6,2},{8,12},{10,14},{12,8},{14,10},{1,5},{3,7},... | collective-permute-start | bytes 196616 | tf_op jit(solution)/shard_map/ppermute | solution.py:583
  20.9 0.6 %collective-permute-done.2.got = bf16[5,64,128]{2,1,0:T(8,128)(2,1)S(1)} collective-permute-done((bf16[5,64,128]{2,1,0:T(8,128)(2,1)S(1)}, bf16[5,64,128]{2,1,0:T(8,128)(2,1)S(1)}, u32[]{:S(2)}, u32[]{:S(2)}) %collective-permute-start.2) | collective-permute-done | bytes 81952 | tf_op jit(solution)/shard_map/ppermute | solution.py:583
  21.6 3.1 %collective-permute-start.3 = (bf16[5,64,128]{2,1,0:T(8,128)(2,1)S(1)}, bf16[5,64,128]{2,1,0:T(8,128)(2,1)S(1)}, u32[]{:S(2)}, u32[]{:S(2)}) collective-permute-start(bf16[5,64,128]{2,1,0:T(8,128)(2,1)S(1)} %get-tuple-element.39), channel_id=1, source_target_pairs={{0,8},{2,10},{4,12},{6,14},{8,0},{10,2},{12,4},{14,6},{1,9},{3,11}... | collective-permute-start | bytes 245768 | tf_op jit(solution)/shard_map/ppermute | solution.py:583
  24.8 2.1 %collective-permute-start.9 = (bf16[2,128,128]{2,1,0:T(8,128)(2,1)S(1)}, bf16[2,128,128]{2,1,0:T(8,128)(2,1)S(1)}, u32[]{:S(2)}, u32[]{:S(2)}) collective-permute-start(bf16[2,128,128]{2,1,0:T(8,128)(2,1)S(1)} %get-tuple-element.52), channel_id=1, source_target_pairs={{0,8},{2,10},{4,12},{6,14},{8,0},{10,2},{12,4},{14,6},{1,9},{3,11}... | collective-permute-start | bytes 196616 | tf_op jit(solution)/shard_map/ppermute | solution.py:583
  26.9 2.3 %collective-permute-done.3.got = bf16[5,64,128]{2,1,0:T(8,128)(2,1)S(1)} collective-permute-done((bf16[5,64,128]{2,1,0:T(8,128)(2,1)S(1)}, bf16[5,64,128]{2,1,0:T(8,128)(2,1)S(1)}, u32[]{:S(2)}, u32[]{:S(2)}) %collective-permute-start.3) | collective-permute-done | bytes 81952 | tf_op jit(solution)/shard_map/ppermute | solution.py:583
  29.2 0.1 collective-permute-start.4
  29.3 0.7 %collective-permute-done.9.got = bf16[2,128,128]{2,1,0:T(8,128)(2,1)S(1)} collective-permute-done((bf16[2,128,128]{2,1,0:T(8,128)(2,1)S(1)}, bf16[2,128,128]{2,1,0:T(8,128)(2,1)S(1)}, u32[]{:S(2)}, u32[]{:S(2)}) %collective-permute-start.9) | collective-permute-done | bytes 65568 | tf_op jit(solution)/shard_map/ppermute | solution.py:583
  30.0 0.1 collective-permute-start.10
  30.1 0.9 %query.3.refs_0_ = bf16[1024,256]{1,0:T(8,128)(2,1)S(1)} custom-call(bf16[1024,1152]{1,0:T(8,128)(2,1)S(1)} %get-tuple-element.31.video.video_in, bf16[1152,1152]{1,0:T(8,128)(2,1)S(1)} %get-tuple-element.32.w), custom_call_target="tpu_custom_call" | custom-call | tf_op jit(solution)/shard_map/query/pallas_call | solution.py:217
  31.0 1.6 %query.4.refs_1_ = bf16[1024,384]{1,0:T(8,128)(2,1)S(1)} custom-call(bf16[1024,1152]{1,0:T(8,128)(2,1)S(1)} %get-tuple-element.31.video.video_in, bf16[1152,1152]{1,0:T(8,128)(2,1)S(1)} %get-tuple-element.32.w), custom_call_target="tpu_custom_call" | custom-call | tf_op jit(solution)/shard_map/query/pallas_call | solution.py:217
  32.5 0.0 copy-start
  32.5 1.7 %query.5 = bf16[1024,512]{1,0:T(8,128)(2,1)S(1)} custom-call(bf16[1024,1152]{1,0:T(8,128)(2,1)S(1)} %get-tuple-element.31.video.video_in, bf16[1152,1152]{1,0:T(8,128)(2,1)S(1)} %get-tuple-element.32.w), custom_call_target="tpu_custom_call" | custom-call | tf_op jit(solution)/shard_map/query/pallas_call | solution.py:217
  34.2 0.0 copy-done
  34.3 2.6 %partial.1 = f32[1024,1152]{1,0:T(8,128)S(1)} custom-call(bf16[1024,1152]{1,0:T(8,128)(2,1)S(1)} %get-tuple-element.31.video.video_in, bf16[1024,256]{1,0:T(8,128)(2,1)S(1)} %query.3.refs_0_, bf16[1024,384]{1,0:T(8,128)(2,1)S(1)} %query.4.refs_1_, bf16[2,5,128,128]{3,2,1,0:T(8,128)(2,1)S(1)} %get-tuple-element.33.parts.refs_2_, ...), custom_call_target="tpu_custom_call" | custom-call | tf_op jit(solution)/shard_map/partial/pallas_call | solution.py:280
  36.9 1.1 %own.1.partial = f32[1024,1152]{1,0:T(8,128)S(1)} custom-call(f32[1024,1152]{1,0:T(8,128)S(1)} %partial.1, bf16[1024,512]{1,0:T(8,128)(2,1)S(1)} %query.5, bf16[2,4,128,128]{3,2,1,0:T(8,128)(2,1)S(1)} %get-tuple-element.44.parts, bf16[2,4,128,128]{3,2,1,0:T(8,128)(2,1)S(1)} %collective-permute-done.5.other_parts, bf16[2,128,128]{2,1,0:T(8,128)(2,1)S(1)} %round.11.carry, ...), custom_call_target="tpu_custom_call" | custom-call | tf_op jit(solution)/shard_map/own/pallas_call | solution.py:336
  38.1 1.9 %latent.1 = bf16[8,160,128]{2,1,0:T(8,128)(2,1)S(1)} custom-call(f32[1024,1152]{1,0:T(8,128)S(1)} %own.1.partial, bf16[1024,512]{1,0:T(8,128)(2,1)S(1)} %query.5, bf16[2,4,128,128]{3,2,1,0:T(8,128)(2,1)S(1)} %get-tuple-element.44.parts, bf16[2,4,128,128]{3,2,1,0:T(8,128)(2,1)S(1)} %collective-permute-done.5.other_parts, ...), custom_call_target="tpu_custom_call" | custom-call | tf_op jit(solution)/shard_map/latent/pallas_call | solution.py:390
  40.0 17.3 %all_to_all.5.blocks = bf16[8,160,128]{2,1,0:T(8,128)(2,1)S(1)} all-to-all(bf16[8,160,128]{2,1,0:T(8,128)(2,1)S(1)} %latent.1), channel_id=1, replica_groups=mesh['groups'=2,'tm'=8,'space'=2] {'tm'}, dimensions={0} | all-to-all | bytes 655360 | tf_op jit(solution)/shard_map/all_to_all | solution.py:632
  57.3 0.1 collective-permute-start.11
  57.4 1.4 %interior.1 = (bf16[16,12,16,256]{3,2,1,0:T(8,128)(2,1)S(1)}, bf16[4,512,256]{2,1,0:T(8,128)(2,1)S(1)}) custom-call(bf16[8,160,128]{2,1,0:T(8,128)(2,1)S(1)} %all_to_all.5.blocks, bf16[3,3,128,256]{3,2,1,0:T(8,128)(2,1)S(1)} %copy-done.1, f32[1,256]{1,0:T(1,128)S(1)} %bitcast.2), custom_call_target="tpu_custom_call" | custom-call | tf_op jit(solution)/shard_map/interior/pallas_call | solution.py:498
  58.9 1.7 %border.1 = bf16[16,16,16,256]{3,2,1,0:T(8,128)(2,1)} custom-call(bf16[8,160,128]{2,1,0:T(8,128)(2,1)S(1)} %all_to_all.5.blocks, bf16[8,20,128]{2,1,0:T(8,128)(2,1)S(1)} %collective-permute-done.11.edge, bf16[16,12,16,256]{3,2,1,0:T(8,128)(2,1)S(1)} %get-tuple-element.55.interior, bf16[4,512,256]{2,1,0:T(8,128)(2,1)S(1)} %get-tuple-element.56.taps, ...), custom_call_target="tpu_custom_call" | custom-call | tf_op jit(solution)/shard_map/border/pallas_call | solution.py:534
  (20 shorter events, 0.2 us)
Async XLA Ops:
  6.8 4.1 %collective-permute-start = (bf16[2,5,128,128]{3,2,1,0:T(8,128)(2,1)S(1)}, bf16[2,5,128,128]{3,2,1,0:T(8,128)(2,1)S(1)}, u32[]{:S(2)}, u32[]{:S(2)}) collective-permute-start(bf16[2,5,128,128]{3,2,1,0:T(8,128)(2,1)S(1)} %get-tuple-element.33.parts.refs_2_), channel_id=1, source_target_pairs={{0,1},{1,0},{2,3},{3,2},{4,5},{5,4},{6,7},{7,6},{8,9},{9,8},{10,11... | collective-permute-start | bytes 983048 | tf_op jit(solution)/shard_map/ppermute | solution.py:606
  11.1 5.7 %collective-permute-start.1 = (bf16[5,64,128]{2,1,0:T(8,128)(2,1)S(1)}, bf16[5,64,128]{2,1,0:T(8,128)(2,1)S(1)}, u32[]{:S(2)}, u32[]{:S(2)}) collective-permute-start(bf16[5,64,128]{2,1,0:T(8,128)(2,1)S(1)} %get-tuple-element.34), channel_id=1, source_target_pairs={{0,2},{2,0},{4,6},{6,4},{8,10},{10,8},{12,14},{14,12},{1,3},{3,1},... | collective-permute-start | bytes 245768 | tf_op jit(solution)/shard_map/ppermute | solution.py:583
  13.6 1.3 %collective-permute-start.6 = (bf16[2,128,128]{2,1,0:T(8,128)(2,1)S(1)}, bf16[2,128,128]{2,1,0:T(8,128)(2,1)S(1)}, u32[]{:S(2)}, u32[]{:S(2)}) collective-permute-start(bf16[2,128,128]{2,1,0:T(8,128)(2,1)S(1)} %get-tuple-element.46), channel_id=1, source_target_pairs={{0,1},{1,0},{2,3},{3,2},{4,5},{5,4},{6,7},{7,6},{8,9},{9,8},{10,11... | collective-permute-start | bytes 196616 | tf_op jit(solution)/shard_map/ppermute | solution.py:608
  14.9 4.3 %collective-permute-start.7 = (bf16[2,128,128]{2,1,0:T(8,128)(2,1)S(1)}, bf16[2,128,128]{2,1,0:T(8,128)(2,1)S(1)}, u32[]{:S(2)}, u32[]{:S(2)}) collective-permute-start(bf16[2,128,128]{2,1,0:T(8,128)(2,1)S(1)} %get-tuple-element.47), channel_id=1, source_target_pairs={{0,2},{2,0},{4,6},{6,4},{8,10},{10,8},{12,14},{14,12},{1,3},{3,1},... | collective-permute-start | bytes 196616 | tf_op jit(solution)/shard_map/ppermute | solution.py:583
  15.2 21.7 %collective-permute-start.5 = (bf16[2,4,128,128]{3,2,1,0:T(8,128)(2,1)S(1)}, bf16[2,4,128,128]{3,2,1,0:T(8,128)(2,1)S(1)}, u32[]{:S(2)}, u32[]{:S(2)}) collective-permute-start(bf16[2,4,128,128]{3,2,1,0:T(8,128)(2,1)S(1)} %get-tuple-element.44.parts), channel_id=1, source_target_pairs={{0,1},{1,0},{2,3},{3,2},{4,5},{5,4},{6,7},{7,6},{8,9},{9,8},{10,11... | collective-permute-start | bytes 786440 | tf_op jit(solution)/shard_map/ppermute | solution.py:609
  16.8 4.8 %collective-permute-start.2 = (bf16[5,64,128]{2,1,0:T(8,128)(2,1)S(1)}, bf16[5,64,128]{2,1,0:T(8,128)(2,1)S(1)}, u32[]{:S(2)}, u32[]{:S(2)}) collective-permute-start(bf16[5,64,128]{2,1,0:T(8,128)(2,1)S(1)} %get-tuple-element.36), channel_id=1, source_target_pairs={{0,4},{2,6},{4,0},{6,2},{8,12},{10,14},{12,8},{14,10},{1,5},{3,7},... | collective-permute-start | bytes 245768 | tf_op jit(solution)/shard_map/ppermute | solution.py:583
  19.3 5.4 %collective-permute-start.8 = (bf16[2,128,128]{2,1,0:T(8,128)(2,1)S(1)}, bf16[2,128,128]{2,1,0:T(8,128)(2,1)S(1)}, u32[]{:S(2)}, u32[]{:S(2)}) collective-permute-start(bf16[2,128,128]{2,1,0:T(8,128)(2,1)S(1)} %get-tuple-element.49), channel_id=1, source_target_pairs={{0,4},{2,6},{4,0},{6,2},{8,12},{10,14},{12,8},{14,10},{1,5},{3,7},... | collective-permute-start | bytes 196616 | tf_op jit(solution)/shard_map/ppermute | solution.py:583
  21.6 7.6 %collective-permute-start.3 = (bf16[5,64,128]{2,1,0:T(8,128)(2,1)S(1)}, bf16[5,64,128]{2,1,0:T(8,128)(2,1)S(1)}, u32[]{:S(2)}, u32[]{:S(2)}) collective-permute-start(bf16[5,64,128]{2,1,0:T(8,128)(2,1)S(1)} %get-tuple-element.39), channel_id=1, source_target_pairs={{0,8},{2,10},{4,12},{6,14},{8,0},{10,2},{12,4},{14,6},{1,9},{3,11}... | collective-permute-start | bytes 245768 | tf_op jit(solution)/shard_map/ppermute | solution.py:583
  24.8 5.2 %collective-permute-start.9 = (bf16[2,128,128]{2,1,0:T(8,128)(2,1)S(1)}, bf16[2,128,128]{2,1,0:T(8,128)(2,1)S(1)}, u32[]{:S(2)}, u32[]{:S(2)}) collective-permute-start(bf16[2,128,128]{2,1,0:T(8,128)(2,1)S(1)} %get-tuple-element.52), channel_id=1, source_target_pairs={{0,8},{2,10},{4,12},{6,14},{8,0},{10,2},{12,4},{14,6},{1,9},{3,11}... | collective-permute-start | bytes 196616 | tf_op jit(solution)/shard_map/ppermute | solution.py:583
  29.2 5.0 %collective-permute-start.4 = (bf16[5,64,128]{2,1,0:T(8,128)(2,1)S(1)}, bf16[5,64,128]{2,1,0:T(8,128)(2,1)S(1)}, u32[]{:S(2)}, u32[]{:S(2)}) collective-permute-start(bf16[5,64,128]{2,1,0:T(8,128)(2,1)S(1)} %round.8.refs_4_), channel_id=1, source_target_pairs={{0,1},{1,0},{2,3},{3,2},{4,5},{5,4},{6,7},{7,6},{8,9},{9,8},{10,11... | collective-permute-start | bytes 245768 | tf_op jit(solution)/shard_map/ppermute | solution.py:625
  30.0 8.1 %collective-permute-start.10 = (bf16[2,128,128]{2,1,0:T(8,128)(2,1)S(1)}, bf16[2,128,128]{2,1,0:T(8,128)(2,1)S(1)}, u32[]{:S(2)}, u32[]{:S(2)}) collective-permute-start(bf16[2,128,128]{2,1,0:T(8,128)(2,1)S(1)} %round.11.carry), channel_id=1, source_target_pairs={{0,1},{1,0},{2,3},{3,2},{4,5},{5,4},{6,7},{7,6},{8,9},{9,8},{10,11... | collective-permute-start | bytes 196616 | tf_op jit(solution)/shard_map/ppermute | solution.py:625
  32.5 1.8 %copy-start = (bf16[1152,1152]{1,0:T(8,128)(2,1)S(1)}, bf16[1152,1152]{1,0:T(8,128)(2,1)}, u32[]{:S(2)}) copy-start(bf16[1152,1152]{1,0:T(8,128)(2,1)} %w_out.3) | copy-start | bytes 7962628
  36.9 1.2 %copy-start.2 = (bf16[1152,128]{1,0:T(8,128)(2,1)S(1)}, bf16[1152,128]{1,0:T(8,128)(2,1)}, u32[]{:S(2)}) copy-start(bf16[1152,128]{1,0:T(8,128)(2,1)} %w_latent.1) | copy-start | bytes 884740
  38.1 19.3 %copy-start.1 = (bf16[3,3,128,256]{3,2,1,0:T(8,128)(2,1)S(1)}, bf16[3,3,128,256]{3,2,1,0:T(8,128)(2,1)}, u32[]{:S(2)}) copy-start(bf16[3,3,128,256]{3,2,1,0:T(8,128)(2,1)} %weight.1) | copy-start | bytes 1769476
  38.1 19.3 %copy-start.3 = (f32[256]{0:T(256)S(1)}, f32[256]{0:T(256)}, u32[]{:S(2)}) copy-start(f32[256]{0:T(256)} %param.15) | copy-start | bytes 3076
  57.3 1.6 %collective-permute-start.11 = (bf16[8,20,128]{2,1,0:T(8,128)(2,1)S(1)}, bf16[8,20,128]{2,1,0:T(8,128)(2,1)S(1)}, u32[]{:S(2)}, u32[]{:S(2)}) collective-permute-start(bf16[8,20,128]{2,1,0:T(8,128)(2,1)S(1)} %edge.1), channel_id=1, source_target_pairs={{0,1},{1,0},{2,3},{3,2},{4,5},{5,4},{6,7},{7,6},{8,9},{9,8},{10,11... | collective-permute-start | bytes 122888 | tf_op jit(solution)/shard_map/ppermute | solution.py:670

commit v12 on v10

--- a/solution.py
+++ b/solution.py
@@ -482,13 +482,24 @@
     ]
 
 
-def interior_call(blocks, weight, bias, frames, tiles, grid_rows, own):
+def taps_call(weight):
     channels, width = weight.shape[2:]
+    return pl.pallas_call(
+        lay_taps,
+        out_shape=shape((4, 4 * channels, width), BF16),
+        in_specs=[IN_VMEM],
+        out_specs=IN_VMEM,
+        name="taps",
+        compiler_params=params(8),
+    )(weight)
+
+
+def interior_call(blocks, taps, bias, frames, tiles, grid_rows, own):
+    channels, width = blocks.shape[2], taps.shape[2]
     total = tiles * frames * own
     count = 3 if (grid_rows - 2) % 3 == 0 else 1
 
-    def kernel(blocks, weight, bias, out, taps, left, middle, right, wide):
-        lay_taps(weight, taps)
+    def kernel(blocks, taps, bias, out, left, middle, right, wide):
         lay_rows(frames, tiles, grid_rows, own, range(grid_rows), blocks, None,
                  left, middle, right)
         for i in range(0, grid_rows - 2, count):
@@ -496,16 +507,13 @@
 
     return pl.pallas_call(
         kernel,
-        out_shape=[
-            shape((tiles * frames, 2 * (grid_rows - 2), 2 * own, width), BF16),
-            shape((4, 4 * channels, width), BF16),
-        ],
+        out_shape=shape((tiles * frames, 2 * (grid_rows - 2), 2 * own, width), BF16),
         in_specs=[IN_VMEM] * 3,
-        out_specs=[IN_VMEM] * 2,
+        out_specs=IN_VMEM,
         scratch_shapes=decode_scratch(grid_rows, count, total, channels, width),
         name="interior",
         compiler_params=params(24),
-    )(blocks, weight, bias)
+    )(blocks, taps, bias)
 
 
 def border_call(blocks, edge, interior, taps, bias, frames, tiles, grid_rows, own):
@@ -624,15 +632,16 @@
         other_carry = lax.ppermute(carry, "space", SWAP)
         ready[name] = (queries, parts, other, carry, other_carry)
 
+    taps = taps_call(conv_weight)
     partial = partial_call(near, ready["a"], w_out, frames)
     chunk_b = (ready["b"][0][0],) + ready["b"][1:]
     partial = own_call(partial, chunk_b, w_out, frames)
     blocks = latent_call(partial, chunk_b, w_out, w_latent, frames, columns, tiles)
     blocks = lax.all_to_all(blocks, "tm", 0, 0, tiled=True)
-    return decode(blocks, conv_weight, conv_bias, frames, grid_rows, own, tiles)
-
-
-def decode(blocks, conv_weight, conv_bias, frames, grid_rows, own, tiles):
+    return decode(blocks, taps, conv_weight, conv_bias, frames, grid_rows, own, tiles)
+
+
+def decode(blocks, taps, conv_weight, conv_bias, frames, grid_rows, own, tiles):
     channels = conv_weight.shape[2]
     width = conv_weight.shape[3]
     group = frames * own
@@ -668,9 +677,7 @@
     )(blocks)
     beside = lax.ppermute(mine, "space", SWAP)
     bias = conv_bias.reshape(1, width)
-    interior, taps = interior_call(
-        blocks, conv_weight, bias, frames, tiles, grid_rows, own
-    )
+    interior = interior_call(blocks, taps, bias, frames, tiles, grid_rows, own)
     return border_call(blocks, beside, interior, taps, bias, frames, tiles, grid_rows, own)
 
 

time: 61.3 us -> 61.4 us (level)
    pallas_call x1 -> x2, Pallas kernels: 1.45 us -> 1.5 us  [the longest x1 1.26 us: interior_call(): pl.pallas_call(kernel, out_shape=shape((tiles * frames, 2 * (grid_rows -...]
where the time goes in v12:
time: 61.4 us; the launch traced here: 61.2 us
  Pallas kernels  24.1 us (39%)
  blocking collectives  17.3 us (28%)
  starting transfers between devices  12.6 us (21%)
  waiting for transfers between devices  6.81 us (11%)
    all_to_all x1, blocking collectives, body(): blocks = lax.all_to_all(blocks, 'tm', 0, 0, tiled=True)  17.3 us
    ppermute x6, starting transfers between devices, prefix_rounds(): got = lax.ppermute(sent, 'tm', [(i, i ^ step) for i in range(tiles)])  11.6 us
    pallas_call x1, Pallas kernels, first_states(): pl.pallas_call(functools.partial(states_kernel, frames, heads, False), ou...  6.82 us
    ppermute x6, waiting for transfers between devices, prefix_rounds(): got = lax.ppermute(sent, 'tm', [(i, i ^ step) for i in range(tiles)])  5.76 us
    pallas_call x3, Pallas kernels, query_call(): pl.pallas_call(kernel, out_shape=shape((video.shape[0], width), BF16), in...  4.1 us
    pallas_call x1, Pallas kernels, second_states(): pl.pallas_call(functools.partial(states_kernel, frames, heads, True), out...  3.92 us
    pallas_call x1, Pallas kernels, partial_call(): pl.pallas_call(kernel, out_shape=shape((tokens, d), F32), in_specs=[IN_VM...  2.64 us
    pallas_call x1, Pallas kernels, latent_call(): pl.pallas_call(functools.partial(latent_kernel, frames, columns, tiles),...  2.01 us
  transfers between devices with their start and end apart: 12, of which 6 were waited for; matrix products, arithmetic and copies ran while one was open for 0% of the time, Pallas kernels for 22%

profile of v12, /device:TPU:0, one launch (start us, length us, event | category | flops | bytes accessed | tf_op | source)
XLA Modules:
  0.0 61.2 jit_solution(4847968702612756981)
XLA Ops:
  0.0 6.8 %states.2 = (bf16[2,5,128,128]{3,2,1,0:T(8,128)(2,1)S(1)}, bf16[1024,1152]{1,0:T(8,128)(2,1)S(1)}, bf16[1152,512]{1,0:T(8,128)(2,1)S(1)}, bf16[1152,512]{1,0:T(8,128)(2,1)S(1)}, bf16[1152,1152]{1,0:T(8,128)(2,1)S(1)}) custom-call(bf16[1024,1152]{1,0:T(8,128)(2,1)} %bitcast.4, bf16[1152,1152]{1,0:T(8,128)(2,1)} %wk_hbm.1, bf16[1152,1152]{1,0:T(8,128)(2,1)} %wv_hbm.1, ...), custom_call_target="tpu_custom_call" | custom-call | tf_op jit(solution)/shard_map/states/pallas_call | solution.py:124
  6.8 0.6 collective-permute-start
  7.4 3.9 %states.3 = (bf16[2,4,128,128]{3,2,1,0:T(8,128)(2,1)S(1)}, f32[2,128,128]{2,1,0:T(8,128)S(1)}, bf16[2,128,128]{2,1,0:T(8,128)(2,1)S(1)}) custom-call(bf16[1024,1152]{1,0:T(8,128)(2,1)S(1)} %get-tuple-element.29.video.video_in, bf16[1152,512]{1,0:T(8,128)(2,1)S(1)} %get-tuple-element.40.wk_hbm, bf16[1152,512]{1,0:T(8,128)(2,1)S(1)} %get-tuple-element.41.wv_hbm), custom_call_target="tpu_custom_call" | custom-call | tf_op jit(solution)/shard_map/states/pallas_call | solution.py:153
  11.3 0.1 total.1
  11.4 2.6 %collective-permute-start.1 = (bf16[5,64,128]{2,1,0:T(8,128)(2,1)S(1)}, bf16[5,64,128]{2,1,0:T(8,128)(2,1)S(1)}, u32[]{:S(2)}, u32[]{:S(2)}) collective-permute-start(bf16[5,64,128]{2,1,0:T(8,128)(2,1)S(1)} %get-tuple-element.32), channel_id=1, source_target_pairs={{0,2},{2,0},{4,6},{6,4},{8,10},{10,8},{12,14},{14,12},{1,3},{3,1},... | collective-permute-start | bytes 245768 | tf_op jit(solution)/shard_map/ppermute | solution.py:590
  14.0 0.2 collective-permute-start.6
  14.2 1.0 %collective-permute-done.6.got = bf16[2,128,128]{2,1,0:T(8,128)(2,1)S(1)} collective-permute-done((bf16[2,128,128]{2,1,0:T(8,128)(2,1)S(1)}, bf16[2,128,128]{2,1,0:T(8,128)(2,1)S(1)}, u32[]{:S(2)}, u32[]{:S(2)}) %collective-permute-start.6) | collective-permute-done | bytes 65568 | tf_op jit(solution)/shard_map/ppermute | solution.py:615
  15.3 0.3 collective-permute-start.7
  15.6 0.1 collective-permute-start.5
  15.6 1.5 %collective-permute-done.1.got = bf16[5,64,128]{2,1,0:T(8,128)(2,1)S(1)} collective-permute-done((bf16[5,64,128]{2,1,0:T(8,128)(2,1)S(1)}, bf16[5,64,128]{2,1,0:T(8,128)(2,1)S(1)}, u32[]{:S(2)}, u32[]{:S(2)}) %collective-permute-start.1) | collective-permute-done | bytes 81952 | tf_op jit(solution)/shard_map/ppermute | solution.py:590
  17.1 1.9 %collective-permute-start.2 = (bf16[5,64,128]{2,1,0:T(8,128)(2,1)S(1)}, bf16[5,64,128]{2,1,0:T(8,128)(2,1)S(1)}, u32[]{:S(2)}, u32[]{:S(2)}) collective-permute-start(bf16[5,64,128]{2,1,0:T(8,128)(2,1)S(1)} %get-tuple-element.34), channel_id=1, source_target_pairs={{0,4},{2,6},{4,0},{6,2},{8,12},{10,14},{12,8},{14,10},{1,5},{3,7},... | collective-permute-start | bytes 245768 | tf_op jit(solution)/shard_map/ppermute | solution.py:590
  19.0 0.6 collective-permute-done.7.got
  19.6 1.6 %collective-permute-start.8 = (bf16[2,128,128]{2,1,0:T(8,128)(2,1)S(1)}, bf16[2,128,128]{2,1,0:T(8,128)(2,1)S(1)}, u32[]{:S(2)}, u32[]{:S(2)}) collective-permute-start(bf16[2,128,128]{2,1,0:T(8,128)(2,1)S(1)} %get-tuple-element.47), channel_id=1, source_target_pairs={{0,4},{2,6},{4,0},{6,2},{8,12},{10,14},{12,8},{14,10},{1,5},{3,7},... | collective-permute-start | bytes 196616 | tf_op jit(solution)/shard_map/ppermute | solution.py:590
  21.3 0.6 %collective-permute-done.2.got = bf16[5,64,128]{2,1,0:T(8,128)(2,1)S(1)} collective-permute-done((bf16[5,64,128]{2,1,0:T(8,128)(2,1)S(1)}, bf16[5,64,128]{2,1,0:T(8,128)(2,1)S(1)}, u32[]{:S(2)}, u32[]{:S(2)}) %collective-permute-start.2) | collective-permute-done | bytes 81952 | tf_op jit(solution)/shard_map/ppermute | solution.py:590
  22.0 3.1 %collective-permute-start.3 = (bf16[5,64,128]{2,1,0:T(8,128)(2,1)S(1)}, bf16[5,64,128]{2,1,0:T(8,128)(2,1)S(1)}, u32[]{:S(2)}, u32[]{:S(2)}) collective-permute-start(bf16[5,64,128]{2,1,0:T(8,128)(2,1)S(1)} %get-tuple-element.37), channel_id=1, source_target_pairs={{0,8},{2,10},{4,12},{6,14},{8,0},{10,2},{12,4},{14,6},{1,9},{3,11}... | collective-permute-start | bytes 245768 | tf_op jit(solution)/shard_map/ppermute | solution.py:590
  25.1 2.1 %collective-permute-start.9 = (bf16[2,128,128]{2,1,0:T(8,128)(2,1)S(1)}, bf16[2,128,128]{2,1,0:T(8,128)(2,1)S(1)}, u32[]{:S(2)}, u32[]{:S(2)}) collective-permute-start(bf16[2,128,128]{2,1,0:T(8,128)(2,1)S(1)} %get-tuple-element.50), channel_id=1, source_target_pairs={{0,8},{2,10},{4,12},{6,14},{8,0},{10,2},{12,4},{14,6},{1,9},{3,11}... | collective-permute-start | bytes 196616 | tf_op jit(solution)/shard_map/ppermute | solution.py:590
  27.2 2.3 %collective-permute-done.3.got = bf16[5,64,128]{2,1,0:T(8,128)(2,1)S(1)} collective-permute-done((bf16[5,64,128]{2,1,0:T(8,128)(2,1)S(1)}, bf16[5,64,128]{2,1,0:T(8,128)(2,1)S(1)}, u32[]{:S(2)}, u32[]{:S(2)}) %collective-permute-start.3) | collective-permute-done | bytes 81952 | tf_op jit(solution)/shard_map/ppermute | solution.py:590
  29.6 0.1 collective-permute-start.4
  29.6 0.7 %collective-permute-done.9.got = bf16[2,128,128]{2,1,0:T(8,128)(2,1)S(1)} collective-permute-done((bf16[2,128,128]{2,1,0:T(8,128)(2,1)S(1)}, bf16[2,128,128]{2,1,0:T(8,128)(2,1)S(1)}, u32[]{:S(2)}, u32[]{:S(2)}) %collective-permute-start.9) | collective-permute-done | bytes 65568 | tf_op jit(solution)/shard_map/ppermute | solution.py:590
  30.4 0.1 collective-permute-start.10
  30.5 0.9 %query.3.refs_0_ = bf16[1024,256]{1,0:T(8,128)(2,1)S(1)} custom-call(bf16[1024,1152]{1,0:T(8,128)(2,1)S(1)} %get-tuple-element.29.video.video_in, bf16[1152,1152]{1,0:T(8,128)(2,1)S(1)} %get-tuple-element.30.w), custom_call_target="tpu_custom_call" | custom-call | tf_op jit(solution)/shard_map/query/pallas_call | solution.py:217
  31.3 1.6 %query.4.refs_1_ = bf16[1024,384]{1,0:T(8,128)(2,1)S(1)} custom-call(bf16[1024,1152]{1,0:T(8,128)(2,1)S(1)} %get-tuple-element.29.video.video_in, bf16[1152,1152]{1,0:T(8,128)(2,1)S(1)} %get-tuple-element.30.w), custom_call_target="tpu_custom_call" | custom-call | tf_op jit(solution)/shard_map/query/pallas_call | solution.py:217
  32.9 1.7 %query.5 = bf16[1024,512]{1,0:T(8,128)(2,1)S(1)} custom-call(bf16[1024,1152]{1,0:T(8,128)(2,1)S(1)} %get-tuple-element.29.video.video_in, bf16[1152,1152]{1,0:T(8,128)(2,1)S(1)} %get-tuple-element.30.w), custom_call_target="tpu_custom_call" | custom-call | tf_op jit(solution)/shard_map/query/pallas_call | solution.py:217
  34.6 0.0 copy-done
  34.6 2.6 %partial.1 = f32[1024,1152]{1,0:T(8,128)S(1)} custom-call(bf16[1024,1152]{1,0:T(8,128)(2,1)S(1)} %get-tuple-element.29.video.video_in, bf16[1024,256]{1,0:T(8,128)(2,1)S(1)} %query.3.refs_0_, bf16[1024,384]{1,0:T(8,128)(2,1)S(1)} %query.4.refs_1_, bf16[2,5,128,128]{3,2,1,0:T(8,128)(2,1)S(1)} %get-tuple-element.31.parts.refs_2_, ...), custom_call_target="tpu_custom_call" | custom-call | tf_op jit(solution)/shard_map/partial/pallas_call | solution.py:280
  37.3 1.1 %own.1.partial = f32[1024,1152]{1,0:T(8,128)S(1)} custom-call(f32[1024,1152]{1,0:T(8,128)S(1)} %partial.1, bf16[1024,512]{1,0:T(8,128)(2,1)S(1)} %query.5, bf16[2,4,128,128]{3,2,1,0:T(8,128)(2,1)S(1)} %get-tuple-element.42.parts, bf16[2,4,128,128]{3,2,1,0:T(8,128)(2,1)S(1)} %collective-permute-done.5.other_parts, bf16[2,128,128]{2,1,0:T(8,128)(2,1)S(1)} %round.11.carry, ...), custom_call_target="tpu_custom_call" | custom-call | tf_op jit(solution)/shard_map/own/pallas_call | solution.py:336
  38.5 2.0 %latent.1 = bf16[8,160,128]{2,1,0:T(8,128)(2,1)S(1)} custom-call(f32[1024,1152]{1,0:T(8,128)S(1)} %own.1.partial, bf16[1024,512]{1,0:T(8,128)(2,1)S(1)} %query.5, bf16[2,4,128,128]{3,2,1,0:T(8,128)(2,1)S(1)} %get-tuple-element.42.parts, bf16[2,4,128,128]{3,2,1,0:T(8,128)(2,1)S(1)} %collective-permute-done.5.other_parts, ...), custom_call_target="tpu_custom_call" | custom-call | tf_op jit(solution)/shard_map/latent/pallas_call | solution.py:389
  40.5 17.3 %all_to_all.5.blocks = bf16[8,160,128]{2,1,0:T(8,128)(2,1)S(1)} all-to-all(bf16[8,160,128]{2,1,0:T(8,128)(2,1)S(1)} %latent.1), channel_id=1, replica_groups=mesh['groups'=2,'tm'=8,'space'=2] {'tm'}, dimensions={0} | all-to-all | bytes 655360 | tf_op jit(solution)/shard_map/all_to_all | solution.py:640
  57.8 0.1 collective-permute-start.11
  57.9 0.2 taps.1
  58.2 1.3 %interior.1 = bf16[16,12,16,256]{3,2,1,0:T(8,128)(2,1)S(1)} custom-call(bf16[8,160,128]{2,1,0:T(8,128)(2,1)S(1)} %all_to_all.5.blocks, bf16[4,512,256]{2,1,0:T(8,128)(2,1)S(1)} %taps.1, f32[1,256]{1,0:T(1,128)S(1)} %bitcast.2), custom_call_target="tpu_custom_call" | custom-call | tf_op jit(solution)/shard_map/interior/pallas_call | solution.py:508
  59.5 1.7 %border.1 = bf16[16,16,16,256]{3,2,1,0:T(8,128)(2,1)} custom-call(bf16[8,160,128]{2,1,0:T(8,128)(2,1)S(1)} %all_to_all.5.blocks, bf16[8,20,128]{2,1,0:T(8,128)(2,1)S(1)} %collective-permute-done.11.edge, bf16[16,12,16,256]{3,2,1,0:T(8,128)(2,1)S(1)} %interior.1, bf16[4,512,256]{2,1,0:T(8,128)(2,1)S(1)} %taps.1, f32[1,256]{1,0:T(1,128)S(1)} %bitcast.3), custom_call_target="tpu_custom_call" | custom-call | tf_op jit(solution)/shard_map/border/pallas_call | solution.py:541
  (21 shorter events, 0.2 us)
Async XLA Ops:
  6.8 4.5 %collective-permute-start = (bf16[2,5,128,128]{3,2,1,0:T(8,128)(2,1)S(1)}, bf16[2,5,128,128]{3,2,1,0:T(8,128)(2,1)S(1)}, u32[]{:S(2)}, u32[]{:S(2)}) collective-permute-start(bf16[2,5,128,128]{3,2,1,0:T(8,128)(2,1)S(1)} %get-tuple-element.31.parts.refs_2_), channel_id=1, source_target_pairs={{0,1},{1,0},{2,3},{3,2},{4,5},{5,4},{6,7},{7,6},{8,9},{9,8},{10,11... | collective-permute-start | bytes 983048 | tf_op jit(solution)/shard_map/ppermute | solution.py:613
  11.4 5.7 %collective-permute-start.1 = (bf16[5,64,128]{2,1,0:T(8,128)(2,1)S(1)}, bf16[5,64,128]{2,1,0:T(8,128)(2,1)S(1)}, u32[]{:S(2)}, u32[]{:S(2)}) collective-permute-start(bf16[5,64,128]{2,1,0:T(8,128)(2,1)S(1)} %get-tuple-element.32), channel_id=1, source_target_pairs={{0,2},{2,0},{4,6},{6,4},{8,10},{10,8},{12,14},{14,12},{1,3},{3,1},... | collective-permute-start | bytes 245768 | tf_op jit(solution)/shard_map/ppermute | solution.py:590
  14.0 1.3 %collective-permute-start.6 = (bf16[2,128,128]{2,1,0:T(8,128)(2,1)S(1)}, bf16[2,128,128]{2,1,0:T(8,128)(2,1)S(1)}, u32[]{:S(2)}, u32[]{:S(2)}) collective-permute-start(bf16[2,128,128]{2,1,0:T(8,128)(2,1)S(1)} %get-tuple-element.44), channel_id=1, source_target_pairs={{0,1},{1,0},{2,3},{3,2},{4,5},{5,4},{6,7},{7,6},{8,9},{9,8},{10,11... | collective-permute-start | bytes 196616 | tf_op jit(solution)/shard_map/ppermute | solution.py:615
  15.3 4.3 %collective-permute-start.7 = (bf16[2,128,128]{2,1,0:T(8,128)(2,1)S(1)}, bf16[2,128,128]{2,1,0:T(8,128)(2,1)S(1)}, u32[]{:S(2)}, u32[]{:S(2)}) collective-permute-start(bf16[2,128,128]{2,1,0:T(8,128)(2,1)S(1)} %get-tuple-element.45), channel_id=1, source_target_pairs={{0,2},{2,0},{4,6},{6,4},{8,10},{10,8},{12,14},{14,12},{1,3},{3,1},... | collective-permute-start | bytes 196616 | tf_op jit(solution)/shard_map/ppermute | solution.py:590
  15.6 21.7 %collective-permute-start.5 = (bf16[2,4,128,128]{3,2,1,0:T(8,128)(2,1)S(1)}, bf16[2,4,128,128]{3,2,1,0:T(8,128)(2,1)S(1)}, u32[]{:S(2)}, u32[]{:S(2)}) collective-permute-start(bf16[2,4,128,128]{3,2,1,0:T(8,128)(2,1)S(1)} %get-tuple-element.42.parts), channel_id=1, source_target_pairs={{0,1},{1,0},{2,3},{3,2},{4,5},{5,4},{6,7},{7,6},{8,9},{9,8},{10,11... | collective-permute-start | bytes 786440 | tf_op jit(solution)/shard_map/ppermute | solution.py:616
  17.1 4.8 %collective-permute-start.2 = (bf16[5,64,128]{2,1,0:T(8,128)(2,1)S(1)}, bf16[5,64,128]{2,1,0:T(8,128)(2,1)S(1)}, u32[]{:S(2)}, u32[]{:S(2)}) collective-permute-start(bf16[5,64,128]{2,1,0:T(8,128)(2,1)S(1)} %get-tuple-element.34), channel_id=1, source_target_pairs={{0,4},{2,6},{4,0},{6,2},{8,12},{10,14},{12,8},{14,10},{1,5},{3,7},... | collective-permute-start | bytes 245768 | tf_op jit(solution)/shard_map/ppermute | solution.py:590
  19.6 5.4 %collective-permute-start.8 = (bf16[2,128,128]{2,1,0:T(8,128)(2,1)S(1)}, bf16[2,128,128]{2,1,0:T(8,128)(2,1)S(1)}, u32[]{:S(2)}, u32[]{:S(2)}) collective-permute-start(bf16[2,128,128]{2,1,0:T(8,128)(2,1)S(1)} %get-tuple-element.47), channel_id=1, source_target_pairs={{0,4},{2,6},{4,0},{6,2},{8,12},{10,14},{12,8},{14,10},{1,5},{3,7},... | collective-permute-start | bytes 196616 | tf_op jit(solution)/shard_map/ppermute | solution.py:590
  22.0 7.6 %collective-permute-start.3 = (bf16[5,64,128]{2,1,0:T(8,128)(2,1)S(1)}, bf16[5,64,128]{2,1,0:T(8,128)(2,1)S(1)}, u32[]{:S(2)}, u32[]{:S(2)}) collective-permute-start(bf16[5,64,128]{2,1,0:T(8,128)(2,1)S(1)} %get-tuple-element.37), channel_id=1, source_target_pairs={{0,8},{2,10},{4,12},{6,14},{8,0},{10,2},{12,4},{14,6},{1,9},{3,11}... | collective-permute-start | bytes 245768 | tf_op jit(solution)/shard_map/ppermute | solution.py:590
  25.1 5.2 %collective-permute-start.9 = (bf16[2,128,128]{2,1,0:T(8,128)(2,1)S(1)}, bf16[2,128,128]{2,1,0:T(8,128)(2,1)S(1)}, u32[]{:S(2)}, u32[]{:S(2)}) collective-permute-start(bf16[2,128,128]{2,1,0:T(8,128)(2,1)S(1)} %get-tuple-element.50), channel_id=1, source_target_pairs={{0,8},{2,10},{4,12},{6,14},{8,0},{10,2},{12,4},{14,6},{1,9},{3,11}... | collective-permute-start | bytes 196616 | tf_op jit(solution)/shard_map/ppermute | solution.py:590
  29.6 5.0 %collective-permute-start.4 = (bf16[5,64,128]{2,1,0:T(8,128)(2,1)S(1)}, bf16[5,64,128]{2,1,0:T(8,128)(2,1)S(1)}, u32[]{:S(2)}, u32[]{:S(2)}) collective-permute-start(bf16[5,64,128]{2,1,0:T(8,128)(2,1)S(1)} %round.8.refs_4_), channel_id=1, source_target_pairs={{0,1},{1,0},{2,3},{3,2},{4,5},{5,4},{6,7},{7,6},{8,9},{9,8},{10,11... | collective-permute-start | bytes 245768 | tf_op jit(solution)/shard_map/ppermute | solution.py:632
  30.4 8.1 %collective-permute-start.10 = (bf16[2,128,128]{2,1,0:T(8,128)(2,1)S(1)}, bf16[2,128,128]{2,1,0:T(8,128)(2,1)S(1)}, u32[]{:S(2)}, u32[]{:S(2)}) collective-permute-start(bf16[2,128,128]{2,1,0:T(8,128)(2,1)S(1)} %round.11.carry), channel_id=1, source_target_pairs={{0,1},{1,0},{2,3},{3,2},{4,5},{5,4},{6,7},{7,6},{8,9},{9,8},{10,11... | collective-permute-start | bytes 196616 | tf_op jit(solution)/shard_map/ppermute | solution.py:632
  32.9 1.8 %copy-start = (bf16[1152,1152]{1,0:T(8,128)(2,1)S(1)}, bf16[1152,1152]{1,0:T(8,128)(2,1)}, u32[]{:S(2)}) copy-start(bf16[1152,1152]{1,0:T(8,128)(2,1)} %w_out.3) | copy-start | bytes 7962628
  37.3 1.2 %copy-start.2 = (bf16[1152,128]{1,0:T(8,128)(2,1)S(1)}, bf16[1152,128]{1,0:T(8,128)(2,1)}, u32[]{:S(2)}) copy-start(bf16[1152,128]{1,0:T(8,128)(2,1)} %w_latent.1) | copy-start | bytes 884740
  38.4 19.5 %copy-start.1 = (bf16[3,3,128,256]{3,2,1,0:T(8,128)(2,1)S(1)}, bf16[3,3,128,256]{3,2,1,0:T(8,128)(2,1)}, u32[]{:S(2)}) copy-start(bf16[3,3,128,256]{3,2,1,0:T(8,128)(2,1)} %weight.1) | copy-start | bytes 1769476
  40.5 17.7 %copy-start.3 = (f32[256]{0:T(256)S(1)}, f32[256]{0:T(256)}, u32[]{:S(2)}) copy-start(f32[256]{0:T(256)} %param.15) | copy-start | bytes 3076
  57.8 1.6 %collective-permute-start.11 = (bf16[8,20,128]{2,1,0:T(8,128)(2,1)S(1)}, bf16[8,20,128]{2,1,0:T(8,128)(2,1)S(1)}, u32[]{:S(2)}, u32[]{:S(2)}) collective-permute-start(bf16[8,20,128]{2,1,0:T(8,128)(2,1)S(1)} %edge.1), channel_id=1, source_target_pairs={{0,1},{1,0},{2,3},{3,2},{4,5},{5,4},{6,7},{7,6},{8,9},{9,8},{10,11... | collective-permute-start | bytes 122888 | tf_op jit(solution)/shard_map/ppermute | solution.py:678
